TPU v7x, 32 devices: a whole 2x2x4 slice. The times are simulated.
32 devices in a mesh: dp: 2 (over x), space: 16 (over z, y, core).
Axes of the slice: x: 2, y: 2, z: 4, core: 2. Of those that a mesh axis runs over, the one named last changes fastest.
Arguments:
- tiles_in: bfloat16 [2, 64, 8, 8, 384], P('dp', 'space'), may hold values from -6 to 6
- upstream: bfloat16 [2, 64, 8, 8, 384], P('dp', 'space'), may hold values from -1.1953125 to 1.1953125
- pool_weight: float32 [2, 64], P('dp', 'space'), may hold values from 0.25 to 4
- slide_cot: float32 [2, 384], P('dp'), may hold values from -6 to 6
- adjacency: int32 [2, 64, 8], P('dp', 'space'), may hold values from -1 to 63, as said below
- counts: int32 [2, 16], P('dp', 'space'), may hold values from 1 to 4, as said below
- kernel: float32 [7, 7, 384], replicated, may hold values from -0.875 to 0.875
- norm_gain: float32 [384], replicated, may hold values from 0.5 to 1.5
- w_in: bfloat16 [384, 1536], replicated, may hold values from -0.3125 to 0.3125
- w_out: bfloat16 [1536, 384], replicated, may hold values from -0.15625 to 0.15625
- layer_scale: float32 [384], replicated, may hold values from 0.1 to 1
Outputs:
- embedding: float32 [2, 384], P('dp')
- grad_tiles: bfloat16 [2, 64, 8, 8, 384], P('dp', 'space')
- grad_w_out: float32 [1536, 384], P('space')
- grad_kernel: float32 [7, 7, 384], replicated
Inputs may be any that keep to these rules, and one draw needn't show every extreme that they name: Slots form blocks of 4; block k of a slide is one row of tiles, its live tiles in its first counts slots in column order; the last block of every slide is full, and often another one too. `adjacency`: tiles lie on a grid: entries 0, 4, 5 name live slots of the block before the tile's own, entries 1, 6, 7 of the block after it, entries 2 and 3 of its own block. The lists are mutual (b is the north neighbour of a exactly when a is the south neighbour of b, and likewise for the other directions). Slots that are not live have no neighbours and are named by none.
All inputs are finite; a program needn't handle non-finite values.
Results may differ from a plain program's by a relative error of at most 0.011.
Values may be sent and summed in bfloat16 or wider, within the bound.
No kernel may reach another device: no remote copies, remote signals or barrier semaphores. Data moves between devices by JAX's collectives and lax.ppermute only.
A program may use at most 64 MiB of HBM per device.

v0:
```python
import functools

import jax
import jax.numpy as jnp
from jax import lax
from jax.experimental import pallas as pl
from jax.experimental.pallas import tpu as pltpu
from jax.sharding import PartitionSpec as P

sqrt_half = 0.7071067811865476
inv_root_two_pi = 0.3989422804014327
f32 = jnp.float32
bf16 = jnp.bfloat16
LANES = 128
SEPARATE = 2

VMEM = pl.BlockSpec(memory_space=pltpu.VMEM)
SMEM = pl.BlockSpec(memory_space=pltpu.SMEM)
HBM = pl.BlockSpec(memory_space=pltpu.HBM)
STATE = 56
TAPS = 49
EDGE_COST = 5_000_000_000


def call(body, out_shape, in_specs, args, flops=0, scratch=(), limit=16 << 20, out_specs=None):
    outs = out_shape if isinstance(out_shape, (list, tuple)) else [out_shape]
    total = sum(a.size * a.dtype.itemsize for a in list(args) + list(outs))
    return pl.pallas_call(
        body,
        out_shape=out_shape,
        in_specs=in_specs,
        out_specs=out_specs or jax.tree.map(lambda _: VMEM, out_shape),
        scratch_shapes=scratch,
        compiler_params=pltpu.CompilerParams(vmem_limit_bytes=limit),
        cost_estimate=pl.CostEstimate(flops=flops, bytes_accessed=total, transcendentals=0),
    )(*args)


def struct(shape, dtype=f32):
    return jax.ShapeDtypeStruct(shape, dtype)


def passed_along(value, axis, steps):
    count = lax.axis_size(axis)
    leading, last = (max(0, -steps), min(count, count - steps))
    return lax.ppermute(value, axis, [(source, source + steps) for source in range(leading, last)])


def swapped(value, axis, bit):
    count = lax.axis_size(axis)
    return lax.ppermute(value, axis, [(source, source ^ bit) for source in range(count)])


def valid(entry):
    return jnp.where(entry >= 0, 1.0, 0.0).astype(f32)


def local(entry, capacity):
    return lax.rem(jnp.maximum(entry, 0), capacity)


def place(pad_ref, tile, row, part, value, parts):
    for lane in range(parts):
        pad_ref[lane, tile, row, pl.ds(part * 8, 8), :] = value[:, lane * LANES : (lane + 1) * LANES]


def fill_middle(pad_ref, own_at, adj_ref, capacity, first_row, parts):
    for tile in range(capacity):
        west, east = adj_ref[tile, 2], adj_ref[tile, 3]
        for row in range(8):
            place(pad_ref, tile, first_row + row, 0, own_at(local(west, capacity), row) * valid(west), parts)
            place(pad_ref, tile, first_row + row, 1, own_at(tile, row), parts)
            place(pad_ref, tile, first_row + row, 2, own_at(local(east, capacity), row) * valid(east), parts)


def fill_edge(pad_ref, edge_ref, adj_ref, capacity, entries, first_row, parts):
    for tile in range(capacity):
        for part, entry in enumerate(entries):
            wanted = adj_ref[tile, entry]
            index, keep = local(wanted, capacity), valid(wanted)
            for row in range(3):
                value = edge_ref[index, row].astype(f32) * keep
                place(pad_ref, tile, first_row + row, part, value, parts)


UPPER, LOWER = (4, 0, 5), (6, 1, 7)


def convolve(pads, tap_row, finish, capacity, parts):
    for lane in range(parts):

        def one_tile(tile, _):
            sums = [None] * 8
            for col in range(7):
                taps = [tap_row(row, col, lane) for row in range(7)]
                for ref, rows, base in pads:
                    for held in range(rows):
                        window = ref[lane, tile, held, pl.ds(5 + col, 8), :]
                        for out in range(8):
                            tap = held + base - out
                            if 0 <= tap < 7:
                                term = window * taps[tap]
                                sums[out] = term if sums[out] is None else sums[out] + term
            finish(tile, lane, sums)
            return 0

        lax.fori_loop(0, capacity, one_tile, 0)


def lanes(lane):
    return slice(lane * LANES, (lane + 1) * LANES)


def edge_kernel(tiles_ref, north_ref, south_ref):
    north_ref[...] = tiles_ref[:, 5:8]
    south_ref[...] = tiles_ref[:, 0:3]


def early_kernel(
    adj_ref, counts_ref, pool_ref, cot_ref, scale_ref, kern_ref, tiles_ref, up_ref, w_out_ref,
    pad_ref, conv_ref, mixed_ref, act_grad_ref, own_sum_ref,
):
    capacity, parts = tiles_ref.shape[0], tiles_ref.shape[3] // LANES
    pixels = 64
    channels = tiles_ref.shape[3]
    fill_middle(pad_ref, lambda t, r: tiles_ref[t, r].astype(f32), adj_ref, capacity, 0, parts)
    own_sum = jnp.zeros((1, channels), f32)
    scale = scale_ref[...].reshape(1, channels)
    for tile in range(capacity):
        live = jnp.where(tile < counts_ref[0, 0], 1.0, 0.0).astype(f32)
        pool = pool_ref[0, tile]
        rows = slice(tile * pixels, (tile + 1) * pixels)
        out_grad = live * (up_ref[rows, :].astype(f32) + pool * cot_ref[...] * 0.125)
        mixed_ref[rows, 0:channels] = (out_grad * scale).astype(bf16)
        column = lax.broadcasted_iota(jnp.int32, (pixels, LANES), 1)
        mixed_ref[rows, channels:] = jnp.where(column == tile, 1.0, 0.0).astype(bf16)
        own = tiles_ref[tile].astype(f32)
        own_sum += live * pool * jnp.sum(own.reshape(pixels, channels), axis=0, keepdims=True)
    own_sum_ref[...] = own_sum
    act_grad_ref[...] = lax.dot_general(
        mixed_ref[:, 0:channels], w_out_ref[...], (((1,), (1,)), ((), ())), preferred_element_type=f32
    )

    def finish(tile, lane, sums):
        for row in range(8):
            conv_ref[pl.ds(tile * pixels + row * 8, 8), lanes(lane)] = sums[row]

    convolve(
        [(pad_ref, 8, 3)],
        lambda row, col, lane: kern_ref[row, col : col + 1, lanes(lane)],
        finish, capacity, parts,
    )


def split_pieces(value_ref, rows, place, stage, keep_ref, send_ref):
    side = lax.rem(lax.div(place, 1 << stage), 2)
    for pair in range(value_ref.shape[0] // (2 * rows)):
        here = pl.ds(pair * rows, rows)
        mine = pl.ds(pl.multiple_of((2 * pair + side) * rows, 8), rows)
        other = pl.ds(pl.multiple_of((2 * pair + 1 - side) * rows, 8), rows)
        keep_ref[here, :] = value_ref[mine, :]
        send_ref[here, :] = value_ref[other, :].astype(bf16)


def forward_kernel(
    rows, adj_ref, place_ref, north_ref, south_ref, conv_ref, kern_ref, gain_ref, w_in_ref, mixed_ref, act_grad_ref,
    edge_ref, normed_ref, inv_ref, pre_grad_ref, keep_ref, send_ref, pooled_ref, whole_ref, weight_ref,
):
    capacity, parts = adj_ref.shape[0], conv_ref.shape[1] // LANES
    channels = conv_ref.shape[1]
    pixels = 64
    fill_edge(edge_ref, north_ref, adj_ref, capacity, UPPER, 0, parts)
    fill_edge(edge_ref, south_ref, adj_ref, capacity, LOWER, 3, parts)

    def finish(tile, lane, sums):
        for row in range(8):
            at = pl.ds(tile * pixels + row * 8, 8)
            total = conv_ref[at, lanes(lane)]
            if sums[row] is not None:
                total = total + sums[row]
            whole_ref[at, lanes(lane)] = total

    convolve(
        [(edge_ref.at[:, :, 0:3], 3, 0), (edge_ref.at[:, :, 3:6], 3, 11)],
        lambda row, col, lane: kern_ref[row, col : col + 1, lanes(lane)],
        finish, capacity, parts,
    )
    conv = whole_ref[...]
    centred = conv - jnp.mean(conv, axis=-1, keepdims=True)
    inv_std = lax.rsqrt(jnp.mean(centred * centred, axis=-1, keepdims=True) + 1e-06)
    normed = centred * inv_std
    normed_ref[...] = normed
    inv_ref[...] = inv_std
    lifted = (normed * gain_ref[...].reshape(1, channels)).astype(bf16)
    hidden = w_in_ref.shape[1]
    chunk = hidden // 4 if hidden % 512 == 0 else hidden
    for first in range(0, hidden, chunk):
        at = slice(first, first + chunk)
        pre = jnp.dot(lifted, w_in_ref[:, at], preferred_element_type=f32)
        cdf = 0.5 * (1.0 + lax.erf(pre * sqrt_half))
        activated = (pre * cdf).astype(bf16)
        density = jnp.exp(-0.5 * pre * pre) * inv_root_two_pi
        pre_grad_ref[:, at] = (act_grad_ref[:, at] * (cdf + pre * density)).astype(bf16)
        both = lax.dot_general(
            activated, mixed_ref[...], (((0,), (0,)), ((), ())), preferred_element_type=f32
        )
        weight_ref[at, :] = both[:, 0:channels]
        pooled_ref[at, :] = both[:, channels:]
    split_pieces(weight_ref, rows, place_ref[0, 0], 0, keep_ref, send_ref)


def back_kernel(
    counts_ref, pool_ref, pre_grad_ref, w_in_ref, normed_ref, inv_ref, gain_ref, pooled_ref, w_out_ref,
    scale_ref, own_sum_ref, grad_ref, north_ref, south_ref, emb_ref,
):
    channels = normed_ref.shape[1]
    capacity = north_ref.shape[0]
    lift = lax.dot_general(
        pre_grad_ref[...], w_in_ref[...], (((1,), (1,)), ((), ())), preferred_element_type=f32
    )
    grad_normed = lift * gain_ref[...].reshape(1, channels)
    normed = normed_ref[...]
    grad = inv_ref[...] * (
        grad_normed
        - jnp.mean(grad_normed, axis=-1, keepdims=True)
        - normed * jnp.mean(grad_normed * normed, axis=-1, keepdims=True)
    )
    grad_ref[...] = grad
    shaped = grad.reshape(capacity, 8, 8, channels)
    north_ref[...] = shaped[:, 5:8].astype(bf16)
    south_ref[...] = shaped[:, 0:3].astype(bf16)
    column = lax.broadcasted_iota(jnp.int32, (1, LANES), 1)
    weights = jnp.zeros((1, LANES), f32)
    for tile in range(capacity):
        amount = jnp.where(tile < counts_ref[0, 0], pool_ref[0, tile], 0.0)
        weights = jnp.where(column == tile, amount, weights)
    hidden = jnp.sum(pooled_ref[...] * weights, axis=1, keepdims=True)
    mixed = jnp.sum(hidden * w_out_ref[...].astype(f32), axis=0, keepdims=True)
    emb_ref[...] = (own_sum_ref[...] + scale_ref[...].reshape(1, channels) * mixed) * 0.125


def taps_kernel(pad_ref, edge_ref, grad_ref, emb_ref, state_ref, pack_ref, part_ref):
    parts, capacity = pad_ref.shape[0], pad_ref.shape[1]
    for lane in range(parts):

        def one_column(col):
            def one_tile(tile, sums):
                sums = list(sums)
                grads = [grad_ref[pl.ds(tile * 64 + row * 8, 8), lanes(lane)] for row in range(8)]
                for held in range(14):
                    if 3 <= held < 11:
                        window = pad_ref[lane, tile, held - 3, pl.ds(5 + col, 8), :]
                    else:
                        row = held if held < 3 else held - 8
                        window = edge_ref[lane, tile, row, pl.ds(5 + col, 8), :]
                    for out in range(8):
                        tap = held - out
                        if 0 <= tap < 7:
                            sums[tap] = sums[tap] + window * grads[out]
                return tuple(sums)

            sums = lax.fori_loop(0, capacity, one_tile, tuple(jnp.zeros((8, LANES), f32) for _ in range(7)))
            for row in range(7):
                part_ref[row * 7 + col, :, lanes(lane)] = sums[row]
            return 0

        for col in range(7):
            one_column(col)
    state_ref[0:TAPS, :] = jnp.sum(part_ref[...], axis=1)
    state_ref[TAPS : TAPS + 1, :] = emb_ref[...]
    state_ref[TAPS + 1 :, :] = jnp.zeros((STATE - TAPS - 1, emb_ref.shape[1]), f32)
    pack_ref[...] = packed(state_ref)


def packed(state_ref):
    state = state_ref[...]
    high = state.astype(bf16)
    low = pltpu.roll(state - high.astype(f32), 1, 0)
    row = lax.broadcasted_iota(jnp.int32, state.shape, 0)
    return jnp.where(row == TAPS + 1, low, high.astype(f32)).astype(bf16)


def merged(state_ref, got):
    total = packed(state_ref).astype(f32) + got.astype(f32)
    row = lax.broadcasted_iota(jnp.int32, total.shape, 0)
    moved = pltpu.roll(total, STATE - 1, 0)
    total = jnp.where(row == TAPS, total + moved, total)
    return jnp.where(row > TAPS, 0.0, total)


def state_kernel(state_ref, got_ref, new_ref, pack_ref):
    new_ref[...] = merged(state_ref, got_ref[...])
    pack_ref[...] = packed(new_ref)


def merge_kernel(rows, stage, with_state, joins, symmetric, place_ref, keep_ref, got_ref, *refs):
    count = keep_ref.shape[0]
    refs = list(refs)
    state_ref = refs.pop(0) if with_state else None
    new_ref, send_ref = refs.pop(0), refs.pop(0)
    next_ref = refs.pop(0) if with_state else None
    value = keep_ref[...]
    if symmetric:
        value = value.astype(bf16).astype(f32)
    total = value + got_ref[0:count, :].astype(f32)
    if stage is None:
        new_ref[...] = total
        send_ref[0:count, :] = total.astype(bf16)
        sent = count
    else:
        sum_ref = refs.pop(0)
        sum_ref[...] = total
        split_pieces(sum_ref, rows, place_ref[0, 0], stage, new_ref, send_ref.at[0 : count // 2])
        sent = count // 2
    if with_state:
        next_ref[...] = merged(state_ref, got_ref[count:, :]) if joins else state_ref[...]
        send_ref[sent:, :] = packed(next_ref)


def finish_kernel(keep_ref, got_ref, state_ref, share_ref, taps_ref):
    count = keep_ref.shape[0]
    share_ref[...] = keep_ref[...].astype(bf16).astype(f32) + got_ref[0:count, :].astype(f32)
    total = packed(state_ref).astype(f32) + got_ref[count:, :].astype(f32)
    for row in range(7):
        taps_ref[row] = total[row * 7 : row * 7 + 7, :]


def final_kernel(
    adj_ref, counts_ref, pool_ref, grad_ref, north_ref, south_ref, kern_ref, up_ref, cot_ref,
    out_ref, pad_ref,
):
    capacity, parts = adj_ref.shape[0], grad_ref.shape[1] // LANES

    def own_at(tile, row):
        at = tile * 64 + row * 8
        return grad_ref[pl.ds(at if isinstance(at, int) else pl.multiple_of(at, 8), 8), :]

    fill_middle(pad_ref, own_at, adj_ref, capacity, 3, parts)
    fill_edge(pad_ref, north_ref, adj_ref, capacity, UPPER, 0, parts)
    fill_edge(pad_ref, south_ref, adj_ref, capacity, LOWER, 11, parts)

    def finish(tile, lane, sums):
        live = jnp.where(tile < counts_ref[0, 0], 1.0, 0.0).astype(f32)
        extra = pool_ref[0, tile] * cot_ref[:, lanes(lane)] * 0.125
        for row in range(8):
            at = pl.ds(tile * 64 + row * 8, 8)
            out_grad = live * (up_ref[at, lanes(lane)].astype(f32) + extra)
            out_ref[at, lanes(lane)] = (live * (out_grad + sums[row])).astype(bf16)

    convolve(
        [(pad_ref, 14, 0)],
        lambda row, col, lane: kern_ref[6 - row, 6 - col : 7 - col, lanes(lane)],
        finish, capacity, parts,
    )


def whole_pass(
    tiles_in, upstream, pool_weight, slide_cot, adjacency, counts, kernel, norm_gain, w_in, w_out,
    layer_scale,
):
    own = tiles_in[0]
    capacity, _, _, channels = own.shape
    parts = channels // LANES
    hidden = w_in.shape[1]
    pixels = capacity * 64
    up = upstream.reshape(pixels, channels)
    wanted = adjacency[0]
    edge_shape = (capacity, 3, 8, channels)
    count = lax.axis_size("space")
    stages = count.bit_length() - 1
    rows = hidden // count
    place = lax.axis_index("space").astype(jnp.int32).reshape(1, 1)

    north, south = call(edge_kernel, [struct(edge_shape, bf16)] * 2, [VMEM], [own], flops=EDGE_COST)
    north = passed_along(north, "space", 1)
    south = passed_along(south, "space", -1)

    pad, conv, mixed, act_grad, own_sum = call(
        early_kernel,
        [
            struct((parts, capacity, 8, 24, LANES)),
            struct((pixels, channels)),
            struct((pixels, channels + LANES), bf16),
            struct((pixels, hidden)),
            struct((1, channels)),
        ],
        [SMEM] * 3 + [VMEM] * 6,
        [wanted, counts, pool_weight, slide_cot, layer_scale, kernel, own, up, w_out],
        flops=2 * pixels * channels * hidden,
    )
    edge, normed, inv, pre_grad, keep, send, pooled = call(
        functools.partial(forward_kernel, rows),
        [
            struct((parts, capacity, 6, 24, LANES)),
            struct((pixels, channels)),
            struct((pixels, 1)),
            struct((pixels, hidden), bf16),
            struct((hidden // 2, channels)),
            struct((hidden // 2, channels), bf16),
            struct((hidden, LANES)),
        ],
        [SMEM] * 2 + [VMEM] * 8,
        [wanted, place, north, south, conv, kernel, norm_gain, w_in, mixed, act_grad],
        flops=4 * pixels * channels * hidden,
        scratch=[pltpu.VMEM((pixels, channels), f32), pltpu.VMEM((hidden, channels), f32)],
    )
    got = swapped(send, "space", 1)

    grad, grad_north, grad_south, emb = call(
        back_kernel,
        [
            struct((pixels, channels)),
            struct(edge_shape, bf16),
            struct(edge_shape, bf16),
            struct((1, channels)),
        ],
        [SMEM] * 2 + [VMEM] * 9,
        [counts, pool_weight, pre_grad, w_in, normed, inv, norm_gain, pooled, w_out, layer_scale, own_sum],
        flops=2 * pixels * channels * hidden,
    )
    grad_north = passed_along(grad_north, "space", 1)
    grad_south = passed_along(grad_south, "space", -1)

    state, pack = call(
        taps_kernel, [struct((STATE, channels)), struct((STATE, channels), bf16)],
        [VMEM] * 4, [pad, edge, grad, emb],
        scratch=[pltpu.VMEM((TAPS, 8, channels), f32)],
    )
    for stage in range(min(SEPARATE, stages)):
        new = swapped(pack, "space", 1 << stage)
        state, pack = call(
            state_kernel, [struct((STATE, channels)), struct((STATE, channels), bf16)],
            [VMEM] * 2, [state, new],
        )

    for stage in range(1, stages + 1):
        last = stage == stages
        with_state = stage >= SEPARATE
        held = hidden >> stage
        sent = held if last else held // 2
        shapes = [
            struct((sent, channels)),
            struct((sent + (STATE if with_state else 0), channels), bf16),
        ]
        operands = [place, keep, got]
        if with_state:
            shapes.append(struct((STATE, channels)))
            operands.append(state)
        results = call(
            functools.partial(
                merge_kernel, rows, None if last else stage, with_state, stage > SEPARATE, False
            ),
            shapes, [SMEM] + [VMEM] * (len(operands) - 1), operands,
            scratch=[] if last else [pltpu.VMEM((held, channels), f32)],
        )
        keep, send = results[:2]
        if with_state:
            state = results[2]
        if not last:
            got = swapped(send, "space", 1 << stage)
    embedding = state[TAPS : TAPS + 1]
    groups = lax.axis_size("dp")
    bit = 1
    while bit < groups:
        got = swapped(send, "dp", bit)
        bit *= 2
        if bit < groups:
            keep, send, state = call(
                functools.partial(merge_kernel, rows, None, True, True, True),
                [struct(keep.shape), struct(send.shape, bf16), struct(state.shape)],
                [SMEM] + [VMEM] * 3, [place, keep, got, state],
            )
    share, tap_grad = call(
        finish_kernel, [struct((rows, channels)), struct(kernel.shape)],
        [VMEM] * 3, [keep, got, state],
    )

    grad_tiles = call(
        final_kernel, struct((pixels, channels), bf16),
        [SMEM] * 3 + [VMEM] * 6,
        [wanted, counts, pool_weight, grad, grad_north, grad_south, kernel, up, slide_cot],
        scratch=[pltpu.VMEM((parts, capacity, 14, 24, LANES), f32)],
    )
    return (
        embedding,
        grad_tiles.reshape(tiles_in.shape),
        share,
        tap_grad,
    )


def solution(mesh):
    return jax.shard_map(
        whole_pass,
        mesh=mesh,
        in_specs=(
            P("dp", "space", None, None, None),
            P("dp", "space", None, None, None),
            P("dp", "space"),
            P("dp", None),
            P("dp", "space", None),
            P("dp", "space"),
            P(),
            P(),
            P(),
            P(),
            P(),
        ),
        out_specs=(P("dp", None), P("dp", "space", None, None, None), P("space", None), P()),
        check_vma=False,
    )
```

profile of v0, /device:TPU:1, one launch (start us, length us, event | category | flops | bytes accessed | tf_op | source)
XLA Modules:
  0.0 58.6 jit_solution(202286289197624705)
XLA Ops:
  0.6 0.0 copy-start.4
  0.6 0.9 %copy-done.4 = bf16[1,4,8,8,384]{4,3,2,1,0:T(8,128)(2,1)S(1)} copy-done((bf16[1,4,8,8,384]{4,3,2,1,0:T(8,128)(2,1)S(1)}, bf16[1,4,8,8,384]{4,3,2,1,0:T(8,128)(2,1)}, u32[]{:S(2)}) %copy-start.4) | copy-done | bytes 196632
  1.6 0.0 copy-start.6
  1.6 0.0 copy-start.7
  1.6 0.0 copy-start.9
  1.6 0.0 copy-start.10
  1.6 0.0 copy-start.1
  1.6 0.0 copy-start.8
  1.7 4.8 %collective-permute-start = (bf16[4,3,8,384]{3,2,1,0:T(8,128)(2,1)S(1)}, bf16[4,3,8,384]{3,2,1,0:T(8,128)(2,1)S(1)}, u32[]{:S(2)}, u32[]{:S(2)}) collective-permute-start(bf16[4,3,8,384]{3,2,1,0:T(8,128)(2,1)S(1)} %get-tuple-element.40), channel_id=1, source_target_pairs={{0,1},{1,2},{2,3},{3,4},{4,5},{5,6},{6,7},{7,8},{8,9},{9,10},{10,1... | collective-permute-start | bytes 221192 | tf_op jit(solution)/shard_map/ppermute | solution.py:46
  6.5 1.9 %collective-permute-start.1 = (bf16[4,3,8,384]{3,2,1,0:T(8,128)(2,1)S(1)}, bf16[4,3,8,384]{3,2,1,0:T(8,128)(2,1)S(1)}, u32[]{:S(2)}, u32[]{:S(2)}) collective-permute-start(bf16[4,3,8,384]{3,2,1,0:T(8,128)(2,1)S(1)} %get-tuple-element.41), channel_id=1, source_target_pairs={{1,0},{2,1},{3,2},{4,3},{5,4},{6,5},{7,6},{8,7},{9,8},{10,9},{11,1... | collective-permute-start | bytes 221192 | tf_op jit(solution)/shard_map/ppermute | solution.py:46
  9.0 0.0 copy-done
  9.0 0.0 copy-done.2
  9.1 0.0 copy-done.3
  9.1 0.0 copy-done.5
  9.1 0.0 copy-done.6
  9.1 0.0 copy-done.7
  9.1 0.0 copy-done.9
  9.1 2.3 %shard_map.139 = (f32[3,4,8,24,128]{4,3,2,1,0:T(8,128)S(1)}, f32[256,384]{1,0:T(8,128)S(1)}, bf16[256,512]{1,0:T(8,128)(2,1)S(1)}, f32[256,1536]{1,0:T(8,128)S(1)}, f32[1,384]{1,0:T(1,128)S(1)}) custom-call(s32[4,8]{1,0:T(4,128)S(1)} %bitcast.9, s32[1,1]{1,0:T(1,128)S(6)} %copy.15.counts_ref, f32[1,4]{1,0:T(1,128)S(1)} %copy-done.10, ...), custom_call_target="tpu_custom_call" | custom-call | flops 301989888 | bytes 5060756 | tf_op jit(solution)/shard_map/pallas_call | solution.py:28
  11.4 0.0 collective-permute-done.north_ref
  11.4 0.7 %collective-permute-done.1.south_ref = bf16[4,3,8,384]{3,2,1,0:T(8,128)(2,1)S(1)} collective-permute-done((bf16[4,3,8,384]{3,2,1,0:T(8,128)(2,1)S(1)}, bf16[4,3,8,384]{3,2,1,0:T(8,128)(2,1)S(1)}, u32[]{:S(2)}, u32[]{:S(2)}) %collective-permute-start.1) | collective-permute-done | bytes 73760 | tf_op jit(solution)/shard_map/ppermute | solution.py:46
  12.1 3.7 %shard_map.140 = (f32[3,4,6,24,128]{4,3,2,1,0:T(8,128)S(1)}, f32[256,384]{1,0:T(8,128)S(1)}, f32[256,1]{1,0:T(8,128)S(1)}, bf16[256,1536]{1,0:T(8,128)(2,1)S(1)}...) custom-call(s32[4,8]{1,0:T(4,128)S(1)} %bitcast.10, s32[1,1]{1,0:T(1,128)} %bitcast.place_ref, ...), custom_call_target="tpu_custom_call" | custom-call | flops 603979776 | bytes 8253572 | tf_op jit(solution)/shard_map/pallas_call | solution.py:28
  15.8 0.1 collective-permute-start.2
  15.9 2.0 %collective-permute-done.2.got_ref = bf16[768,384]{1,0:T(8,128)(2,1)S(1)} collective-permute-done((bf16[768,384]{1,0:T(8,128)(2,1)S(1)}, bf16[768,384]{1,0:T(8,128)(2,1)S(1)}, u32[]{:S(2)}, u32[]{:S(2)}) %collective-permute-start.2) | collective-permute-done | bytes 589856 | tf_op jit(solution)/shard_map/ppermute | solution.py:51
  17.9 0.3 shard_map.141
  18.2 2.2 %collective-permute-start.3 = (bf16[384,384]{1,0:T(8,128)(2,1)S(1)}, bf16[384,384]{1,0:T(8,128)(2,1)S(1)}, u32[]{:S(2)}, u32[]{:S(2)}) collective-permute-start(bf16[384,384]{1,0:T(8,128)(2,1)S(1)} %get-tuple-element.48), channel_id=1, source_target_pairs={{0,2},{1,3},{2,0},{3,1},{4,6},{5,7},{6,4},{7,5},{8,10},{9,11},{10,... | collective-permute-start | bytes 884744 | tf_op jit(solution)/shard_map/ppermute | solution.py:51
  20.4 1.3 %shard_map.142 = (f32[256,384]{1,0:T(8,128)S(1)}, bf16[4,3,8,384]{3,2,1,0:T(8,128)(2,1)S(1)}, bf16[4,3,8,384]{3,2,1,0:T(8,128)(2,1)S(1)}, f32[1,384]{1,0:T(1,128)S(1)}) custom-call(s32[1,1]{1,0:T(1,128)S(6)} %copy.15.counts_ref, f32[1,4]{1,0:T(1,128)S(1)} %copy-done.10, bf16[256,1536]{1,0:T(8,128)(2,1)S(1)} %get-tuple-element.51.pre_grad_ref, ...), custom_call_target="tpu_custom_call" | custom-call | flops 301989888 | bytes 4873236 | tf_op jit(solution)/shard_map/pallas_call | solution.py:28
  21.6 2.4 %shard_map.143 = (f32[56,384]{1,0:T(8,128)S(1)}, bf16[56,384]{1,0:T(8,128)(2,1)S(1)}) custom-call(f32[3,4,8,24,128]{4,3,2,1,0:T(8,128)S(1)} %get-tuple-element.49.pad_ref, f32[3,4,6,24,128]{4,3,2,1,0:T(8,128)S(1)} %get-tuple-element.50.edge_ref, f32[256,384]{1,0:T(8,128)S(1)} %get-tuple-element.56.grad_ref, f32[1,384]{1,0:T(1,128)S(1)} %get-tuple-element.57.emb_ref), custom_call_target="tpu_custom_call" | custom-call | bytes 2588160 | tf_op jit(solution)/shard_map/pallas_call | solution.py:28
  24.1 0.5 collective-permute-start.4
  24.6 0.9 %collective-permute-done.4.got_ref = bf16[56,384]{1,0:T(8,128)(2,1)S(1)} collective-permute-done((bf16[56,384]{1,0:T(8,128)(2,1)S(1)}, bf16[56,384]{1,0:T(8,128)(2,1)S(1)}, u32[]{:S(2)}, u32[]{:S(2)}) %collective-permute-start.4) | collective-permute-done | bytes 43040 | tf_op jit(solution)/shard_map/ppermute | solution.py:51
  25.5 0.1 collective-permute-start.5
  25.6 2.9 %collective-permute-done.5.got_ref = bf16[56,384]{1,0:T(8,128)(2,1)S(1)} collective-permute-done((bf16[56,384]{1,0:T(8,128)(2,1)S(1)}, bf16[56,384]{1,0:T(8,128)(2,1)S(1)}, u32[]{:S(2)}, u32[]{:S(2)}) %collective-permute-start.5) | collective-permute-done | bytes 43040 | tf_op jit(solution)/shard_map/ppermute | solution.py:51
  28.4 0.6 %shard_map.145 = (f32[56,384]{1,0:T(8,128)S(1)}, bf16[56,384]{1,0:T(8,128)(2,1)}) custom-call(f32[56,384]{1,0:T(8,128)S(1)} %get-tuple-element.60.state_ref, bf16[56,384]{1,0:T(8,128)(2,1)S(1)} %collective-permute-done.5.got_ref), custom_call_target="tpu_custom_call" | custom-call | bytes 258048 | tf_op jit(solution)/shard_map/pallas_call | solution.py:28
  29.1 0.0 collective-permute-done.3.got_ref
  29.1 0.1 shard_map.146
  29.2 1.4 %collective-permute-start.6 = (bf16[248,384]{1,0:T(8,128)(2,1)S(1)}, bf16[248,384]{1,0:T(8,128)(2,1)S(1)}, u32[]{:S(2)}, u32[]{:S(2)}) collective-permute-start(bf16[248,384]{1,0:T(8,128)(2,1)S(1)} %get-tuple-element.64), channel_id=1, source_target_pairs={{0,4},{1,5},{2,6},{3,7},{4,0},{5,1},{6,2},{7,3},{8,12},{9,13},{10,... | collective-permute-start | bytes 571400 | tf_op jit(solution)/shard_map/ppermute | solution.py:51
  30.6 3.5 %collective-permute-done.6.got_ref = bf16[248,384]{1,0:T(8,128)(2,1)S(1)} collective-permute-done((bf16[248,384]{1,0:T(8,128)(2,1)S(1)}, bf16[248,384]{1,0:T(8,128)(2,1)S(1)}, u32[]{:S(2)}, u32[]{:S(2)}) %collective-permute-start.6) | collective-permute-done | bytes 190496 | tf_op jit(solution)/shard_map/ppermute | solution.py:51
  34.1 0.1 shard_map.147
  34.2 2.4 %collective-permute-start.7 = (bf16[152,384]{1,0:T(8,128)(2,1)S(1)}, bf16[152,384]{1,0:T(8,128)(2,1)S(1)}, u32[]{:S(2)}, u32[]{:S(2)}) collective-permute-start(bf16[152,384]{1,0:T(8,128)(2,1)S(1)} %get-tuple-element.67), channel_id=1, source_target_pairs={{0,8},{1,9},{2,10},{3,11},{4,12},{5,13},{6,14},{7,15},{8,0},{9,1},... | collective-permute-start | bytes 350216 | tf_op jit(solution)/shard_map/ppermute | solution.py:51
  36.6 3.5 %collective-permute-done.7.got_ref = bf16[152,384]{1,0:T(8,128)(2,1)S(1)} collective-permute-done((bf16[152,384]{1,0:T(8,128)(2,1)S(1)}, bf16[152,384]{1,0:T(8,128)(2,1)S(1)}, u32[]{:S(2)}, u32[]{:S(2)}) %collective-permute-start.7) | collective-permute-done | bytes 116768 | tf_op jit(solution)/shard_map/ppermute | solution.py:51
  40.1 1.3 %collective-permute-start.10 = (bf16[152,384]{1,0:T(8,128)(2,1)S(1)}, bf16[152,384]{1,0:T(8,128)(2,1)S(1)}, u32[]{:S(2)}, u32[]{:S(2)}) collective-permute-start(bf16[152,384]{1,0:T(8,128)(2,1)S(1)} %get-tuple-element.73), channel_id=1, source_target_pairs={{0,16},{16,0},{1,17},{17,1},{2,18},{18,2},{3,19},{19,3},{4,20},{20... | collective-permute-start | bytes 350216 | tf_op jit(solution)/shard_map/ppermute | solution.py:51
  41.4 7.0 %collective-permute-start.8 = (bf16[4,3,8,384]{3,2,1,0:T(8,128)(2,1)S(1)}, bf16[4,3,8,384]{3,2,1,0:T(8,128)(2,1)S(1)}, u32[]{:S(2)}, u32[]{:S(2)}) collective-permute-start(bf16[4,3,8,384]{3,2,1,0:T(8,128)(2,1)S(1)} %get-tuple-element.70), channel_id=1, source_target_pairs={{0,1},{1,2},{2,3},{3,4},{4,5},{5,6},{6,7},{7,8},{8,9},{9,10},{10,1... | collective-permute-start | bytes 221192 | tf_op jit(solution)/shard_map/ppermute | solution.py:46
  48.5 1.9 %collective-permute-start.9 = (bf16[4,3,8,384]{3,2,1,0:T(8,128)(2,1)S(1)}, bf16[4,3,8,384]{3,2,1,0:T(8,128)(2,1)S(1)}, u32[]{:S(2)}, u32[]{:S(2)}) collective-permute-start(bf16[4,3,8,384]{3,2,1,0:T(8,128)(2,1)S(1)} %get-tuple-element.71), channel_id=1, source_target_pairs={{1,0},{2,1},{3,2},{4,3},{5,4},{6,5},{7,6},{8,7},{9,8},{10,9},{11,1... | collective-permute-start | bytes 221192 | tf_op jit(solution)/shard_map/ppermute | solution.py:46
  50.4 0.0 collective-permute-done.8.north_ref
  50.4 3.7 %collective-permute-done.9.south_ref = bf16[4,3,8,384]{3,2,1,0:T(8,128)(2,1)S(1)} collective-permute-done((bf16[4,3,8,384]{3,2,1,0:T(8,128)(2,1)S(1)}, bf16[4,3,8,384]{3,2,1,0:T(8,128)(2,1)S(1)}, u32[]{:S(2)}, u32[]{:S(2)}) %collective-permute-start.9) | collective-permute-done | bytes 73760 | tf_op jit(solution)/shard_map/ppermute | solution.py:46
  54.1 3.2 %shard_map.149 = bf16[256,384]{1,0:T(8,128)(2,1)} custom-call(s32[4,8]{1,0:T(4,128)S(1)} %bitcast.11, s32[1,1]{1,0:T(1,128)S(6)} %copy.15.counts_ref, f32[1,4]{1,0:T(1,128)S(1)} %copy-done.10, f32[256,384]{1,0:T(8,128)S(1)} %get-tuple-element.56.grad_ref, bf16[4,3,8,384]{3,2,1,0:T(8,128)(2,1)S(1)} %collective-permute-done.8.north_ref, ...), custom_call_target="tpu_custom_call" | custom-call | bytes 1010836 | tf_op jit(solution)/shard_map/pallas_call | solution.py:28
  57.3 0.6 slice.3
  57.9 0.0 collective-permute-done.10.got_ref
  57.9 0.7 %shard_map.150 = (f32[96,384]{1,0:T(8,128)}, f32[7,7,384]{2,1,0:T(8,128)}) custom-call(f32[96,384]{1,0:T(8,128)S(1)} %get-tuple-element.72.keep_ref, bf16[152,384]{1,0:T(8,128)(2,1)S(1)} %collective-permute-done.10.got_ref, f32[56,384]{1,0:T(8,128)S(1)} %get-tuple-element.69.state_ref), custom_call_target="tpu_custom_call" | custom-call | bytes 572928 | tf_op jit(solution)/shard_map/pallas_call | solution.py:28
  (10 shorter events, 0.1 us)
Async XLA Ops:
  0.6 0.9 %copy-start.4 = (bf16[1,4,8,8,384]{4,3,2,1,0:T(8,128)(2,1)S(1)}, bf16[1,4,8,8,384]{4,3,2,1,0:T(8,128)(2,1)}, u32[]{:S(2)}) copy-start(bf16[1,4,8,8,384]{4,3,2,1,0:T(8,128)(2,1)} %param.11) | copy-start | bytes 589828
  1.6 7.5 %copy-start = (bf16[1536,384]{1,0:T(8,128)(2,1)S(1)}, bf16[1536,384]{1,0:T(8,128)(2,1)}, u32[]{:S(2)}) copy-start(bf16[1536,384]{1,0:T(8,128)(2,1)} %w_out_ref.3) | copy-start | bytes 3538948
  1.6 7.5 %copy-start.2 = (bf16[1,4,8,8,384]{4,3,2,1,0:T(8,128)(2,1)S(1)}, bf16[1,4,8,8,384]{4,3,2,1,0:T(8,128)(2,1)}, u32[]{:S(2)}) copy-start(bf16[1,4,8,8,384]{4,3,2,1,0:T(8,128)(2,1)} %param.12) | copy-start | bytes 589828
  1.6 7.5 %copy-start.3 = (f32[7,7,384]{2,1,0:T(8,128)S(1)}, f32[7,7,384]{2,1,0:T(8,128)}, u32[]{:S(2)}) copy-start(f32[7,7,384]{2,1,0:T(8,128)} %kern_ref.5) | copy-start | bytes 225796
  1.6 7.5 %copy-start.5 = (bf16[1,4,8,8,384]{4,3,2,1,0:T(8,128)(2,1)S(1)}, bf16[1,4,8,8,384]{4,3,2,1,0:T(8,128)(2,1)}, u32[]{:S(2)}) copy-start(bf16[1,4,8,8,384]{4,3,2,1,0:T(8,128)(2,1)} %param.11) | copy-start | bytes 589828
  1.6 7.5 %copy-start.6 = (s32[1,4,8]{2,1,0:T(4,128)S(1)}, s32[1,4,8]{2,1,0:T(4,128)}, u32[]{:S(2)}) copy-start(s32[1,4,8]{2,1,0:T(4,128)} %param.15) | copy-start | bytes 388
  1.6 7.5 %copy-start.7 = (f32[384]{0:T(512)S(1)}, f32[384]{0:T(512)}, u32[]{:S(2)}) copy-start(f32[384]{0:T(512)} %scale_ref.3) | copy-start | bytes 4612
  1.6 7.5 %copy-start.9 = (f32[1,384]{1,0:T(1,128)S(1)}, f32[1,384]{1,0:T(1,128)}, u32[]{:S(2)}) copy-start(f32[1,384]{1,0:T(1,128)} %cot_ref.3) | copy-start | bytes 4612
  1.6 7.5 %copy-start.10 = (f32[1,4]{1,0:T(1,128)S(1)}, f32[1,4]{1,0:T(1,128)}, u32[]{:S(2)}) copy-start(f32[1,4]{1,0:T(1,128)} %pool_ref.5) | copy-start | bytes 52
  1.6 10.5 %copy-start.1 = (bf16[384,1536]{1,0:T(8,128)(2,1)S(1)}, bf16[384,1536]{1,0:T(8,128)(2,1)}, u32[]{:S(2)}) copy-start(bf16[384,1536]{1,0:T(8,128)(2,1)} %w_in_ref.3) | copy-start | bytes 3538948
  1.6 10.5 %copy-start.8 = (f32[384]{0:T(512)S(1)}, f32[384]{0:T(512)}, u32[]{:S(2)}) copy-start(f32[384]{0:T(512)} %gain_ref.3) | copy-start | bytes 4612
  1.7 9.8 %collective-permute-start = (bf16[4,3,8,384]{3,2,1,0:T(8,128)(2,1)S(1)}, bf16[4,3,8,384]{3,2,1,0:T(8,128)(2,1)S(1)}, u32[]{:S(2)}, u32[]{:S(2)}) collective-permute-start(bf16[4,3,8,384]{3,2,1,0:T(8,128)(2,1)S(1)} %get-tuple-element.40), channel_id=1, source_target_pairs={{0,1},{1,2},{2,3},{3,4},{4,5},{5,6},{6,7},{7,8},{8,9},{9,10},{10,1... | collective-permute-start | bytes 221192 | tf_op jit(solution)/shard_map/ppermute | solution.py:46
  6.5 5.7 %collective-permute-start.1 = (bf16[4,3,8,384]{3,2,1,0:T(8,128)(2,1)S(1)}, bf16[4,3,8,384]{3,2,1,0:T(8,128)(2,1)S(1)}, u32[]{:S(2)}, u32[]{:S(2)}) collective-permute-start(bf16[4,3,8,384]{3,2,1,0:T(8,128)(2,1)S(1)} %get-tuple-element.41), channel_id=1, source_target_pairs={{1,0},{2,1},{3,2},{4,3},{5,4},{6,5},{7,6},{8,7},{9,8},{10,9},{11,1... | collective-permute-start | bytes 221192 | tf_op jit(solution)/shard_map/ppermute | solution.py:46
  15.8 2.1 %collective-permute-start.2 = (bf16[768,384]{1,0:T(8,128)(2,1)S(1)}, bf16[768,384]{1,0:T(8,128)(2,1)S(1)}, u32[]{:S(2)}, u32[]{:S(2)}) collective-permute-start(bf16[768,384]{1,0:T(8,128)(2,1)S(1)} %get-tuple-element.46), channel_id=1, source_target_pairs={{0,1},{1,0},{2,3},{3,2},{4,5},{5,4},{6,7},{7,6},{8,9},{9,8},{10,11... | collective-permute-start | bytes 1769480 | tf_op jit(solution)/shard_map/ppermute | solution.py:51
  18.2 10.9 %collective-permute-start.3 = (bf16[384,384]{1,0:T(8,128)(2,1)S(1)}, bf16[384,384]{1,0:T(8,128)(2,1)S(1)}, u32[]{:S(2)}, u32[]{:S(2)}) collective-permute-start(bf16[384,384]{1,0:T(8,128)(2,1)S(1)} %get-tuple-element.48), channel_id=1, source_target_pairs={{0,2},{1,3},{2,0},{3,1},{4,6},{5,7},{6,4},{7,5},{8,10},{9,11},{10,... | collective-permute-start | bytes 884744 | tf_op jit(solution)/shard_map/ppermute | solution.py:51
  24.1 1.4 %collective-permute-start.4 = (bf16[56,384]{1,0:T(8,128)(2,1)S(1)}, bf16[56,384]{1,0:T(8,128)(2,1)S(1)}, u32[]{:S(2)}, u32[]{:S(2)}) collective-permute-start(bf16[56,384]{1,0:T(8,128)(2,1)S(1)} %get-tuple-element.59), channel_id=1, source_target_pairs={{0,1},{1,0},{2,3},{3,2},{4,5},{5,4},{6,7},{7,6},{8,9},{9,8},{10,11... | collective-permute-start | bytes 129032 | tf_op jit(solution)/shard_map/ppermute | solution.py:51
  25.5 2.9 %collective-permute-start.5 = (bf16[56,384]{1,0:T(8,128)(2,1)S(1)}, bf16[56,384]{1,0:T(8,128)(2,1)S(1)}, u32[]{:S(2)}, u32[]{:S(2)}) collective-permute-start(bf16[56,384]{1,0:T(8,128)(2,1)S(1)} %get-tuple-element.61), channel_id=1, source_target_pairs={{0,2},{1,3},{2,0},{3,1},{4,6},{5,7},{6,4},{7,5},{8,10},{9,11},{10,... | collective-permute-start | bytes 129032 | tf_op jit(solution)/shard_map/ppermute | solution.py:51
  29.2 4.9 %collective-permute-start.6 = (bf16[248,384]{1,0:T(8,128)(2,1)S(1)}, bf16[248,384]{1,0:T(8,128)(2,1)S(1)}, u32[]{:S(2)}, u32[]{:S(2)}) collective-permute-start(bf16[248,384]{1,0:T(8,128)(2,1)S(1)} %get-tuple-element.64), channel_id=1, source_target_pairs={{0,4},{1,5},{2,6},{3,7},{4,0},{5,1},{6,2},{7,3},{8,12},{9,13},{10,... | collective-permute-start | bytes 571400 | tf_op jit(solution)/shard_map/ppermute | solution.py:51
  34.2 5.9 %collective-permute-start.7 = (bf16[152,384]{1,0:T(8,128)(2,1)S(1)}, bf16[152,384]{1,0:T(8,128)(2,1)S(1)}, u32[]{:S(2)}, u32[]{:S(2)}) collective-permute-start(bf16[152,384]{1,0:T(8,128)(2,1)S(1)} %get-tuple-element.67), channel_id=1, source_target_pairs={{0,8},{1,9},{2,10},{3,11},{4,12},{5,13},{6,14},{7,15},{8,0},{9,1},... | collective-permute-start | bytes 350216 | tf_op jit(solution)/shard_map/ppermute | solution.py:51
  40.1 17.7 %collective-permute-start.10 = (bf16[152,384]{1,0:T(8,128)(2,1)S(1)}, bf16[152,384]{1,0:T(8,128)(2,1)S(1)}, u32[]{:S(2)}, u32[]{:S(2)}) collective-permute-start(bf16[152,384]{1,0:T(8,128)(2,1)S(1)} %get-tuple-element.73), channel_id=1, source_target_pairs={{0,16},{16,0},{1,17},{17,1},{2,18},{18,2},{3,19},{19,3},{4,20},{20... | collective-permute-start | bytes 350216 | tf_op jit(solution)/shard_map/ppermute | solution.py:51
  41.4 9.0 %collective-permute-start.8 = (bf16[4,3,8,384]{3,2,1,0:T(8,128)(2,1)S(1)}, bf16[4,3,8,384]{3,2,1,0:T(8,128)(2,1)S(1)}, u32[]{:S(2)}, u32[]{:S(2)}) collective-permute-start(bf16[4,3,8,384]{3,2,1,0:T(8,128)(2,1)S(1)} %get-tuple-element.70), channel_id=1, source_target_pairs={{0,1},{1,2},{2,3},{3,4},{4,5},{5,6},{6,7},{7,8},{8,9},{9,10},{10,1... | collective-permute-start | bytes 221192 | tf_op jit(solution)/shard_map/ppermute | solution.py:46
  48.5 5.7 %collective-permute-start.9 = (bf16[4,3,8,384]{3,2,1,0:T(8,128)(2,1)S(1)}, bf16[4,3,8,384]{3,2,1,0:T(8,128)(2,1)S(1)}, u32[]{:S(2)}, u32[]{:S(2)}) collective-permute-start(bf16[4,3,8,384]{3,2,1,0:T(8,128)(2,1)S(1)} %get-tuple-element.71), channel_id=1, source_target_pairs={{1,0},{2,1},{3,2},{4,3},{5,4},{6,5},{7,6},{8,7},{9,8},{10,9},{11,1... | collective-permute-start | bytes 221192 | tf_op jit(solution)/shard_map/ppermute | solution.py:46
where the time goes:
time: 58.8 us; the launch traced here: 58.6 us
  starting transfers between devices  23.5 us (40%)
  waiting for transfers between devices  17.2 us (29%)
  Pallas kernels  14.8 us (25%)
  local copies, waits for them, and re-layouts  1.53 us (3%)
  between operations  1.53 us (3%)
    ppermute x4, starting transfers between devices, passed_along(): lax.ppermute(value, axis, [(source, source + steps) for source in range(l...  15.7 us
    pallas_call x13, Pallas kernels, call(): pl.pallas_call(body, out_shape=out_shape, in_specs=in_specs, out_specs=ou...  14.8 us
    ppermute x7, waiting for transfers between devices, swapped(): lax.ppermute(value, axis, [(source, source ^ bit) for source in range(cou...  12.8 us
    ppermute x7, starting transfers between devices, swapped(): lax.ppermute(value, axis, [(source, source ^ bit) for source in range(cou...  7.85 us
    ppermute x4, waiting for transfers between devices, passed_along(): lax.ppermute(value, axis, [(source, source + steps) for source in range(l...  4.43 us
  transfers between devices with their start and end apart: 11, of which 7 were waited for; matrix products, arithmetic and copies ran while one was open for 1% of the time, Pallas kernels for 17%

commit v1 on v0

--- a/solution.py
+++ b/solution.py
@@ -12,7 +12,6 @@
 f32 = jnp.float32
 bf16 = jnp.bfloat16
 LANES = 128
-SEPARATE = 2
 
 VMEM = pl.BlockSpec(memory_space=pltpu.VMEM)
 SMEM = pl.BlockSpec(memory_space=pltpu.SMEM)
@@ -40,15 +39,17 @@
     return jax.ShapeDtypeStruct(shape, dtype)
 
 
-def passed_along(value, axis, steps):
-    count = lax.axis_size(axis)
-    leading, last = (max(0, -steps), min(count, count - steps))
-    return lax.ppermute(value, axis, [(source, source + steps) for source in range(leading, last)])
-
-
 def swapped(value, axis, bit):
     count = lax.axis_size(axis)
     return lax.ppermute(value, axis, [(source, source ^ bit) for source in range(count)])
+
+
+def crossed(value, axis):
+    count = lax.axis_size(axis)
+    firsts = range(1, count - 1, 2)
+    return lax.ppermute(
+        value, axis, [(n, n + 1) for n in firsts] + [(n + 1, n) for n in firsts]
+    )
 
 
 def valid(entry):
@@ -73,14 +74,19 @@
             place(pad_ref, tile, first_row + row, 2, own_at(local(east, capacity), row) * valid(east), parts)
 
 
-def fill_edge(pad_ref, edge_ref, adj_ref, capacity, entries, first_row, parts):
+def fill_edge(pad_ref, odd_ref, even_ref, odd, adj_ref, capacity, entries, first_row, parts):
     for tile in range(capacity):
         for part, entry in enumerate(entries):
             wanted = adj_ref[tile, entry]
             index, keep = local(wanted, capacity), valid(wanted)
             for row in range(3):
-                value = edge_ref[index, row].astype(f32) * keep
+                value = odd_ref[index, row].astype(f32) * (keep * odd)
+                value = value + even_ref[index, row].astype(f32) * (keep * (1.0 - odd))
                 place(pad_ref, tile, first_row + row, part, value, parts)
+
+
+def is_odd(place_ref):
+    return lax.rem(place_ref[0, 0], 2).astype(f32)
 
 
 UPPER, LOWER = (4, 0, 5), (6, 1, 7)
@@ -111,9 +117,15 @@
     return slice(lane * LANES, (lane + 1) * LANES)
 
 
-def edge_kernel(tiles_ref, north_ref, south_ref):
-    north_ref[...] = tiles_ref[:, 5:8]
-    south_ref[...] = tiles_ref[:, 0:3]
+def swap_edges(last, first, odd, core_ref, cross_ref):
+    core_ref[...] = (first * odd + last * (1.0 - odd)).astype(bf16)
+    cross_ref[...] = (last * odd + first * (1.0 - odd)).astype(bf16)
+
+
+def edge_kernel(place_ref, tiles_ref, core_ref, cross_ref):
+    swap_edges(
+        tiles_ref[:, 5:8].astype(f32), tiles_ref[:, 0:3].astype(f32), is_odd(place_ref), core_ref, cross_ref
+    )
 
 
 def early_kernel(
@@ -152,8 +164,8 @@
     )
 
 
-def split_pieces(value_ref, rows, place, stage, keep_ref, send_ref):
-    side = lax.rem(lax.div(place, 1 << stage), 2)
+def split_pieces(value_ref, rows, place_ref, stage, keep_ref, send_ref):
+    side = lax.rem(lax.div(place_ref[0, 0], 1 << stage), 2)
     for pair in range(value_ref.shape[0] // (2 * rows)):
         here = pl.ds(pair * rows, rows)
         mine = pl.ds(pl.multiple_of((2 * pair + side) * rows, 8), rows)
@@ -163,14 +175,15 @@
 
 
 def forward_kernel(
-    rows, adj_ref, place_ref, north_ref, south_ref, conv_ref, kern_ref, gain_ref, w_in_ref, mixed_ref, act_grad_ref,
+    rows, adj_ref, place_ref, core_ref, cross_ref, conv_ref, kern_ref, gain_ref, w_in_ref, mixed_ref, act_grad_ref,
     edge_ref, normed_ref, inv_ref, pre_grad_ref, keep_ref, send_ref, pooled_ref, whole_ref, weight_ref,
 ):
     capacity, parts = adj_ref.shape[0], conv_ref.shape[1] // LANES
     channels = conv_ref.shape[1]
     pixels = 64
-    fill_edge(edge_ref, north_ref, adj_ref, capacity, UPPER, 0, parts)
-    fill_edge(edge_ref, south_ref, adj_ref, capacity, LOWER, 3, parts)
+    odd = is_odd(place_ref)
+    fill_edge(edge_ref, core_ref, cross_ref, odd, adj_ref, capacity, UPPER, 0, parts)
+    fill_edge(edge_ref, cross_ref, core_ref, odd, adj_ref, capacity, LOWER, 3, parts)
 
     def finish(tile, lane, sums):
         for row in range(8):
@@ -206,15 +219,15 @@
         )
         weight_ref[at, :] = both[:, 0:channels]
         pooled_ref[at, :] = both[:, channels:]
-    split_pieces(weight_ref, rows, place_ref[0, 0], 0, keep_ref, send_ref)
+    split_pieces(weight_ref, rows, place_ref, 0, keep_ref, send_ref)
 
 
 def back_kernel(
-    counts_ref, pool_ref, pre_grad_ref, w_in_ref, normed_ref, inv_ref, gain_ref, pooled_ref, w_out_ref,
-    scale_ref, own_sum_ref, grad_ref, north_ref, south_ref, emb_ref,
+    place_ref, counts_ref, pool_ref, pre_grad_ref, w_in_ref, normed_ref, inv_ref, gain_ref, pooled_ref, w_out_ref,
+    scale_ref, own_sum_ref, grad_ref, core_ref, cross_ref, emb_ref,
 ):
     channels = normed_ref.shape[1]
-    capacity = north_ref.shape[0]
+    capacity = core_ref.shape[0]
     lift = lax.dot_general(
         pre_grad_ref[...], w_in_ref[...], (((1,), (1,)), ((), ())), preferred_element_type=f32
     )
@@ -227,8 +240,7 @@
     )
     grad_ref[...] = grad
     shaped = grad.reshape(capacity, 8, 8, channels)
-    north_ref[...] = shaped[:, 5:8].astype(bf16)
-    south_ref[...] = shaped[:, 0:3].astype(bf16)
+    swap_edges(shaped[:, 5:8], shaped[:, 0:3], is_odd(place_ref), core_ref, cross_ref)
     column = lax.broadcasted_iota(jnp.int32, (1, LANES), 1)
     weights = jnp.zeros((1, LANES), f32)
     for tile in range(capacity):
@@ -280,53 +292,53 @@
     return jnp.where(row == TAPS + 1, low, high.astype(f32)).astype(bf16)
 
 
-def merged(state_ref, got):
+def merged(state_ref, got, with_embedding=True):
     total = packed(state_ref).astype(f32) + got.astype(f32)
     row = lax.broadcasted_iota(jnp.int32, total.shape, 0)
-    moved = pltpu.roll(total, STATE - 1, 0)
-    total = jnp.where(row == TAPS, total + moved, total)
-    return jnp.where(row > TAPS, 0.0, total)
-
-
-def state_kernel(state_ref, got_ref, new_ref, pack_ref):
-    new_ref[...] = merged(state_ref, got_ref[...])
+    if with_embedding:
+        embedding = total + pltpu.roll(total, STATE - 1, 0)
+    else:
+        embedding = state_ref[...]
+    return jnp.where(row < TAPS, total, jnp.where(row == TAPS, embedding, 0.0))
+
+
+def state_kernel(with_embedding, state_ref, got_ref, new_ref, pack_ref):
+    new_ref[...] = merged(state_ref, got_ref[...], with_embedding)
     pack_ref[...] = packed(new_ref)
 
 
-def merge_kernel(rows, stage, with_state, joins, symmetric, place_ref, keep_ref, got_ref, *refs):
-    count = keep_ref.shape[0]
-    refs = list(refs)
-    state_ref = refs.pop(0) if with_state else None
-    new_ref, send_ref = refs.pop(0), refs.pop(0)
-    next_ref = refs.pop(0) if with_state else None
-    value = keep_ref[...]
-    if symmetric:
-        value = value.astype(bf16).astype(f32)
-    total = value + got_ref[0:count, :].astype(f32)
-    if stage is None:
-        new_ref[...] = total
-        send_ref[0:count, :] = total.astype(bf16)
-        sent = count
-    else:
-        sum_ref = refs.pop(0)
-        sum_ref[...] = total
-        split_pieces(sum_ref, rows, place_ref[0, 0], stage, new_ref, send_ref.at[0 : count // 2])
-        sent = count // 2
-    if with_state:
-        next_ref[...] = merged(state_ref, got_ref[count:, :]) if joins else state_ref[...]
-        send_ref[sent:, :] = packed(next_ref)
-
-
-def finish_kernel(keep_ref, got_ref, state_ref, share_ref, taps_ref):
-    count = keep_ref.shape[0]
-    share_ref[...] = keep_ref[...].astype(bf16).astype(f32) + got_ref[0:count, :].astype(f32)
-    total = packed(state_ref).astype(f32) + got_ref[count:, :].astype(f32)
+def merge_kernel(splits, terms, place_ref, *refs):
+    sums, refs = refs[: 2 * terms], refs[2 * terms :]
+    outs = max(1, len(splits))
+    keeps, sends, sum_ref = refs[0 : 2 * outs : 2], refs[1 : 2 * outs : 2], refs[2 * outs]
+    first = 0
+    for keep_ref, got_ref in zip(sums[0::2], sums[1::2]):
+        count = keep_ref.shape[0]
+        sum_ref[first : first + count, :] = keep_ref[...] + got_ref[...].astype(f32)
+        first += count
+    for keep_ref, send_ref, (start, count, rows, bit) in zip(keeps, sends, splits):
+        split_pieces(sum_ref.at[start : start + count], rows, place_ref, bit, keep_ref, send_ref)
+    if not splits:
+        keeps[0][...] = sum_ref[...]
+        sends[0][...] = sum_ref[...].astype(bf16)
+
+
+def pair_kernel(keep_ref, got_ref, new_ref, send_ref):
+    total = keep_ref[...].astype(bf16).astype(f32) + got_ref[...].astype(f32)
+    new_ref[...] = total
+    send_ref[...] = total.astype(bf16)
+
+
+def finish_kernel(keep_ref, got_ref, state_ref, new_ref, share_ref, taps_ref, emb_ref):
+    share_ref[...] = keep_ref[...].astype(bf16).astype(f32) + got_ref[...].astype(f32)
+    total = merged(state_ref, new_ref[...])
     for row in range(7):
         taps_ref[row] = total[row * 7 : row * 7 + 7, :]
+    emb_ref[...] = total[TAPS : TAPS + 1, :]
 
 
 def final_kernel(
-    adj_ref, counts_ref, pool_ref, grad_ref, north_ref, south_ref, kern_ref, up_ref, cot_ref,
+    adj_ref, place_ref, counts_ref, pool_ref, grad_ref, core_ref, cross_ref, kern_ref, up_ref, cot_ref,
     out_ref, pad_ref,
 ):
     capacity, parts = adj_ref.shape[0], grad_ref.shape[1] // LANES
@@ -336,8 +348,9 @@
         return grad_ref[pl.ds(at if isinstance(at, int) else pl.multiple_of(at, 8), 8), :]
 
     fill_middle(pad_ref, own_at, adj_ref, capacity, 3, parts)
-    fill_edge(pad_ref, north_ref, adj_ref, capacity, UPPER, 0, parts)
-    fill_edge(pad_ref, south_ref, adj_ref, capacity, LOWER, 11, parts)
+    odd = is_odd(place_ref)
+    fill_edge(pad_ref, core_ref, cross_ref, odd, adj_ref, capacity, UPPER, 0, parts)
+    fill_edge(pad_ref, cross_ref, core_ref, odd, adj_ref, capacity, LOWER, 11, parts)
 
     def finish(tile, lane, sums):
         live = jnp.where(tile < counts_ref[0, 0], 1.0, 0.0).astype(f32)
@@ -371,9 +384,9 @@
     rows = hidden // count
     place = lax.axis_index("space").astype(jnp.int32).reshape(1, 1)
 
-    north, south = call(edge_kernel, [struct(edge_shape, bf16)] * 2, [VMEM], [own], flops=EDGE_COST)
-    north = passed_along(north, "space", 1)
-    south = passed_along(south, "space", -1)
+    core, cross = call(edge_kernel, [struct(edge_shape, bf16)] * 2, [SMEM, VMEM], [place, own], flops=EDGE_COST)
+    cross = crossed(cross, "space")
+    core = swapped(core, "space", 1)
 
     pad, conv, mixed, act_grad, own_sum = call(
         early_kernel,
@@ -400,13 +413,13 @@
             struct((hidden, LANES)),
         ],
         [SMEM] * 2 + [VMEM] * 8,
-        [wanted, place, north, south, conv, kernel, norm_gain, w_in, mixed, act_grad],
+        [wanted, place, core, cross, conv, kernel, norm_gain, w_in, mixed, act_grad],
         flops=4 * pixels * channels * hidden,
         scratch=[pltpu.VMEM((pixels, channels), f32), pltpu.VMEM((hidden, channels), f32)],
     )
     got = swapped(send, "space", 1)
 
-    grad, grad_north, grad_south, emb = call(
+    grad, core, cross, emb = call(
         back_kernel,
         [
             struct((pixels, channels)),
@@ -414,71 +427,76 @@
             struct(edge_shape, bf16),
             struct((1, channels)),
         ],
-        [SMEM] * 2 + [VMEM] * 9,
-        [counts, pool_weight, pre_grad, w_in, normed, inv, norm_gain, pooled, w_out, layer_scale, own_sum],
+        [SMEM] * 3 + [VMEM] * 9,
+        [place, counts, pool_weight, pre_grad, w_in, normed, inv, norm_gain, pooled, w_out, layer_scale, own_sum],
         flops=2 * pixels * channels * hidden,
     )
-    grad_north = passed_along(grad_north, "space", 1)
-    grad_south = passed_along(grad_south, "space", -1)
-
-    state, pack = call(
-        taps_kernel, [struct((STATE, channels)), struct((STATE, channels), bf16)],
-        [VMEM] * 4, [pad, edge, grad, emb],
-        scratch=[pltpu.VMEM((TAPS, 8, channels), f32)],
-    )
-    for stage in range(min(SEPARATE, stages)):
-        new = swapped(pack, "space", 1 << stage)
-        state, pack = call(
-            state_kernel, [struct((STATE, channels)), struct((STATE, channels), bf16)],
-            [VMEM] * 2, [state, new],
+    cross = crossed(cross, "space")
+    core = swapped(core, "space", 1)
+
+    def merge(parts_, splits):
+        held = sum(keep.shape[0] for keep, _ in parts_)
+        shapes = []
+        for size in [count // 2 for _, count, _, _ in splits] or [held]:
+            shapes += [struct((size, channels)), struct((size, channels), bf16)]
+        operands = [array for pair in parts_ for array in pair]
+        out = call(
+            functools.partial(merge_kernel, splits, len(parts_)), shapes,
+            [SMEM] + [VMEM] * len(operands), [place] + operands,
+            scratch=[pltpu.VMEM((held, channels), f32)],
         )
-
-    for stage in range(1, stages + 1):
-        last = stage == stages
-        with_state = stage >= SEPARATE
-        held = hidden >> stage
-        sent = held if last else held // 2
-        shapes = [
-            struct((sent, channels)),
-            struct((sent + (STATE if with_state else 0), channels), bf16),
-        ]
-        operands = [place, keep, got]
-        if with_state:
-            shapes.append(struct((STATE, channels)))
-            operands.append(state)
-        results = call(
-            functools.partial(
-                merge_kernel, rows, None if last else stage, with_state, stage > SEPARATE, False
-            ),
-            shapes, [SMEM] + [VMEM] * (len(operands) - 1), operands,
-            scratch=[] if last else [pltpu.VMEM((held, channels), f32)],
-        )
-        keep, send = results[:2]
-        if with_state:
-            state = results[2]
-        if not last:
-            got = swapped(send, "space", 1 << stage)
-    embedding = state[TAPS : TAPS + 1]
+        return list(zip(out[0::2], out[1::2]))
+
+    half = hidden // 4
+    (keep_a, send_a), (keep_b, send_b) = merge([(keep, got)], [(0, half, rows, 1), (half, half, 2 * rows, 2)])
+    got_a = swapped(send_a, "space", 2)
+    got_b = swapped(send_b, "space", 4)
+    half //= 2
+    (keep_a, send_a), (keep_b, send_b) = merge(
+        [(keep_a, got_a), (keep_b, got_b)], [(0, half, rows, 2), (half, half, rows, 1)]
+    )
+    got_a = swapped(send_a, "space", 4)
+    got_b = swapped(send_b, "space", 2)
+    held = [(keep_a, got_a), (keep_b, got_b)]
+    for stage in range(3, stages):
+        size = hidden >> stage
+        ((keep, send),) = merge(held, [(0, size, rows, stage)])
+        got = swapped(send, "space", 1 << stage)
+        held = [(keep, got)]
+    ((share, send),) = merge(held, [])
     groups = lax.axis_size("dp")
     bit = 1
     while bit < groups:
         got = swapped(send, "dp", bit)
         bit *= 2
         if bit < groups:
-            keep, send, state = call(
-                functools.partial(merge_kernel, rows, None, True, True, True),
-                [struct(keep.shape), struct(send.shape, bf16), struct(state.shape)],
-                [SMEM] + [VMEM] * 3, [place, keep, got, state],
+            share, send = call(pair_kernel, [struct(share.shape), struct(send.shape, bf16)], [VMEM] * 2, [share, got])
+
+    state, pack = call(
+        taps_kernel, [struct((STATE, channels)), struct((STATE, channels), bf16)],
+        [VMEM] * 4, [pad, edge, grad, emb],
+        scratch=[pltpu.VMEM((TAPS, 8, channels), f32)],
+    )
+    steps = [("space", 1)] + [("dp", 1 << n) for n in range(groups.bit_length() - 1)]
+    steps += [("space", 1 << n) for n in range(1, stages)]
+    for axis, bit in steps:
+        new = swapped(pack, axis, bit)
+        if (axis, bit) != steps[-1]:
+            state, pack = call(
+                functools.partial(state_kernel, axis == "space"),
+                [struct((STATE, channels)), struct((STATE, channels), bf16)],
+                [VMEM] * 2, [state, new],
             )
-    share, tap_grad = call(
-        finish_kernel, [struct((rows, channels)), struct(kernel.shape)],
-        [VMEM] * 3, [keep, got, state],
+
+    share, tap_grad, embedding = call(
+        finish_kernel, [struct((rows, channels)), struct(kernel.shape), struct((1, channels))],
+        [VMEM] * 4, [share, got, state, new],
     )
 
     grad_tiles = call(
         final_kernel, struct((pixels, channels), bf16),
-        [SMEM] * 3 + [VMEM] * 6,
-        [wanted, counts, pool_weight, grad, grad_north, grad_south, kernel, up, slide_cot],
+        [SMEM] * 4 + [VMEM] * 6,
+        [wanted, place, counts, pool_weight, grad, core, cross, kernel, up, slide_cot],
         scratch=[pltpu.VMEM((parts, capacity, 14, 24, LANES), f32)],
     )
     return (

time: 58.8 us -> 51.7 us (0.88)
  the two profiles are of different devices: /device:TPU:1 before, /device:TPU:0 now
where the time goes in v1:
time: 51.7 us; the launch traced here: 51.5 us
  starting transfers between devices  23.2 us (45%)
  Pallas kernels  14.5 us (28%)
  waiting for transfers between devices  11.2 us (22%)
  between operations  1.55 us (3%)
  local copies, waits for them, and re-layouts  0.96 us (2%)
    ppermute x14, starting transfers between devices, swapped(): lax.ppermute(value, axis, [(source, source ^ bit) for source in range(cou...  21.8 us
    pallas_call x15, Pallas kernels, call(): pl.pallas_call(body, out_shape=out_shape, in_specs=in_specs, out_specs=ou...  14.5 us
    ppermute x14, waiting for transfers between devices, swapped(): lax.ppermute(value, axis, [(source, source ^ bit) for source in range(cou...  11.2 us
    ppermute x2, starting transfers between devices, crossed(): lax.ppermute(value, axis, [(n, n + 1) for n in firsts] + [(n + 1, n) for...  1.44 us
  transfers between devices with their start and end apart: 16, of which 6 were waited for; matrix products, arithmetic and copies ran while one was open for 0% of the time, Pallas kernels for 19%

profile of v1, /device:TPU:0, one launch (start us, length us, event | category | flops | bytes accessed | tf_op | source)
XLA Modules:
  0.0 51.5 jit_solution(7907743460324989652)
XLA Ops:
  0.6 0.9 %copy-done.4 = bf16[1,4,8,8,384]{4,3,2,1,0:T(8,128)(2,1)S(1)} copy-done((bf16[1,4,8,8,384]{4,3,2,1,0:T(8,128)(2,1)S(1)}, bf16[1,4,8,8,384]{4,3,2,1,0:T(8,128)(2,1)}, u32[]{:S(2)}) %copy-start.4) | copy-done | bytes 196632
  1.6 0.0 copy-start.6
  1.6 0.0 copy-start.7
  1.6 0.0 copy-start.9
  1.6 0.1 shard_map.138
  1.7 0.0 copy-start.1
  1.7 0.0 copy-start.8
  1.7 0.6 %collective-permute-start = (bf16[4,3,8,384]{3,2,1,0:T(8,128)(2,1)S(1)}, bf16[4,3,8,384]{3,2,1,0:T(8,128)(2,1)S(1)}, u32[]{:S(2)}, u32[]{:S(2)}) collective-permute-start(bf16[4,3,8,384]{3,2,1,0:T(8,128)(2,1)S(1)} %get-tuple-element.47), channel_id=1, source_target_pairs={{0,1},{1,0},{2,3},{3,2},{4,5},{5,4},{6,7},{7,6},{8,9},{9,8},{10,11... | collective-permute-start | bytes 221192 | tf_op jit(solution)/shard_map/ppermute | solution.py:44
  2.3 0.8 %collective-permute-start.1 = (bf16[4,3,8,384]{3,2,1,0:T(8,128)(2,1)S(1)}, bf16[4,3,8,384]{3,2,1,0:T(8,128)(2,1)S(1)}, u32[]{:S(2)}, u32[]{:S(2)}) collective-permute-start(bf16[4,3,8,384]{3,2,1,0:T(8,128)(2,1)S(1)} %get-tuple-element.48), channel_id=1, source_target_pairs={{1,2},{3,4},{5,6},{7,8},{9,10},{11,12},{13,14},{2,1},{4,3},{6,5},{... | collective-permute-start | bytes 221192 | tf_op jit(solution)/shard_map/ppermute | solution.py:50
  3.8 2.3 %shard_map.139 = (f32[3,4,8,24,128]{4,3,2,1,0:T(8,128)S(1)}, f32[256,384]{1,0:T(8,128)S(1)}, bf16[256,512]{1,0:T(8,128)(2,1)S(1)}, f32[256,1536]{1,0:T(8,128)S(1)}, f32[1,384]{1,0:T(1,128)S(1)}) custom-call(s32[4,8]{1,0:T(4,128)S(1)} %bitcast.9, s32[1,1]{1,0:T(1,128)S(6)} %copy.15.counts_ref, f32[1,4]{1,0:T(1,128)S(1)} %copy-done.10, ...), custom_call_target="tpu_custom_call" | custom-call | flops 301989888 | bytes 5060756 | tf_op jit(solution)/shard_map/pallas_call | solution.py:27
  6.1 0.0 collective-permute-done.core_ref
  6.1 0.0 collective-permute-done.1.cross_ref
  6.2 3.8 %shard_map.140 = (f32[3,4,6,24,128]{4,3,2,1,0:T(8,128)S(1)}, f32[256,384]{1,0:T(8,128)S(1)}, f32[256,1]{1,0:T(8,128)S(1)}, bf16[256,1536]{1,0:T(8,128)(2,1)S(1)}...) custom-call(s32[4,8]{1,0:T(4,128)S(1)} %bitcast.10, s32[1,1]{1,0:T(1,128)} %bitcast.place_ref, ...), custom_call_target="tpu_custom_call" | custom-call | flops 603979776 | bytes 8253572 | tf_op jit(solution)/shard_map/pallas_call | solution.py:27
  10.0 4.0 %collective-permute-start.2 = (bf16[768,384]{1,0:T(8,128)(2,1)S(1)}, bf16[768,384]{1,0:T(8,128)(2,1)S(1)}, u32[]{:S(2)}, u32[]{:S(2)}) collective-permute-start(bf16[768,384]{1,0:T(8,128)(2,1)S(1)} %get-tuple-element.53), channel_id=1, source_target_pairs={{0,1},{1,0},{2,3},{3,2},{4,5},{5,4},{6,7},{7,6},{8,9},{9,8},{10,11... | collective-permute-start | bytes 1769480 | tf_op jit(solution)/shard_map/ppermute | solution.py:44
  14.0 1.6 %collective-permute-done.2.refs_1_ = bf16[768,384]{1,0:T(8,128)(2,1)S(1)} collective-permute-done((bf16[768,384]{1,0:T(8,128)(2,1)S(1)}, bf16[768,384]{1,0:T(8,128)(2,1)S(1)}, u32[]{:S(2)}, u32[]{:S(2)}) %collective-permute-start.2) | collective-permute-done | bytes 589856 | tf_op jit(solution)/shard_map/ppermute | solution.py:44
  15.6 0.3 shard_map.141
  15.9 2.0 %collective-permute-start.3 = (bf16[192,384]{1,0:T(8,128)(2,1)S(1)}, bf16[192,384]{1,0:T(8,128)(2,1)S(1)}, u32[]{:S(2)}, u32[]{:S(2)}) collective-permute-start(bf16[192,384]{1,0:T(8,128)(2,1)S(1)} %get-tuple-element.55), channel_id=1, source_target_pairs={{0,2},{1,3},{2,0},{3,1},{4,6},{5,7},{6,4},{7,5},{8,10},{9,11},{10,... | collective-permute-start | bytes 442376 | tf_op jit(solution)/shard_map/ppermute | solution.py:44
  17.8 1.6 %collective-permute-start.4 = (bf16[192,384]{1,0:T(8,128)(2,1)S(1)}, bf16[192,384]{1,0:T(8,128)(2,1)S(1)}, u32[]{:S(2)}, u32[]{:S(2)}) collective-permute-start(bf16[192,384]{1,0:T(8,128)(2,1)S(1)} %get-tuple-element.57), channel_id=1, source_target_pairs={{0,4},{1,5},{2,6},{3,7},{4,0},{5,1},{6,2},{7,3},{8,12},{9,13},{10,... | collective-permute-start | bytes 442376 | tf_op jit(solution)/shard_map/ppermute | solution.py:44
  19.4 2.8 %collective-permute-done.3.refs_1_ = bf16[192,384]{1,0:T(8,128)(2,1)S(1)} collective-permute-done((bf16[192,384]{1,0:T(8,128)(2,1)S(1)}, bf16[192,384]{1,0:T(8,128)(2,1)S(1)}, u32[]{:S(2)}, u32[]{:S(2)}) %collective-permute-start.3) | collective-permute-done | bytes 147488 | tf_op jit(solution)/shard_map/ppermute | solution.py:44
  22.2 1.5 %collective-permute-done.4.refs_3_ = bf16[192,384]{1,0:T(8,128)(2,1)S(1)} collective-permute-done((bf16[192,384]{1,0:T(8,128)(2,1)S(1)}, bf16[192,384]{1,0:T(8,128)(2,1)S(1)}, u32[]{:S(2)}, u32[]{:S(2)}) %collective-permute-start.4) | collective-permute-done | bytes 147488 | tf_op jit(solution)/shard_map/ppermute | solution.py:44
  23.7 0.1 shard_map.142
  23.8 1.6 %collective-permute-start.5 = (bf16[96,384]{1,0:T(8,128)(2,1)S(1)}, bf16[96,384]{1,0:T(8,128)(2,1)S(1)}, u32[]{:S(2)}, u32[]{:S(2)}) collective-permute-start(bf16[96,384]{1,0:T(8,128)(2,1)S(1)} %get-tuple-element.59), channel_id=1, source_target_pairs={{0,4},{1,5},{2,6},{3,7},{4,0},{5,1},{6,2},{7,3},{8,12},{9,13},{10,... | collective-permute-start | bytes 221192 | tf_op jit(solution)/shard_map/ppermute | solution.py:44
  25.4 0.4 collective-permute-start.6
  25.8 1.3 %shard_map.145 = (f32[256,384]{1,0:T(8,128)S(1)}, bf16[4,3,8,384]{3,2,1,0:T(8,128)(2,1)S(1)}, bf16[4,3,8,384]{3,2,1,0:T(8,128)(2,1)S(1)}, f32[1,384]{1,0:T(1,128)S(1)}) custom-call(s32[1,1]{1,0:T(1,128)} %bitcast.place_ref, s32[1,1]{1,0:T(1,128)S(6)} %copy.15.counts_ref, f32[1,4]{1,0:T(1,128)S(1)} %copy-done.10, ...), custom_call_target="tpu_custom_call" | custom-call | flops 301989888 | bytes 4873240 | tf_op jit(solution)/shard_map/pallas_call | solution.py:27
  27.2 2.4 %shard_map.146 = (f32[56,384]{1,0:T(8,128)S(1)}, bf16[56,384]{1,0:T(8,128)(2,1)S(1)}) custom-call(f32[3,4,8,24,128]{4,3,2,1,0:T(8,128)S(1)} %get-tuple-element.66.pad_ref, f32[3,4,6,24,128]{4,3,2,1,0:T(8,128)S(1)} %get-tuple-element.67.edge_ref, f32[256,384]{1,0:T(8,128)S(1)} %get-tuple-element.73.grad_ref, f32[1,384]{1,0:T(1,128)S(1)} %get-tuple-element.74.emb_ref), custom_call_target="tpu_custom_call" | custom-call | bytes 2588160 | tf_op jit(solution)/shard_map/pallas_call | solution.py:27
  29.6 0.1 collective-permute-start.9
  29.7 1.2 %collective-permute-done.9.got_ref = bf16[56,384]{1,0:T(8,128)(2,1)S(1)} collective-permute-done((bf16[56,384]{1,0:T(8,128)(2,1)S(1)}, bf16[56,384]{1,0:T(8,128)(2,1)S(1)}, u32[]{:S(2)}, u32[]{:S(2)}) %collective-permute-start.9) | collective-permute-done | bytes 43040 | tf_op jit(solution)/shard_map/ppermute | solution.py:44
  31.0 1.6 %collective-permute-start.10 = (bf16[56,384]{1,0:T(8,128)(2,1)S(1)}, bf16[56,384]{1,0:T(8,128)(2,1)S(1)}, u32[]{:S(2)}, u32[]{:S(2)}) collective-permute-start(bf16[56,384]{1,0:T(8,128)(2,1)S(1)} %get-tuple-element.78), channel_id=1, source_target_pairs={{0,16},{16,0},{1,17},{17,1},{2,18},{18,2},{3,19},{19,3},{4,20},{20... | collective-permute-start | bytes 129032 | tf_op jit(solution)/shard_map/ppermute | solution.py:44
  32.5 0.0 collective-permute-done.5.refs_1_
  32.5 0.0 collective-permute-done.6.refs_3_
  32.5 0.1 shard_map.143
  32.6 2.7 %collective-permute-start.7 = (bf16[96,384]{1,0:T(8,128)(2,1)S(1)}, bf16[96,384]{1,0:T(8,128)(2,1)S(1)}, u32[]{:S(2)}, u32[]{:S(2)}) collective-permute-start(bf16[96,384]{1,0:T(8,128)(2,1)S(1)} %get-tuple-element.63), channel_id=1, source_target_pairs={{0,8},{1,9},{2,10},{3,11},{4,12},{5,13},{6,14},{7,15},{8,0},{9,1},... | collective-permute-start | bytes 221192 | tf_op jit(solution)/shard_map/ppermute | solution.py:44
  35.2 0.0 collective-permute-done.10.got_ref
  35.3 1.5 %collective-permute-start.11 = (bf16[56,384]{1,0:T(8,128)(2,1)S(1)}, bf16[56,384]{1,0:T(8,128)(2,1)S(1)}, u32[]{:S(2)}, u32[]{:S(2)}) collective-permute-start(bf16[56,384]{1,0:T(8,128)(2,1)S(1)} %get-tuple-element.80), channel_id=1, source_target_pairs={{0,2},{1,3},{2,0},{3,1},{4,6},{5,7},{6,4},{7,5},{8,10},{9,11},{10,... | collective-permute-start | bytes 129032 | tf_op jit(solution)/shard_map/ppermute | solution.py:44
  36.8 2.6 %collective-permute-done.11.got_ref = bf16[56,384]{1,0:T(8,128)(2,1)S(1)} collective-permute-done((bf16[56,384]{1,0:T(8,128)(2,1)S(1)}, bf16[56,384]{1,0:T(8,128)(2,1)S(1)}, u32[]{:S(2)}, u32[]{:S(2)}) %collective-permute-start.11) | collective-permute-done | bytes 43040 | tf_op jit(solution)/shard_map/ppermute | solution.py:44
  39.4 0.5 collective-permute-start.12
  39.9 0.0 collective-permute-start.14
  39.9 0.7 %collective-permute-start.15 = (bf16[4,3,8,384]{3,2,1,0:T(8,128)(2,1)S(1)}, bf16[4,3,8,384]{3,2,1,0:T(8,128)(2,1)S(1)}, u32[]{:S(2)}, u32[]{:S(2)}) collective-permute-start(bf16[4,3,8,384]{3,2,1,0:T(8,128)(2,1)S(1)} %get-tuple-element.87), channel_id=1, source_target_pairs={{1,2},{3,4},{5,6},{7,8},{9,10},{11,12},{13,14},{2,1},{4,3},{6,5},{... | collective-permute-start | bytes 221192 | tf_op jit(solution)/shard_map/ppermute | solution.py:50
  40.6 0.0 collective-permute-done.7.refs_1_
  40.6 1.3 %collective-permute-start.8 = (bf16[96,384]{1,0:T(8,128)(2,1)S(1)}, bf16[96,384]{1,0:T(8,128)(2,1)S(1)}, u32[]{:S(2)}, u32[]{:S(2)}) collective-permute-start(bf16[96,384]{1,0:T(8,128)(2,1)S(1)} %get-tuple-element.65), channel_id=1, source_target_pairs={{0,16},{16,0},{1,17},{17,1},{2,18},{18,2},{3,19},{19,3},{4,20},{20... | collective-permute-start | bytes 221192 | tf_op jit(solution)/shard_map/ppermute | solution.py:44
  42.0 1.5 %collective-permute-done.12.got_ref = bf16[56,384]{1,0:T(8,128)(2,1)S(1)} collective-permute-done((bf16[56,384]{1,0:T(8,128)(2,1)S(1)}, bf16[56,384]{1,0:T(8,128)(2,1)S(1)}, u32[]{:S(2)}, u32[]{:S(2)}) %collective-permute-start.12) | collective-permute-done | bytes 43040 | tf_op jit(solution)/shard_map/ppermute | solution.py:44
  43.5 4.0 %collective-permute-start.13 = (bf16[56,384]{1,0:T(8,128)(2,1)S(1)}, bf16[56,384]{1,0:T(8,128)(2,1)S(1)}, u32[]{:S(2)}, u32[]{:S(2)}) collective-permute-start(bf16[56,384]{1,0:T(8,128)(2,1)S(1)} %get-tuple-element.84), channel_id=1, source_target_pairs={{0,8},{1,9},{2,10},{3,11},{4,12},{5,13},{6,14},{7,15},{8,0},{9,1},... | collective-permute-start | bytes 129032 | tf_op jit(solution)/shard_map/ppermute | solution.py:44
  47.5 0.0 collective-permute-done.14.core_ref
  47.5 0.0 collective-permute-done.15.cross_ref
  47.5 3.2 %shard_map.152 = bf16[256,384]{1,0:T(8,128)(2,1)} custom-call(s32[4,8]{1,0:T(4,128)S(1)} %bitcast.11, s32[1,1]{1,0:T(1,128)} %bitcast.place_ref, s32[1,1]{1,0:T(1,128)S(6)} %copy.15.counts_ref, f32[1,4]{1,0:T(1,128)S(1)} %copy-done.10, f32[256,384]{1,0:T(8,128)S(1)} %get-tuple-element.73.grad_ref, ...), custom_call_target="tpu_custom_call" | custom-call | bytes 1010840 | tf_op jit(solution)/shard_map/pallas_call | solution.py:27
  50.8 0.0 collective-permute-done.13.new_ref
  50.8 0.0 collective-permute-done.8.got_ref
  50.8 0.7 %shard_map.151 = (f32[96,384]{1,0:T(8,128)}, f32[7,7,384]{2,1,0:T(8,128)}, f32[1,384]{1,0:T(1,128)}) custom-call(f32[96,384]{1,0:T(8,128)S(1)} %get-tuple-element.64.keep_ref, bf16[96,384]{1,0:T(8,128)(2,1)S(1)} %collective-permute-done.8.got_ref, f32[56,384]{1,0:T(8,128)S(1)} %get-tuple-element.83.state_ref, bf16[56,384]{1,0:T(8,128)(2,1)S(1)} %collective-permute-done.13.new_ref), custom_call_target="tpu_custom_call" | custom-call | bytes 574464 | tf_op jit(solution)/shard_map/pallas_call | solution.py:27
  (21 shorter events, 0.2 us)
Async XLA Ops:
  0.6 0.9 %copy-start.4 = (bf16[1,4,8,8,384]{4,3,2,1,0:T(8,128)(2,1)S(1)}, bf16[1,4,8,8,384]{4,3,2,1,0:T(8,128)(2,1)}, u32[]{:S(2)}) copy-start(bf16[1,4,8,8,384]{4,3,2,1,0:T(8,128)(2,1)} %param.11) | copy-start | bytes 589828
  1.6 2.1 %copy-start = (bf16[1536,384]{1,0:T(8,128)(2,1)S(1)}, bf16[1536,384]{1,0:T(8,128)(2,1)}, u32[]{:S(2)}) copy-start(bf16[1536,384]{1,0:T(8,128)(2,1)} %w_out_ref.3) | copy-start | bytes 3538948
  1.6 2.2 %copy-start.2 = (bf16[1,4,8,8,384]{4,3,2,1,0:T(8,128)(2,1)S(1)}, bf16[1,4,8,8,384]{4,3,2,1,0:T(8,128)(2,1)}, u32[]{:S(2)}) copy-start(bf16[1,4,8,8,384]{4,3,2,1,0:T(8,128)(2,1)} %param.12) | copy-start | bytes 589828
  1.6 2.2 %copy-start.3 = (f32[7,7,384]{2,1,0:T(8,128)S(1)}, f32[7,7,384]{2,1,0:T(8,128)}, u32[]{:S(2)}) copy-start(f32[7,7,384]{2,1,0:T(8,128)} %kern_ref.5) | copy-start | bytes 225796
  1.6 2.2 %copy-start.5 = (bf16[1,4,8,8,384]{4,3,2,1,0:T(8,128)(2,1)S(1)}, bf16[1,4,8,8,384]{4,3,2,1,0:T(8,128)(2,1)}, u32[]{:S(2)}) copy-start(bf16[1,4,8,8,384]{4,3,2,1,0:T(8,128)(2,1)} %param.11) | copy-start | bytes 589828
  1.6 2.2 %copy-start.6 = (s32[1,4,8]{2,1,0:T(4,128)S(1)}, s32[1,4,8]{2,1,0:T(4,128)}, u32[]{:S(2)}) copy-start(s32[1,4,8]{2,1,0:T(4,128)} %param.15) | copy-start | bytes 388
  1.6 2.2 %copy-start.7 = (f32[384]{0:T(512)S(1)}, f32[384]{0:T(512)}, u32[]{:S(2)}) copy-start(f32[384]{0:T(512)} %scale_ref.3) | copy-start | bytes 4612
  1.6 2.2 %copy-start.9 = (f32[1,384]{1,0:T(1,128)S(1)}, f32[1,384]{1,0:T(1,128)}, u32[]{:S(2)}) copy-start(f32[1,384]{1,0:T(1,128)} %cot_ref.3) | copy-start | bytes 4612
  1.6 2.2 %copy-start.10 = (f32[1,4]{1,0:T(1,128)S(1)}, f32[1,4]{1,0:T(1,128)}, u32[]{:S(2)}) copy-start(f32[1,4]{1,0:T(1,128)} %pool_ref.5) | copy-start | bytes 52
  1.7 4.5 %copy-start.1 = (bf16[384,1536]{1,0:T(8,128)(2,1)S(1)}, bf16[384,1536]{1,0:T(8,128)(2,1)}, u32[]{:S(2)}) copy-start(bf16[384,1536]{1,0:T(8,128)(2,1)} %w_in_ref.3) | copy-start | bytes 3538948
  1.7 4.5 %copy-start.8 = (f32[384]{0:T(512)S(1)}, f32[384]{0:T(512)}, u32[]{:S(2)}) copy-start(f32[384]{0:T(512)} %gain_ref.3) | copy-start | bytes 4612
  1.7 4.4 %collective-permute-start = (bf16[4,3,8,384]{3,2,1,0:T(8,128)(2,1)S(1)}, bf16[4,3,8,384]{3,2,1,0:T(8,128)(2,1)S(1)}, u32[]{:S(2)}, u32[]{:S(2)}) collective-permute-start(bf16[4,3,8,384]{3,2,1,0:T(8,128)(2,1)S(1)} %get-tuple-element.47), channel_id=1, source_target_pairs={{0,1},{1,0},{2,3},{3,2},{4,5},{5,4},{6,7},{7,6},{8,9},{9,8},{10,11... | collective-permute-start | bytes 221192 | tf_op jit(solution)/shard_map/ppermute | solution.py:44
  2.3 3.9 %collective-permute-start.1 = (bf16[4,3,8,384]{3,2,1,0:T(8,128)(2,1)S(1)}, bf16[4,3,8,384]{3,2,1,0:T(8,128)(2,1)S(1)}, u32[]{:S(2)}, u32[]{:S(2)}) collective-permute-start(bf16[4,3,8,384]{3,2,1,0:T(8,128)(2,1)S(1)} %get-tuple-element.48), channel_id=1, source_target_pairs={{1,2},{3,4},{5,6},{7,8},{9,10},{11,12},{13,14},{2,1},{4,3},{6,5},{... | collective-permute-start | bytes 221192 | tf_op jit(solution)/shard_map/ppermute | solution.py:50
  10.0 5.6 %collective-permute-start.2 = (bf16[768,384]{1,0:T(8,128)(2,1)S(1)}, bf16[768,384]{1,0:T(8,128)(2,1)S(1)}, u32[]{:S(2)}, u32[]{:S(2)}) collective-permute-start(bf16[768,384]{1,0:T(8,128)(2,1)S(1)} %get-tuple-element.53), channel_id=1, source_target_pairs={{0,1},{1,0},{2,3},{3,2},{4,5},{5,4},{6,7},{7,6},{8,9},{9,8},{10,11... | collective-permute-start | bytes 1769480 | tf_op jit(solution)/shard_map/ppermute | solution.py:44
  15.9 6.4 %collective-permute-start.3 = (bf16[192,384]{1,0:T(8,128)(2,1)S(1)}, bf16[192,384]{1,0:T(8,128)(2,1)S(1)}, u32[]{:S(2)}, u32[]{:S(2)}) collective-permute-start(bf16[192,384]{1,0:T(8,128)(2,1)S(1)} %get-tuple-element.55), channel_id=1, source_target_pairs={{0,2},{1,3},{2,0},{3,1},{4,6},{5,7},{6,4},{7,5},{8,10},{9,11},{10,... | collective-permute-start | bytes 442376 | tf_op jit(solution)/shard_map/ppermute | solution.py:44
  17.8 5.8 %collective-permute-start.4 = (bf16[192,384]{1,0:T(8,128)(2,1)S(1)}, bf16[192,384]{1,0:T(8,128)(2,1)S(1)}, u32[]{:S(2)}, u32[]{:S(2)}) collective-permute-start(bf16[192,384]{1,0:T(8,128)(2,1)S(1)} %get-tuple-element.57), channel_id=1, source_target_pairs={{0,4},{1,5},{2,6},{3,7},{4,0},{5,1},{6,2},{7,3},{8,12},{9,13},{10,... | collective-permute-start | bytes 442376 | tf_op jit(solution)/shard_map/ppermute | solution.py:44
  23.8 8.7 %collective-permute-start.5 = (bf16[96,384]{1,0:T(8,128)(2,1)S(1)}, bf16[96,384]{1,0:T(8,128)(2,1)S(1)}, u32[]{:S(2)}, u32[]{:S(2)}) collective-permute-start(bf16[96,384]{1,0:T(8,128)(2,1)S(1)} %get-tuple-element.59), channel_id=1, source_target_pairs={{0,4},{1,5},{2,6},{3,7},{4,0},{5,1},{6,2},{7,3},{8,12},{9,13},{10,... | collective-permute-start | bytes 221192 | tf_op jit(solution)/shard_map/ppermute | solution.py:44
  25.4 7.1 %collective-permute-start.6 = (bf16[96,384]{1,0:T(8,128)(2,1)S(1)}, bf16[96,384]{1,0:T(8,128)(2,1)S(1)}, u32[]{:S(2)}, u32[]{:S(2)}) collective-permute-start(bf16[96,384]{1,0:T(8,128)(2,1)S(1)} %get-tuple-element.61), channel_id=1, source_target_pairs={{0,2},{1,3},{2,0},{3,1},{4,6},{5,7},{6,4},{7,5},{8,10},{9,11},{10,... | collective-permute-start | bytes 221192 | tf_op jit(solution)/shard_map/ppermute | solution.py:44
  29.6 1.3 %collective-permute-start.9 = (bf16[56,384]{1,0:T(8,128)(2,1)S(1)}, bf16[56,384]{1,0:T(8,128)(2,1)S(1)}, u32[]{:S(2)}, u32[]{:S(2)}) collective-permute-start(bf16[56,384]{1,0:T(8,128)(2,1)S(1)} %get-tuple-element.76), channel_id=1, source_target_pairs={{0,1},{1,0},{2,3},{3,2},{4,5},{5,4},{6,7},{7,6},{8,9},{9,8},{10,11... | collective-permute-start | bytes 129032 | tf_op jit(solution)/shard_map/ppermute | solution.py:44
  31.0 4.3 %collective-permute-start.10 = (bf16[56,384]{1,0:T(8,128)(2,1)S(1)}, bf16[56,384]{1,0:T(8,128)(2,1)S(1)}, u32[]{:S(2)}, u32[]{:S(2)}) collective-permute-start(bf16[56,384]{1,0:T(8,128)(2,1)S(1)} %get-tuple-element.78), channel_id=1, source_target_pairs={{0,16},{16,0},{1,17},{17,1},{2,18},{18,2},{3,19},{19,3},{4,20},{20... | collective-permute-start | bytes 129032 | tf_op jit(solution)/shard_map/ppermute | solution.py:44
  32.6 8.0 %collective-permute-start.7 = (bf16[96,384]{1,0:T(8,128)(2,1)S(1)}, bf16[96,384]{1,0:T(8,128)(2,1)S(1)}, u32[]{:S(2)}, u32[]{:S(2)}) collective-permute-start(bf16[96,384]{1,0:T(8,128)(2,1)S(1)} %get-tuple-element.63), channel_id=1, source_target_pairs={{0,8},{1,9},{2,10},{3,11},{4,12},{5,13},{6,14},{7,15},{8,0},{9,1},... | collective-permute-start | bytes 221192 | tf_op jit(solution)/shard_map/ppermute | solution.py:44
  35.3 4.1 %collective-permute-start.11 = (bf16[56,384]{1,0:T(8,128)(2,1)S(1)}, bf16[56,384]{1,0:T(8,128)(2,1)S(1)}, u32[]{:S(2)}, u32[]{:S(2)}) collective-permute-start(bf16[56,384]{1,0:T(8,128)(2,1)S(1)} %get-tuple-element.80), channel_id=1, source_target_pairs={{0,2},{1,3},{2,0},{3,1},{4,6},{5,7},{6,4},{7,5},{8,10},{9,11},{10,... | collective-permute-start | bytes 129032 | tf_op jit(solution)/shard_map/ppermute | solution.py:44
  39.4 4.1 %collective-permute-start.12 = (bf16[56,384]{1,0:T(8,128)(2,1)S(1)}, bf16[56,384]{1,0:T(8,128)(2,1)S(1)}, u32[]{:S(2)}, u32[]{:S(2)}) collective-permute-start(bf16[56,384]{1,0:T(8,128)(2,1)S(1)} %get-tuple-element.82), channel_id=1, source_target_pairs={{0,4},{1,5},{2,6},{3,7},{4,0},{5,1},{6,2},{7,3},{8,12},{9,13},{10,... | collective-permute-start | bytes 129032 | tf_op jit(solution)/shard_map/ppermute | solution.py:44
  39.9 7.6 %collective-permute-start.14 = (bf16[4,3,8,384]{3,2,1,0:T(8,128)(2,1)S(1)}, bf16[4,3,8,384]{3,2,1,0:T(8,128)(2,1)S(1)}, u32[]{:S(2)}, u32[]{:S(2)}) collective-permute-start(bf16[4,3,8,384]{3,2,1,0:T(8,128)(2,1)S(1)} %get-tuple-element.86), channel_id=1, source_target_pairs={{0,1},{1,0},{2,3},{3,2},{4,5},{5,4},{6,7},{7,6},{8,9},{9,8},{10,11... | collective-permute-start | bytes 221192 | tf_op jit(solution)/shard_map/ppermute | solution.py:44
  39.9 7.6 %collective-permute-start.15 = (bf16[4,3,8,384]{3,2,1,0:T(8,128)(2,1)S(1)}, bf16[4,3,8,384]{3,2,1,0:T(8,128)(2,1)S(1)}, u32[]{:S(2)}, u32[]{:S(2)}) collective-permute-start(bf16[4,3,8,384]{3,2,1,0:T(8,128)(2,1)S(1)} %get-tuple-element.87), channel_id=1, source_target_pairs={{1,2},{3,4},{5,6},{7,8},{9,10},{11,12},{13,14},{2,1},{4,3},{6,5},{... | collective-permute-start | bytes 221192 | tf_op jit(solution)/shard_map/ppermute | solution.py:50
  40.6 10.2 %collective-permute-start.8 = (bf16[96,384]{1,0:T(8,128)(2,1)S(1)}, bf16[96,384]{1,0:T(8,128)(2,1)S(1)}, u32[]{:S(2)}, u32[]{:S(2)}) collective-permute-start(bf16[96,384]{1,0:T(8,128)(2,1)S(1)} %get-tuple-element.65), channel_id=1, source_target_pairs={{0,16},{16,0},{1,17},{17,1},{2,18},{18,2},{3,19},{19,3},{4,20},{20... | collective-permute-start | bytes 221192 | tf_op jit(solution)/shard_map/ppermute | solution.py:44
  43.5 7.3 %collective-permute-start.13 = (bf16[56,384]{1,0:T(8,128)(2,1)S(1)}, bf16[56,384]{1,0:T(8,128)(2,1)S(1)}, u32[]{:S(2)}, u32[]{:S(2)}) collective-permute-start(bf16[56,384]{1,0:T(8,128)(2,1)S(1)} %get-tuple-element.84), channel_id=1, source_target_pairs={{0,8},{1,9},{2,10},{3,11},{4,12},{5,13},{6,14},{7,15},{8,0},{9,1},... | collective-permute-start | bytes 129032 | tf_op jit(solution)/shard_map/ppermute | solution.py:44

commit v2 on v1

--- a/solution.py
+++ b/solution.py
@@ -18,6 +18,8 @@
 HBM = pl.BlockSpec(memory_space=pltpu.HBM)
 STATE = 56
 TAPS = 49
+CHUNK = 384
+BACK_CHUNK = 512
 EDGE_COST = 5_000_000_000
 
 
@@ -85,6 +87,10 @@
                 place(pad_ref, tile, first_row + row, part, value, parts)
 
 
+def is_live(counts_ref, tile):
+    return jnp.where(tile < counts_ref[...], 1.0, 0.0).astype(f32)
+
+
 def is_odd(place_ref):
     return lax.rem(place_ref[0, 0], 2).astype(f32)
 
@@ -95,7 +101,7 @@
 def convolve(pads, tap_row, finish, capacity, parts):
     for lane in range(parts):
 
-        def one_tile(tile, _):
+        def one_tile(tile):
             sums = [None] * 8
             for col in range(7):
                 taps = [tap_row(row, col, lane) for row in range(7)]
@@ -110,7 +116,8 @@
             finish(tile, lane, sums)
             return 0
 
-        lax.fori_loop(0, capacity, one_tile, 0)
+        for tile in range(capacity):
+            one_tile(tile)
 
 
 def lanes(lane):
@@ -122,7 +129,7 @@
     cross_ref[...] = (last * odd + first * (1.0 - odd)).astype(bf16)
 
 
-def edge_kernel(place_ref, tiles_ref, core_ref, cross_ref):
+def edge_kernel(place_ref, counts_ref, tiles_ref, core_ref, cross_ref):
     swap_edges(
         tiles_ref[:, 5:8].astype(f32), tiles_ref[:, 0:3].astype(f32), is_odd(place_ref), core_ref, cross_ref
     )
@@ -139,7 +146,7 @@
     own_sum = jnp.zeros((1, channels), f32)
     scale = scale_ref[...].reshape(1, channels)
     for tile in range(capacity):
-        live = jnp.where(tile < counts_ref[0, 0], 1.0, 0.0).astype(f32)
+        live = is_live(counts_ref, tile)
         pool = pool_ref[0, tile]
         rows = slice(tile * pixels, (tile + 1) * pixels)
         out_grad = live * (up_ref[rows, :].astype(f32) + pool * cot_ref[...] * 0.125)
@@ -175,8 +182,8 @@
 
 
 def forward_kernel(
-    rows, adj_ref, place_ref, core_ref, cross_ref, conv_ref, kern_ref, gain_ref, w_in_ref, mixed_ref, act_grad_ref,
-    edge_ref, normed_ref, inv_ref, pre_grad_ref, keep_ref, send_ref, pooled_ref, whole_ref, weight_ref,
+    rows, adj_ref, place_ref, core_ref, cross_ref, conv_ref, kern_ref, gain_ref, w_in_ref, mixed_ref,
+    edge_ref, normed_ref, inv_ref, pre_ref, cdf_ref, keep_ref, send_ref, pooled_ref, whole_ref,
 ):
     capacity, parts = adj_ref.shape[0], conv_ref.shape[1] // LANES
     channels = conv_ref.shape[1]
@@ -206,31 +213,52 @@
     inv_ref[...] = inv_std
     lifted = (normed * gain_ref[...].reshape(1, channels)).astype(bf16)
     hidden = w_in_ref.shape[1]
-    chunk = hidden // 4 if hidden % 512 == 0 else hidden
+    side = lax.rem(place_ref[0, 0], 2)
+    chunk = CHUNK if hidden % CHUNK == 0 and CHUNK % (2 * rows) == 0 else hidden
+
+    def project(first):
+        return jnp.dot(lifted, w_in_ref[:, first : first + chunk], preferred_element_type=f32)
+
+    following = project(0)
     for first in range(0, hidden, chunk):
         at = slice(first, first + chunk)
-        pre = jnp.dot(lifted, w_in_ref[:, at], preferred_element_type=f32)
+        pre = following
+        if first + chunk < hidden:
+            following = project(first + chunk)
         cdf = 0.5 * (1.0 + lax.erf(pre * sqrt_half))
+        pre_ref[:, at] = pre
+        cdf_ref[:, at] = cdf
         activated = (pre * cdf).astype(bf16)
-        density = jnp.exp(-0.5 * pre * pre) * inv_root_two_pi
-        pre_grad_ref[:, at] = (act_grad_ref[:, at] * (cdf + pre * density)).astype(bf16)
         both = lax.dot_general(
             activated, mixed_ref[...], (((0,), (0,)), ((), ())), preferred_element_type=f32
         )
-        weight_ref[at, :] = both[:, 0:channels]
         pooled_ref[at, :] = both[:, channels:]
-    split_pieces(weight_ref, rows, place_ref, 0, keep_ref, send_ref)
+        for block in range(0, chunk, 2 * rows):
+            even = both[block : block + rows, 0:channels]
+            odd_rows = both[block + rows : block + 2 * rows, 0:channels]
+            out = pl.ds((first + block) // 2, rows)
+            keep_ref[out, :] = jnp.where(side == 0, even, odd_rows)
+            send_ref[out, :] = jnp.where(side == 0, odd_rows, even).astype(bf16)
 
 
 def back_kernel(
-    place_ref, counts_ref, pool_ref, pre_grad_ref, w_in_ref, normed_ref, inv_ref, gain_ref, pooled_ref, w_out_ref,
+    place_ref, counts_ref, pool_ref, pre_ref, cdf_ref, act_grad_ref, w_in_ref, normed_ref, inv_ref, gain_ref, pooled_ref, w_out_ref,
     scale_ref, own_sum_ref, grad_ref, core_ref, cross_ref, emb_ref,
 ):
     channels = normed_ref.shape[1]
     capacity = core_ref.shape[0]
-    lift = lax.dot_general(
-        pre_grad_ref[...], w_in_ref[...], (((1,), (1,)), ((), ())), preferred_element_type=f32
-    )
+    hidden = w_in_ref.shape[1]
+    chunk = BACK_CHUNK if hidden % BACK_CHUNK == 0 else hidden
+    lift = None
+    for first in range(0, hidden, chunk):
+        at = slice(first, first + chunk)
+        pre = pre_ref[:, at]
+        density = jnp.exp(-0.5 * pre * pre) * inv_root_two_pi
+        pre_grad = (act_grad_ref[:, at] * (cdf_ref[:, at] + pre * density)).astype(bf16)
+        term = lax.dot_general(
+            pre_grad, w_in_ref[:, at], (((1,), (1,)), ((), ())), preferred_element_type=f32
+        )
+        lift = term if lift is None else lift + term
     grad_normed = lift * gain_ref[...].reshape(1, channels)
     normed = normed_ref[...]
     grad = inv_ref[...] * (
@@ -244,7 +272,7 @@
     column = lax.broadcasted_iota(jnp.int32, (1, LANES), 1)
     weights = jnp.zeros((1, LANES), f32)
     for tile in range(capacity):
-        amount = jnp.where(tile < counts_ref[0, 0], pool_ref[0, tile], 0.0)
+        amount = is_live(counts_ref, tile) * pool_ref[0, tile]
         weights = jnp.where(column == tile, amount, weights)
     hidden = jnp.sum(pooled_ref[...] * weights, axis=1, keepdims=True)
     mixed = jnp.sum(hidden * w_out_ref[...].astype(f32), axis=0, keepdims=True)
@@ -271,7 +299,9 @@
                             sums[tap] = sums[tap] + window * grads[out]
                 return tuple(sums)
 
-            sums = lax.fori_loop(0, capacity, one_tile, tuple(jnp.zeros((8, LANES), f32) for _ in range(7)))
+            sums = tuple(jnp.zeros((8, LANES), f32) for _ in range(7))
+            for tile in range(capacity):
+                sums = one_tile(tile, sums)
             for row in range(7):
                 part_ref[row * 7 + col, :, lanes(lane)] = sums[row]
             return 0
@@ -337,31 +367,47 @@
     emb_ref[...] = total[TAPS : TAPS + 1, :]
 
 
-def final_kernel(
-    adj_ref, place_ref, counts_ref, pool_ref, grad_ref, core_ref, cross_ref, kern_ref, up_ref, cot_ref,
-    out_ref, pad_ref,
-):
+def middle_kernel(adj_ref, grad_ref, kern_ref, out_ref, pad_ref):
     capacity, parts = adj_ref.shape[0], grad_ref.shape[1] // LANES
 
     def own_at(tile, row):
         at = tile * 64 + row * 8
         return grad_ref[pl.ds(at if isinstance(at, int) else pl.multiple_of(at, 8), 8), :]
 
-    fill_middle(pad_ref, own_at, adj_ref, capacity, 3, parts)
+    fill_middle(pad_ref, own_at, adj_ref, capacity, 0, parts)
+
+    def finish(tile, lane, sums):
+        for row in range(8):
+            out_ref[pl.ds(tile * 64 + row * 8, 8), lanes(lane)] = sums[row]
+
+    convolve(
+        [(pad_ref, 8, 3)],
+        lambda row, col, lane: kern_ref[6 - row, 6 - col : 7 - col, lanes(lane)],
+        finish, capacity, parts,
+    )
+
+
+def outer_kernel(
+    adj_ref, place_ref, counts_ref, pool_ref, part_ref, core_ref, cross_ref, kern_ref, up_ref, cot_ref,
+    out_ref, pad_ref,
+):
+    capacity, parts = adj_ref.shape[0], part_ref.shape[1] // LANES
     odd = is_odd(place_ref)
     fill_edge(pad_ref, core_ref, cross_ref, odd, adj_ref, capacity, UPPER, 0, parts)
-    fill_edge(pad_ref, cross_ref, core_ref, odd, adj_ref, capacity, LOWER, 11, parts)
+    fill_edge(pad_ref, cross_ref, core_ref, odd, adj_ref, capacity, LOWER, 3, parts)
 
     def finish(tile, lane, sums):
-        live = jnp.where(tile < counts_ref[0, 0], 1.0, 0.0).astype(f32)
+        live = is_live(counts_ref, tile)
         extra = pool_ref[0, tile] * cot_ref[:, lanes(lane)] * 0.125
         for row in range(8):
             at = pl.ds(tile * 64 + row * 8, 8)
-            out_grad = live * (up_ref[at, lanes(lane)].astype(f32) + extra)
-            out_ref[at, lanes(lane)] = (live * (out_grad + sums[row])).astype(bf16)
+            total = live * (up_ref[at, lanes(lane)].astype(f32) + extra) + part_ref[at, lanes(lane)]
+            if sums[row] is not None:
+                total = total + sums[row]
+            out_ref[at, lanes(lane)] = (live * total).astype(bf16)
 
     convolve(
-        [(pad_ref, 14, 0)],
+        [(pad_ref.at[:, :, 0:3], 3, 0), (pad_ref.at[:, :, 3:6], 3, 11)],
         lambda row, col, lane: kern_ref[6 - row, 6 - col : 7 - col, lanes(lane)],
         finish, capacity, parts,
     )
@@ -384,7 +430,10 @@
     rows = hidden // count
     place = lax.axis_index("space").astype(jnp.int32).reshape(1, 1)
 
-    core, cross = call(edge_kernel, [struct(edge_shape, bf16)] * 2, [SMEM, VMEM], [place, own], flops=EDGE_COST)
+    core, cross = call(
+        edge_kernel, [struct(edge_shape, bf16)] * 2, [SMEM, VMEM, VMEM], [place, counts, own],
+        flops=EDGE_COST,
+    )
     cross = crossed(cross, "space")
     core = swapped(core, "space", 1)
 
@@ -397,25 +446,26 @@
             struct((pixels, hidden)),
             struct((1, channels)),
         ],
-        [SMEM] * 3 + [VMEM] * 6,
+        [SMEM, VMEM, SMEM] + [VMEM] * 6,
         [wanted, counts, pool_weight, slide_cot, layer_scale, kernel, own, up, w_out],
         flops=2 * pixels * channels * hidden,
     )
-    edge, normed, inv, pre_grad, keep, send, pooled = call(
+    edge, normed, inv, pre, cdf, keep, send, pooled = call(
         functools.partial(forward_kernel, rows),
         [
             struct((parts, capacity, 6, 24, LANES)),
             struct((pixels, channels)),
             struct((pixels, 1)),
-            struct((pixels, hidden), bf16),
+            struct((pixels, hidden)),
+            struct((pixels, hidden)),
             struct((hidden // 2, channels)),
             struct((hidden // 2, channels), bf16),
             struct((hidden, LANES)),
         ],
-        [SMEM] * 2 + [VMEM] * 8,
-        [wanted, place, core, cross, conv, kernel, norm_gain, w_in, mixed, act_grad],
+        [SMEM] * 2 + [VMEM] * 7,
+        [wanted, place, core, cross, conv, kernel, norm_gain, w_in, mixed],
         flops=4 * pixels * channels * hidden,
-        scratch=[pltpu.VMEM((pixels, channels), f32), pltpu.VMEM((hidden, channels), f32)],
+        scratch=[pltpu.VMEM((pixels, channels), f32)],
     )
     got = swapped(send, "space", 1)
 
@@ -427,8 +477,8 @@
             struct(edge_shape, bf16),
             struct((1, channels)),
         ],
-        [SMEM] * 3 + [VMEM] * 9,
-        [place, counts, pool_weight, pre_grad, w_in, normed, inv, norm_gain, pooled, w_out, layer_scale, own_sum],
+        [SMEM, VMEM, SMEM] + [VMEM] * 11,
+        [place, counts, pool_weight, pre, cdf, act_grad, w_in, normed, inv, norm_gain, pooled, w_out, layer_scale, own_sum],
         flops=2 * pixels * channels * hidden,
     )
     cross = crossed(cross, "space")
@@ -493,11 +543,15 @@
         [VMEM] * 4, [share, got, state, new],
     )
 
+    part = call(
+        middle_kernel, struct((pixels, channels)), [SMEM] + [VMEM] * 2, [wanted, grad, kernel],
+        scratch=[pltpu.VMEM((parts, capacity, 8, 24, LANES), f32)],
+    )
     grad_tiles = call(
-        final_kernel, struct((pixels, channels), bf16),
-        [SMEM] * 4 + [VMEM] * 6,
-        [wanted, place, counts, pool_weight, grad, core, cross, kernel, up, slide_cot],
-        scratch=[pltpu.VMEM((parts, capacity, 14, 24, LANES), f32)],
+        outer_kernel, struct((pixels, channels), bf16),
+        [SMEM] * 2 + [VMEM, SMEM] + [VMEM] * 6,
+        [wanted, place, counts, pool_weight, part, core, cross, kernel, up, slide_cot],
+        scratch=[pltpu.VMEM((parts, capacity, 6, 24, LANES), f32)],
     )
     return (
         embedding,

time: 51.7 us -> 50.4 us (0.975)
  Pallas kernels: 14.5 us -> 12.4 us
  starting transfers between devices: 23.2 us -> 24 us
    pallas_call x15 -> x16, Pallas kernels: 14.5 us -> 12.4 us  [call(): pl.pallas_call(body, out_shape=out_shape, in_specs=in_specs, out_specs=ou...]
    ppermute x14, starting transfers between devices: 21.8 us -> 22.6 us  [swapped(): lax.ppermute(value, axis, [(source, source ^ bit) for source in range(cou...]
  transfers between devices with their start and end apart: 16 -> 16, of which waited for: 6 -> 6; matrix products, arithmetic and copies ran while one was open for 0% -> 0% of each run, Pallas kernels for 19% -> 17%
where the time goes in v2:
time: 50.4 us; the launch traced here: 50.2 us
  starting transfers between devices  24 us (48%)
  Pallas kernels  12.4 us (25%)
  waiting for transfers between devices  11.3 us (22%)
  between operations  1.57 us (3%)
  local copies, waits for them, and re-layouts  0.96 us (2%)
    ppermute x14, starting transfers between devices, swapped(): lax.ppermute(value, axis, [(source, source ^ bit) for source in range(cou...  22.6 us
    pallas_call x16, Pallas kernels, call(): pl.pallas_call(body, out_shape=out_shape, in_specs=in_specs, out_specs=ou...  12.4 us
    ppermute x14, waiting for transfers between devices, swapped(): lax.ppermute(value, axis, [(source, source ^ bit) for source in range(cou...  11.2 us
    ppermute x2, starting transfers between devices, crossed(): lax.ppermute(value, axis, [(n, n + 1) for n in firsts] + [(n + 1, n) for...  1.44 us
  transfers between devices with their start and end apart: 16, of which 6 were waited for; matrix products, arithmetic and copies ran while one was open for 0% of the time, Pallas kernels for 17%

profile of v2, /device:TPU:0, one launch (start us, length us, event | category | flops | bytes accessed | tf_op | source)
XLA Modules:
  0.0 50.2 jit_solution(3520000213551263153)
XLA Ops:
  1.3 0.9 %copy-done.4 = bf16[1,4,8,8,384]{4,3,2,1,0:T(8,128)(2,1)S(1)} copy-done((bf16[1,4,8,8,384]{4,3,2,1,0:T(8,128)(2,1)S(1)}, bf16[1,4,8,8,384]{4,3,2,1,0:T(8,128)(2,1)}, u32[]{:S(2)}) %copy-start.4) | copy-done | bytes 196632
  2.3 0.1 shard_map.138
  2.3 0.0 copy-start.1
  2.3 0.0 copy-start.10
  2.4 0.6 %collective-permute-start = (bf16[4,3,8,384]{3,2,1,0:T(8,128)(2,1)S(1)}, bf16[4,3,8,384]{3,2,1,0:T(8,128)(2,1)S(1)}, u32[]{:S(2)}, u32[]{:S(2)}) collective-permute-start(bf16[4,3,8,384]{3,2,1,0:T(8,128)(2,1)S(1)} %get-tuple-element.48), channel_id=1, source_target_pairs={{0,1},{1,0},{2,3},{3,2},{4,5},{5,4},{6,7},{7,6},{8,9},{9,8},{10,11... | collective-permute-start | bytes 221192 | tf_op jit(solution)/shard_map/ppermute | solution.py:46
  2.9 0.8 %collective-permute-start.1 = (bf16[4,3,8,384]{3,2,1,0:T(8,128)(2,1)S(1)}, bf16[4,3,8,384]{3,2,1,0:T(8,128)(2,1)S(1)}, u32[]{:S(2)}, u32[]{:S(2)}) collective-permute-start(bf16[4,3,8,384]{3,2,1,0:T(8,128)(2,1)S(1)} %get-tuple-element.49), channel_id=1, source_target_pairs={{1,2},{3,4},{5,6},{7,8},{9,10},{11,12},{13,14},{2,1},{4,3},{6,5},{... | collective-permute-start | bytes 221192 | tf_op jit(solution)/shard_map/ppermute | solution.py:52
  3.7 0.0 copy-done
  3.7 0.0 copy-done.2
  3.7 0.0 copy-done.3
  3.8 2.2 %shard_map.139 = (f32[3,4,8,24,128]{4,3,2,1,0:T(8,128)S(1)}, f32[256,384]{1,0:T(8,128)S(1)}, bf16[256,512]{1,0:T(8,128)(2,1)S(1)}, f32[256,1536]{1,0:T(8,128)S(1)}, f32[1,384]{1,0:T(1,128)S(1)}) custom-call(s32[4,8]{1,0:T(4,128)S(1)} %bitcast.9, s32[1,1]{1,0:T(1,128)S(6)} %copy.15.counts_ref, f32[1,4]{1,0:T(1,128)S(1)} %copy-done.9, f32[1,384]{1,0:T(1,128)S(1)} %copy-done.8, ...), custom_call_target="tpu_custom_call" | custom-call | flops 301989888 | bytes 5060756 | tf_op jit(solution)/shard_map/pallas_call | solution.py:29
  6.0 0.0 collective-permute-done.core_ref
  6.0 0.0 collective-permute-done.1.cross_ref
  6.0 2.6 %shard_map.140 = (f32[3,4,6,24,128]{4,3,2,1,0:T(8,128)S(1)}, f32[256,384]{1,0:T(8,128)S(1)}, f32[256,1]{1,0:T(8,128)S(1)}, f32[256,1536]{1,0:T(8,128)S(1)}, f32[...) custom-call(s32[4,8]{1,0:T(4,128)S(1)} %bitcast.10, ...), custom_call_target="tpu_custom_call" | custom-call | flops 603979776 | bytes 9040004 | tf_op jit(solution)/shard_map/pallas_call | solution.py:29
  8.6 4.0 %collective-permute-start.2 = (bf16[768,384]{1,0:T(8,128)(2,1)S(1)}, bf16[768,384]{1,0:T(8,128)(2,1)S(1)}, u32[]{:S(2)}, u32[]{:S(2)}) collective-permute-start(bf16[768,384]{1,0:T(8,128)(2,1)S(1)} %get-tuple-element.53), channel_id=1, source_target_pairs={{0,1},{1,0},{2,3},{3,2},{4,5},{5,4},{6,7},{7,6},{8,9},{9,8},{10,11... | collective-permute-start | bytes 1769480 | tf_op jit(solution)/shard_map/ppermute | solution.py:46
  12.5 1.6 %collective-permute-done.2.refs_1_ = bf16[768,384]{1,0:T(8,128)(2,1)S(1)} collective-permute-done((bf16[768,384]{1,0:T(8,128)(2,1)S(1)}, bf16[768,384]{1,0:T(8,128)(2,1)S(1)}, u32[]{:S(2)}, u32[]{:S(2)}) %collective-permute-start.2) | collective-permute-done | bytes 589856 | tf_op jit(solution)/shard_map/ppermute | solution.py:46
  14.2 0.3 shard_map.141
  14.4 2.8 %collective-permute-start.3 = (bf16[192,384]{1,0:T(8,128)(2,1)S(1)}, bf16[192,384]{1,0:T(8,128)(2,1)S(1)}, u32[]{:S(2)}, u32[]{:S(2)}) collective-permute-start(bf16[192,384]{1,0:T(8,128)(2,1)S(1)} %get-tuple-element.55), channel_id=1, source_target_pairs={{0,2},{1,3},{2,0},{3,1},{4,6},{5,7},{6,4},{7,5},{8,10},{9,11},{10,... | collective-permute-start | bytes 442376 | tf_op jit(solution)/shard_map/ppermute | solution.py:46
  17.2 1.6 %collective-permute-start.4 = (bf16[192,384]{1,0:T(8,128)(2,1)S(1)}, bf16[192,384]{1,0:T(8,128)(2,1)S(1)}, u32[]{:S(2)}, u32[]{:S(2)}) collective-permute-start(bf16[192,384]{1,0:T(8,128)(2,1)S(1)} %get-tuple-element.57), channel_id=1, source_target_pairs={{0,4},{1,5},{2,6},{3,7},{4,0},{5,1},{6,2},{7,3},{8,12},{9,13},{10,... | collective-permute-start | bytes 442376 | tf_op jit(solution)/shard_map/ppermute | solution.py:46
  18.8 2.8 %collective-permute-done.3.refs_1_ = bf16[192,384]{1,0:T(8,128)(2,1)S(1)} collective-permute-done((bf16[192,384]{1,0:T(8,128)(2,1)S(1)}, bf16[192,384]{1,0:T(8,128)(2,1)S(1)}, u32[]{:S(2)}, u32[]{:S(2)}) %collective-permute-start.3) | collective-permute-done | bytes 147488 | tf_op jit(solution)/shard_map/ppermute | solution.py:46
  21.6 1.5 %collective-permute-done.4.refs_3_ = bf16[192,384]{1,0:T(8,128)(2,1)S(1)} collective-permute-done((bf16[192,384]{1,0:T(8,128)(2,1)S(1)}, bf16[192,384]{1,0:T(8,128)(2,1)S(1)}, u32[]{:S(2)}, u32[]{:S(2)}) %collective-permute-start.4) | collective-permute-done | bytes 147488 | tf_op jit(solution)/shard_map/ppermute | solution.py:46
  23.0 0.1 shard_map.142
  23.2 1.6 %collective-permute-start.5 = (bf16[96,384]{1,0:T(8,128)(2,1)S(1)}, bf16[96,384]{1,0:T(8,128)(2,1)S(1)}, u32[]{:S(2)}, u32[]{:S(2)}) collective-permute-start(bf16[96,384]{1,0:T(8,128)(2,1)S(1)} %get-tuple-element.59), channel_id=1, source_target_pairs={{0,4},{1,5},{2,6},{3,7},{4,0},{5,1},{6,2},{7,3},{8,12},{9,13},{10,... | collective-permute-start | bytes 221192 | tf_op jit(solution)/shard_map/ppermute | solution.py:46
  24.8 0.4 collective-permute-start.6
  25.2 1.6 %shard_map.145 = (f32[256,384]{1,0:T(8,128)S(1)}, bf16[4,3,8,384]{3,2,1,0:T(8,128)(2,1)S(1)}, bf16[4,3,8,384]{3,2,1,0:T(8,128)(2,1)S(1)}, f32[1,384]{1,0:T(1,128)S(1)}) custom-call(s32[1,1]{1,0:T(1,128)} %bitcast.place_ref, s32[1,1]{1,0:T(1,128)S(6)} %copy.15.counts_ref, f32[1,4]{1,0:T(1,128)S(1)} %copy-done.9, f32[256,1536]{1,0:T(8,128)S(1)} %get-tuple-element.68.pre_ref, ...), custom_call_target="tpu_custom_call" | custom-call | flops 301989888 | bytes 8805400 | tf_op jit(solution)/shard_map/pallas_call | solution.py:29
  26.8 1.4 %shard_map.146 = (f32[56,384]{1,0:T(8,128)S(1)}, bf16[56,384]{1,0:T(8,128)(2,1)S(1)}) custom-call(f32[3,4,8,24,128]{4,3,2,1,0:T(8,128)S(1)} %get-tuple-element.66.pad_ref, f32[3,4,6,24,128]{4,3,2,1,0:T(8,128)S(1)} %get-tuple-element.67.edge_ref, f32[256,384]{1,0:T(8,128)S(1)} %get-tuple-element.75.grad_ref, f32[1,384]{1,0:T(1,128)S(1)} %get-tuple-element.76.emb_ref), custom_call_target="tpu_custom_call" | custom-call | bytes 2588160 | tf_op jit(solution)/shard_map/pallas_call | solution.py:29
  28.1 0.1 collective-permute-start.9
  28.2 1.2 %collective-permute-done.9.got_ref = bf16[56,384]{1,0:T(8,128)(2,1)S(1)} collective-permute-done((bf16[56,384]{1,0:T(8,128)(2,1)S(1)}, bf16[56,384]{1,0:T(8,128)(2,1)S(1)}, u32[]{:S(2)}, u32[]{:S(2)}) %collective-permute-start.9) | collective-permute-done | bytes 43040 | tf_op jit(solution)/shard_map/ppermute | solution.py:46
  29.5 1.6 %collective-permute-start.10 = (bf16[56,384]{1,0:T(8,128)(2,1)S(1)}, bf16[56,384]{1,0:T(8,128)(2,1)S(1)}, u32[]{:S(2)}, u32[]{:S(2)}) collective-permute-start(bf16[56,384]{1,0:T(8,128)(2,1)S(1)} %get-tuple-element.80), channel_id=1, source_target_pairs={{0,16},{16,0},{1,17},{17,1},{2,18},{18,2},{3,19},{19,3},{4,20},{20... | collective-permute-start | bytes 129032 | tf_op jit(solution)/shard_map/ppermute | solution.py:46
  31.0 0.0 collective-permute-done.5.refs_1_
  31.0 0.0 collective-permute-done.6.refs_3_
  31.1 2.7 %collective-permute-start.7 = (bf16[96,384]{1,0:T(8,128)(2,1)S(1)}, bf16[96,384]{1,0:T(8,128)(2,1)S(1)}, u32[]{:S(2)}, u32[]{:S(2)}) collective-permute-start(bf16[96,384]{1,0:T(8,128)(2,1)S(1)} %get-tuple-element.63), channel_id=1, source_target_pairs={{0,8},{1,9},{2,10},{3,11},{4,12},{5,13},{6,14},{7,15},{8,0},{9,1},... | collective-permute-start | bytes 221192 | tf_op jit(solution)/shard_map/ppermute | solution.py:46
  33.7 0.0 collective-permute-done.10.got_ref
  33.8 1.5 %collective-permute-start.11 = (bf16[56,384]{1,0:T(8,128)(2,1)S(1)}, bf16[56,384]{1,0:T(8,128)(2,1)S(1)}, u32[]{:S(2)}, u32[]{:S(2)}) collective-permute-start(bf16[56,384]{1,0:T(8,128)(2,1)S(1)} %get-tuple-element.82), channel_id=1, source_target_pairs={{0,2},{1,3},{2,0},{3,1},{4,6},{5,7},{6,4},{7,5},{8,10},{9,11},{10,... | collective-permute-start | bytes 129032 | tf_op jit(solution)/shard_map/ppermute | solution.py:46
  35.3 2.6 %collective-permute-done.11.got_ref = bf16[56,384]{1,0:T(8,128)(2,1)S(1)} collective-permute-done((bf16[56,384]{1,0:T(8,128)(2,1)S(1)}, bf16[56,384]{1,0:T(8,128)(2,1)S(1)}, u32[]{:S(2)}, u32[]{:S(2)}) %collective-permute-start.11) | collective-permute-done | bytes 43040 | tf_op jit(solution)/shard_map/ppermute | solution.py:46
  37.9 0.5 %collective-permute-start.12 = (bf16[56,384]{1,0:T(8,128)(2,1)S(1)}, bf16[56,384]{1,0:T(8,128)(2,1)S(1)}, u32[]{:S(2)}, u32[]{:S(2)}) collective-permute-start(bf16[56,384]{1,0:T(8,128)(2,1)S(1)} %get-tuple-element.84), channel_id=1, source_target_pairs={{0,4},{1,5},{2,6},{3,7},{4,0},{5,1},{6,2},{7,3},{8,12},{9,13},{10,... | collective-permute-start | bytes 129032 | tf_op jit(solution)/shard_map/ppermute | solution.py:46
  38.4 0.0 collective-permute-start.14
  38.4 0.7 %collective-permute-start.15 = (bf16[4,3,8,384]{3,2,1,0:T(8,128)(2,1)S(1)}, bf16[4,3,8,384]{3,2,1,0:T(8,128)(2,1)S(1)}, u32[]{:S(2)}, u32[]{:S(2)}) collective-permute-start(bf16[4,3,8,384]{3,2,1,0:T(8,128)(2,1)S(1)} %get-tuple-element.89), channel_id=1, source_target_pairs={{1,2},{3,4},{5,6},{7,8},{9,10},{11,12},{13,14},{2,1},{4,3},{6,5},{... | collective-permute-start | bytes 221192 | tf_op jit(solution)/shard_map/ppermute | solution.py:52
  39.1 0.0 collective-permute-done.7.refs_1_
  39.1 1.3 %collective-permute-start.8 = (bf16[96,384]{1,0:T(8,128)(2,1)S(1)}, bf16[96,384]{1,0:T(8,128)(2,1)S(1)}, u32[]{:S(2)}, u32[]{:S(2)}) collective-permute-start(bf16[96,384]{1,0:T(8,128)(2,1)S(1)} %get-tuple-element.65), channel_id=1, source_target_pairs={{0,16},{16,0},{1,17},{17,1},{2,18},{18,2},{3,19},{19,3},{4,20},{20... | collective-permute-start | bytes 221192 | tf_op jit(solution)/shard_map/ppermute | solution.py:46
  40.4 1.5 %collective-permute-done.12.got_ref = bf16[56,384]{1,0:T(8,128)(2,1)S(1)} collective-permute-done((bf16[56,384]{1,0:T(8,128)(2,1)S(1)}, bf16[56,384]{1,0:T(8,128)(2,1)S(1)}, u32[]{:S(2)}, u32[]{:S(2)}) %collective-permute-start.12) | collective-permute-done | bytes 43040 | tf_op jit(solution)/shard_map/ppermute | solution.py:46
  42.0 4.0 %collective-permute-start.13 = (bf16[56,384]{1,0:T(8,128)(2,1)S(1)}, bf16[56,384]{1,0:T(8,128)(2,1)S(1)}, u32[]{:S(2)}, u32[]{:S(2)}) collective-permute-start(bf16[56,384]{1,0:T(8,128)(2,1)S(1)} %get-tuple-element.86), channel_id=1, source_target_pairs={{0,8},{1,9},{2,10},{3,11},{4,12},{5,13},{6,14},{7,15},{8,0},{9,1},... | collective-permute-start | bytes 129032 | tf_op jit(solution)/shard_map/ppermute | solution.py:46
  46.0 1.6 %shard_map.152.part_ref = f32[256,384]{1,0:T(8,128)S(1)} custom-call(s32[4,8]{1,0:T(4,128)S(1)} %bitcast.11, f32[256,384]{1,0:T(8,128)S(1)} %get-tuple-element.75.grad_ref, f32[7,7,384]{2,1,0:T(8,128)S(1)} %copy-done.3), custom_call_target="tpu_custom_call" | custom-call | bytes 861824 | tf_op jit(solution)/shard_map/pallas_call | solution.py:29
  47.7 0.0 collective-permute-done.14.core_ref
  47.7 0.0 collective-permute-done.15.cross_ref
  47.7 1.8 %shard_map.153 = bf16[256,384]{1,0:T(8,128)(2,1)} custom-call(s32[4,8]{1,0:T(4,128)S(1)} %bitcast.12, s32[1,1]{1,0:T(1,128)} %bitcast.place_ref, s32[1,1]{1,0:T(1,128)S(6)} %copy.15.counts_ref, f32[1,4]{1,0:T(1,128)S(1)} %copy-done.9, f32[256,384]{1,0:T(8,128)S(1)} %shard_map.152.part_ref, bf16[4,3,8,384]{3,2,1,0:T(8,128)(2,1)S(1)} %collective-permute-done.14.core_ref, ...), custom_call_target="tpu_custom_call" | custom-call | bytes 1010840 | tf_op jit(solution)/shard_map/pallas_call | solution.py:29
  49.5 0.0 collective-permute-done.13.new_ref
  49.5 0.0 collective-permute-done.8.got_ref
  49.5 0.7 %shard_map.151 = (f32[96,384]{1,0:T(8,128)}, f32[7,7,384]{2,1,0:T(8,128)}, f32[1,384]{1,0:T(1,128)}) custom-call(f32[96,384]{1,0:T(8,128)S(1)} %get-tuple-element.64.keep_ref, bf16[96,384]{1,0:T(8,128)(2,1)S(1)} %collective-permute-done.8.got_ref, f32[56,384]{1,0:T(8,128)S(1)} %get-tuple-element.85.state_ref, bf16[56,384]{1,0:T(8,128)(2,1)S(1)} %collective-permute-done.13.new_ref), custom_call_target="tpu_custom_call" | custom-call | bytes 574464 | tf_op jit(solution)/shard_map/pallas_call | solution.py:29
  (22 shorter events, 0.2 us)
Async XLA Ops:
  1.3 0.9 %copy-start.4 = (bf16[1,4,8,8,384]{4,3,2,1,0:T(8,128)(2,1)S(1)}, bf16[1,4,8,8,384]{4,3,2,1,0:T(8,128)(2,1)}, u32[]{:S(2)}) copy-start(bf16[1,4,8,8,384]{4,3,2,1,0:T(8,128)(2,1)} %param.11) | copy-start | bytes 589828
  2.2 1.5 %copy-start = (bf16[1536,384]{1,0:T(8,128)(2,1)S(1)}, bf16[1536,384]{1,0:T(8,128)(2,1)}, u32[]{:S(2)}) copy-start(bf16[1536,384]{1,0:T(8,128)(2,1)} %w_out_ref.3) | copy-start | bytes 3538948
  2.2 1.5 %copy-start.2 = (bf16[1,4,8,8,384]{4,3,2,1,0:T(8,128)(2,1)S(1)}, bf16[1,4,8,8,384]{4,3,2,1,0:T(8,128)(2,1)}, u32[]{:S(2)}) copy-start(bf16[1,4,8,8,384]{4,3,2,1,0:T(8,128)(2,1)} %param.12) | copy-start | bytes 589828
  2.2 1.5 %copy-start.3 = (f32[7,7,384]{2,1,0:T(8,128)S(1)}, f32[7,7,384]{2,1,0:T(8,128)}, u32[]{:S(2)}) copy-start(f32[7,7,384]{2,1,0:T(8,128)} %kern_ref.7) | copy-start | bytes 225796
  2.2 1.5 %copy-start.5 = (bf16[1,4,8,8,384]{4,3,2,1,0:T(8,128)(2,1)S(1)}, bf16[1,4,8,8,384]{4,3,2,1,0:T(8,128)(2,1)}, u32[]{:S(2)}) copy-start(bf16[1,4,8,8,384]{4,3,2,1,0:T(8,128)(2,1)} %param.11) | copy-start | bytes 589828
  2.2 1.5 %copy-start.6 = (s32[1,4,8]{2,1,0:T(4,128)S(1)}, s32[1,4,8]{2,1,0:T(4,128)}, u32[]{:S(2)}) copy-start(s32[1,4,8]{2,1,0:T(4,128)} %param.15) | copy-start | bytes 388
  2.2 1.5 %copy-start.7 = (f32[384]{0:T(512)S(1)}, f32[384]{0:T(512)}, u32[]{:S(2)}) copy-start(f32[384]{0:T(512)} %scale_ref.3) | copy-start | bytes 4612
  2.2 1.5 %copy-start.8 = (f32[1,384]{1,0:T(1,128)S(1)}, f32[1,384]{1,0:T(1,128)}, u32[]{:S(2)}) copy-start(f32[1,384]{1,0:T(1,128)} %cot_ref.3) | copy-start | bytes 4612
  2.3 1.5 %copy-start.9 = (f32[1,4]{1,0:T(1,128)S(1)}, f32[1,4]{1,0:T(1,128)}, u32[]{:S(2)}) copy-start(f32[1,4]{1,0:T(1,128)} %pool_ref.5) | copy-start | bytes 52
  2.3 3.7 %copy-start.1 = (bf16[384,1536]{1,0:T(8,128)(2,1)S(1)}, bf16[384,1536]{1,0:T(8,128)(2,1)}, u32[]{:S(2)}) copy-start(bf16[384,1536]{1,0:T(8,128)(2,1)} %w_in_ref.3) | copy-start | bytes 3538948
  2.3 3.7 %copy-start.10 = (f32[384]{0:T(512)S(1)}, f32[384]{0:T(512)}, u32[]{:S(2)}) copy-start(f32[384]{0:T(512)} %gain_ref.3) | copy-start | bytes 4612
  2.4 3.6 %collective-permute-start = (bf16[4,3,8,384]{3,2,1,0:T(8,128)(2,1)S(1)}, bf16[4,3,8,384]{3,2,1,0:T(8,128)(2,1)S(1)}, u32[]{:S(2)}, u32[]{:S(2)}) collective-permute-start(bf16[4,3,8,384]{3,2,1,0:T(8,128)(2,1)S(1)} %get-tuple-element.48), channel_id=1, source_target_pairs={{0,1},{1,0},{2,3},{3,2},{4,5},{5,4},{6,7},{7,6},{8,9},{9,8},{10,11... | collective-permute-start | bytes 221192 | tf_op jit(solution)/shard_map/ppermute | solution.py:46
  2.9 3.1 %collective-permute-start.1 = (bf16[4,3,8,384]{3,2,1,0:T(8,128)(2,1)S(1)}, bf16[4,3,8,384]{3,2,1,0:T(8,128)(2,1)S(1)}, u32[]{:S(2)}, u32[]{:S(2)}) collective-permute-start(bf16[4,3,8,384]{3,2,1,0:T(8,128)(2,1)S(1)} %get-tuple-element.49), channel_id=1, source_target_pairs={{1,2},{3,4},{5,6},{7,8},{9,10},{11,12},{13,14},{2,1},{4,3},{6,5},{... | collective-permute-start | bytes 221192 | tf_op jit(solution)/shard_map/ppermute | solution.py:52
  8.6 5.6 %collective-permute-start.2 = (bf16[768,384]{1,0:T(8,128)(2,1)S(1)}, bf16[768,384]{1,0:T(8,128)(2,1)S(1)}, u32[]{:S(2)}, u32[]{:S(2)}) collective-permute-start(bf16[768,384]{1,0:T(8,128)(2,1)S(1)} %get-tuple-element.53), channel_id=1, source_target_pairs={{0,1},{1,0},{2,3},{3,2},{4,5},{5,4},{6,7},{7,6},{8,9},{9,8},{10,11... | collective-permute-start | bytes 1769480 | tf_op jit(solution)/shard_map/ppermute | solution.py:46
  14.4 7.2 %collective-permute-start.3 = (bf16[192,384]{1,0:T(8,128)(2,1)S(1)}, bf16[192,384]{1,0:T(8,128)(2,1)S(1)}, u32[]{:S(2)}, u32[]{:S(2)}) collective-permute-start(bf16[192,384]{1,0:T(8,128)(2,1)S(1)} %get-tuple-element.55), channel_id=1, source_target_pairs={{0,2},{1,3},{2,0},{3,1},{4,6},{5,7},{6,4},{7,5},{8,10},{9,11},{10,... | collective-permute-start | bytes 442376 | tf_op jit(solution)/shard_map/ppermute | solution.py:46
  17.2 5.8 %collective-permute-start.4 = (bf16[192,384]{1,0:T(8,128)(2,1)S(1)}, bf16[192,384]{1,0:T(8,128)(2,1)S(1)}, u32[]{:S(2)}, u32[]{:S(2)}) collective-permute-start(bf16[192,384]{1,0:T(8,128)(2,1)S(1)} %get-tuple-element.57), channel_id=1, source_target_pairs={{0,4},{1,5},{2,6},{3,7},{4,0},{5,1},{6,2},{7,3},{8,12},{9,13},{10,... | collective-permute-start | bytes 442376 | tf_op jit(solution)/shard_map/ppermute | solution.py:46
  23.2 7.9 %collective-permute-start.5 = (bf16[96,384]{1,0:T(8,128)(2,1)S(1)}, bf16[96,384]{1,0:T(8,128)(2,1)S(1)}, u32[]{:S(2)}, u32[]{:S(2)}) collective-permute-start(bf16[96,384]{1,0:T(8,128)(2,1)S(1)} %get-tuple-element.59), channel_id=1, source_target_pairs={{0,4},{1,5},{2,6},{3,7},{4,0},{5,1},{6,2},{7,3},{8,12},{9,13},{10,... | collective-permute-start | bytes 221192 | tf_op jit(solution)/shard_map/ppermute | solution.py:46
  24.8 6.2 %collective-permute-start.6 = (bf16[96,384]{1,0:T(8,128)(2,1)S(1)}, bf16[96,384]{1,0:T(8,128)(2,1)S(1)}, u32[]{:S(2)}, u32[]{:S(2)}) collective-permute-start(bf16[96,384]{1,0:T(8,128)(2,1)S(1)} %get-tuple-element.61), channel_id=1, source_target_pairs={{0,2},{1,3},{2,0},{3,1},{4,6},{5,7},{6,4},{7,5},{8,10},{9,11},{10,... | collective-permute-start | bytes 221192 | tf_op jit(solution)/shard_map/ppermute | solution.py:46
  28.1 1.3 %collective-permute-start.9 = (bf16[56,384]{1,0:T(8,128)(2,1)S(1)}, bf16[56,384]{1,0:T(8,128)(2,1)S(1)}, u32[]{:S(2)}, u32[]{:S(2)}) collective-permute-start(bf16[56,384]{1,0:T(8,128)(2,1)S(1)} %get-tuple-element.78), channel_id=1, source_target_pairs={{0,1},{1,0},{2,3},{3,2},{4,5},{5,4},{6,7},{7,6},{8,9},{9,8},{10,11... | collective-permute-start | bytes 129032 | tf_op jit(solution)/shard_map/ppermute | solution.py:46
  29.5 4.3 %collective-permute-start.10 = (bf16[56,384]{1,0:T(8,128)(2,1)S(1)}, bf16[56,384]{1,0:T(8,128)(2,1)S(1)}, u32[]{:S(2)}, u32[]{:S(2)}) collective-permute-start(bf16[56,384]{1,0:T(8,128)(2,1)S(1)} %get-tuple-element.80), channel_id=1, source_target_pairs={{0,16},{16,0},{1,17},{17,1},{2,18},{18,2},{3,19},{19,3},{4,20},{20... | collective-permute-start | bytes 129032 | tf_op jit(solution)/shard_map/ppermute | solution.py:46
  31.1 8.0 %collective-permute-start.7 = (bf16[96,384]{1,0:T(8,128)(2,1)S(1)}, bf16[96,384]{1,0:T(8,128)(2,1)S(1)}, u32[]{:S(2)}, u32[]{:S(2)}) collective-permute-start(bf16[96,384]{1,0:T(8,128)(2,1)S(1)} %get-tuple-element.63), channel_id=1, source_target_pairs={{0,8},{1,9},{2,10},{3,11},{4,12},{5,13},{6,14},{7,15},{8,0},{9,1},... | collective-permute-start | bytes 221192 | tf_op jit(solution)/shard_map/ppermute | solution.py:46
  33.8 4.1 %collective-permute-start.11 = (bf16[56,384]{1,0:T(8,128)(2,1)S(1)}, bf16[56,384]{1,0:T(8,128)(2,1)S(1)}, u32[]{:S(2)}, u32[]{:S(2)}) collective-permute-start(bf16[56,384]{1,0:T(8,128)(2,1)S(1)} %get-tuple-element.82), channel_id=1, source_target_pairs={{0,2},{1,3},{2,0},{3,1},{4,6},{5,7},{6,4},{7,5},{8,10},{9,11},{10,... | collective-permute-start | bytes 129032 | tf_op jit(solution)/shard_map/ppermute | solution.py:46
  37.9 4.1 %collective-permute-start.12 = (bf16[56,384]{1,0:T(8,128)(2,1)S(1)}, bf16[56,384]{1,0:T(8,128)(2,1)S(1)}, u32[]{:S(2)}, u32[]{:S(2)}) collective-permute-start(bf16[56,384]{1,0:T(8,128)(2,1)S(1)} %get-tuple-element.84), channel_id=1, source_target_pairs={{0,4},{1,5},{2,6},{3,7},{4,0},{5,1},{6,2},{7,3},{8,12},{9,13},{10,... | collective-permute-start | bytes 129032 | tf_op jit(solution)/shard_map/ppermute | solution.py:46
  38.4 9.3 %collective-permute-start.14 = (bf16[4,3,8,384]{3,2,1,0:T(8,128)(2,1)S(1)}, bf16[4,3,8,384]{3,2,1,0:T(8,128)(2,1)S(1)}, u32[]{:S(2)}, u32[]{:S(2)}) collective-permute-start(bf16[4,3,8,384]{3,2,1,0:T(8,128)(2,1)S(1)} %get-tuple-element.88), channel_id=1, source_target_pairs={{0,1},{1,0},{2,3},{3,2},{4,5},{5,4},{6,7},{7,6},{8,9},{9,8},{10,11... | collective-permute-start | bytes 221192 | tf_op jit(solution)/shard_map/ppermute | solution.py:46
  38.4 9.3 %collective-permute-start.15 = (bf16[4,3,8,384]{3,2,1,0:T(8,128)(2,1)S(1)}, bf16[4,3,8,384]{3,2,1,0:T(8,128)(2,1)S(1)}, u32[]{:S(2)}, u32[]{:S(2)}) collective-permute-start(bf16[4,3,8,384]{3,2,1,0:T(8,128)(2,1)S(1)} %get-tuple-element.89), channel_id=1, source_target_pairs={{1,2},{3,4},{5,6},{7,8},{9,10},{11,12},{13,14},{2,1},{4,3},{6,5},{... | collective-permute-start | bytes 221192 | tf_op jit(solution)/shard_map/ppermute | solution.py:52
  39.1 10.4 %collective-permute-start.8 = (bf16[96,384]{1,0:T(8,128)(2,1)S(1)}, bf16[96,384]{1,0:T(8,128)(2,1)S(1)}, u32[]{:S(2)}, u32[]{:S(2)}) collective-permute-start(bf16[96,384]{1,0:T(8,128)(2,1)S(1)} %get-tuple-element.65), channel_id=1, source_target_pairs={{0,16},{16,0},{1,17},{17,1},{2,18},{18,2},{3,19},{19,3},{4,20},{20... | collective-permute-start | bytes 221192 | tf_op jit(solution)/shard_map/ppermute | solution.py:46
  42.0 7.5 %collective-permute-start.13 = (bf16[56,384]{1,0:T(8,128)(2,1)S(1)}, bf16[56,384]{1,0:T(8,128)(2,1)S(1)}, u32[]{:S(2)}, u32[]{:S(2)}) collective-permute-start(bf16[56,384]{1,0:T(8,128)(2,1)S(1)} %get-tuple-element.86), channel_id=1, source_target_pairs={{0,8},{1,9},{2,10},{3,11},{4,12},{5,13},{6,14},{7,15},{8,0},{9,1},... | collective-permute-start | bytes 129032 | tf_op jit(solution)/shard_map/ppermute | solution.py:46

commit v3 on v2

--- a/solution.py
+++ b/solution.py
@@ -98,7 +98,7 @@
 UPPER, LOWER = (4, 0, 5), (6, 1, 7)
 
 
-def convolve(pads, tap_row, finish, capacity, parts):
+def convolve(pads, tap_row, finish, capacity, parts, between=()):
     for lane in range(parts):
 
         def one_tile(tile):
@@ -118,6 +118,8 @@
 
         for tile in range(capacity):
             one_tile(tile)
+            if lane * capacity + tile < len(between):
+                between[lane * capacity + tile]()
 
 
 def lanes(lane):
@@ -129,7 +131,7 @@
     cross_ref[...] = (last * odd + first * (1.0 - odd)).astype(bf16)
 
 
-def edge_kernel(place_ref, counts_ref, tiles_ref, core_ref, cross_ref):
+def edge_kernel(place_ref, tiles_ref, core_ref, cross_ref):
     swap_edges(
         tiles_ref[:, 5:8].astype(f32), tiles_ref[:, 0:3].astype(f32), is_odd(place_ref), core_ref, cross_ref
     )
@@ -156,9 +158,15 @@
         own = tiles_ref[tile].astype(f32)
         own_sum += live * pool * jnp.sum(own.reshape(pixels, channels), axis=0, keepdims=True)
     own_sum_ref[...] = own_sum
-    act_grad_ref[...] = lax.dot_general(
-        mixed_ref[:, 0:channels], w_out_ref[...], (((1,), (1,)), ((), ())), preferred_element_type=f32
-    )
+
+    def product(at):
+        act_grad_ref[:, at] = lax.dot_general(
+            mixed_ref[:, 0:channels], w_out_ref[at, :], (((1,), (1,)), ((), ())), preferred_element_type=f32
+        )
+
+    hidden = w_out_ref.shape[0]
+    step = 256 if hidden % 256 == 0 else hidden
+    products = [functools.partial(product, slice(n, n + step)) for n in range(0, hidden, step)]
 
     def finish(tile, lane, sums):
         for row in range(8):
@@ -167,7 +175,7 @@
     convolve(
         [(pad_ref, 8, 3)],
         lambda row, col, lane: kern_ref[row, col : col + 1, lanes(lane)],
-        finish, capacity, parts,
+        finish, capacity, parts, products,
     )
 
 
@@ -431,7 +439,7 @@
     place = lax.axis_index("space").astype(jnp.int32).reshape(1, 1)
 
     core, cross = call(
-        edge_kernel, [struct(edge_shape, bf16)] * 2, [SMEM, VMEM, VMEM], [place, counts, own],
+        edge_kernel, [struct(edge_shape, bf16)] * 2, [SMEM, VMEM], [place, own],
         flops=EDGE_COST,
     )
     cross = crossed(cross, "space")

time: 50.4 us -> 49.8 us (0.988)
  no operation moved by 1% of the time
where the time goes in v3:
time: 49.8 us; the launch traced here: 49.6 us
  starting transfers between devices  23.5 us (47%)
  Pallas kernels  12.3 us (25%)
  waiting for transfers between devices  11.2 us (22%)
  between operations  1.57 us (3%)
  local copies, waits for them, and re-layouts  0.96 us (2%)
    ppermute x14, starting transfers between devices, swapped(): lax.ppermute(value, axis, [(source, source ^ bit) for source in range(cou...  22.1 us
    pallas_call x16, Pallas kernels, call(): pl.pallas_call(body, out_shape=out_shape, in_specs=in_specs, out_specs=ou...  12.3 us
    ppermute x14, waiting for transfers between devices, swapped(): lax.ppermute(value, axis, [(source, source ^ bit) for source in range(cou...  11.2 us
    ppermute x2, starting transfers between devices, crossed(): lax.ppermute(value, axis, [(n, n + 1) for n in firsts] + [(n + 1, n) for...  1.44 us
  transfers between devices with their start and end apart: 16, of which 6 were waited for; matrix products, arithmetic and copies ran while one was open for 0% of the time, Pallas kernels for 17%

profile of v3, /device:TPU:0, one launch (start us, length us, event | category | flops | bytes accessed | tf_op | source)
XLA Modules:
  0.0 49.6 jit_solution(5350438923144340114)
XLA Ops:
  0.6 0.9 %copy-done.4 = bf16[1,4,8,8,384]{4,3,2,1,0:T(8,128)(2,1)S(1)} copy-done((bf16[1,4,8,8,384]{4,3,2,1,0:T(8,128)(2,1)S(1)}, bf16[1,4,8,8,384]{4,3,2,1,0:T(8,128)(2,1)}, u32[]{:S(2)}) %copy-start.4) | copy-done | bytes 196632
  1.6 0.0 copy-start.6
  1.6 0.0 copy-start.7
  1.6 0.0 copy-start.8
  1.6 0.1 shard_map.138
  1.7 0.0 copy-start.1
  1.7 0.0 copy-start.10
  1.7 0.6 %collective-permute-start = (bf16[4,3,8,384]{3,2,1,0:T(8,128)(2,1)S(1)}, bf16[4,3,8,384]{3,2,1,0:T(8,128)(2,1)S(1)}, u32[]{:S(2)}, u32[]{:S(2)}) collective-permute-start(bf16[4,3,8,384]{3,2,1,0:T(8,128)(2,1)S(1)} %get-tuple-element.48), channel_id=1, source_target_pairs={{0,1},{1,0},{2,3},{3,2},{4,5},{5,4},{6,7},{7,6},{8,9},{9,8},{10,11... | collective-permute-start | bytes 221192 | tf_op jit(solution)/shard_map/ppermute | solution.py:46
  2.3 0.8 %collective-permute-start.1 = (bf16[4,3,8,384]{3,2,1,0:T(8,128)(2,1)S(1)}, bf16[4,3,8,384]{3,2,1,0:T(8,128)(2,1)S(1)}, u32[]{:S(2)}, u32[]{:S(2)}) collective-permute-start(bf16[4,3,8,384]{3,2,1,0:T(8,128)(2,1)S(1)} %get-tuple-element.49), channel_id=1, source_target_pairs={{1,2},{3,4},{5,6},{7,8},{9,10},{11,12},{13,14},{2,1},{4,3},{6,5},{... | collective-permute-start | bytes 221192 | tf_op jit(solution)/shard_map/ppermute | solution.py:52
  3.8 2.1 %shard_map.139 = (f32[3,4,8,24,128]{4,3,2,1,0:T(8,128)S(1)}, f32[256,384]{1,0:T(8,128)S(1)}, bf16[256,512]{1,0:T(8,128)(2,1)S(1)}, f32[256,1536]{1,0:T(8,128)S(1)}, f32[1,384]{1,0:T(1,128)S(1)}) custom-call(s32[4,8]{1,0:T(4,128)S(1)} %bitcast.9, s32[1,1]{1,0:T(1,128)S(6)} %copy.15.counts_ref, f32[1,4]{1,0:T(1,128)S(1)} %copy-done.9, f32[1,384]{1,0:T(1,128)S(1)} %copy-done.8, ...), custom_call_target="tpu_custom_call" | custom-call | flops 301989888 | bytes 5060756 | tf_op jit(solution)/shard_map/pallas_call | solution.py:29
  5.8 0.0 collective-permute-done.core_ref
  5.9 0.0 collective-permute-done.1.cross_ref
  5.9 2.6 %shard_map.140 = (f32[3,4,6,24,128]{4,3,2,1,0:T(8,128)S(1)}, f32[256,384]{1,0:T(8,128)S(1)}, f32[256,1]{1,0:T(8,128)S(1)}, f32[256,1536]{1,0:T(8,128)S(1)}, f32[...) custom-call(s32[4,8]{1,0:T(4,128)S(1)} %bitcast.10, ...), custom_call_target="tpu_custom_call" | custom-call | flops 603979776 | bytes 9040004 | tf_op jit(solution)/shard_map/pallas_call | solution.py:29
  8.4 4.0 %collective-permute-start.2 = (bf16[768,384]{1,0:T(8,128)(2,1)S(1)}, bf16[768,384]{1,0:T(8,128)(2,1)S(1)}, u32[]{:S(2)}, u32[]{:S(2)}) collective-permute-start(bf16[768,384]{1,0:T(8,128)(2,1)S(1)} %get-tuple-element.53), channel_id=1, source_target_pairs={{0,1},{1,0},{2,3},{3,2},{4,5},{5,4},{6,7},{7,6},{8,9},{9,8},{10,11... | collective-permute-start | bytes 1769480 | tf_op jit(solution)/shard_map/ppermute | solution.py:46
  12.4 1.6 %collective-permute-done.2.refs_1_ = bf16[768,384]{1,0:T(8,128)(2,1)S(1)} collective-permute-done((bf16[768,384]{1,0:T(8,128)(2,1)S(1)}, bf16[768,384]{1,0:T(8,128)(2,1)S(1)}, u32[]{:S(2)}, u32[]{:S(2)}) %collective-permute-start.2) | collective-permute-done | bytes 589856 | tf_op jit(solution)/shard_map/ppermute | solution.py:46
  14.0 0.3 shard_map.141
  14.3 2.3 %collective-permute-start.3 = (bf16[192,384]{1,0:T(8,128)(2,1)S(1)}, bf16[192,384]{1,0:T(8,128)(2,1)S(1)}, u32[]{:S(2)}, u32[]{:S(2)}) collective-permute-start(bf16[192,384]{1,0:T(8,128)(2,1)S(1)} %get-tuple-element.55), channel_id=1, source_target_pairs={{0,2},{1,3},{2,0},{3,1},{4,6},{5,7},{6,4},{7,5},{8,10},{9,11},{10,... | collective-permute-start | bytes 442376 | tf_op jit(solution)/shard_map/ppermute | solution.py:46
  16.6 1.6 %collective-permute-start.4 = (bf16[192,384]{1,0:T(8,128)(2,1)S(1)}, bf16[192,384]{1,0:T(8,128)(2,1)S(1)}, u32[]{:S(2)}, u32[]{:S(2)}) collective-permute-start(bf16[192,384]{1,0:T(8,128)(2,1)S(1)} %get-tuple-element.57), channel_id=1, source_target_pairs={{0,4},{1,5},{2,6},{3,7},{4,0},{5,1},{6,2},{7,3},{8,12},{9,13},{10,... | collective-permute-start | bytes 442376 | tf_op jit(solution)/shard_map/ppermute | solution.py:46
  18.1 2.8 %collective-permute-done.3.refs_1_ = bf16[192,384]{1,0:T(8,128)(2,1)S(1)} collective-permute-done((bf16[192,384]{1,0:T(8,128)(2,1)S(1)}, bf16[192,384]{1,0:T(8,128)(2,1)S(1)}, u32[]{:S(2)}, u32[]{:S(2)}) %collective-permute-start.3) | collective-permute-done | bytes 147488 | tf_op jit(solution)/shard_map/ppermute | solution.py:46
  20.9 1.5 %collective-permute-done.4.refs_3_ = bf16[192,384]{1,0:T(8,128)(2,1)S(1)} collective-permute-done((bf16[192,384]{1,0:T(8,128)(2,1)S(1)}, bf16[192,384]{1,0:T(8,128)(2,1)S(1)}, u32[]{:S(2)}, u32[]{:S(2)}) %collective-permute-start.4) | collective-permute-done | bytes 147488 | tf_op jit(solution)/shard_map/ppermute | solution.py:46
  22.4 0.1 shard_map.142
  22.5 1.6 %collective-permute-start.5 = (bf16[96,384]{1,0:T(8,128)(2,1)S(1)}, bf16[96,384]{1,0:T(8,128)(2,1)S(1)}, u32[]{:S(2)}, u32[]{:S(2)}) collective-permute-start(bf16[96,384]{1,0:T(8,128)(2,1)S(1)} %get-tuple-element.59), channel_id=1, source_target_pairs={{0,4},{1,5},{2,6},{3,7},{4,0},{5,1},{6,2},{7,3},{8,12},{9,13},{10,... | collective-permute-start | bytes 221192 | tf_op jit(solution)/shard_map/ppermute | solution.py:46
  24.2 0.4 collective-permute-start.6
  24.6 1.6 %shard_map.145 = (f32[256,384]{1,0:T(8,128)S(1)}, bf16[4,3,8,384]{3,2,1,0:T(8,128)(2,1)S(1)}, bf16[4,3,8,384]{3,2,1,0:T(8,128)(2,1)S(1)}, f32[1,384]{1,0:T(1,128)S(1)}) custom-call(s32[1,1]{1,0:T(1,128)} %bitcast.place_ref, s32[1,1]{1,0:T(1,128)S(6)} %copy.15.counts_ref, f32[1,4]{1,0:T(1,128)S(1)} %copy-done.9, f32[256,1536]{1,0:T(8,128)S(1)} %get-tuple-element.68.pre_ref, ...), custom_call_target="tpu_custom_call" | custom-call | flops 301989888 | bytes 8805400 | tf_op jit(solution)/shard_map/pallas_call | solution.py:29
  26.1 1.4 %shard_map.146 = (f32[56,384]{1,0:T(8,128)S(1)}, bf16[56,384]{1,0:T(8,128)(2,1)S(1)}) custom-call(f32[3,4,8,24,128]{4,3,2,1,0:T(8,128)S(1)} %get-tuple-element.66.pad_ref, f32[3,4,6,24,128]{4,3,2,1,0:T(8,128)S(1)} %get-tuple-element.67.edge_ref, f32[256,384]{1,0:T(8,128)S(1)} %get-tuple-element.75.grad_ref, f32[1,384]{1,0:T(1,128)S(1)} %get-tuple-element.76.emb_ref), custom_call_target="tpu_custom_call" | custom-call | bytes 2588160 | tf_op jit(solution)/shard_map/pallas_call | solution.py:29
  27.5 0.1 collective-permute-start.9
  27.6 1.2 %collective-permute-done.9.got_ref = bf16[56,384]{1,0:T(8,128)(2,1)S(1)} collective-permute-done((bf16[56,384]{1,0:T(8,128)(2,1)S(1)}, bf16[56,384]{1,0:T(8,128)(2,1)S(1)}, u32[]{:S(2)}, u32[]{:S(2)}) %collective-permute-start.9) | collective-permute-done | bytes 43040 | tf_op jit(solution)/shard_map/ppermute | solution.py:46
  28.8 1.6 %collective-permute-start.10 = (bf16[56,384]{1,0:T(8,128)(2,1)S(1)}, bf16[56,384]{1,0:T(8,128)(2,1)S(1)}, u32[]{:S(2)}, u32[]{:S(2)}) collective-permute-start(bf16[56,384]{1,0:T(8,128)(2,1)S(1)} %get-tuple-element.80), channel_id=1, source_target_pairs={{0,16},{16,0},{1,17},{17,1},{2,18},{18,2},{3,19},{19,3},{4,20},{20... | collective-permute-start | bytes 129032 | tf_op jit(solution)/shard_map/ppermute | solution.py:46
  30.4 0.0 collective-permute-done.5.refs_1_
  30.4 0.0 collective-permute-done.6.refs_3_
  30.4 2.7 %collective-permute-start.7 = (bf16[96,384]{1,0:T(8,128)(2,1)S(1)}, bf16[96,384]{1,0:T(8,128)(2,1)S(1)}, u32[]{:S(2)}, u32[]{:S(2)}) collective-permute-start(bf16[96,384]{1,0:T(8,128)(2,1)S(1)} %get-tuple-element.63), channel_id=1, source_target_pairs={{0,8},{1,9},{2,10},{3,11},{4,12},{5,13},{6,14},{7,15},{8,0},{9,1},... | collective-permute-start | bytes 221192 | tf_op jit(solution)/shard_map/ppermute | solution.py:46
  33.1 0.0 collective-permute-done.10.got_ref
  33.1 1.5 %collective-permute-start.11 = (bf16[56,384]{1,0:T(8,128)(2,1)S(1)}, bf16[56,384]{1,0:T(8,128)(2,1)S(1)}, u32[]{:S(2)}, u32[]{:S(2)}) collective-permute-start(bf16[56,384]{1,0:T(8,128)(2,1)S(1)} %get-tuple-element.82), channel_id=1, source_target_pairs={{0,2},{1,3},{2,0},{3,1},{4,6},{5,7},{6,4},{7,5},{8,10},{9,11},{10,... | collective-permute-start | bytes 129032 | tf_op jit(solution)/shard_map/ppermute | solution.py:46
  34.6 2.6 %collective-permute-done.11.got_ref = bf16[56,384]{1,0:T(8,128)(2,1)S(1)} collective-permute-done((bf16[56,384]{1,0:T(8,128)(2,1)S(1)}, bf16[56,384]{1,0:T(8,128)(2,1)S(1)}, u32[]{:S(2)}, u32[]{:S(2)}) %collective-permute-start.11) | collective-permute-done | bytes 43040 | tf_op jit(solution)/shard_map/ppermute | solution.py:46
  37.2 0.5 %collective-permute-start.12 = (bf16[56,384]{1,0:T(8,128)(2,1)S(1)}, bf16[56,384]{1,0:T(8,128)(2,1)S(1)}, u32[]{:S(2)}, u32[]{:S(2)}) collective-permute-start(bf16[56,384]{1,0:T(8,128)(2,1)S(1)} %get-tuple-element.84), channel_id=1, source_target_pairs={{0,4},{1,5},{2,6},{3,7},{4,0},{5,1},{6,2},{7,3},{8,12},{9,13},{10,... | collective-permute-start | bytes 129032 | tf_op jit(solution)/shard_map/ppermute | solution.py:46
  37.8 0.0 collective-permute-start.14
  37.8 0.7 %collective-permute-start.15 = (bf16[4,3,8,384]{3,2,1,0:T(8,128)(2,1)S(1)}, bf16[4,3,8,384]{3,2,1,0:T(8,128)(2,1)S(1)}, u32[]{:S(2)}, u32[]{:S(2)}) collective-permute-start(bf16[4,3,8,384]{3,2,1,0:T(8,128)(2,1)S(1)} %get-tuple-element.89), channel_id=1, source_target_pairs={{1,2},{3,4},{5,6},{7,8},{9,10},{11,12},{13,14},{2,1},{4,3},{6,5},{... | collective-permute-start | bytes 221192 | tf_op jit(solution)/shard_map/ppermute | solution.py:52
  38.4 0.0 collective-permute-done.7.refs_1_
  38.5 1.3 %collective-permute-start.8 = (bf16[96,384]{1,0:T(8,128)(2,1)S(1)}, bf16[96,384]{1,0:T(8,128)(2,1)S(1)}, u32[]{:S(2)}, u32[]{:S(2)}) collective-permute-start(bf16[96,384]{1,0:T(8,128)(2,1)S(1)} %get-tuple-element.65), channel_id=1, source_target_pairs={{0,16},{16,0},{1,17},{17,1},{2,18},{18,2},{3,19},{19,3},{4,20},{20... | collective-permute-start | bytes 221192 | tf_op jit(solution)/shard_map/ppermute | solution.py:46
  39.8 1.5 %collective-permute-done.12.got_ref = bf16[56,384]{1,0:T(8,128)(2,1)S(1)} collective-permute-done((bf16[56,384]{1,0:T(8,128)(2,1)S(1)}, bf16[56,384]{1,0:T(8,128)(2,1)S(1)}, u32[]{:S(2)}, u32[]{:S(2)}) %collective-permute-start.12) | collective-permute-done | bytes 43040 | tf_op jit(solution)/shard_map/ppermute | solution.py:46
  41.4 4.0 %collective-permute-start.13 = (bf16[56,384]{1,0:T(8,128)(2,1)S(1)}, bf16[56,384]{1,0:T(8,128)(2,1)S(1)}, u32[]{:S(2)}, u32[]{:S(2)}) collective-permute-start(bf16[56,384]{1,0:T(8,128)(2,1)S(1)} %get-tuple-element.86), channel_id=1, source_target_pairs={{0,8},{1,9},{2,10},{3,11},{4,12},{5,13},{6,14},{7,15},{8,0},{9,1},... | collective-permute-start | bytes 129032 | tf_op jit(solution)/shard_map/ppermute | solution.py:46
  45.4 1.6 %shard_map.152.part_ref = f32[256,384]{1,0:T(8,128)S(1)} custom-call(s32[4,8]{1,0:T(4,128)S(1)} %bitcast.11, f32[256,384]{1,0:T(8,128)S(1)} %get-tuple-element.75.grad_ref, f32[7,7,384]{2,1,0:T(8,128)S(1)} %copy-done.3), custom_call_target="tpu_custom_call" | custom-call | bytes 861824 | tf_op jit(solution)/shard_map/pallas_call | solution.py:29
  47.0 0.0 collective-permute-done.14.core_ref
  47.0 0.0 collective-permute-done.15.cross_ref
  47.1 1.8 %shard_map.153 = bf16[256,384]{1,0:T(8,128)(2,1)} custom-call(s32[4,8]{1,0:T(4,128)S(1)} %bitcast.12, s32[1,1]{1,0:T(1,128)} %bitcast.place_ref, s32[1,1]{1,0:T(1,128)S(6)} %copy.15.counts_ref, f32[1,4]{1,0:T(1,128)S(1)} %copy-done.9, f32[256,384]{1,0:T(8,128)S(1)} %shard_map.152.part_ref, bf16[4,3,8,384]{3,2,1,0:T(8,128)(2,1)S(1)} %collective-permute-done.14.core_ref, ...), custom_call_target="tpu_custom_call" | custom-call | bytes 1010840 | tf_op jit(solution)/shard_map/pallas_call | solution.py:29
  48.9 0.0 collective-permute-done.13.new_ref
  48.9 0.0 collective-permute-done.8.got_ref
  48.9 0.7 %shard_map.151 = (f32[96,384]{1,0:T(8,128)}, f32[7,7,384]{2,1,0:T(8,128)}, f32[1,384]{1,0:T(1,128)}) custom-call(f32[96,384]{1,0:T(8,128)S(1)} %get-tuple-element.64.keep_ref, bf16[96,384]{1,0:T(8,128)(2,1)S(1)} %collective-permute-done.8.got_ref, f32[56,384]{1,0:T(8,128)S(1)} %get-tuple-element.85.state_ref, bf16[56,384]{1,0:T(8,128)(2,1)S(1)} %collective-permute-done.13.new_ref), custom_call_target="tpu_custom_call" | custom-call | bytes 574464 | tf_op jit(solution)/shard_map/pallas_call | solution.py:29
  (22 shorter events, 0.2 us)
Async XLA Ops:
  0.6 0.9 %copy-start.4 = (bf16[1,4,8,8,384]{4,3,2,1,0:T(8,128)(2,1)S(1)}, bf16[1,4,8,8,384]{4,3,2,1,0:T(8,128)(2,1)}, u32[]{:S(2)}) copy-start(bf16[1,4,8,8,384]{4,3,2,1,0:T(8,128)(2,1)} %param.11) | copy-start | bytes 589828
  1.6 2.1 %copy-start = (bf16[1536,384]{1,0:T(8,128)(2,1)S(1)}, bf16[1536,384]{1,0:T(8,128)(2,1)}, u32[]{:S(2)}) copy-start(bf16[1536,384]{1,0:T(8,128)(2,1)} %w_out_ref.3) | copy-start | bytes 3538948
  1.6 2.2 %copy-start.2 = (bf16[1,4,8,8,384]{4,3,2,1,0:T(8,128)(2,1)S(1)}, bf16[1,4,8,8,384]{4,3,2,1,0:T(8,128)(2,1)}, u32[]{:S(2)}) copy-start(bf16[1,4,8,8,384]{4,3,2,1,0:T(8,128)(2,1)} %param.12) | copy-start | bytes 589828
  1.6 2.2 %copy-start.3 = (f32[7,7,384]{2,1,0:T(8,128)S(1)}, f32[7,7,384]{2,1,0:T(8,128)}, u32[]{:S(2)}) copy-start(f32[7,7,384]{2,1,0:T(8,128)} %kern_ref.7) | copy-start | bytes 225796
  1.6 2.2 %copy-start.5 = (bf16[1,4,8,8,384]{4,3,2,1,0:T(8,128)(2,1)S(1)}, bf16[1,4,8,8,384]{4,3,2,1,0:T(8,128)(2,1)}, u32[]{:S(2)}) copy-start(bf16[1,4,8,8,384]{4,3,2,1,0:T(8,128)(2,1)} %param.11) | copy-start | bytes 589828
  1.6 2.2 %copy-start.6 = (s32[1,4,8]{2,1,0:T(4,128)S(1)}, s32[1,4,8]{2,1,0:T(4,128)}, u32[]{:S(2)}) copy-start(s32[1,4,8]{2,1,0:T(4,128)} %param.15) | copy-start | bytes 388
  1.6 2.2 %copy-start.7 = (f32[384]{0:T(512)S(1)}, f32[384]{0:T(512)}, u32[]{:S(2)}) copy-start(f32[384]{0:T(512)} %scale_ref.3) | copy-start | bytes 4612
  1.6 2.2 %copy-start.8 = (f32[1,384]{1,0:T(1,128)S(1)}, f32[1,384]{1,0:T(1,128)}, u32[]{:S(2)}) copy-start(f32[1,384]{1,0:T(1,128)} %cot_ref.3) | copy-start | bytes 4612
  1.6 2.2 %copy-start.9 = (f32[1,4]{1,0:T(1,128)S(1)}, f32[1,4]{1,0:T(1,128)}, u32[]{:S(2)}) copy-start(f32[1,4]{1,0:T(1,128)} %pool_ref.5) | copy-start | bytes 52
  1.7 4.2 %copy-start.1 = (bf16[384,1536]{1,0:T(8,128)(2,1)S(1)}, bf16[384,1536]{1,0:T(8,128)(2,1)}, u32[]{:S(2)}) copy-start(bf16[384,1536]{1,0:T(8,128)(2,1)} %w_in_ref.3) | copy-start | bytes 3538948
  1.7 4.2 %copy-start.10 = (f32[384]{0:T(512)S(1)}, f32[384]{0:T(512)}, u32[]{:S(2)}) copy-start(f32[384]{0:T(512)} %gain_ref.3) | copy-start | bytes 4612
  1.7 4.1 %collective-permute-start = (bf16[4,3,8,384]{3,2,1,0:T(8,128)(2,1)S(1)}, bf16[4,3,8,384]{3,2,1,0:T(8,128)(2,1)S(1)}, u32[]{:S(2)}, u32[]{:S(2)}) collective-permute-start(bf16[4,3,8,384]{3,2,1,0:T(8,128)(2,1)S(1)} %get-tuple-element.48), channel_id=1, source_target_pairs={{0,1},{1,0},{2,3},{3,2},{4,5},{5,4},{6,7},{7,6},{8,9},{9,8},{10,11... | collective-permute-start | bytes 221192 | tf_op jit(solution)/shard_map/ppermute | solution.py:46
  2.3 3.6 %collective-permute-start.1 = (bf16[4,3,8,384]{3,2,1,0:T(8,128)(2,1)S(1)}, bf16[4,3,8,384]{3,2,1,0:T(8,128)(2,1)S(1)}, u32[]{:S(2)}, u32[]{:S(2)}) collective-permute-start(bf16[4,3,8,384]{3,2,1,0:T(8,128)(2,1)S(1)} %get-tuple-element.49), channel_id=1, source_target_pairs={{1,2},{3,4},{5,6},{7,8},{9,10},{11,12},{13,14},{2,1},{4,3},{6,5},{... | collective-permute-start | bytes 221192 | tf_op jit(solution)/shard_map/ppermute | solution.py:52
  8.4 5.6 %collective-permute-start.2 = (bf16[768,384]{1,0:T(8,128)(2,1)S(1)}, bf16[768,384]{1,0:T(8,128)(2,1)S(1)}, u32[]{:S(2)}, u32[]{:S(2)}) collective-permute-start(bf16[768,384]{1,0:T(8,128)(2,1)S(1)} %get-tuple-element.53), channel_id=1, source_target_pairs={{0,1},{1,0},{2,3},{3,2},{4,5},{5,4},{6,7},{7,6},{8,9},{9,8},{10,11... | collective-permute-start | bytes 1769480 | tf_op jit(solution)/shard_map/ppermute | solution.py:46
  14.3 6.6 %collective-permute-start.3 = (bf16[192,384]{1,0:T(8,128)(2,1)S(1)}, bf16[192,384]{1,0:T(8,128)(2,1)S(1)}, u32[]{:S(2)}, u32[]{:S(2)}) collective-permute-start(bf16[192,384]{1,0:T(8,128)(2,1)S(1)} %get-tuple-element.55), channel_id=1, source_target_pairs={{0,2},{1,3},{2,0},{3,1},{4,6},{5,7},{6,4},{7,5},{8,10},{9,11},{10,... | collective-permute-start | bytes 442376 | tf_op jit(solution)/shard_map/ppermute | solution.py:46
  16.6 5.8 %collective-permute-start.4 = (bf16[192,384]{1,0:T(8,128)(2,1)S(1)}, bf16[192,384]{1,0:T(8,128)(2,1)S(1)}, u32[]{:S(2)}, u32[]{:S(2)}) collective-permute-start(bf16[192,384]{1,0:T(8,128)(2,1)S(1)} %get-tuple-element.57), channel_id=1, source_target_pairs={{0,4},{1,5},{2,6},{3,7},{4,0},{5,1},{6,2},{7,3},{8,12},{9,13},{10,... | collective-permute-start | bytes 442376 | tf_op jit(solution)/shard_map/ppermute | solution.py:46
  22.5 7.9 %collective-permute-start.5 = (bf16[96,384]{1,0:T(8,128)(2,1)S(1)}, bf16[96,384]{1,0:T(8,128)(2,1)S(1)}, u32[]{:S(2)}, u32[]{:S(2)}) collective-permute-start(bf16[96,384]{1,0:T(8,128)(2,1)S(1)} %get-tuple-element.59), channel_id=1, source_target_pairs={{0,4},{1,5},{2,6},{3,7},{4,0},{5,1},{6,2},{7,3},{8,12},{9,13},{10,... | collective-permute-start | bytes 221192 | tf_op jit(solution)/shard_map/ppermute | solution.py:46
  24.2 6.2 %collective-permute-start.6 = (bf16[96,384]{1,0:T(8,128)(2,1)S(1)}, bf16[96,384]{1,0:T(8,128)(2,1)S(1)}, u32[]{:S(2)}, u32[]{:S(2)}) collective-permute-start(bf16[96,384]{1,0:T(8,128)(2,1)S(1)} %get-tuple-element.61), channel_id=1, source_target_pairs={{0,2},{1,3},{2,0},{3,1},{4,6},{5,7},{6,4},{7,5},{8,10},{9,11},{10,... | collective-permute-start | bytes 221192 | tf_op jit(solution)/shard_map/ppermute | solution.py:46
  27.5 1.3 %collective-permute-start.9 = (bf16[56,384]{1,0:T(8,128)(2,1)S(1)}, bf16[56,384]{1,0:T(8,128)(2,1)S(1)}, u32[]{:S(2)}, u32[]{:S(2)}) collective-permute-start(bf16[56,384]{1,0:T(8,128)(2,1)S(1)} %get-tuple-element.78), channel_id=1, source_target_pairs={{0,1},{1,0},{2,3},{3,2},{4,5},{5,4},{6,7},{7,6},{8,9},{9,8},{10,11... | collective-permute-start | bytes 129032 | tf_op jit(solution)/shard_map/ppermute | solution.py:46
  28.8 4.3 %collective-permute-start.10 = (bf16[56,384]{1,0:T(8,128)(2,1)S(1)}, bf16[56,384]{1,0:T(8,128)(2,1)S(1)}, u32[]{:S(2)}, u32[]{:S(2)}) collective-permute-start(bf16[56,384]{1,0:T(8,128)(2,1)S(1)} %get-tuple-element.80), channel_id=1, source_target_pairs={{0,16},{16,0},{1,17},{17,1},{2,18},{18,2},{3,19},{19,3},{4,20},{20... | collective-permute-start | bytes 129032 | tf_op jit(solution)/shard_map/ppermute | solution.py:46
  30.4 8.0 %collective-permute-start.7 = (bf16[96,384]{1,0:T(8,128)(2,1)S(1)}, bf16[96,384]{1,0:T(8,128)(2,1)S(1)}, u32[]{:S(2)}, u32[]{:S(2)}) collective-permute-start(bf16[96,384]{1,0:T(8,128)(2,1)S(1)} %get-tuple-element.63), channel_id=1, source_target_pairs={{0,8},{1,9},{2,10},{3,11},{4,12},{5,13},{6,14},{7,15},{8,0},{9,1},... | collective-permute-start | bytes 221192 | tf_op jit(solution)/shard_map/ppermute | solution.py:46
  33.1 4.1 %collective-permute-start.11 = (bf16[56,384]{1,0:T(8,128)(2,1)S(1)}, bf16[56,384]{1,0:T(8,128)(2,1)S(1)}, u32[]{:S(2)}, u32[]{:S(2)}) collective-permute-start(bf16[56,384]{1,0:T(8,128)(2,1)S(1)} %get-tuple-element.82), channel_id=1, source_target_pairs={{0,2},{1,3},{2,0},{3,1},{4,6},{5,7},{6,4},{7,5},{8,10},{9,11},{10,... | collective-permute-start | bytes 129032 | tf_op jit(solution)/shard_map/ppermute | solution.py:46
  37.2 4.1 %collective-permute-start.12 = (bf16[56,384]{1,0:T(8,128)(2,1)S(1)}, bf16[56,384]{1,0:T(8,128)(2,1)S(1)}, u32[]{:S(2)}, u32[]{:S(2)}) collective-permute-start(bf16[56,384]{1,0:T(8,128)(2,1)S(1)} %get-tuple-element.84), channel_id=1, source_target_pairs={{0,4},{1,5},{2,6},{3,7},{4,0},{5,1},{6,2},{7,3},{8,12},{9,13},{10,... | collective-permute-start | bytes 129032 | tf_op jit(solution)/shard_map/ppermute | solution.py:46
  37.8 9.3 %collective-permute-start.14 = (bf16[4,3,8,384]{3,2,1,0:T(8,128)(2,1)S(1)}, bf16[4,3,8,384]{3,2,1,0:T(8,128)(2,1)S(1)}, u32[]{:S(2)}, u32[]{:S(2)}) collective-permute-start(bf16[4,3,8,384]{3,2,1,0:T(8,128)(2,1)S(1)} %get-tuple-element.88), channel_id=1, source_target_pairs={{0,1},{1,0},{2,3},{3,2},{4,5},{5,4},{6,7},{7,6},{8,9},{9,8},{10,11... | collective-permute-start | bytes 221192 | tf_op jit(solution)/shard_map/ppermute | solution.py:46
  37.8 9.3 %collective-permute-start.15 = (bf16[4,3,8,384]{3,2,1,0:T(8,128)(2,1)S(1)}, bf16[4,3,8,384]{3,2,1,0:T(8,128)(2,1)S(1)}, u32[]{:S(2)}, u32[]{:S(2)}) collective-permute-start(bf16[4,3,8,384]{3,2,1,0:T(8,128)(2,1)S(1)} %get-tuple-element.89), channel_id=1, source_target_pairs={{1,2},{3,4},{5,6},{7,8},{9,10},{11,12},{13,14},{2,1},{4,3},{6,5},{... | collective-permute-start | bytes 221192 | tf_op jit(solution)/shard_map/ppermute | solution.py:52
  38.5 10.4 %collective-permute-start.8 = (bf16[96,384]{1,0:T(8,128)(2,1)S(1)}, bf16[96,384]{1,0:T(8,128)(2,1)S(1)}, u32[]{:S(2)}, u32[]{:S(2)}) collective-permute-start(bf16[96,384]{1,0:T(8,128)(2,1)S(1)} %get-tuple-element.65), channel_id=1, source_target_pairs={{0,16},{16,0},{1,17},{17,1},{2,18},{18,2},{3,19},{19,3},{4,20},{20... | collective-permute-start | bytes 221192 | tf_op jit(solution)/shard_map/ppermute | solution.py:46
  41.4 7.5 %collective-permute-start.13 = (bf16[56,384]{1,0:T(8,128)(2,1)S(1)}, bf16[56,384]{1,0:T(8,128)(2,1)S(1)}, u32[]{:S(2)}, u32[]{:S(2)}) collective-permute-start(bf16[56,384]{1,0:T(8,128)(2,1)S(1)} %get-tuple-element.86), channel_id=1, source_target_pairs={{0,8},{1,9},{2,10},{3,11},{4,12},{5,13},{6,14},{7,15},{8,0},{9,1},... | collective-permute-start | bytes 129032 | tf_op jit(solution)/shard_map/ppermute | solution.py:46

commit v4 on v3

--- a/solution.py
+++ b/solution.py
@@ -46,12 +46,17 @@
     return lax.ppermute(value, axis, [(source, source ^ bit) for source in range(count)])
 
 
-def crossed(value, axis):
-    count = lax.axis_size(axis)
-    firsts = range(1, count - 1, 2)
-    return lax.ppermute(
-        value, axis, [(n, n + 1) for n in firsts] + [(n + 1, n) for n in firsts]
-    )
+def crossed(value):
+    groups, count = lax.axis_size("dp"), lax.axis_size("space")
+    targets = []
+    for group in range(groups):
+        for n in range(count):
+            step = 1 if n % 2 else -1
+            if 0 <= n + step < count:
+                targets.append((group * count + n, group * count + n + step))
+            elif (group ^ 1) < groups:
+                targets.append((group * count + n, (group ^ 1) * count + n))
+    return lax.ppermute(value, ("dp", "space"), targets)
 
 
 def valid(entry):
@@ -442,7 +447,7 @@
         edge_kernel, [struct(edge_shape, bf16)] * 2, [SMEM, VMEM], [place, own],
         flops=EDGE_COST,
     )
-    cross = crossed(cross, "space")
+    cross = crossed(cross)
     core = swapped(core, "space", 1)
 
     pad, conv, mixed, act_grad, own_sum = call(
@@ -489,7 +494,7 @@
         [place, counts, pool_weight, pre, cdf, act_grad, w_in, normed, inv, norm_gain, pooled, w_out, layer_scale, own_sum],
         flops=2 * pixels * channels * hidden,
     )
-    cross = crossed(cross, "space")
+    cross = crossed(cross)
     core = swapped(core, "space", 1)
 
     def merge(parts_, splits):

time: 49.8 us -> 46.2 us (0.928)
  starting transfers between devices: 23.5 us -> 19.8 us
    ppermute x14, starting transfers between devices: 22.1 us -> 16 us  [swapped(): lax.ppermute(value, axis, [(source, source ^ bit) for source in range(cou...]
    ppermute x2, starting transfers between devices: 1.44 us -> 3.83 us  [crossed(): return lax.ppermute(value, ('dp', 'space'), targets)]
  transfers between devices with their start and end apart: 16 -> 16, of which waited for: 6 -> 6; matrix products, arithmetic and copies ran while one was open for 0% -> 0% of each run, Pallas kernels for 17% -> 19%
where the time goes in v4:
time: 46.2 us; the launch traced here: 46 us
  starting transfers between devices  19.8 us (43%)
  Pallas kernels  12.3 us (27%)
  waiting for transfers between devices  11.4 us (25%)
  between operations  1.55 us (3%)
  local copies, waits for them, and re-layouts  0.96 us (2%)
    ppermute x14, starting transfers between devices, swapped(): lax.ppermute(value, axis, [(source, source ^ bit) for source in range(cou...  16 us
    pallas_call x16, Pallas kernels, call(): pl.pallas_call(body, out_shape=out_shape, in_specs=in_specs, out_specs=ou...  12.3 us
    ppermute x14, waiting for transfers between devices, swapped(): lax.ppermute(value, axis, [(source, source ^ bit) for source in range(cou...  11.4 us
    ppermute x2, starting transfers between devices, crossed(): return lax.ppermute(value, ('dp', 'space'), targets)  3.83 us
    unnamed x22, local copies, waits for them, and re-layouts  0.96 us
  transfers between devices with their start and end apart: 16, of which 6 were waited for; matrix products, arithmetic and copies ran while one was open for 0% of the time, Pallas kernels for 19%

profile of v4, /device:TPU:0, one launch (start us, length us, event | category | flops | bytes accessed | tf_op | source)
XLA Modules:
  0.0 46.0 jit_solution(11511118708366455609)
XLA Ops:
  0.6 0.9 %copy-done.4 = bf16[1,4,8,8,384]{4,3,2,1,0:T(8,128)(2,1)S(1)} copy-done((bf16[1,4,8,8,384]{4,3,2,1,0:T(8,128)(2,1)S(1)}, bf16[1,4,8,8,384]{4,3,2,1,0:T(8,128)(2,1)}, u32[]{:S(2)}) %copy-start.4) | copy-done | bytes 196632
  1.6 0.0 copy-start.6
  1.6 0.0 copy-start.7
  1.6 0.0 copy-start.8
  1.6 0.1 shard_map.138
  1.7 0.0 copy-start.1
  1.7 0.0 copy-start.10
  1.7 0.6 %collective-permute-start = (bf16[4,3,8,384]{3,2,1,0:T(8,128)(2,1)S(1)}, bf16[4,3,8,384]{3,2,1,0:T(8,128)(2,1)S(1)}, u32[]{:S(2)}, u32[]{:S(2)}) collective-permute-start(bf16[4,3,8,384]{3,2,1,0:T(8,128)(2,1)S(1)} %get-tuple-element.48), channel_id=1, source_target_pairs={{0,1},{1,0},{2,3},{3,2},{4,5},{5,4},{6,7},{7,6},{8,9},{9,8},{10,11... | collective-permute-start | bytes 221192 | tf_op jit(solution)/shard_map/ppermute | solution.py:46
  2.3 2.6 %collective-permute-start.1 = (bf16[4,3,8,384]{3,2,1,0:T(8,128)(2,1)S(1)}, bf16[4,3,8,384]{3,2,1,0:T(8,128)(2,1)S(1)}, u32[]{:S(2)}, u32[]{:S(2)}) collective-permute-start(bf16[4,3,8,384]{3,2,1,0:T(8,128)(2,1)S(1)} %get-tuple-element.49), channel_id=1, source_target_pairs={{0,16},{1,2},{2,1},{3,4},{4,3},{5,6},{6,5},{7,8},{8,7},{9,10},{10,... | collective-permute-start | bytes 221192 | tf_op jit(solution)/shard_map/ppermute | solution.py:59
  5.6 2.0 %shard_map.139 = (f32[3,4,8,24,128]{4,3,2,1,0:T(8,128)S(1)}, f32[256,384]{1,0:T(8,128)S(1)}, bf16[256,512]{1,0:T(8,128)(2,1)S(1)}, f32[256,1536]{1,0:T(8,128)S(1)}, f32[1,384]{1,0:T(1,128)S(1)}) custom-call(s32[4,8]{1,0:T(4,128)S(1)} %bitcast.9, s32[1,1]{1,0:T(1,128)S(6)} %copy.15.counts_ref, f32[1,4]{1,0:T(1,128)S(1)} %copy-done.9, f32[1,384]{1,0:T(1,128)S(1)} %copy-done.8, ...), custom_call_target="tpu_custom_call" | custom-call | flops 301989888 | bytes 5060756 | tf_op jit(solution)/shard_map/pallas_call | solution.py:29
  7.6 0.0 collective-permute-done.core_ref
  7.6 0.0 collective-permute-done.1.cross_ref
  7.6 2.6 %shard_map.140 = (f32[3,4,6,24,128]{4,3,2,1,0:T(8,128)S(1)}, f32[256,384]{1,0:T(8,128)S(1)}, f32[256,1]{1,0:T(8,128)S(1)}, f32[256,1536]{1,0:T(8,128)S(1)}, f32[...) custom-call(s32[4,8]{1,0:T(4,128)S(1)} %bitcast.10, ...), custom_call_target="tpu_custom_call" | custom-call | flops 603979776 | bytes 9040004 | tf_op jit(solution)/shard_map/pallas_call | solution.py:29
  10.2 0.2 collective-permute-start.2
  10.4 1.9 %collective-permute-done.2.refs_1_ = bf16[768,384]{1,0:T(8,128)(2,1)S(1)} collective-permute-done((bf16[768,384]{1,0:T(8,128)(2,1)S(1)}, bf16[768,384]{1,0:T(8,128)(2,1)S(1)}, u32[]{:S(2)}, u32[]{:S(2)}) %collective-permute-start.2) | collective-permute-done | bytes 589856 | tf_op jit(solution)/shard_map/ppermute | solution.py:46
  12.3 0.3 shard_map.141
  12.5 2.0 %collective-permute-start.3 = (bf16[192,384]{1,0:T(8,128)(2,1)S(1)}, bf16[192,384]{1,0:T(8,128)(2,1)S(1)}, u32[]{:S(2)}, u32[]{:S(2)}) collective-permute-start(bf16[192,384]{1,0:T(8,128)(2,1)S(1)} %get-tuple-element.55), channel_id=1, source_target_pairs={{0,2},{1,3},{2,0},{3,1},{4,6},{5,7},{6,4},{7,5},{8,10},{9,11},{10,... | collective-permute-start | bytes 442376 | tf_op jit(solution)/shard_map/ppermute | solution.py:46
  14.5 1.6 %collective-permute-start.4 = (bf16[192,384]{1,0:T(8,128)(2,1)S(1)}, bf16[192,384]{1,0:T(8,128)(2,1)S(1)}, u32[]{:S(2)}, u32[]{:S(2)}) collective-permute-start(bf16[192,384]{1,0:T(8,128)(2,1)S(1)} %get-tuple-element.57), channel_id=1, source_target_pairs={{0,4},{1,5},{2,6},{3,7},{4,0},{5,1},{6,2},{7,3},{8,12},{9,13},{10,... | collective-permute-start | bytes 442376 | tf_op jit(solution)/shard_map/ppermute | solution.py:46
  16.1 2.8 %collective-permute-done.3.refs_1_ = bf16[192,384]{1,0:T(8,128)(2,1)S(1)} collective-permute-done((bf16[192,384]{1,0:T(8,128)(2,1)S(1)}, bf16[192,384]{1,0:T(8,128)(2,1)S(1)}, u32[]{:S(2)}, u32[]{:S(2)}) %collective-permute-start.3) | collective-permute-done | bytes 147488 | tf_op jit(solution)/shard_map/ppermute | solution.py:46
  18.9 1.5 %collective-permute-done.4.refs_3_ = bf16[192,384]{1,0:T(8,128)(2,1)S(1)} collective-permute-done((bf16[192,384]{1,0:T(8,128)(2,1)S(1)}, bf16[192,384]{1,0:T(8,128)(2,1)S(1)}, u32[]{:S(2)}, u32[]{:S(2)}) %collective-permute-start.4) | collective-permute-done | bytes 147488 | tf_op jit(solution)/shard_map/ppermute | solution.py:46
  20.4 0.1 shard_map.142
  20.5 1.6 %collective-permute-start.5 = (bf16[96,384]{1,0:T(8,128)(2,1)S(1)}, bf16[96,384]{1,0:T(8,128)(2,1)S(1)}, u32[]{:S(2)}, u32[]{:S(2)}) collective-permute-start(bf16[96,384]{1,0:T(8,128)(2,1)S(1)} %get-tuple-element.59), channel_id=1, source_target_pairs={{0,4},{1,5},{2,6},{3,7},{4,0},{5,1},{6,2},{7,3},{8,12},{9,13},{10,... | collective-permute-start | bytes 221192 | tf_op jit(solution)/shard_map/ppermute | solution.py:46
  22.1 0.4 collective-permute-start.6
  22.5 1.6 %shard_map.145 = (f32[256,384]{1,0:T(8,128)S(1)}, bf16[4,3,8,384]{3,2,1,0:T(8,128)(2,1)S(1)}, bf16[4,3,8,384]{3,2,1,0:T(8,128)(2,1)S(1)}, f32[1,384]{1,0:T(1,128)S(1)}) custom-call(s32[1,1]{1,0:T(1,128)} %bitcast.place_ref, s32[1,1]{1,0:T(1,128)S(6)} %copy.15.counts_ref, f32[1,4]{1,0:T(1,128)S(1)} %copy-done.9, f32[256,1536]{1,0:T(8,128)S(1)} %get-tuple-element.68.pre_ref, ...), custom_call_target="tpu_custom_call" | custom-call | flops 301989888 | bytes 8805400 | tf_op jit(solution)/shard_map/pallas_call | solution.py:29
  24.1 1.4 %shard_map.146 = (f32[56,384]{1,0:T(8,128)S(1)}, bf16[56,384]{1,0:T(8,128)(2,1)S(1)}) custom-call(f32[3,4,8,24,128]{4,3,2,1,0:T(8,128)S(1)} %get-tuple-element.66.pad_ref, f32[3,4,6,24,128]{4,3,2,1,0:T(8,128)S(1)} %get-tuple-element.67.edge_ref, f32[256,384]{1,0:T(8,128)S(1)} %get-tuple-element.75.grad_ref, f32[1,384]{1,0:T(1,128)S(1)} %get-tuple-element.76.emb_ref), custom_call_target="tpu_custom_call" | custom-call | bytes 2588160 | tf_op jit(solution)/shard_map/pallas_call | solution.py:29
  25.5 0.1 collective-permute-start.9
  25.6 1.2 %collective-permute-done.9.got_ref = bf16[56,384]{1,0:T(8,128)(2,1)S(1)} collective-permute-done((bf16[56,384]{1,0:T(8,128)(2,1)S(1)}, bf16[56,384]{1,0:T(8,128)(2,1)S(1)}, u32[]{:S(2)}, u32[]{:S(2)}) %collective-permute-start.9) | collective-permute-done | bytes 43040 | tf_op jit(solution)/shard_map/ppermute | solution.py:46
  26.8 1.6 %collective-permute-start.10 = (bf16[56,384]{1,0:T(8,128)(2,1)S(1)}, bf16[56,384]{1,0:T(8,128)(2,1)S(1)}, u32[]{:S(2)}, u32[]{:S(2)}) collective-permute-start(bf16[56,384]{1,0:T(8,128)(2,1)S(1)} %get-tuple-element.80), channel_id=1, source_target_pairs={{0,16},{16,0},{1,17},{17,1},{2,18},{18,2},{3,19},{19,3},{4,20},{20... | collective-permute-start | bytes 129032 | tf_op jit(solution)/shard_map/ppermute | solution.py:46
  28.4 0.0 collective-permute-done.5.refs_1_
  28.4 0.0 collective-permute-done.6.refs_3_
  28.4 2.7 %collective-permute-start.7 = (bf16[96,384]{1,0:T(8,128)(2,1)S(1)}, bf16[96,384]{1,0:T(8,128)(2,1)S(1)}, u32[]{:S(2)}, u32[]{:S(2)}) collective-permute-start(bf16[96,384]{1,0:T(8,128)(2,1)S(1)} %get-tuple-element.63), channel_id=1, source_target_pairs={{0,8},{1,9},{2,10},{3,11},{4,12},{5,13},{6,14},{7,15},{8,0},{9,1},... | collective-permute-start | bytes 221192 | tf_op jit(solution)/shard_map/ppermute | solution.py:46
  31.1 0.0 collective-permute-done.10.got_ref
  31.1 1.5 %collective-permute-start.11 = (bf16[56,384]{1,0:T(8,128)(2,1)S(1)}, bf16[56,384]{1,0:T(8,128)(2,1)S(1)}, u32[]{:S(2)}, u32[]{:S(2)}) collective-permute-start(bf16[56,384]{1,0:T(8,128)(2,1)S(1)} %get-tuple-element.82), channel_id=1, source_target_pairs={{0,2},{1,3},{2,0},{3,1},{4,6},{5,7},{6,4},{7,5},{8,10},{9,11},{10,... | collective-permute-start | bytes 129032 | tf_op jit(solution)/shard_map/ppermute | solution.py:46
  32.6 2.6 %collective-permute-done.11.got_ref = bf16[56,384]{1,0:T(8,128)(2,1)S(1)} collective-permute-done((bf16[56,384]{1,0:T(8,128)(2,1)S(1)}, bf16[56,384]{1,0:T(8,128)(2,1)S(1)}, u32[]{:S(2)}, u32[]{:S(2)}) %collective-permute-start.11) | collective-permute-done | bytes 43040 | tf_op jit(solution)/shard_map/ppermute | solution.py:46
  35.2 0.5 %collective-permute-start.12 = (bf16[56,384]{1,0:T(8,128)(2,1)S(1)}, bf16[56,384]{1,0:T(8,128)(2,1)S(1)}, u32[]{:S(2)}, u32[]{:S(2)}) collective-permute-start(bf16[56,384]{1,0:T(8,128)(2,1)S(1)} %get-tuple-element.84), channel_id=1, source_target_pairs={{0,4},{1,5},{2,6},{3,7},{4,0},{5,1},{6,2},{7,3},{8,12},{9,13},{10,... | collective-permute-start | bytes 129032 | tf_op jit(solution)/shard_map/ppermute | solution.py:46
  35.7 0.0 collective-permute-start.14
  35.7 1.3 %collective-permute-start.15 = (bf16[4,3,8,384]{3,2,1,0:T(8,128)(2,1)S(1)}, bf16[4,3,8,384]{3,2,1,0:T(8,128)(2,1)S(1)}, u32[]{:S(2)}, u32[]{:S(2)}) collective-permute-start(bf16[4,3,8,384]{3,2,1,0:T(8,128)(2,1)S(1)} %get-tuple-element.89), channel_id=1, source_target_pairs={{0,16},{1,2},{2,1},{3,4},{4,3},{5,6},{6,5},{7,8},{8,7},{9,10},{10,... | collective-permute-start | bytes 221192 | tf_op jit(solution)/shard_map/ppermute | solution.py:59
  37.0 0.0 collective-permute-done.7.refs_1_
  37.1 0.8 %collective-permute-start.8 = (bf16[96,384]{1,0:T(8,128)(2,1)S(1)}, bf16[96,384]{1,0:T(8,128)(2,1)S(1)}, u32[]{:S(2)}, u32[]{:S(2)}) collective-permute-start(bf16[96,384]{1,0:T(8,128)(2,1)S(1)} %get-tuple-element.65), channel_id=1, source_target_pairs={{0,16},{16,0},{1,17},{17,1},{2,18},{18,2},{3,19},{19,3},{4,20},{20... | collective-permute-start | bytes 221192 | tf_op jit(solution)/shard_map/ppermute | solution.py:46
  37.9 1.4 %collective-permute-done.12.got_ref = bf16[56,384]{1,0:T(8,128)(2,1)S(1)} collective-permute-done((bf16[56,384]{1,0:T(8,128)(2,1)S(1)}, bf16[56,384]{1,0:T(8,128)(2,1)S(1)}, u32[]{:S(2)}, u32[]{:S(2)}) %collective-permute-start.12) | collective-permute-done | bytes 43040 | tf_op jit(solution)/shard_map/ppermute | solution.py:46
  39.4 2.5 %collective-permute-start.13 = (bf16[56,384]{1,0:T(8,128)(2,1)S(1)}, bf16[56,384]{1,0:T(8,128)(2,1)S(1)}, u32[]{:S(2)}, u32[]{:S(2)}) collective-permute-start(bf16[56,384]{1,0:T(8,128)(2,1)S(1)} %get-tuple-element.86), channel_id=1, source_target_pairs={{0,8},{1,9},{2,10},{3,11},{4,12},{5,13},{6,14},{7,15},{8,0},{9,1},... | collective-permute-start | bytes 129032 | tf_op jit(solution)/shard_map/ppermute | solution.py:46
  41.8 1.6 %shard_map.152.part_ref = f32[256,384]{1,0:T(8,128)S(1)} custom-call(s32[4,8]{1,0:T(4,128)S(1)} %bitcast.11, f32[256,384]{1,0:T(8,128)S(1)} %get-tuple-element.75.grad_ref, f32[7,7,384]{2,1,0:T(8,128)S(1)} %copy-done.3), custom_call_target="tpu_custom_call" | custom-call | bytes 861824 | tf_op jit(solution)/shard_map/pallas_call | solution.py:29
  43.5 0.0 collective-permute-done.14.core_ref
  43.5 0.0 collective-permute-done.15.cross_ref
  43.5 1.8 %shard_map.153 = bf16[256,384]{1,0:T(8,128)(2,1)} custom-call(s32[4,8]{1,0:T(4,128)S(1)} %bitcast.12, s32[1,1]{1,0:T(1,128)} %bitcast.place_ref, s32[1,1]{1,0:T(1,128)S(6)} %copy.15.counts_ref, f32[1,4]{1,0:T(1,128)S(1)} %copy-done.9, f32[256,384]{1,0:T(8,128)S(1)} %shard_map.152.part_ref, bf16[4,3,8,384]{3,2,1,0:T(8,128)(2,1)S(1)} %collective-permute-done.14.core_ref, ...), custom_call_target="tpu_custom_call" | custom-call | bytes 1010840 | tf_op jit(solution)/shard_map/pallas_call | solution.py:29
  45.3 0.0 collective-permute-done.13.new_ref
  45.3 0.0 collective-permute-done.8.got_ref
  45.3 0.7 %shard_map.151 = (f32[96,384]{1,0:T(8,128)}, f32[7,7,384]{2,1,0:T(8,128)}, f32[1,384]{1,0:T(1,128)}) custom-call(f32[96,384]{1,0:T(8,128)S(1)} %get-tuple-element.64.keep_ref, bf16[96,384]{1,0:T(8,128)(2,1)S(1)} %collective-permute-done.8.got_ref, f32[56,384]{1,0:T(8,128)S(1)} %get-tuple-element.85.state_ref, bf16[56,384]{1,0:T(8,128)(2,1)S(1)} %collective-permute-done.13.new_ref), custom_call_target="tpu_custom_call" | custom-call | bytes 574464 | tf_op jit(solution)/shard_map/pallas_call | solution.py:29
  (22 shorter events, 0.2 us)
Async XLA Ops:
  0.6 0.9 %copy-start.4 = (bf16[1,4,8,8,384]{4,3,2,1,0:T(8,128)(2,1)S(1)}, bf16[1,4,8,8,384]{4,3,2,1,0:T(8,128)(2,1)}, u32[]{:S(2)}) copy-start(bf16[1,4,8,8,384]{4,3,2,1,0:T(8,128)(2,1)} %param.11) | copy-start | bytes 589828
  1.6 3.9 %copy-start = (bf16[1536,384]{1,0:T(8,128)(2,1)S(1)}, bf16[1536,384]{1,0:T(8,128)(2,1)}, u32[]{:S(2)}) copy-start(bf16[1536,384]{1,0:T(8,128)(2,1)} %w_out_ref.3) | copy-start | bytes 3538948
  1.6 3.9 %copy-start.2 = (bf16[1,4,8,8,384]{4,3,2,1,0:T(8,128)(2,1)S(1)}, bf16[1,4,8,8,384]{4,3,2,1,0:T(8,128)(2,1)}, u32[]{:S(2)}) copy-start(bf16[1,4,8,8,384]{4,3,2,1,0:T(8,128)(2,1)} %param.12) | copy-start | bytes 589828
  1.6 3.9 %copy-start.3 = (f32[7,7,384]{2,1,0:T(8,128)S(1)}, f32[7,7,384]{2,1,0:T(8,128)}, u32[]{:S(2)}) copy-start(f32[7,7,384]{2,1,0:T(8,128)} %kern_ref.7) | copy-start | bytes 225796
  1.6 3.9 %copy-start.5 = (bf16[1,4,8,8,384]{4,3,2,1,0:T(8,128)(2,1)S(1)}, bf16[1,4,8,8,384]{4,3,2,1,0:T(8,128)(2,1)}, u32[]{:S(2)}) copy-start(bf16[1,4,8,8,384]{4,3,2,1,0:T(8,128)(2,1)} %param.11) | copy-start | bytes 589828
  1.6 3.9 %copy-start.6 = (s32[1,4,8]{2,1,0:T(4,128)S(1)}, s32[1,4,8]{2,1,0:T(4,128)}, u32[]{:S(2)}) copy-start(s32[1,4,8]{2,1,0:T(4,128)} %param.15) | copy-start | bytes 388
  1.6 3.9 %copy-start.7 = (f32[384]{0:T(512)S(1)}, f32[384]{0:T(512)}, u32[]{:S(2)}) copy-start(f32[384]{0:T(512)} %scale_ref.3) | copy-start | bytes 4612
  1.6 3.9 %copy-start.8 = (f32[1,384]{1,0:T(1,128)S(1)}, f32[1,384]{1,0:T(1,128)}, u32[]{:S(2)}) copy-start(f32[1,384]{1,0:T(1,128)} %cot_ref.3) | copy-start | bytes 4612
  1.6 3.9 %copy-start.9 = (f32[1,4]{1,0:T(1,128)S(1)}, f32[1,4]{1,0:T(1,128)}, u32[]{:S(2)}) copy-start(f32[1,4]{1,0:T(1,128)} %pool_ref.5) | copy-start | bytes 52
  1.7 5.9 %copy-start.1 = (bf16[384,1536]{1,0:T(8,128)(2,1)S(1)}, bf16[384,1536]{1,0:T(8,128)(2,1)}, u32[]{:S(2)}) copy-start(bf16[384,1536]{1,0:T(8,128)(2,1)} %w_in_ref.3) | copy-start | bytes 3538948
  1.7 5.9 %copy-start.10 = (f32[384]{0:T(512)S(1)}, f32[384]{0:T(512)}, u32[]{:S(2)}) copy-start(f32[384]{0:T(512)} %gain_ref.3) | copy-start | bytes 4612
  1.7 5.9 %collective-permute-start = (bf16[4,3,8,384]{3,2,1,0:T(8,128)(2,1)S(1)}, bf16[4,3,8,384]{3,2,1,0:T(8,128)(2,1)S(1)}, u32[]{:S(2)}, u32[]{:S(2)}) collective-permute-start(bf16[4,3,8,384]{3,2,1,0:T(8,128)(2,1)S(1)} %get-tuple-element.48), channel_id=1, source_target_pairs={{0,1},{1,0},{2,3},{3,2},{4,5},{5,4},{6,7},{7,6},{8,9},{9,8},{10,11... | collective-permute-start | bytes 221192 | tf_op jit(solution)/shard_map/ppermute | solution.py:46
  2.3 5.4 %collective-permute-start.1 = (bf16[4,3,8,384]{3,2,1,0:T(8,128)(2,1)S(1)}, bf16[4,3,8,384]{3,2,1,0:T(8,128)(2,1)S(1)}, u32[]{:S(2)}, u32[]{:S(2)}) collective-permute-start(bf16[4,3,8,384]{3,2,1,0:T(8,128)(2,1)S(1)} %get-tuple-element.49), channel_id=1, source_target_pairs={{0,16},{1,2},{2,1},{3,4},{4,3},{5,6},{6,5},{7,8},{8,7},{9,10},{10,... | collective-permute-start | bytes 221192 | tf_op jit(solution)/shard_map/ppermute | solution.py:59
  10.2 2.1 %collective-permute-start.2 = (bf16[768,384]{1,0:T(8,128)(2,1)S(1)}, bf16[768,384]{1,0:T(8,128)(2,1)S(1)}, u32[]{:S(2)}, u32[]{:S(2)}) collective-permute-start(bf16[768,384]{1,0:T(8,128)(2,1)S(1)} %get-tuple-element.53), channel_id=1, source_target_pairs={{0,1},{1,0},{2,3},{3,2},{4,5},{5,4},{6,7},{7,6},{8,9},{9,8},{10,11... | collective-permute-start | bytes 1769480 | tf_op jit(solution)/shard_map/ppermute | solution.py:46
  12.5 6.4 %collective-permute-start.3 = (bf16[192,384]{1,0:T(8,128)(2,1)S(1)}, bf16[192,384]{1,0:T(8,128)(2,1)S(1)}, u32[]{:S(2)}, u32[]{:S(2)}) collective-permute-start(bf16[192,384]{1,0:T(8,128)(2,1)S(1)} %get-tuple-element.55), channel_id=1, source_target_pairs={{0,2},{1,3},{2,0},{3,1},{4,6},{5,7},{6,4},{7,5},{8,10},{9,11},{10,... | collective-permute-start | bytes 442376 | tf_op jit(solution)/shard_map/ppermute | solution.py:46
  14.5 5.8 %collective-permute-start.4 = (bf16[192,384]{1,0:T(8,128)(2,1)S(1)}, bf16[192,384]{1,0:T(8,128)(2,1)S(1)}, u32[]{:S(2)}, u32[]{:S(2)}) collective-permute-start(bf16[192,384]{1,0:T(8,128)(2,1)S(1)} %get-tuple-element.57), channel_id=1, source_target_pairs={{0,4},{1,5},{2,6},{3,7},{4,0},{5,1},{6,2},{7,3},{8,12},{9,13},{10,... | collective-permute-start | bytes 442376 | tf_op jit(solution)/shard_map/ppermute | solution.py:46
  20.5 7.9 %collective-permute-start.5 = (bf16[96,384]{1,0:T(8,128)(2,1)S(1)}, bf16[96,384]{1,0:T(8,128)(2,1)S(1)}, u32[]{:S(2)}, u32[]{:S(2)}) collective-permute-start(bf16[96,384]{1,0:T(8,128)(2,1)S(1)} %get-tuple-element.59), channel_id=1, source_target_pairs={{0,4},{1,5},{2,6},{3,7},{4,0},{5,1},{6,2},{7,3},{8,12},{9,13},{10,... | collective-permute-start | bytes 221192 | tf_op jit(solution)/shard_map/ppermute | solution.py:46
  22.1 6.2 %collective-permute-start.6 = (bf16[96,384]{1,0:T(8,128)(2,1)S(1)}, bf16[96,384]{1,0:T(8,128)(2,1)S(1)}, u32[]{:S(2)}, u32[]{:S(2)}) collective-permute-start(bf16[96,384]{1,0:T(8,128)(2,1)S(1)} %get-tuple-element.61), channel_id=1, source_target_pairs={{0,2},{1,3},{2,0},{3,1},{4,6},{5,7},{6,4},{7,5},{8,10},{9,11},{10,... | collective-permute-start | bytes 221192 | tf_op jit(solution)/shard_map/ppermute | solution.py:46
  25.5 1.3 %collective-permute-start.9 = (bf16[56,384]{1,0:T(8,128)(2,1)S(1)}, bf16[56,384]{1,0:T(8,128)(2,1)S(1)}, u32[]{:S(2)}, u32[]{:S(2)}) collective-permute-start(bf16[56,384]{1,0:T(8,128)(2,1)S(1)} %get-tuple-element.78), channel_id=1, source_target_pairs={{0,1},{1,0},{2,3},{3,2},{4,5},{5,4},{6,7},{7,6},{8,9},{9,8},{10,11... | collective-permute-start | bytes 129032 | tf_op jit(solution)/shard_map/ppermute | solution.py:46
  26.8 4.3 %collective-permute-start.10 = (bf16[56,384]{1,0:T(8,128)(2,1)S(1)}, bf16[56,384]{1,0:T(8,128)(2,1)S(1)}, u32[]{:S(2)}, u32[]{:S(2)}) collective-permute-start(bf16[56,384]{1,0:T(8,128)(2,1)S(1)} %get-tuple-element.80), channel_id=1, source_target_pairs={{0,16},{16,0},{1,17},{17,1},{2,18},{18,2},{3,19},{19,3},{4,20},{20... | collective-permute-start | bytes 129032 | tf_op jit(solution)/shard_map/ppermute | solution.py:46
  28.4 8.6 %collective-permute-start.7 = (bf16[96,384]{1,0:T(8,128)(2,1)S(1)}, bf16[96,384]{1,0:T(8,128)(2,1)S(1)}, u32[]{:S(2)}, u32[]{:S(2)}) collective-permute-start(bf16[96,384]{1,0:T(8,128)(2,1)S(1)} %get-tuple-element.63), channel_id=1, source_target_pairs={{0,8},{1,9},{2,10},{3,11},{4,12},{5,13},{6,14},{7,15},{8,0},{9,1},... | collective-permute-start | bytes 221192 | tf_op jit(solution)/shard_map/ppermute | solution.py:46
  31.1 4.1 %collective-permute-start.11 = (bf16[56,384]{1,0:T(8,128)(2,1)S(1)}, bf16[56,384]{1,0:T(8,128)(2,1)S(1)}, u32[]{:S(2)}, u32[]{:S(2)}) collective-permute-start(bf16[56,384]{1,0:T(8,128)(2,1)S(1)} %get-tuple-element.82), channel_id=1, source_target_pairs={{0,2},{1,3},{2,0},{3,1},{4,6},{5,7},{6,4},{7,5},{8,10},{9,11},{10,... | collective-permute-start | bytes 129032 | tf_op jit(solution)/shard_map/ppermute | solution.py:46
  35.2 4.1 %collective-permute-start.12 = (bf16[56,384]{1,0:T(8,128)(2,1)S(1)}, bf16[56,384]{1,0:T(8,128)(2,1)S(1)}, u32[]{:S(2)}, u32[]{:S(2)}) collective-permute-start(bf16[56,384]{1,0:T(8,128)(2,1)S(1)} %get-tuple-element.84), channel_id=1, source_target_pairs={{0,4},{1,5},{2,6},{3,7},{4,0},{5,1},{6,2},{7,3},{8,12},{9,13},{10,... | collective-permute-start | bytes 129032 | tf_op jit(solution)/shard_map/ppermute | solution.py:46
  35.7 7.7 %collective-permute-start.14 = (bf16[4,3,8,384]{3,2,1,0:T(8,128)(2,1)S(1)}, bf16[4,3,8,384]{3,2,1,0:T(8,128)(2,1)S(1)}, u32[]{:S(2)}, u32[]{:S(2)}) collective-permute-start(bf16[4,3,8,384]{3,2,1,0:T(8,128)(2,1)S(1)} %get-tuple-element.88), channel_id=1, source_target_pairs={{0,1},{1,0},{2,3},{3,2},{4,5},{5,4},{6,7},{7,6},{8,9},{9,8},{10,11... | collective-permute-start | bytes 221192 | tf_op jit(solution)/shard_map/ppermute | solution.py:46
  35.7 7.7 %collective-permute-start.15 = (bf16[4,3,8,384]{3,2,1,0:T(8,128)(2,1)S(1)}, bf16[4,3,8,384]{3,2,1,0:T(8,128)(2,1)S(1)}, u32[]{:S(2)}, u32[]{:S(2)}) collective-permute-start(bf16[4,3,8,384]{3,2,1,0:T(8,128)(2,1)S(1)} %get-tuple-element.89), channel_id=1, source_target_pairs={{0,16},{1,2},{2,1},{3,4},{4,3},{5,6},{6,5},{7,8},{8,7},{9,10},{10,... | collective-permute-start | bytes 221192 | tf_op jit(solution)/shard_map/ppermute | solution.py:59
  37.1 8.2 %collective-permute-start.8 = (bf16[96,384]{1,0:T(8,128)(2,1)S(1)}, bf16[96,384]{1,0:T(8,128)(2,1)S(1)}, u32[]{:S(2)}, u32[]{:S(2)}) collective-permute-start(bf16[96,384]{1,0:T(8,128)(2,1)S(1)} %get-tuple-element.65), channel_id=1, source_target_pairs={{0,16},{16,0},{1,17},{17,1},{2,18},{18,2},{3,19},{19,3},{4,20},{20... | collective-permute-start | bytes 221192 | tf_op jit(solution)/shard_map/ppermute | solution.py:46
  39.4 5.9 %collective-permute-start.13 = (bf16[56,384]{1,0:T(8,128)(2,1)S(1)}, bf16[56,384]{1,0:T(8,128)(2,1)S(1)}, u32[]{:S(2)}, u32[]{:S(2)}) collective-permute-start(bf16[56,384]{1,0:T(8,128)(2,1)S(1)} %get-tuple-element.86), channel_id=1, source_target_pairs={{0,8},{1,9},{2,10},{3,11},{4,12},{5,13},{6,14},{7,15},{8,0},{9,1},... | collective-permute-start | bytes 129032 | tf_op jit(solution)/shard_map/ppermute | solution.py:46

commit v5 on v4

--- a/solution.py
+++ b/solution.py
@@ -19,7 +19,7 @@
 STATE = 56
 TAPS = 49
 CHUNK = 384
-BACK_CHUNK = 512
+BACK_CHUNK = 384
 EDGE_COST = 5_000_000_000
 
 
@@ -196,8 +196,9 @@
 
 def forward_kernel(
     rows, adj_ref, place_ref, core_ref, cross_ref, conv_ref, kern_ref, gain_ref, w_in_ref, mixed_ref,
-    edge_ref, normed_ref, inv_ref, pre_ref, cdf_ref, keep_ref, send_ref, pooled_ref, whole_ref,
+    edge_ref, normed_ref, inv_ref, lifted_ref, *outs,
 ):
+    *outs, whole_ref = outs
     capacity, parts = adj_ref.shape[0], conv_ref.shape[1] // LANES
     channels = conv_ref.shape[1]
     pixels = 64
@@ -224,13 +225,23 @@
     normed = centred * inv_std
     normed_ref[...] = normed
     inv_ref[...] = inv_std
-    lifted = (normed * gain_ref[...].reshape(1, channels)).astype(bf16)
-    hidden = w_in_ref.shape[1]
+    lifted_ref[...] = (normed * gain_ref[...].reshape(1, channels)).astype(bf16)
+    expand(rows, 0, place_ref, lifted_ref, w_in_ref, mixed_ref, *outs)
+
+
+def rest_kernel(rows, place_ref, lifted_ref, w_in_ref, mixed_ref, *outs):
+    expand(rows, w_in_ref.shape[1] // 2, place_ref, lifted_ref, w_in_ref, mixed_ref, *outs)
+
+
+def expand(rows, base, place_ref, lifted_ref, w_in_ref, mixed_ref, pre_ref, cdf_ref, keep_ref, send_ref, pooled_ref):
+    channels = lifted_ref.shape[1]
+    hidden = pre_ref.shape[1]
     side = lax.rem(place_ref[0, 0], 2)
     chunk = CHUNK if hidden % CHUNK == 0 and CHUNK % (2 * rows) == 0 else hidden
+    lifted = lifted_ref[...]
 
     def project(first):
-        return jnp.dot(lifted, w_in_ref[:, first : first + chunk], preferred_element_type=f32)
+        return jnp.dot(lifted, w_in_ref[:, base + first : base + first + chunk], preferred_element_type=f32)
 
     following = project(0)
     for first in range(0, hidden, chunk):
@@ -255,23 +266,26 @@
 
 
 def back_kernel(
-    place_ref, counts_ref, pool_ref, pre_ref, cdf_ref, act_grad_ref, w_in_ref, normed_ref, inv_ref, gain_ref, pooled_ref, w_out_ref,
+    place_ref, counts_ref, pool_ref, pre_a_ref, cdf_a_ref, pre_b_ref, cdf_b_ref, act_grad_ref, w_in_ref,
+    normed_ref, inv_ref, gain_ref, pooled_a_ref, pooled_b_ref, w_out_ref,
     scale_ref, own_sum_ref, grad_ref, core_ref, cross_ref, emb_ref,
 ):
     channels = normed_ref.shape[1]
     capacity = core_ref.shape[0]
-    hidden = w_in_ref.shape[1]
-    chunk = BACK_CHUNK if hidden % BACK_CHUNK == 0 else hidden
+    half = w_in_ref.shape[1] // 2
+    chunk = BACK_CHUNK if half % BACK_CHUNK == 0 else half
     lift = None
-    for first in range(0, hidden, chunk):
-        at = slice(first, first + chunk)
-        pre = pre_ref[:, at]
-        density = jnp.exp(-0.5 * pre * pre) * inv_root_two_pi
-        pre_grad = (act_grad_ref[:, at] * (cdf_ref[:, at] + pre * density)).astype(bf16)
-        term = lax.dot_general(
-            pre_grad, w_in_ref[:, at], (((1,), (1,)), ((), ())), preferred_element_type=f32
-        )
-        lift = term if lift is None else lift + term
+    for base, pre_ref, cdf_ref in ((0, pre_a_ref, cdf_a_ref), (half, pre_b_ref, cdf_b_ref)):
+        for first in range(0, half, chunk):
+            at = slice(first, first + chunk)
+            whole = slice(base + first, base + first + chunk)
+            pre = pre_ref[:, at]
+            density = jnp.exp(-0.5 * pre * pre) * inv_root_two_pi
+            pre_grad = (act_grad_ref[:, whole] * (cdf_ref[:, at] + pre * density)).astype(bf16)
+            term = lax.dot_general(
+                pre_grad, w_in_ref[:, whole], (((1,), (1,)), ((), ())), preferred_element_type=f32
+            )
+            lift = term if lift is None else lift + term
     grad_normed = lift * gain_ref[...].reshape(1, channels)
     normed = normed_ref[...]
     grad = inv_ref[...] * (
@@ -287,8 +301,10 @@
     for tile in range(capacity):
         amount = is_live(counts_ref, tile) * pool_ref[0, tile]
         weights = jnp.where(column == tile, amount, weights)
-    hidden = jnp.sum(pooled_ref[...] * weights, axis=1, keepdims=True)
-    mixed = jnp.sum(hidden * w_out_ref[...].astype(f32), axis=0, keepdims=True)
+    mixed = jnp.zeros((1, channels), f32)
+    for base, pooled_ref in ((0, pooled_a_ref), (half, pooled_b_ref)):
+        hidden = jnp.sum(pooled_ref[...] * weights, axis=1, keepdims=True)
+        mixed += jnp.sum(hidden * w_out_ref[base : base + half, :].astype(f32), axis=0, keepdims=True)
     emb_ref[...] = (own_sum_ref[...] + scale_ref[...].reshape(1, channels) * mixed) * 0.125
 
 
@@ -463,24 +479,33 @@
         [wanted, counts, pool_weight, slide_cot, layer_scale, kernel, own, up, w_out],
         flops=2 * pixels * channels * hidden,
     )
-    edge, normed, inv, pre, cdf, keep, send, pooled = call(
+    half = hidden // 2
+    expanded = [
+        struct((pixels, half)),
+        struct((pixels, half)),
+        struct((half // 2, channels)),
+        struct((half // 2, channels), bf16),
+        struct((half, LANES)),
+    ]
+    edge, normed, inv, lifted, pre_a, cdf_a, keep_a, send_a, pooled_a = call(
         functools.partial(forward_kernel, rows),
         [
             struct((parts, capacity, 6, 24, LANES)),
             struct((pixels, channels)),
             struct((pixels, 1)),
-            struct((pixels, hidden)),
-            struct((pixels, hidden)),
-            struct((hidden // 2, channels)),
-            struct((hidden // 2, channels), bf16),
-            struct((hidden, LANES)),
-        ],
+            struct((pixels, channels), bf16),
+        ] + expanded,
         [SMEM] * 2 + [VMEM] * 7,
         [wanted, place, core, cross, conv, kernel, norm_gain, w_in, mixed],
-        flops=4 * pixels * channels * hidden,
+        flops=2 * pixels * channels * hidden,
         scratch=[pltpu.VMEM((pixels, channels), f32)],
     )
-    got = swapped(send, "space", 1)
+    got_a = swapped(send_a, "space", 1)
+    pre_b, cdf_b, keep_b, send_b, pooled_b = call(
+        functools.partial(rest_kernel, rows), expanded, [SMEM] + [VMEM] * 3, [place, lifted, w_in, mixed],
+        flops=2 * pixels * channels * hidden,
+    )
+    got_b = swapped(send_b, "space", 1)
 
     grad, core, cross, emb = call(
         back_kernel,
@@ -490,8 +515,9 @@
             struct(edge_shape, bf16),
             struct((1, channels)),
         ],
-        [SMEM, VMEM, SMEM] + [VMEM] * 11,
-        [place, counts, pool_weight, pre, cdf, act_grad, w_in, normed, inv, norm_gain, pooled, w_out, layer_scale, own_sum],
+        [SMEM, VMEM, SMEM] + [VMEM] * 14,
+        [place, counts, pool_weight, pre_a, cdf_a, pre_b, cdf_b, act_grad, w_in, normed, inv, norm_gain,
+         pooled_a, pooled_b, w_out, layer_scale, own_sum],
         flops=2 * pixels * channels * hidden,
     )
     cross = crossed(cross)
@@ -511,8 +537,9 @@
         return list(zip(out[0::2], out[1::2]))
 
     half = hidden // 4
-    (keep_a, send_a), (keep_b, send_b) = merge([(keep, got)], [(0, half, rows, 1), (half, half, 2 * rows, 2)])
+    ((keep_a, send_a),) = merge([(keep_a, got_a)], [(0, half, rows, 1)])
     got_a = swapped(send_a, "space", 2)
+    ((keep_b, send_b),) = merge([(keep_b, got_b)], [(0, half, 2 * rows, 2)])
     got_b = swapped(send_b, "space", 4)
     half //= 2
     (keep_a, send_a), (keep_b, send_b) = merge(

time: 46.2 us -> 45.5 us (0.985)
  waiting for transfers between devices: 11.4 us -> 10.4 us
    ppermute x14 -> x15, waiting for transfers between devices: 11.4 us -> 10.4 us  [swapped(): lax.ppermute(value, axis, [(source, source ^ bit) for source in range(cou...]
    pallas_call x16 -> x18, Pallas kernels: 12.3 us -> 12.7 us  [call(): pl.pallas_call(body, out_shape=out_shape, in_specs=in_specs, out_specs=ou...]
    ppermute x14 -> x15, starting transfers between devices: 16 us -> 15.9 us  [swapped(): lax.ppermute(value, axis, [(source, source ^ bit) for source in range(cou...]
  transfers between devices with their start and end apart: 16 -> 17, of which waited for: 6 -> 7; matrix products, arithmetic and copies ran while one was open for 0% -> 0% of each run, Pallas kernels for 19% -> 22%
where the time goes in v5:
time: 45.5 us; the launch traced here: 45.4 us
  starting transfers between devices  19.7 us (43%)
  Pallas kernels  12.7 us (28%)
  waiting for transfers between devices  10.4 us (23%)
  between operations  1.56 us (3%)
  local copies, waits for them, and re-layouts  0.96 us (2%)
    ppermute x15, starting transfers between devices, swapped(): lax.ppermute(value, axis, [(source, source ^ bit) for source in range(cou...  15.9 us
    pallas_call x18, Pallas kernels, call(): pl.pallas_call(body, out_shape=out_shape, in_specs=in_specs, out_specs=ou...  12.7 us
    ppermute x15, waiting for transfers between devices, swapped(): lax.ppermute(value, axis, [(source, source ^ bit) for source in range(cou...  10.4 us
    ppermute x2, starting transfers between devices, crossed(): return lax.ppermute(value, ('dp', 'space'), targets)  3.85 us
    unnamed x22, local copies, waits for them, and re-layouts  0.96 us
  transfers between devices with their start and end apart: 17, of which 7 were waited for; matrix products, arithmetic and copies ran while one was open for 0% of the time, Pallas kernels for 22%

profile of v5, /device:TPU:0, one launch (start us, length us, event | category | flops | bytes accessed | tf_op | source)
XLA Modules:
  0.0 45.4 jit_solution(13158498099808428860)
XLA Ops:
  0.6 0.9 %copy-done.4 = bf16[1,4,8,8,384]{4,3,2,1,0:T(8,128)(2,1)S(1)} copy-done((bf16[1,4,8,8,384]{4,3,2,1,0:T(8,128)(2,1)S(1)}, bf16[1,4,8,8,384]{4,3,2,1,0:T(8,128)(2,1)}, u32[]{:S(2)}) %copy-start.4) | copy-done | bytes 196632
  1.6 0.1 shard_map.138
  1.7 0.0 copy-start
  1.7 0.0 copy-start.8
  1.7 0.6 %collective-permute-start = (bf16[4,3,8,384]{3,2,1,0:T(8,128)(2,1)S(1)}, bf16[4,3,8,384]{3,2,1,0:T(8,128)(2,1)S(1)}, u32[]{:S(2)}, u32[]{:S(2)}) collective-permute-start(bf16[4,3,8,384]{3,2,1,0:T(8,128)(2,1)S(1)} %get-tuple-element.54), channel_id=1, source_target_pairs={{0,1},{1,0},{2,3},{3,2},{4,5},{5,4},{6,7},{7,6},{8,9},{9,8},{10,11... | collective-permute-start | bytes 221192 | tf_op jit(solution)/shard_map/ppermute | solution.py:46
  2.3 2.6 %collective-permute-start.1 = (bf16[4,3,8,384]{3,2,1,0:T(8,128)(2,1)S(1)}, bf16[4,3,8,384]{3,2,1,0:T(8,128)(2,1)S(1)}, u32[]{:S(2)}, u32[]{:S(2)}) collective-permute-start(bf16[4,3,8,384]{3,2,1,0:T(8,128)(2,1)S(1)} %get-tuple-element.55), channel_id=1, source_target_pairs={{0,16},{1,2},{2,1},{3,4},{4,3},{5,6},{6,5},{7,8},{8,7},{9,10},{10,... | collective-permute-start | bytes 221192 | tf_op jit(solution)/shard_map/ppermute | solution.py:59
  5.6 2.0 %shard_map.139 = (f32[3,4,8,24,128]{4,3,2,1,0:T(8,128)S(1)}, f32[256,384]{1,0:T(8,128)S(1)}, bf16[256,512]{1,0:T(8,128)(2,1)S(1)}, f32[256,1536]{1,0:T(8,128)S(1)}, f32[1,384]{1,0:T(1,128)S(1)}) custom-call(s32[4,8]{1,0:T(4,128)S(1)} %bitcast.9, s32[1,1]{1,0:T(1,128)S(6)} %copy.15.counts_ref, f32[1,4]{1,0:T(1,128)S(1)} %copy-done.10, ...), custom_call_target="tpu_custom_call" | custom-call | flops 301989888 | bytes 5060756 | tf_op jit(solution)/shard_map/pallas_call | solution.py:29
  7.6 0.0 collective-permute-done.core_ref
  7.6 0.0 collective-permute-done.1.cross_ref
  7.6 2.0 %shard_map.140 = (f32[3,4,6,24,128]{4,3,2,1,0:T(8,128)S(1)}, f32[256,384]{1,0:T(8,128)S(1)}, f32[256,1]{1,0:T(8,128)S(1)}, bf16[256,384]{1,0:T(8,128)(2,1)S(1)},...) custom-call(s32[4,8]{1,0:T(4,128)S(1)} %bitcast.10, ...), custom_call_target="tpu_custom_call" | custom-call | flops 301989888 | bytes 6385796 | tf_op jit(solution)/shard_map/pallas_call | solution.py:29
  9.7 0.2 collective-permute-start.2
  9.9 0.7 %shard_map.142 = (f32[256,768]{1,0:T(8,128)S(1)}, f32[256,768]{1,0:T(8,128)S(1)}, f32[384,384]{1,0:T(8,128)S(1)}, bf16[384,384]{1,0:T(8,128)(2,1)S(1)}, f32[768,128]{1,0:T(8,128)S(1)}) custom-call(s32[1,1]{1,0:T(1,128)} %bitcast.place_ref, bf16[256,384]{1,0:T(8,128)(2,1)S(1)} %get-tuple-element.62.lifted_ref, bf16[384,1536]{1,0:T(8,128)(2,1)S(1)} %copy-done, ...), custom_call_target="tpu_custom_call" | custom-call | flops 301989888 | bytes 4489220 | tf_op jit(solution)/shard_map/pallas_call | solution.py:29
  10.6 0.4 collective-permute-start.4
  11.0 0.3 collective-permute-done.2.refs_1_
  11.3 0.1 shard_map.141
  11.4 2.0 %collective-permute-start.3 = (bf16[192,384]{1,0:T(8,128)(2,1)S(1)}, bf16[192,384]{1,0:T(8,128)(2,1)S(1)}, u32[]{:S(2)}, u32[]{:S(2)}) collective-permute-start(bf16[192,384]{1,0:T(8,128)(2,1)S(1)} %get-tuple-element.61), channel_id=1, source_target_pairs={{0,2},{1,3},{2,0},{3,1},{4,6},{5,7},{6,4},{7,5},{8,10},{9,11},{10,... | collective-permute-start | bytes 442376 | tf_op jit(solution)/shard_map/ppermute | solution.py:46
  13.5 0.0 collective-permute-done.4.refs_1_
  13.5 0.1 shard_map.143
  13.6 1.6 %collective-permute-start.5 = (bf16[192,384]{1,0:T(8,128)(2,1)S(1)}, bf16[192,384]{1,0:T(8,128)(2,1)S(1)}, u32[]{:S(2)}, u32[]{:S(2)}) collective-permute-start(bf16[192,384]{1,0:T(8,128)(2,1)S(1)} %get-tuple-element.66), channel_id=1, source_target_pairs={{0,4},{1,5},{2,6},{3,7},{4,0},{5,1},{6,2},{7,3},{8,12},{9,13},{10,... | collective-permute-start | bytes 442376 | tf_op jit(solution)/shard_map/ppermute | solution.py:46
  15.2 2.6 %collective-permute-done.3.refs_1_ = bf16[192,384]{1,0:T(8,128)(2,1)S(1)} collective-permute-done((bf16[192,384]{1,0:T(8,128)(2,1)S(1)}, bf16[192,384]{1,0:T(8,128)(2,1)S(1)}, u32[]{:S(2)}, u32[]{:S(2)}) %collective-permute-start.3) | collective-permute-done | bytes 147488 | tf_op jit(solution)/shard_map/ppermute | solution.py:46
  17.8 1.7 %collective-permute-done.5.refs_3_ = bf16[192,384]{1,0:T(8,128)(2,1)S(1)} collective-permute-done((bf16[192,384]{1,0:T(8,128)(2,1)S(1)}, bf16[192,384]{1,0:T(8,128)(2,1)S(1)}, u32[]{:S(2)}, u32[]{:S(2)}) %collective-permute-start.5) | collective-permute-done | bytes 147488 | tf_op jit(solution)/shard_map/ppermute | solution.py:46
  19.5 0.1 shard_map.144
  19.6 1.6 %collective-permute-start.6 = (bf16[96,384]{1,0:T(8,128)(2,1)S(1)}, bf16[96,384]{1,0:T(8,128)(2,1)S(1)}, u32[]{:S(2)}, u32[]{:S(2)}) collective-permute-start(bf16[96,384]{1,0:T(8,128)(2,1)S(1)} %get-tuple-element.68), channel_id=1, source_target_pairs={{0,4},{1,5},{2,6},{3,7},{4,0},{5,1},{6,2},{7,3},{8,12},{9,13},{10,... | collective-permute-start | bytes 221192 | tf_op jit(solution)/shard_map/ppermute | solution.py:46
  21.3 1.0 %collective-permute-start.7 = (bf16[96,384]{1,0:T(8,128)(2,1)S(1)}, bf16[96,384]{1,0:T(8,128)(2,1)S(1)}, u32[]{:S(2)}, u32[]{:S(2)}) collective-permute-start(bf16[96,384]{1,0:T(8,128)(2,1)S(1)} %get-tuple-element.70), channel_id=1, source_target_pairs={{0,2},{1,3},{2,0},{3,1},{4,6},{5,7},{6,4},{7,5},{8,10},{9,11},{10,... | collective-permute-start | bytes 221192 | tf_op jit(solution)/shard_map/ppermute | solution.py:46
  22.2 1.7 %shard_map.147 = (f32[256,384]{1,0:T(8,128)S(1)}, bf16[4,3,8,384]{3,2,1,0:T(8,128)(2,1)S(1)}, bf16[4,3,8,384]{3,2,1,0:T(8,128)(2,1)S(1)}, f32[1,384]{1,0:T(1,128)S(1)}) custom-call(s32[1,1]{1,0:T(1,128)} %bitcast.place_ref, s32[1,1]{1,0:T(1,128)S(6)} %copy.15.counts_ref, f32[1,4]{1,0:T(1,128)S(1)} %copy-done.10, f32[256,768]{1,0:T(8,128)S(1)} %get-tuple-element.77.pre_a_ref, ...), custom_call_target="tpu_custom_call" | custom-call | flops 301989888 | bytes 8805400 | tf_op jit(solution)/shard_map/pallas_call | solution.py:29
  24.0 1.5 %shard_map.148 = (f32[56,384]{1,0:T(8,128)S(1)}, bf16[56,384]{1,0:T(8,128)(2,1)S(1)}) custom-call(f32[3,4,8,24,128]{4,3,2,1,0:T(8,128)S(1)} %get-tuple-element.75.pad_ref, f32[3,4,6,24,128]{4,3,2,1,0:T(8,128)S(1)} %get-tuple-element.76.edge_ref, f32[256,384]{1,0:T(8,128)S(1)} %get-tuple-element.87.grad_ref, f32[1,384]{1,0:T(1,128)S(1)} %get-tuple-element.88.emb_ref), custom_call_target="tpu_custom_call" | custom-call | bytes 2588160 | tf_op jit(solution)/shard_map/pallas_call | solution.py:29
  25.4 0.1 collective-permute-start.10
  25.5 1.2 %collective-permute-done.10.got_ref = bf16[56,384]{1,0:T(8,128)(2,1)S(1)} collective-permute-done((bf16[56,384]{1,0:T(8,128)(2,1)S(1)}, bf16[56,384]{1,0:T(8,128)(2,1)S(1)}, u32[]{:S(2)}, u32[]{:S(2)}) %collective-permute-start.10) | collective-permute-done | bytes 43040 | tf_op jit(solution)/shard_map/ppermute | solution.py:46
  26.7 1.6 %collective-permute-start.11 = (bf16[56,384]{1,0:T(8,128)(2,1)S(1)}, bf16[56,384]{1,0:T(8,128)(2,1)S(1)}, u32[]{:S(2)}, u32[]{:S(2)}) collective-permute-start(bf16[56,384]{1,0:T(8,128)(2,1)S(1)} %get-tuple-element.92), channel_id=1, source_target_pairs={{0,16},{16,0},{1,17},{17,1},{2,18},{18,2},{3,19},{19,3},{4,20},{20... | collective-permute-start | bytes 129032 | tf_op jit(solution)/shard_map/ppermute | solution.py:46
  28.3 0.0 collective-permute-done.6.refs_1_
  28.3 0.0 collective-permute-done.7.refs_3_
  28.3 2.1 %collective-permute-start.8 = (bf16[96,384]{1,0:T(8,128)(2,1)S(1)}, bf16[96,384]{1,0:T(8,128)(2,1)S(1)}, u32[]{:S(2)}, u32[]{:S(2)}) collective-permute-start(bf16[96,384]{1,0:T(8,128)(2,1)S(1)} %get-tuple-element.72), channel_id=1, source_target_pairs={{0,8},{1,9},{2,10},{3,11},{4,12},{5,13},{6,14},{7,15},{8,0},{9,1},... | collective-permute-start | bytes 221192 | tf_op jit(solution)/shard_map/ppermute | solution.py:46
  30.4 0.4 collective-permute-done.11.got_ref
  30.8 1.1 %collective-permute-start.12 = (bf16[56,384]{1,0:T(8,128)(2,1)S(1)}, bf16[56,384]{1,0:T(8,128)(2,1)S(1)}, u32[]{:S(2)}, u32[]{:S(2)}) collective-permute-start(bf16[56,384]{1,0:T(8,128)(2,1)S(1)} %get-tuple-element.94), channel_id=1, source_target_pairs={{0,2},{1,3},{2,0},{3,1},{4,6},{5,7},{6,4},{7,5},{8,10},{9,11},{10,... | collective-permute-start | bytes 129032 | tf_op jit(solution)/shard_map/ppermute | solution.py:46
  32.0 3.0 %collective-permute-done.12.got_ref = bf16[56,384]{1,0:T(8,128)(2,1)S(1)} collective-permute-done((bf16[56,384]{1,0:T(8,128)(2,1)S(1)}, bf16[56,384]{1,0:T(8,128)(2,1)S(1)}, u32[]{:S(2)}, u32[]{:S(2)}) %collective-permute-start.12) | collective-permute-done | bytes 43040 | tf_op jit(solution)/shard_map/ppermute | solution.py:46
  35.0 0.7 %collective-permute-start.13 = (bf16[56,384]{1,0:T(8,128)(2,1)S(1)}, bf16[56,384]{1,0:T(8,128)(2,1)S(1)}, u32[]{:S(2)}, u32[]{:S(2)}) collective-permute-start(bf16[56,384]{1,0:T(8,128)(2,1)S(1)} %get-tuple-element.96), channel_id=1, source_target_pairs={{0,4},{1,5},{2,6},{3,7},{4,0},{5,1},{6,2},{7,3},{8,12},{9,13},{10,... | collective-permute-start | bytes 129032 | tf_op jit(solution)/shard_map/ppermute | solution.py:46
  35.7 0.0 collective-permute-start.15
  35.7 1.3 %collective-permute-start.16 = (bf16[4,3,8,384]{3,2,1,0:T(8,128)(2,1)S(1)}, bf16[4,3,8,384]{3,2,1,0:T(8,128)(2,1)S(1)}, u32[]{:S(2)}, u32[]{:S(2)}) collective-permute-start(bf16[4,3,8,384]{3,2,1,0:T(8,128)(2,1)S(1)} %get-tuple-element.101), channel_id=1, source_target_pairs={{0,16},{1,2},{2,1},{3,4},{4,3},{5,6},{6,5},{7,8},{8,7},{9,10},{10,... | collective-permute-start | bytes 221192 | tf_op jit(solution)/shard_map/ppermute | solution.py:59
  37.0 0.0 collective-permute-done.8.refs_1_
  37.0 0.8 %collective-permute-start.9 = (bf16[96,384]{1,0:T(8,128)(2,1)S(1)}, bf16[96,384]{1,0:T(8,128)(2,1)S(1)}, u32[]{:S(2)}, u32[]{:S(2)}) collective-permute-start(bf16[96,384]{1,0:T(8,128)(2,1)S(1)} %get-tuple-element.74), channel_id=1, source_target_pairs={{0,16},{16,0},{1,17},{17,1},{2,18},{18,2},{3,19},{19,3},{4,20},{20... | collective-permute-start | bytes 221192 | tf_op jit(solution)/shard_map/ppermute | solution.py:46
  37.8 1.3 %collective-permute-done.13.got_ref = bf16[56,384]{1,0:T(8,128)(2,1)S(1)} collective-permute-done((bf16[56,384]{1,0:T(8,128)(2,1)S(1)}, bf16[56,384]{1,0:T(8,128)(2,1)S(1)}, u32[]{:S(2)}, u32[]{:S(2)}) %collective-permute-start.13) | collective-permute-done | bytes 43040 | tf_op jit(solution)/shard_map/ppermute | solution.py:46
  39.1 2.1 %collective-permute-start.14 = (bf16[56,384]{1,0:T(8,128)(2,1)S(1)}, bf16[56,384]{1,0:T(8,128)(2,1)S(1)}, u32[]{:S(2)}, u32[]{:S(2)}) collective-permute-start(bf16[56,384]{1,0:T(8,128)(2,1)S(1)} %get-tuple-element.98), channel_id=1, source_target_pairs={{0,8},{1,9},{2,10},{3,11},{4,12},{5,13},{6,14},{7,15},{8,0},{9,1},... | collective-permute-start | bytes 129032 | tf_op jit(solution)/shard_map/ppermute | solution.py:46
  41.2 1.6 %shard_map.154.part_ref = f32[256,384]{1,0:T(8,128)S(1)} custom-call(s32[4,8]{1,0:T(4,128)S(1)} %bitcast.11, f32[256,384]{1,0:T(8,128)S(1)} %get-tuple-element.87.grad_ref, f32[7,7,384]{2,1,0:T(8,128)S(1)} %copy-done.2), custom_call_target="tpu_custom_call" | custom-call | bytes 861824 | tf_op jit(solution)/shard_map/pallas_call | solution.py:29
  42.8 0.0 collective-permute-done.15.core_ref
  42.8 1.8 %shard_map.155 = bf16[256,384]{1,0:T(8,128)(2,1)} custom-call(s32[4,8]{1,0:T(4,128)S(1)} %bitcast.12, s32[1,1]{1,0:T(1,128)} %bitcast.place_ref, s32[1,1]{1,0:T(1,128)S(6)} %copy.15.counts_ref, f32[1,4]{1,0:T(1,128)S(1)} %copy-done.10, f32[256,384]{1,0:T(8,128)S(1)} %shard_map.154.part_ref, bf16[4,3,8,384]{3,2,1,0:T(8,128)(2,1)S(1)} %collective-permute-done.15.core_ref, ...), custom_call_target="tpu_custom_call" | custom-call | bytes 1010840 | tf_op jit(solution)/shard_map/pallas_call | solution.py:29
  44.6 0.0 collective-permute-done.14.new_ref
  44.6 0.0 collective-permute-done.9.got_ref
  44.6 0.7 %shard_map.153 = (f32[96,384]{1,0:T(8,128)}, f32[7,7,384]{2,1,0:T(8,128)}, f32[1,384]{1,0:T(1,128)}) custom-call(f32[96,384]{1,0:T(8,128)S(1)} %get-tuple-element.73.keep_ref, bf16[96,384]{1,0:T(8,128)(2,1)S(1)} %collective-permute-done.9.got_ref, f32[56,384]{1,0:T(8,128)S(1)} %get-tuple-element.97.state_ref, bf16[56,384]{1,0:T(8,128)(2,1)S(1)} %collective-permute-done.14.new_ref), custom_call_target="tpu_custom_call" | custom-call | bytes 574464 | tf_op jit(solution)/shard_map/pallas_call | solution.py:29
  (26 shorter events, 0.2 us)
Async XLA Ops:
  0.6 0.9 %copy-start.4 = (bf16[1,4,8,8,384]{4,3,2,1,0:T(8,128)(2,1)S(1)}, bf16[1,4,8,8,384]{4,3,2,1,0:T(8,128)(2,1)}, u32[]{:S(2)}) copy-start(bf16[1,4,8,8,384]{4,3,2,1,0:T(8,128)(2,1)} %param.11) | copy-start | bytes 589828
  1.6 3.9 %copy-start.1 = (bf16[1536,384]{1,0:T(8,128)(2,1)S(1)}, bf16[1536,384]{1,0:T(8,128)(2,1)}, u32[]{:S(2)}) copy-start(bf16[1536,384]{1,0:T(8,128)(2,1)} %w_out_ref.3) | copy-start | bytes 3538948
  1.6 3.9 %copy-start.2 = (f32[7,7,384]{2,1,0:T(8,128)S(1)}, f32[7,7,384]{2,1,0:T(8,128)}, u32[]{:S(2)}) copy-start(f32[7,7,384]{2,1,0:T(8,128)} %kern_ref.7) | copy-start | bytes 225796
  1.6 3.9 %copy-start.3 = (bf16[1,4,8,8,384]{4,3,2,1,0:T(8,128)(2,1)S(1)}, bf16[1,4,8,8,384]{4,3,2,1,0:T(8,128)(2,1)}, u32[]{:S(2)}) copy-start(bf16[1,4,8,8,384]{4,3,2,1,0:T(8,128)(2,1)} %param.12) | copy-start | bytes 589828
  1.6 3.9 %copy-start.5 = (bf16[1,4,8,8,384]{4,3,2,1,0:T(8,128)(2,1)S(1)}, bf16[1,4,8,8,384]{4,3,2,1,0:T(8,128)(2,1)}, u32[]{:S(2)}) copy-start(bf16[1,4,8,8,384]{4,3,2,1,0:T(8,128)(2,1)} %param.11) | copy-start | bytes 589828
  1.6 3.9 %copy-start.6 = (s32[1,4,8]{2,1,0:T(4,128)S(1)}, s32[1,4,8]{2,1,0:T(4,128)}, u32[]{:S(2)}) copy-start(s32[1,4,8]{2,1,0:T(4,128)} %param.15) | copy-start | bytes 388
  1.6 3.9 %copy-start.7 = (f32[384]{0:T(512)S(1)}, f32[384]{0:T(512)}, u32[]{:S(2)}) copy-start(f32[384]{0:T(512)} %scale_ref.3) | copy-start | bytes 4612
  1.6 3.9 %copy-start.9 = (f32[1,384]{1,0:T(1,128)S(1)}, f32[1,384]{1,0:T(1,128)}, u32[]{:S(2)}) copy-start(f32[1,384]{1,0:T(1,128)} %cot_ref.3) | copy-start | bytes 4612
  1.6 3.9 %copy-start.10 = (f32[1,4]{1,0:T(1,128)S(1)}, f32[1,4]{1,0:T(1,128)}, u32[]{:S(2)}) copy-start(f32[1,4]{1,0:T(1,128)} %pool_ref.5) | copy-start | bytes 52
  1.7 5.9 %copy-start = (bf16[384,1536]{1,0:T(8,128)(2,1)S(1)}, bf16[384,1536]{1,0:T(8,128)(2,1)}, u32[]{:S(2)}) copy-start(bf16[384,1536]{1,0:T(8,128)(2,1)} %w_in_ref.5) | copy-start | bytes 3538948
  1.7 5.9 %copy-start.8 = (f32[384]{0:T(512)S(1)}, f32[384]{0:T(512)}, u32[]{:S(2)}) copy-start(f32[384]{0:T(512)} %gain_ref.3) | copy-start | bytes 4612
  1.7 5.9 %collective-permute-start = (bf16[4,3,8,384]{3,2,1,0:T(8,128)(2,1)S(1)}, bf16[4,3,8,384]{3,2,1,0:T(8,128)(2,1)S(1)}, u32[]{:S(2)}, u32[]{:S(2)}) collective-permute-start(bf16[4,3,8,384]{3,2,1,0:T(8,128)(2,1)S(1)} %get-tuple-element.54), channel_id=1, source_target_pairs={{0,1},{1,0},{2,3},{3,2},{4,5},{5,4},{6,7},{7,6},{8,9},{9,8},{10,11... | collective-permute-start | bytes 221192 | tf_op jit(solution)/shard_map/ppermute | solution.py:46
  2.3 5.3 %collective-permute-start.1 = (bf16[4,3,8,384]{3,2,1,0:T(8,128)(2,1)S(1)}, bf16[4,3,8,384]{3,2,1,0:T(8,128)(2,1)S(1)}, u32[]{:S(2)}, u32[]{:S(2)}) collective-permute-start(bf16[4,3,8,384]{3,2,1,0:T(8,128)(2,1)S(1)} %get-tuple-element.55), channel_id=1, source_target_pairs={{0,16},{1,2},{2,1},{3,4},{4,3},{5,6},{6,5},{7,8},{8,7},{9,10},{10,... | collective-permute-start | bytes 221192 | tf_op jit(solution)/shard_map/ppermute | solution.py:59
  9.7 1.6 %collective-permute-start.2 = (bf16[384,384]{1,0:T(8,128)(2,1)S(1)}, bf16[384,384]{1,0:T(8,128)(2,1)S(1)}, u32[]{:S(2)}, u32[]{:S(2)}) collective-permute-start(bf16[384,384]{1,0:T(8,128)(2,1)S(1)} %get-tuple-element.59), channel_id=1, source_target_pairs={{0,1},{1,0},{2,3},{3,2},{4,5},{5,4},{6,7},{7,6},{8,9},{9,8},{10,11... | collective-permute-start | bytes 884744 | tf_op jit(solution)/shard_map/ppermute | solution.py:46
  10.6 2.9 %collective-permute-start.4 = (bf16[384,384]{1,0:T(8,128)(2,1)S(1)}, bf16[384,384]{1,0:T(8,128)(2,1)S(1)}, u32[]{:S(2)}, u32[]{:S(2)}) collective-permute-start(bf16[384,384]{1,0:T(8,128)(2,1)S(1)} %get-tuple-element.64), channel_id=1, source_target_pairs={{0,1},{1,0},{2,3},{3,2},{4,5},{5,4},{6,7},{7,6},{8,9},{9,8},{10,11... | collective-permute-start | bytes 884744 | tf_op jit(solution)/shard_map/ppermute | solution.py:46
  11.4 6.4 %collective-permute-start.3 = (bf16[192,384]{1,0:T(8,128)(2,1)S(1)}, bf16[192,384]{1,0:T(8,128)(2,1)S(1)}, u32[]{:S(2)}, u32[]{:S(2)}) collective-permute-start(bf16[192,384]{1,0:T(8,128)(2,1)S(1)} %get-tuple-element.61), channel_id=1, source_target_pairs={{0,2},{1,3},{2,0},{3,1},{4,6},{5,7},{6,4},{7,5},{8,10},{9,11},{10,... | collective-permute-start | bytes 442376 | tf_op jit(solution)/shard_map/ppermute | solution.py:46
  13.6 5.9 %collective-permute-start.5 = (bf16[192,384]{1,0:T(8,128)(2,1)S(1)}, bf16[192,384]{1,0:T(8,128)(2,1)S(1)}, u32[]{:S(2)}, u32[]{:S(2)}) collective-permute-start(bf16[192,384]{1,0:T(8,128)(2,1)S(1)} %get-tuple-element.66), channel_id=1, source_target_pairs={{0,4},{1,5},{2,6},{3,7},{4,0},{5,1},{6,2},{7,3},{8,12},{9,13},{10,... | collective-permute-start | bytes 442376 | tf_op jit(solution)/shard_map/ppermute | solution.py:46
  19.6 8.7 %collective-permute-start.6 = (bf16[96,384]{1,0:T(8,128)(2,1)S(1)}, bf16[96,384]{1,0:T(8,128)(2,1)S(1)}, u32[]{:S(2)}, u32[]{:S(2)}) collective-permute-start(bf16[96,384]{1,0:T(8,128)(2,1)S(1)} %get-tuple-element.68), channel_id=1, source_target_pairs={{0,4},{1,5},{2,6},{3,7},{4,0},{5,1},{6,2},{7,3},{8,12},{9,13},{10,... | collective-permute-start | bytes 221192 | tf_op jit(solution)/shard_map/ppermute | solution.py:46
  21.3 7.0 %collective-permute-start.7 = (bf16[96,384]{1,0:T(8,128)(2,1)S(1)}, bf16[96,384]{1,0:T(8,128)(2,1)S(1)}, u32[]{:S(2)}, u32[]{:S(2)}) collective-permute-start(bf16[96,384]{1,0:T(8,128)(2,1)S(1)} %get-tuple-element.70), channel_id=1, source_target_pairs={{0,2},{1,3},{2,0},{3,1},{4,6},{5,7},{6,4},{7,5},{8,10},{9,11},{10,... | collective-permute-start | bytes 221192 | tf_op jit(solution)/shard_map/ppermute | solution.py:46
  25.4 1.3 %collective-permute-start.10 = (bf16[56,384]{1,0:T(8,128)(2,1)S(1)}, bf16[56,384]{1,0:T(8,128)(2,1)S(1)}, u32[]{:S(2)}, u32[]{:S(2)}) collective-permute-start(bf16[56,384]{1,0:T(8,128)(2,1)S(1)} %get-tuple-element.90), channel_id=1, source_target_pairs={{0,1},{1,0},{2,3},{3,2},{4,5},{5,4},{6,7},{7,6},{8,9},{9,8},{10,11... | collective-permute-start | bytes 129032 | tf_op jit(solution)/shard_map/ppermute | solution.py:46
  26.7 4.1 %collective-permute-start.11 = (bf16[56,384]{1,0:T(8,128)(2,1)S(1)}, bf16[56,384]{1,0:T(8,128)(2,1)S(1)}, u32[]{:S(2)}, u32[]{:S(2)}) collective-permute-start(bf16[56,384]{1,0:T(8,128)(2,1)S(1)} %get-tuple-element.92), channel_id=1, source_target_pairs={{0,16},{16,0},{1,17},{17,1},{2,18},{18,2},{3,19},{19,3},{4,20},{20... | collective-permute-start | bytes 129032 | tf_op jit(solution)/shard_map/ppermute | solution.py:46
  28.3 8.6 %collective-permute-start.8 = (bf16[96,384]{1,0:T(8,128)(2,1)S(1)}, bf16[96,384]{1,0:T(8,128)(2,1)S(1)}, u32[]{:S(2)}, u32[]{:S(2)}) collective-permute-start(bf16[96,384]{1,0:T(8,128)(2,1)S(1)} %get-tuple-element.72), channel_id=1, source_target_pairs={{0,8},{1,9},{2,10},{3,11},{4,12},{5,13},{6,14},{7,15},{8,0},{9,1},... | collective-permute-start | bytes 221192 | tf_op jit(solution)/shard_map/ppermute | solution.py:46
  30.8 4.1 %collective-permute-start.12 = (bf16[56,384]{1,0:T(8,128)(2,1)S(1)}, bf16[56,384]{1,0:T(8,128)(2,1)S(1)}, u32[]{:S(2)}, u32[]{:S(2)}) collective-permute-start(bf16[56,384]{1,0:T(8,128)(2,1)S(1)} %get-tuple-element.94), channel_id=1, source_target_pairs={{0,2},{1,3},{2,0},{3,1},{4,6},{5,7},{6,4},{7,5},{8,10},{9,11},{10,... | collective-permute-start | bytes 129032 | tf_op jit(solution)/shard_map/ppermute | solution.py:46
  35.0 4.1 %collective-permute-start.13 = (bf16[56,384]{1,0:T(8,128)(2,1)S(1)}, bf16[56,384]{1,0:T(8,128)(2,1)S(1)}, u32[]{:S(2)}, u32[]{:S(2)}) collective-permute-start(bf16[56,384]{1,0:T(8,128)(2,1)S(1)} %get-tuple-element.96), channel_id=1, source_target_pairs={{0,4},{1,5},{2,6},{3,7},{4,0},{5,1},{6,2},{7,3},{8,12},{9,13},{10,... | collective-permute-start | bytes 129032 | tf_op jit(solution)/shard_map/ppermute | solution.py:46
  35.7 7.1 %collective-permute-start.15 = (bf16[4,3,8,384]{3,2,1,0:T(8,128)(2,1)S(1)}, bf16[4,3,8,384]{3,2,1,0:T(8,128)(2,1)S(1)}, u32[]{:S(2)}, u32[]{:S(2)}) collective-permute-start(bf16[4,3,8,384]{3,2,1,0:T(8,128)(2,1)S(1)} %get-tuple-element.100), channel_id=1, source_target_pairs={{0,1},{1,0},{2,3},{3,2},{4,5},{5,4},{6,7},{7,6},{8,9},{9,8},{10,11... | collective-permute-start | bytes 221192 | tf_op jit(solution)/shard_map/ppermute | solution.py:46
  35.7 7.1 %collective-permute-start.16 = (bf16[4,3,8,384]{3,2,1,0:T(8,128)(2,1)S(1)}, bf16[4,3,8,384]{3,2,1,0:T(8,128)(2,1)S(1)}, u32[]{:S(2)}, u32[]{:S(2)}) collective-permute-start(bf16[4,3,8,384]{3,2,1,0:T(8,128)(2,1)S(1)} %get-tuple-element.101), channel_id=1, source_target_pairs={{0,16},{1,2},{2,1},{3,4},{4,3},{5,6},{6,5},{7,8},{8,7},{9,10},{10,... | collective-permute-start | bytes 221192 | tf_op jit(solution)/shard_map/ppermute | solution.py:59
  37.0 7.6 %collective-permute-start.9 = (bf16[96,384]{1,0:T(8,128)(2,1)S(1)}, bf16[96,384]{1,0:T(8,128)(2,1)S(1)}, u32[]{:S(2)}, u32[]{:S(2)}) collective-permute-start(bf16[96,384]{1,0:T(8,128)(2,1)S(1)} %get-tuple-element.74), channel_id=1, source_target_pairs={{0,16},{16,0},{1,17},{17,1},{2,18},{18,2},{3,19},{19,3},{4,20},{20... | collective-permute-start | bytes 221192 | tf_op jit(solution)/shard_map/ppermute | solution.py:46
  39.1 5.5 %collective-permute-start.14 = (bf16[56,384]{1,0:T(8,128)(2,1)S(1)}, bf16[56,384]{1,0:T(8,128)(2,1)S(1)}, u32[]{:S(2)}, u32[]{:S(2)}) collective-permute-start(bf16[56,384]{1,0:T(8,128)(2,1)S(1)} %get-tuple-element.98), channel_id=1, source_target_pairs={{0,8},{1,9},{2,10},{3,11},{4,12},{5,13},{6,14},{7,15},{8,0},{9,1},... | collective-permute-start | bytes 129032 | tf_op jit(solution)/shard_map/ppermute | solution.py:46

commit v6 on v5

--- a/solution.py
+++ b/solution.py
@@ -542,9 +542,8 @@
     ((keep_b, send_b),) = merge([(keep_b, got_b)], [(0, half, 2 * rows, 2)])
     got_b = swapped(send_b, "space", 4)
     half //= 2
-    (keep_a, send_a), (keep_b, send_b) = merge(
-        [(keep_a, got_a), (keep_b, got_b)], [(0, half, rows, 2), (half, half, rows, 1)]
-    )
+    ((keep_a, send_a),) = merge([(keep_a, got_a)], [(0, half, rows, 2)])
+    ((keep_b, send_b),) = merge([(keep_b, got_b)], [(0, half, rows, 1)])
     got_a = swapped(send_a, "space", 4)
     got_b = swapped(send_b, "space", 2)
     held = [(keep_a, got_a), (keep_b, got_b)]
@@ -568,7 +567,7 @@
         scratch=[pltpu.VMEM((TAPS, 8, channels), f32)],
     )
     steps = [("space", 1)] + [("dp", 1 << n) for n in range(groups.bit_length() - 1)]
-    steps += [("space", 1 << n) for n in range(1, stages)]
+    steps += [("space", 4), ("space", 2)] + [("space", 1 << n) for n in range(3, stages)]
     for axis, bit in steps:
         new = swapped(pack, axis, bit)
         if (axis, bit) != steps[-1]:

time: 45.5 us -> 45.1 us (level)
    pallas_call x18 -> x19, Pallas kernels: 12.7 us -> 12.7 us  [call(): pl.pallas_call(body, out_shape=out_shape, in_specs=in_specs, out_specs=ou...]
where the time goes in v6:
time: 45.1 us; the launch traced here: 44.9 us
  starting transfers between devices  19.3 us (43%)
  Pallas kernels  12.7 us (28%)
  waiting for transfers between devices  10.4 us (23%)
  between operations  1.56 us (3%)
  local copies, waits for them, and re-layouts  0.96 us (2%)
    ppermute x15, starting transfers between devices, swapped(): lax.ppermute(value, axis, [(source, source ^ bit) for source in range(cou...  15.8 us
    pallas_call x19, Pallas kernels, call(): pl.pallas_call(body, out_shape=out_shape, in_specs=in_specs, out_specs=ou...  12.7 us
    ppermute x15, waiting for transfers between devices, swapped(): lax.ppermute(value, axis, [(source, source ^ bit) for source in range(cou...  10.4 us
    ppermute x2, starting transfers between devices, crossed(): return lax.ppermute(value, ('dp', 'space'), targets)  3.51 us
    unnamed x22, local copies, waits for them, and re-layouts  0.96 us
  transfers between devices with their start and end apart: 17, of which 7 were waited for; matrix products, arithmetic and copies ran while one was open for 0% of the time, Pallas kernels for 22%

profile of v6, /device:TPU:0, one launch (start us, length us, event | category | flops | bytes accessed | tf_op | source)
XLA Modules:
  0.0 44.9 jit_solution(18180589040477250168)
XLA Ops:
  0.6 0.9 %copy-done.4 = bf16[1,4,8,8,384]{4,3,2,1,0:T(8,128)(2,1)S(1)} copy-done((bf16[1,4,8,8,384]{4,3,2,1,0:T(8,128)(2,1)S(1)}, bf16[1,4,8,8,384]{4,3,2,1,0:T(8,128)(2,1)}, u32[]{:S(2)}) %copy-start.4) | copy-done | bytes 196632
  1.6 0.1 shard_map.138
  1.7 0.0 copy-start
  1.7 0.0 copy-start.8
  1.7 0.6 %collective-permute-start = (bf16[4,3,8,384]{3,2,1,0:T(8,128)(2,1)S(1)}, bf16[4,3,8,384]{3,2,1,0:T(8,128)(2,1)S(1)}, u32[]{:S(2)}, u32[]{:S(2)}) collective-permute-start(bf16[4,3,8,384]{3,2,1,0:T(8,128)(2,1)S(1)} %get-tuple-element.54), channel_id=1, source_target_pairs={{0,1},{1,0},{2,3},{3,2},{4,5},{5,4},{6,7},{7,6},{8,9},{9,8},{10,11... | collective-permute-start | bytes 221192 | tf_op jit(solution)/shard_map/ppermute | solution.py:46
  2.3 2.6 %collective-permute-start.1 = (bf16[4,3,8,384]{3,2,1,0:T(8,128)(2,1)S(1)}, bf16[4,3,8,384]{3,2,1,0:T(8,128)(2,1)S(1)}, u32[]{:S(2)}, u32[]{:S(2)}) collective-permute-start(bf16[4,3,8,384]{3,2,1,0:T(8,128)(2,1)S(1)} %get-tuple-element.55), channel_id=1, source_target_pairs={{0,16},{1,2},{2,1},{3,4},{4,3},{5,6},{6,5},{7,8},{8,7},{9,10},{10,... | collective-permute-start | bytes 221192 | tf_op jit(solution)/shard_map/ppermute | solution.py:59
  5.6 2.0 %shard_map.139 = (f32[3,4,8,24,128]{4,3,2,1,0:T(8,128)S(1)}, f32[256,384]{1,0:T(8,128)S(1)}, bf16[256,512]{1,0:T(8,128)(2,1)S(1)}, f32[256,1536]{1,0:T(8,128)S(1)}, f32[1,384]{1,0:T(1,128)S(1)}) custom-call(s32[4,8]{1,0:T(4,128)S(1)} %bitcast.9, s32[1,1]{1,0:T(1,128)S(6)} %copy.15.counts_ref, f32[1,4]{1,0:T(1,128)S(1)} %copy-done.10, ...), custom_call_target="tpu_custom_call" | custom-call | flops 301989888 | bytes 5060756 | tf_op jit(solution)/shard_map/pallas_call | solution.py:29
  7.6 0.0 collective-permute-done.core_ref
  7.6 0.0 collective-permute-done.1.cross_ref
  7.6 2.0 %shard_map.140 = (f32[3,4,6,24,128]{4,3,2,1,0:T(8,128)S(1)}, f32[256,384]{1,0:T(8,128)S(1)}, f32[256,1]{1,0:T(8,128)S(1)}, bf16[256,384]{1,0:T(8,128)(2,1)S(1)},...) custom-call(s32[4,8]{1,0:T(4,128)S(1)} %bitcast.10, ...), custom_call_target="tpu_custom_call" | custom-call | flops 301989888 | bytes 6385796 | tf_op jit(solution)/shard_map/pallas_call | solution.py:29
  9.7 0.2 collective-permute-start.2
  9.9 0.7 %shard_map.143 = (f32[256,768]{1,0:T(8,128)S(1)}, f32[256,768]{1,0:T(8,128)S(1)}, f32[384,384]{1,0:T(8,128)S(1)}, bf16[384,384]{1,0:T(8,128)(2,1)S(1)}, f32[768,128]{1,0:T(8,128)S(1)}) custom-call(s32[1,1]{1,0:T(1,128)} %bitcast.place_ref, bf16[256,384]{1,0:T(8,128)(2,1)S(1)} %get-tuple-element.64.lifted_ref, bf16[384,1536]{1,0:T(8,128)(2,1)S(1)} %copy-done, ...), custom_call_target="tpu_custom_call" | custom-call | flops 301989888 | bytes 4489220 | tf_op jit(solution)/shard_map/pallas_call | solution.py:29
  10.6 0.4 collective-permute-start.5
  11.0 0.3 collective-permute-done.2.refs_1_
  11.3 0.1 shard_map.141
  11.4 2.0 %collective-permute-start.3 = (bf16[192,384]{1,0:T(8,128)(2,1)S(1)}, bf16[192,384]{1,0:T(8,128)(2,1)S(1)}, u32[]{:S(2)}, u32[]{:S(2)}) collective-permute-start(bf16[192,384]{1,0:T(8,128)(2,1)S(1)} %get-tuple-element.61), channel_id=1, source_target_pairs={{0,2},{1,3},{2,0},{3,1},{4,6},{5,7},{6,4},{7,5},{8,10},{9,11},{10,... | collective-permute-start | bytes 442376 | tf_op jit(solution)/shard_map/ppermute | solution.py:46
  13.5 0.0 collective-permute-done.5.refs_1_
  13.5 0.1 shard_map.144
  13.6 1.6 %collective-permute-start.6 = (bf16[192,384]{1,0:T(8,128)(2,1)S(1)}, bf16[192,384]{1,0:T(8,128)(2,1)S(1)}, u32[]{:S(2)}, u32[]{:S(2)}) collective-permute-start(bf16[192,384]{1,0:T(8,128)(2,1)S(1)} %get-tuple-element.68), channel_id=1, source_target_pairs={{0,4},{1,5},{2,6},{3,7},{4,0},{5,1},{6,2},{7,3},{8,12},{9,13},{10,... | collective-permute-start | bytes 442376 | tf_op jit(solution)/shard_map/ppermute | solution.py:46
  15.2 2.6 %collective-permute-done.3.refs_1_ = bf16[192,384]{1,0:T(8,128)(2,1)S(1)} collective-permute-done((bf16[192,384]{1,0:T(8,128)(2,1)S(1)}, bf16[192,384]{1,0:T(8,128)(2,1)S(1)}, u32[]{:S(2)}, u32[]{:S(2)}) %collective-permute-start.3) | collective-permute-done | bytes 147488 | tf_op jit(solution)/shard_map/ppermute | solution.py:46
  17.8 0.1 shard_map.142
  17.9 1.8 %collective-permute-start.4 = (bf16[96,384]{1,0:T(8,128)(2,1)S(1)}, bf16[96,384]{1,0:T(8,128)(2,1)S(1)}, u32[]{:S(2)}, u32[]{:S(2)}) collective-permute-start(bf16[96,384]{1,0:T(8,128)(2,1)S(1)} %get-tuple-element.63), channel_id=1, source_target_pairs={{0,4},{1,5},{2,6},{3,7},{4,0},{5,1},{6,2},{7,3},{8,12},{9,13},{10,... | collective-permute-start | bytes 221192 | tf_op jit(solution)/shard_map/ppermute | solution.py:46
  19.6 0.0 collective-permute-done.6.refs_1_
  19.6 0.1 shard_map.145
  19.7 1.7 %collective-permute-start.7 = (bf16[96,384]{1,0:T(8,128)(2,1)S(1)}, bf16[96,384]{1,0:T(8,128)(2,1)S(1)}, u32[]{:S(2)}, u32[]{:S(2)}) collective-permute-start(bf16[96,384]{1,0:T(8,128)(2,1)S(1)} %get-tuple-element.70), channel_id=1, source_target_pairs={{0,2},{1,3},{2,0},{3,1},{4,6},{5,7},{6,4},{7,5},{8,10},{9,11},{10,... | collective-permute-start | bytes 221192 | tf_op jit(solution)/shard_map/ppermute | solution.py:46
  21.4 1.7 %shard_map.148 = (f32[256,384]{1,0:T(8,128)S(1)}, bf16[4,3,8,384]{3,2,1,0:T(8,128)(2,1)S(1)}, bf16[4,3,8,384]{3,2,1,0:T(8,128)(2,1)S(1)}, f32[1,384]{1,0:T(1,128)S(1)}) custom-call(s32[1,1]{1,0:T(1,128)} %bitcast.place_ref, s32[1,1]{1,0:T(1,128)S(6)} %copy.15.counts_ref, f32[1,4]{1,0:T(1,128)S(1)} %copy-done.10, f32[256,768]{1,0:T(8,128)S(1)} %get-tuple-element.77.pre_a_ref, ...), custom_call_target="tpu_custom_call" | custom-call | flops 301989888 | bytes 8805400 | tf_op jit(solution)/shard_map/pallas_call | solution.py:29
  23.1 1.5 %shard_map.149 = (f32[56,384]{1,0:T(8,128)S(1)}, bf16[56,384]{1,0:T(8,128)(2,1)S(1)}) custom-call(f32[3,4,8,24,128]{4,3,2,1,0:T(8,128)S(1)} %get-tuple-element.75.pad_ref, f32[3,4,6,24,128]{4,3,2,1,0:T(8,128)S(1)} %get-tuple-element.76.edge_ref, f32[256,384]{1,0:T(8,128)S(1)} %get-tuple-element.87.grad_ref, f32[1,384]{1,0:T(1,128)S(1)} %get-tuple-element.88.emb_ref), custom_call_target="tpu_custom_call" | custom-call | bytes 2588160 | tf_op jit(solution)/shard_map/pallas_call | solution.py:29
  24.6 0.1 collective-permute-start.10
  24.7 1.2 %collective-permute-done.10.got_ref = bf16[56,384]{1,0:T(8,128)(2,1)S(1)} collective-permute-done((bf16[56,384]{1,0:T(8,128)(2,1)S(1)}, bf16[56,384]{1,0:T(8,128)(2,1)S(1)}, u32[]{:S(2)}, u32[]{:S(2)}) %collective-permute-start.10) | collective-permute-done | bytes 43040 | tf_op jit(solution)/shard_map/ppermute | solution.py:46
  25.9 1.6 %collective-permute-start.11 = (bf16[56,384]{1,0:T(8,128)(2,1)S(1)}, bf16[56,384]{1,0:T(8,128)(2,1)S(1)}, u32[]{:S(2)}, u32[]{:S(2)}) collective-permute-start(bf16[56,384]{1,0:T(8,128)(2,1)S(1)} %get-tuple-element.92), channel_id=1, source_target_pairs={{0,16},{16,0},{1,17},{17,1},{2,18},{18,2},{3,19},{19,3},{4,20},{20... | collective-permute-start | bytes 129032 | tf_op jit(solution)/shard_map/ppermute | solution.py:46
  27.5 0.0 collective-permute-done.4.refs_1_
  27.5 0.0 collective-permute-done.7.refs_3_
  27.5 1.8 %collective-permute-start.8 = (bf16[96,384]{1,0:T(8,128)(2,1)S(1)}, bf16[96,384]{1,0:T(8,128)(2,1)S(1)}, u32[]{:S(2)}, u32[]{:S(2)}) collective-permute-start(bf16[96,384]{1,0:T(8,128)(2,1)S(1)} %get-tuple-element.72), channel_id=1, source_target_pairs={{0,8},{1,9},{2,10},{3,11},{4,12},{5,13},{6,14},{7,15},{8,0},{9,1},... | collective-permute-start | bytes 221192 | tf_op jit(solution)/shard_map/ppermute | solution.py:46
  29.4 0.6 %collective-permute-done.11.got_ref = bf16[56,384]{1,0:T(8,128)(2,1)S(1)} collective-permute-done((bf16[56,384]{1,0:T(8,128)(2,1)S(1)}, bf16[56,384]{1,0:T(8,128)(2,1)S(1)}, u32[]{:S(2)}, u32[]{:S(2)}) %collective-permute-start.11) | collective-permute-done | bytes 43040 | tf_op jit(solution)/shard_map/ppermute | solution.py:46
  30.0 0.8 %collective-permute-start.12 = (bf16[56,384]{1,0:T(8,128)(2,1)S(1)}, bf16[56,384]{1,0:T(8,128)(2,1)S(1)}, u32[]{:S(2)}, u32[]{:S(2)}) collective-permute-start(bf16[56,384]{1,0:T(8,128)(2,1)S(1)} %get-tuple-element.94), channel_id=1, source_target_pairs={{0,4},{1,5},{2,6},{3,7},{4,0},{5,1},{6,2},{7,3},{8,12},{9,13},{10,... | collective-permute-start | bytes 129032 | tf_op jit(solution)/shard_map/ppermute | solution.py:46
  30.9 3.7 %collective-permute-done.12.got_ref = bf16[56,384]{1,0:T(8,128)(2,1)S(1)} collective-permute-done((bf16[56,384]{1,0:T(8,128)(2,1)S(1)}, bf16[56,384]{1,0:T(8,128)(2,1)S(1)}, u32[]{:S(2)}, u32[]{:S(2)}) %collective-permute-start.12) | collective-permute-done | bytes 43040 | tf_op jit(solution)/shard_map/ppermute | solution.py:46
  34.6 0.5 %collective-permute-start.13 = (bf16[56,384]{1,0:T(8,128)(2,1)S(1)}, bf16[56,384]{1,0:T(8,128)(2,1)S(1)}, u32[]{:S(2)}, u32[]{:S(2)}) collective-permute-start(bf16[56,384]{1,0:T(8,128)(2,1)S(1)} %get-tuple-element.96), channel_id=1, source_target_pairs={{0,2},{1,3},{2,0},{3,1},{4,6},{5,7},{6,4},{7,5},{8,10},{9,11},{10,... | collective-permute-start | bytes 129032 | tf_op jit(solution)/shard_map/ppermute | solution.py:46
  35.1 0.0 collective-permute-start.15
  35.1 1.0 %collective-permute-start.16 = (bf16[4,3,8,384]{3,2,1,0:T(8,128)(2,1)S(1)}, bf16[4,3,8,384]{3,2,1,0:T(8,128)(2,1)S(1)}, u32[]{:S(2)}, u32[]{:S(2)}) collective-permute-start(bf16[4,3,8,384]{3,2,1,0:T(8,128)(2,1)S(1)} %get-tuple-element.101), channel_id=1, source_target_pairs={{0,16},{1,2},{2,1},{3,4},{4,3},{5,6},{6,5},{7,8},{8,7},{9,10},{10,... | collective-permute-start | bytes 221192 | tf_op jit(solution)/shard_map/ppermute | solution.py:59
  36.1 0.0 collective-permute-done.8.refs_1_
  36.1 1.1 %collective-permute-start.9 = (bf16[96,384]{1,0:T(8,128)(2,1)S(1)}, bf16[96,384]{1,0:T(8,128)(2,1)S(1)}, u32[]{:S(2)}, u32[]{:S(2)}) collective-permute-start(bf16[96,384]{1,0:T(8,128)(2,1)S(1)} %get-tuple-element.74), channel_id=1, source_target_pairs={{0,16},{16,0},{1,17},{17,1},{2,18},{18,2},{3,19},{19,3},{4,20},{20... | collective-permute-start | bytes 221192 | tf_op jit(solution)/shard_map/ppermute | solution.py:46
  37.3 1.4 %collective-permute-done.13.got_ref = bf16[56,384]{1,0:T(8,128)(2,1)S(1)} collective-permute-done((bf16[56,384]{1,0:T(8,128)(2,1)S(1)}, bf16[56,384]{1,0:T(8,128)(2,1)S(1)}, u32[]{:S(2)}, u32[]{:S(2)}) %collective-permute-start.13) | collective-permute-done | bytes 43040 | tf_op jit(solution)/shard_map/ppermute | solution.py:46
  38.7 1.5 %collective-permute-start.14 = (bf16[56,384]{1,0:T(8,128)(2,1)S(1)}, bf16[56,384]{1,0:T(8,128)(2,1)S(1)}, u32[]{:S(2)}, u32[]{:S(2)}) collective-permute-start(bf16[56,384]{1,0:T(8,128)(2,1)S(1)} %get-tuple-element.98), channel_id=1, source_target_pairs={{0,8},{1,9},{2,10},{3,11},{4,12},{5,13},{6,14},{7,15},{8,0},{9,1},... | collective-permute-start | bytes 129032 | tf_op jit(solution)/shard_map/ppermute | solution.py:46
  40.3 1.6 %shard_map.155.part_ref = f32[256,384]{1,0:T(8,128)S(1)} custom-call(s32[4,8]{1,0:T(4,128)S(1)} %bitcast.11, f32[256,384]{1,0:T(8,128)S(1)} %get-tuple-element.87.grad_ref, f32[7,7,384]{2,1,0:T(8,128)S(1)} %copy-done.2), custom_call_target="tpu_custom_call" | custom-call | bytes 861824 | tf_op jit(solution)/shard_map/pallas_call | solution.py:29
  41.9 0.0 collective-permute-done.15.core_ref
  41.9 1.8 %shard_map.156 = bf16[256,384]{1,0:T(8,128)(2,1)} custom-call(s32[4,8]{1,0:T(4,128)S(1)} %bitcast.12, s32[1,1]{1,0:T(1,128)} %bitcast.place_ref, s32[1,1]{1,0:T(1,128)S(6)} %copy.15.counts_ref, f32[1,4]{1,0:T(1,128)S(1)} %copy-done.10, f32[256,384]{1,0:T(8,128)S(1)} %shard_map.155.part_ref, bf16[4,3,8,384]{3,2,1,0:T(8,128)(2,1)S(1)} %collective-permute-done.15.core_ref, ...), custom_call_target="tpu_custom_call" | custom-call | bytes 1010840 | tf_op jit(solution)/shard_map/pallas_call | solution.py:29
  43.7 0.5 %collective-permute-done.14.new_ref = bf16[56,384]{1,0:T(8,128)(2,1)S(1)} collective-permute-done((bf16[56,384]{1,0:T(8,128)(2,1)S(1)}, bf16[56,384]{1,0:T(8,128)(2,1)S(1)}, u32[]{:S(2)}, u32[]{:S(2)}) %collective-permute-start.14) | collective-permute-done | bytes 43040 | tf_op jit(solution)/shard_map/ppermute | solution.py:46
  44.2 0.7 %shard_map.154 = (f32[96,384]{1,0:T(8,128)}, f32[7,7,384]{2,1,0:T(8,128)}, f32[1,384]{1,0:T(1,128)}) custom-call(f32[96,384]{1,0:T(8,128)S(1)} %get-tuple-element.73.keep_ref, bf16[96,384]{1,0:T(8,128)(2,1)S(1)} %collective-permute-done.9.got_ref, f32[56,384]{1,0:T(8,128)S(1)} %get-tuple-element.97.state_ref, bf16[56,384]{1,0:T(8,128)(2,1)S(1)} %collective-permute-done.14.new_ref), custom_call_target="tpu_custom_call" | custom-call | bytes 574464 | tf_op jit(solution)/shard_map/pallas_call | solution.py:29
  (27 shorter events, 0.2 us)
Async XLA Ops:
  0.6 0.9 %copy-start.4 = (bf16[1,4,8,8,384]{4,3,2,1,0:T(8,128)(2,1)S(1)}, bf16[1,4,8,8,384]{4,3,2,1,0:T(8,128)(2,1)}, u32[]{:S(2)}) copy-start(bf16[1,4,8,8,384]{4,3,2,1,0:T(8,128)(2,1)} %param.11) | copy-start | bytes 589828
  1.6 3.9 %copy-start.1 = (bf16[1536,384]{1,0:T(8,128)(2,1)S(1)}, bf16[1536,384]{1,0:T(8,128)(2,1)}, u32[]{:S(2)}) copy-start(bf16[1536,384]{1,0:T(8,128)(2,1)} %w_out_ref.3) | copy-start | bytes 3538948
  1.6 3.9 %copy-start.2 = (f32[7,7,384]{2,1,0:T(8,128)S(1)}, f32[7,7,384]{2,1,0:T(8,128)}, u32[]{:S(2)}) copy-start(f32[7,7,384]{2,1,0:T(8,128)} %kern_ref.7) | copy-start | bytes 225796
  1.6 3.9 %copy-start.3 = (bf16[1,4,8,8,384]{4,3,2,1,0:T(8,128)(2,1)S(1)}, bf16[1,4,8,8,384]{4,3,2,1,0:T(8,128)(2,1)}, u32[]{:S(2)}) copy-start(bf16[1,4,8,8,384]{4,3,2,1,0:T(8,128)(2,1)} %param.12) | copy-start | bytes 589828
  1.6 3.9 %copy-start.5 = (bf16[1,4,8,8,384]{4,3,2,1,0:T(8,128)(2,1)S(1)}, bf16[1,4,8,8,384]{4,3,2,1,0:T(8,128)(2,1)}, u32[]{:S(2)}) copy-start(bf16[1,4,8,8,384]{4,3,2,1,0:T(8,128)(2,1)} %param.11) | copy-start | bytes 589828
  1.6 3.9 %copy-start.6 = (s32[1,4,8]{2,1,0:T(4,128)S(1)}, s32[1,4,8]{2,1,0:T(4,128)}, u32[]{:S(2)}) copy-start(s32[1,4,8]{2,1,0:T(4,128)} %param.15) | copy-start | bytes 388
  1.6 3.9 %copy-start.7 = (f32[384]{0:T(512)S(1)}, f32[384]{0:T(512)}, u32[]{:S(2)}) copy-start(f32[384]{0:T(512)} %scale_ref.3) | copy-start | bytes 4612
  1.6 3.9 %copy-start.9 = (f32[1,384]{1,0:T(1,128)S(1)}, f32[1,384]{1,0:T(1,128)}, u32[]{:S(2)}) copy-start(f32[1,384]{1,0:T(1,128)} %cot_ref.3) | copy-start | bytes 4612
  1.6 3.9 %copy-start.10 = (f32[1,4]{1,0:T(1,128)S(1)}, f32[1,4]{1,0:T(1,128)}, u32[]{:S(2)}) copy-start(f32[1,4]{1,0:T(1,128)} %pool_ref.5) | copy-start | bytes 52
  1.7 5.9 %copy-start = (bf16[384,1536]{1,0:T(8,128)(2,1)S(1)}, bf16[384,1536]{1,0:T(8,128)(2,1)}, u32[]{:S(2)}) copy-start(bf16[384,1536]{1,0:T(8,128)(2,1)} %w_in_ref.5) | copy-start | bytes 3538948
  1.7 5.9 %copy-start.8 = (f32[384]{0:T(512)S(1)}, f32[384]{0:T(512)}, u32[]{:S(2)}) copy-start(f32[384]{0:T(512)} %gain_ref.3) | copy-start | bytes 4612
  1.7 5.9 %collective-permute-start = (bf16[4,3,8,384]{3,2,1,0:T(8,128)(2,1)S(1)}, bf16[4,3,8,384]{3,2,1,0:T(8,128)(2,1)S(1)}, u32[]{:S(2)}, u32[]{:S(2)}) collective-permute-start(bf16[4,3,8,384]{3,2,1,0:T(8,128)(2,1)S(1)} %get-tuple-element.54), channel_id=1, source_target_pairs={{0,1},{1,0},{2,3},{3,2},{4,5},{5,4},{6,7},{7,6},{8,9},{9,8},{10,11... | collective-permute-start | bytes 221192 | tf_op jit(solution)/shard_map/ppermute | solution.py:46
  2.3 5.3 %collective-permute-start.1 = (bf16[4,3,8,384]{3,2,1,0:T(8,128)(2,1)S(1)}, bf16[4,3,8,384]{3,2,1,0:T(8,128)(2,1)S(1)}, u32[]{:S(2)}, u32[]{:S(2)}) collective-permute-start(bf16[4,3,8,384]{3,2,1,0:T(8,128)(2,1)S(1)} %get-tuple-element.55), channel_id=1, source_target_pairs={{0,16},{1,2},{2,1},{3,4},{4,3},{5,6},{6,5},{7,8},{8,7},{9,10},{10,... | collective-permute-start | bytes 221192 | tf_op jit(solution)/shard_map/ppermute | solution.py:59
  9.7 1.6 %collective-permute-start.2 = (bf16[384,384]{1,0:T(8,128)(2,1)S(1)}, bf16[384,384]{1,0:T(8,128)(2,1)S(1)}, u32[]{:S(2)}, u32[]{:S(2)}) collective-permute-start(bf16[384,384]{1,0:T(8,128)(2,1)S(1)} %get-tuple-element.59), channel_id=1, source_target_pairs={{0,1},{1,0},{2,3},{3,2},{4,5},{5,4},{6,7},{7,6},{8,9},{9,8},{10,11... | collective-permute-start | bytes 884744 | tf_op jit(solution)/shard_map/ppermute | solution.py:46
  10.6 2.9 %collective-permute-start.5 = (bf16[384,384]{1,0:T(8,128)(2,1)S(1)}, bf16[384,384]{1,0:T(8,128)(2,1)S(1)}, u32[]{:S(2)}, u32[]{:S(2)}) collective-permute-start(bf16[384,384]{1,0:T(8,128)(2,1)S(1)} %get-tuple-element.66), channel_id=1, source_target_pairs={{0,1},{1,0},{2,3},{3,2},{4,5},{5,4},{6,7},{7,6},{8,9},{9,8},{10,11... | collective-permute-start | bytes 884744 | tf_op jit(solution)/shard_map/ppermute | solution.py:46
  11.4 6.4 %collective-permute-start.3 = (bf16[192,384]{1,0:T(8,128)(2,1)S(1)}, bf16[192,384]{1,0:T(8,128)(2,1)S(1)}, u32[]{:S(2)}, u32[]{:S(2)}) collective-permute-start(bf16[192,384]{1,0:T(8,128)(2,1)S(1)} %get-tuple-element.61), channel_id=1, source_target_pairs={{0,2},{1,3},{2,0},{3,1},{4,6},{5,7},{6,4},{7,5},{8,10},{9,11},{10,... | collective-permute-start | bytes 442376 | tf_op jit(solution)/shard_map/ppermute | solution.py:46
  13.6 6.1 %collective-permute-start.6 = (bf16[192,384]{1,0:T(8,128)(2,1)S(1)}, bf16[192,384]{1,0:T(8,128)(2,1)S(1)}, u32[]{:S(2)}, u32[]{:S(2)}) collective-permute-start(bf16[192,384]{1,0:T(8,128)(2,1)S(1)} %get-tuple-element.68), channel_id=1, source_target_pairs={{0,4},{1,5},{2,6},{3,7},{4,0},{5,1},{6,2},{7,3},{8,12},{9,13},{10,... | collective-permute-start | bytes 442376 | tf_op jit(solution)/shard_map/ppermute | solution.py:46
  17.9 9.6 %collective-permute-start.4 = (bf16[96,384]{1,0:T(8,128)(2,1)S(1)}, bf16[96,384]{1,0:T(8,128)(2,1)S(1)}, u32[]{:S(2)}, u32[]{:S(2)}) collective-permute-start(bf16[96,384]{1,0:T(8,128)(2,1)S(1)} %get-tuple-element.63), channel_id=1, source_target_pairs={{0,4},{1,5},{2,6},{3,7},{4,0},{5,1},{6,2},{7,3},{8,12},{9,13},{10,... | collective-permute-start | bytes 221192 | tf_op jit(solution)/shard_map/ppermute | solution.py:46
  19.7 7.8 %collective-permute-start.7 = (bf16[96,384]{1,0:T(8,128)(2,1)S(1)}, bf16[96,384]{1,0:T(8,128)(2,1)S(1)}, u32[]{:S(2)}, u32[]{:S(2)}) collective-permute-start(bf16[96,384]{1,0:T(8,128)(2,1)S(1)} %get-tuple-element.70), channel_id=1, source_target_pairs={{0,2},{1,3},{2,0},{3,1},{4,6},{5,7},{6,4},{7,5},{8,10},{9,11},{10,... | collective-permute-start | bytes 221192 | tf_op jit(solution)/shard_map/ppermute | solution.py:46
  24.6 1.3 %collective-permute-start.10 = (bf16[56,384]{1,0:T(8,128)(2,1)S(1)}, bf16[56,384]{1,0:T(8,128)(2,1)S(1)}, u32[]{:S(2)}, u32[]{:S(2)}) collective-permute-start(bf16[56,384]{1,0:T(8,128)(2,1)S(1)} %get-tuple-element.90), channel_id=1, source_target_pairs={{0,1},{1,0},{2,3},{3,2},{4,5},{5,4},{6,7},{7,6},{8,9},{9,8},{10,11... | collective-permute-start | bytes 129032 | tf_op jit(solution)/shard_map/ppermute | solution.py:46
  25.9 4.1 %collective-permute-start.11 = (bf16[56,384]{1,0:T(8,128)(2,1)S(1)}, bf16[56,384]{1,0:T(8,128)(2,1)S(1)}, u32[]{:S(2)}, u32[]{:S(2)}) collective-permute-start(bf16[56,384]{1,0:T(8,128)(2,1)S(1)} %get-tuple-element.92), channel_id=1, source_target_pairs={{0,16},{16,0},{1,17},{17,1},{2,18},{18,2},{3,19},{19,3},{4,20},{20... | collective-permute-start | bytes 129032 | tf_op jit(solution)/shard_map/ppermute | solution.py:46
  27.5 8.6 %collective-permute-start.8 = (bf16[96,384]{1,0:T(8,128)(2,1)S(1)}, bf16[96,384]{1,0:T(8,128)(2,1)S(1)}, u32[]{:S(2)}, u32[]{:S(2)}) collective-permute-start(bf16[96,384]{1,0:T(8,128)(2,1)S(1)} %get-tuple-element.72), channel_id=1, source_target_pairs={{0,8},{1,9},{2,10},{3,11},{4,12},{5,13},{6,14},{7,15},{8,0},{9,1},... | collective-permute-start | bytes 221192 | tf_op jit(solution)/shard_map/ppermute | solution.py:46
  30.0 4.6 %collective-permute-start.12 = (bf16[56,384]{1,0:T(8,128)(2,1)S(1)}, bf16[56,384]{1,0:T(8,128)(2,1)S(1)}, u32[]{:S(2)}, u32[]{:S(2)}) collective-permute-start(bf16[56,384]{1,0:T(8,128)(2,1)S(1)} %get-tuple-element.94), channel_id=1, source_target_pairs={{0,4},{1,5},{2,6},{3,7},{4,0},{5,1},{6,2},{7,3},{8,12},{9,13},{10,... | collective-permute-start | bytes 129032 | tf_op jit(solution)/shard_map/ppermute | solution.py:46
  34.6 4.1 %collective-permute-start.13 = (bf16[56,384]{1,0:T(8,128)(2,1)S(1)}, bf16[56,384]{1,0:T(8,128)(2,1)S(1)}, u32[]{:S(2)}, u32[]{:S(2)}) collective-permute-start(bf16[56,384]{1,0:T(8,128)(2,1)S(1)} %get-tuple-element.96), channel_id=1, source_target_pairs={{0,2},{1,3},{2,0},{3,1},{4,6},{5,7},{6,4},{7,5},{8,10},{9,11},{10,... | collective-permute-start | bytes 129032 | tf_op jit(solution)/shard_map/ppermute | solution.py:46
  35.1 6.8 %collective-permute-start.15 = (bf16[4,3,8,384]{3,2,1,0:T(8,128)(2,1)S(1)}, bf16[4,3,8,384]{3,2,1,0:T(8,128)(2,1)S(1)}, u32[]{:S(2)}, u32[]{:S(2)}) collective-permute-start(bf16[4,3,8,384]{3,2,1,0:T(8,128)(2,1)S(1)} %get-tuple-element.100), channel_id=1, source_target_pairs={{0,1},{1,0},{2,3},{3,2},{4,5},{5,4},{6,7},{7,6},{8,9},{9,8},{10,11... | collective-permute-start | bytes 221192 | tf_op jit(solution)/shard_map/ppermute | solution.py:46
  35.1 6.8 %collective-permute-start.16 = (bf16[4,3,8,384]{3,2,1,0:T(8,128)(2,1)S(1)}, bf16[4,3,8,384]{3,2,1,0:T(8,128)(2,1)S(1)}, u32[]{:S(2)}, u32[]{:S(2)}) collective-permute-start(bf16[4,3,8,384]{3,2,1,0:T(8,128)(2,1)S(1)} %get-tuple-element.101), channel_id=1, source_target_pairs={{0,16},{1,2},{2,1},{3,4},{4,3},{5,6},{6,5},{7,8},{8,7},{9,10},{10,... | collective-permute-start | bytes 221192 | tf_op jit(solution)/shard_map/ppermute | solution.py:59
  36.1 8.1 %collective-permute-start.9 = (bf16[96,384]{1,0:T(8,128)(2,1)S(1)}, bf16[96,384]{1,0:T(8,128)(2,1)S(1)}, u32[]{:S(2)}, u32[]{:S(2)}) collective-permute-start(bf16[96,384]{1,0:T(8,128)(2,1)S(1)} %get-tuple-element.74), channel_id=1, source_target_pairs={{0,16},{16,0},{1,17},{17,1},{2,18},{18,2},{3,19},{19,3},{4,20},{20... | collective-permute-start | bytes 221192 | tf_op jit(solution)/shard_map/ppermute | solution.py:46
  38.7 5.4 %collective-permute-start.14 = (bf16[56,384]{1,0:T(8,128)(2,1)S(1)}, bf16[56,384]{1,0:T(8,128)(2,1)S(1)}, u32[]{:S(2)}, u32[]{:S(2)}) collective-permute-start(bf16[56,384]{1,0:T(8,128)(2,1)S(1)} %get-tuple-element.98), channel_id=1, source_target_pairs={{0,8},{1,9},{2,10},{3,11},{4,12},{5,13},{6,14},{7,15},{8,0},{9,1},... | collective-permute-start | bytes 129032 | tf_op jit(solution)/shard_map/ppermute | solution.py:46

commit v7 on v4

--- a/solution.py
+++ b/solution.py
@@ -9,6 +9,7 @@
 
 sqrt_half = 0.7071067811865476
 inv_root_two_pi = 0.3989422804014327
+half_log2_e = -0.7213475204444817
 f32 = jnp.float32
 bf16 = jnp.bfloat16
 LANES = 128
@@ -81,15 +82,24 @@
             place(pad_ref, tile, first_row + row, 2, own_at(local(east, capacity), row) * valid(east), parts)
 
 
-def fill_edge(pad_ref, odd_ref, even_ref, odd, adj_ref, capacity, entries, first_row, parts):
+def fill_edge(pad_ref, edge_ref, adj_ref, capacity, entries, first_row, parts):
     for tile in range(capacity):
         for part, entry in enumerate(entries):
             wanted = adj_ref[tile, entry]
             index, keep = local(wanted, capacity), valid(wanted)
             for row in range(3):
-                value = odd_ref[index, row].astype(f32) * (keep * odd)
-                value = value + even_ref[index, row].astype(f32) * (keep * (1.0 - odd))
+                value = edge_ref[index, row].astype(f32) * keep
                 place(pad_ref, tile, first_row + row, part, value, parts)
+
+
+def fill_edges(pad_ref, core_ref, cross_ref, place_ref, adj_ref, capacity, parts):
+    odd = lax.rem(place_ref[0, 0], 2)
+    for parity, upper_ref, lower_ref in ((1, core_ref, cross_ref), (0, cross_ref, core_ref)):
+
+        @pl.when(odd == parity)
+        def _():
+            fill_edge(pad_ref, upper_ref, adj_ref, capacity, UPPER, 0, parts)
+            fill_edge(pad_ref, lower_ref, adj_ref, capacity, LOWER, 3, parts)
 
 
 def is_live(counts_ref, tile):
@@ -201,9 +211,7 @@
     capacity, parts = adj_ref.shape[0], conv_ref.shape[1] // LANES
     channels = conv_ref.shape[1]
     pixels = 64
-    odd = is_odd(place_ref)
-    fill_edge(edge_ref, core_ref, cross_ref, odd, adj_ref, capacity, UPPER, 0, parts)
-    fill_edge(edge_ref, cross_ref, core_ref, odd, adj_ref, capacity, LOWER, 3, parts)
+    fill_edges(edge_ref, core_ref, cross_ref, place_ref, adj_ref, capacity, parts)
 
     def finish(tile, lane, sums):
         for row in range(8):
@@ -266,7 +274,7 @@
     for first in range(0, hidden, chunk):
         at = slice(first, first + chunk)
         pre = pre_ref[:, at]
-        density = jnp.exp(-0.5 * pre * pre) * inv_root_two_pi
+        density = jnp.exp2(pre * pre * half_log2_e) * inv_root_two_pi
         pre_grad = (act_grad_ref[:, at] * (cdf_ref[:, at] + pre * density)).astype(bf16)
         term = lax.dot_general(
             pre_grad, w_in_ref[:, at], (((1,), (1,)), ((), ())), preferred_element_type=f32
@@ -405,9 +413,7 @@
     out_ref, pad_ref,
 ):
     capacity, parts = adj_ref.shape[0], part_ref.shape[1] // LANES
-    odd = is_odd(place_ref)
-    fill_edge(pad_ref, core_ref, cross_ref, odd, adj_ref, capacity, UPPER, 0, parts)
-    fill_edge(pad_ref, cross_ref, core_ref, odd, adj_ref, capacity, LOWER, 3, parts)
+    fill_edges(pad_ref, core_ref, cross_ref, place_ref, adj_ref, capacity, parts)
 
     def finish(tile, lane, sums):
         live = is_live(counts_ref, tile)

time: 46.2 us -> 46 us (level)
  no operation moved by 1% of the time
where the time goes in v7:
time: 46 us; the launch traced here: 45.8 us
  starting transfers between devices  19.8 us (43%)
  Pallas kernels  12.1 us (26%)
  waiting for transfers between devices  11.4 us (25%)
  between operations  1.55 us (3%)
  local copies, waits for them, and re-layouts  0.96 us (2%)
    ppermute x14, starting transfers between devices, swapped(): lax.ppermute(value, axis, [(source, source ^ bit) for source in range(cou...  16 us
    pallas_call x16, Pallas kernels, call(): pl.pallas_call(body, out_shape=out_shape, in_specs=in_specs, out_specs=ou...  12.1 us
    ppermute x14, waiting for transfers between devices, swapped(): lax.ppermute(value, axis, [(source, source ^ bit) for source in range(cou...  11.4 us
    ppermute x2, starting transfers between devices, crossed(): return lax.ppermute(value, ('dp', 'space'), targets)  3.81 us
    unnamed x22, local copies, waits for them, and re-layouts  0.96 us
  transfers between devices with their start and end apart: 16, of which 6 were waited for; matrix products, arithmetic and copies ran while one was open for 0% of the time, Pallas kernels for 19%

profile of v7, /device:TPU:0, one launch (start us, length us, event | category | flops | bytes accessed | tf_op | source)
XLA Modules:
  0.0 45.8 jit_solution(6432569995265159071)
XLA Ops:
  0.6 0.9 %copy-done.4 = bf16[1,4,8,8,384]{4,3,2,1,0:T(8,128)(2,1)S(1)} copy-done((bf16[1,4,8,8,384]{4,3,2,1,0:T(8,128)(2,1)S(1)}, bf16[1,4,8,8,384]{4,3,2,1,0:T(8,128)(2,1)}, u32[]{:S(2)}) %copy-start.4) | copy-done | bytes 196632
  1.6 0.0 copy-start.6
  1.6 0.0 copy-start.7
  1.6 0.0 copy-start.8
  1.6 0.1 shard_map.138
  1.7 0.0 copy-start.1
  1.7 0.0 copy-start.10
  1.7 0.6 %collective-permute-start = (bf16[4,3,8,384]{3,2,1,0:T(8,128)(2,1)S(1)}, bf16[4,3,8,384]{3,2,1,0:T(8,128)(2,1)S(1)}, u32[]{:S(2)}, u32[]{:S(2)}) collective-permute-start(bf16[4,3,8,384]{3,2,1,0:T(8,128)(2,1)S(1)} %get-tuple-element.48), channel_id=1, source_target_pairs={{0,1},{1,0},{2,3},{3,2},{4,5},{5,4},{6,7},{7,6},{8,9},{9,8},{10,11... | collective-permute-start | bytes 221192 | tf_op jit(solution)/shard_map/ppermute | solution.py:47
  2.3 2.6 %collective-permute-start.1 = (bf16[4,3,8,384]{3,2,1,0:T(8,128)(2,1)S(1)}, bf16[4,3,8,384]{3,2,1,0:T(8,128)(2,1)S(1)}, u32[]{:S(2)}, u32[]{:S(2)}) collective-permute-start(bf16[4,3,8,384]{3,2,1,0:T(8,128)(2,1)S(1)} %get-tuple-element.49), channel_id=1, source_target_pairs={{0,16},{1,2},{2,1},{3,4},{4,3},{5,6},{6,5},{7,8},{8,7},{9,10},{10,... | collective-permute-start | bytes 221192 | tf_op jit(solution)/shard_map/ppermute | solution.py:60
  5.6 2.0 %shard_map.139 = (f32[3,4,8,24,128]{4,3,2,1,0:T(8,128)S(1)}, f32[256,384]{1,0:T(8,128)S(1)}, bf16[256,512]{1,0:T(8,128)(2,1)S(1)}, f32[256,1536]{1,0:T(8,128)S(1)}, f32[1,384]{1,0:T(1,128)S(1)}) custom-call(s32[4,8]{1,0:T(4,128)S(1)} %bitcast.9, s32[1,1]{1,0:T(1,128)S(6)} %copy.15.counts_ref, f32[1,4]{1,0:T(1,128)S(1)} %copy-done.9, f32[1,384]{1,0:T(1,128)S(1)} %copy-done.8, ...), custom_call_target="tpu_custom_call" | custom-call | flops 301989888 | bytes 5060756 | tf_op jit(solution)/shard_map/pallas_call | solution.py:30
  7.6 0.0 collective-permute-done.core_ref
  7.6 0.0 collective-permute-done.1.cross_ref
  7.6 2.5 %shard_map.140 = (f32[3,4,6,24,128]{4,3,2,1,0:T(8,128)S(1)}, f32[256,384]{1,0:T(8,128)S(1)}, f32[256,1]{1,0:T(8,128)S(1)}, f32[256,1536]{1,0:T(8,128)S(1)}, f32[...) custom-call(s32[4,8]{1,0:T(4,128)S(1)} %bitcast.10, ...), custom_call_target="tpu_custom_call" | custom-call | flops 603979776 | bytes 9040004 | tf_op jit(solution)/shard_map/pallas_call | solution.py:30
  10.1 0.2 collective-permute-start.2
  10.3 1.9 %collective-permute-done.2.refs_1_ = bf16[768,384]{1,0:T(8,128)(2,1)S(1)} collective-permute-done((bf16[768,384]{1,0:T(8,128)(2,1)S(1)}, bf16[768,384]{1,0:T(8,128)(2,1)S(1)}, u32[]{:S(2)}, u32[]{:S(2)}) %collective-permute-start.2) | collective-permute-done | bytes 589856 | tf_op jit(solution)/shard_map/ppermute | solution.py:47
  12.2 0.3 shard_map.141
  12.5 2.0 %collective-permute-start.3 = (bf16[192,384]{1,0:T(8,128)(2,1)S(1)}, bf16[192,384]{1,0:T(8,128)(2,1)S(1)}, u32[]{:S(2)}, u32[]{:S(2)}) collective-permute-start(bf16[192,384]{1,0:T(8,128)(2,1)S(1)} %get-tuple-element.55), channel_id=1, source_target_pairs={{0,2},{1,3},{2,0},{3,1},{4,6},{5,7},{6,4},{7,5},{8,10},{9,11},{10,... | collective-permute-start | bytes 442376 | tf_op jit(solution)/shard_map/ppermute | solution.py:47
  14.5 1.6 %collective-permute-start.4 = (bf16[192,384]{1,0:T(8,128)(2,1)S(1)}, bf16[192,384]{1,0:T(8,128)(2,1)S(1)}, u32[]{:S(2)}, u32[]{:S(2)}) collective-permute-start(bf16[192,384]{1,0:T(8,128)(2,1)S(1)} %get-tuple-element.57), channel_id=1, source_target_pairs={{0,4},{1,5},{2,6},{3,7},{4,0},{5,1},{6,2},{7,3},{8,12},{9,13},{10,... | collective-permute-start | bytes 442376 | tf_op jit(solution)/shard_map/ppermute | solution.py:47
  16.0 2.8 %collective-permute-done.3.refs_1_ = bf16[192,384]{1,0:T(8,128)(2,1)S(1)} collective-permute-done((bf16[192,384]{1,0:T(8,128)(2,1)S(1)}, bf16[192,384]{1,0:T(8,128)(2,1)S(1)}, u32[]{:S(2)}, u32[]{:S(2)}) %collective-permute-start.3) | collective-permute-done | bytes 147488 | tf_op jit(solution)/shard_map/ppermute | solution.py:47
  18.8 1.5 %collective-permute-done.4.refs_3_ = bf16[192,384]{1,0:T(8,128)(2,1)S(1)} collective-permute-done((bf16[192,384]{1,0:T(8,128)(2,1)S(1)}, bf16[192,384]{1,0:T(8,128)(2,1)S(1)}, u32[]{:S(2)}, u32[]{:S(2)}) %collective-permute-start.4) | collective-permute-done | bytes 147488 | tf_op jit(solution)/shard_map/ppermute | solution.py:47
  20.3 0.1 shard_map.142
  20.4 1.6 %collective-permute-start.5 = (bf16[96,384]{1,0:T(8,128)(2,1)S(1)}, bf16[96,384]{1,0:T(8,128)(2,1)S(1)}, u32[]{:S(2)}, u32[]{:S(2)}) collective-permute-start(bf16[96,384]{1,0:T(8,128)(2,1)S(1)} %get-tuple-element.59), channel_id=1, source_target_pairs={{0,4},{1,5},{2,6},{3,7},{4,0},{5,1},{6,2},{7,3},{8,12},{9,13},{10,... | collective-permute-start | bytes 221192 | tf_op jit(solution)/shard_map/ppermute | solution.py:47
  22.1 0.4 collective-permute-start.6
  22.5 1.5 %shard_map.145 = (f32[256,384]{1,0:T(8,128)S(1)}, bf16[4,3,8,384]{3,2,1,0:T(8,128)(2,1)S(1)}, bf16[4,3,8,384]{3,2,1,0:T(8,128)(2,1)S(1)}, f32[1,384]{1,0:T(1,128)S(1)}) custom-call(s32[1,1]{1,0:T(1,128)} %bitcast.place_ref, s32[1,1]{1,0:T(1,128)S(6)} %copy.15.counts_ref, f32[1,4]{1,0:T(1,128)S(1)} %copy-done.9, f32[256,1536]{1,0:T(8,128)S(1)} %get-tuple-element.68.pre_ref, ...), custom_call_target="tpu_custom_call" | custom-call | flops 301989888 | bytes 8805400 | tf_op jit(solution)/shard_map/pallas_call | solution.py:30
  24.0 1.4 %shard_map.146 = (f32[56,384]{1,0:T(8,128)S(1)}, bf16[56,384]{1,0:T(8,128)(2,1)S(1)}) custom-call(f32[3,4,8,24,128]{4,3,2,1,0:T(8,128)S(1)} %get-tuple-element.66.pad_ref, f32[3,4,6,24,128]{4,3,2,1,0:T(8,128)S(1)} %get-tuple-element.67.edge_ref, f32[256,384]{1,0:T(8,128)S(1)} %get-tuple-element.75.grad_ref, f32[1,384]{1,0:T(1,128)S(1)} %get-tuple-element.76.emb_ref), custom_call_target="tpu_custom_call" | custom-call | bytes 2588160 | tf_op jit(solution)/shard_map/pallas_call | solution.py:30
  25.4 0.1 collective-permute-start.9
  25.4 1.2 %collective-permute-done.9.got_ref = bf16[56,384]{1,0:T(8,128)(2,1)S(1)} collective-permute-done((bf16[56,384]{1,0:T(8,128)(2,1)S(1)}, bf16[56,384]{1,0:T(8,128)(2,1)S(1)}, u32[]{:S(2)}, u32[]{:S(2)}) %collective-permute-start.9) | collective-permute-done | bytes 43040 | tf_op jit(solution)/shard_map/ppermute | solution.py:47
  26.7 1.6 %collective-permute-start.10 = (bf16[56,384]{1,0:T(8,128)(2,1)S(1)}, bf16[56,384]{1,0:T(8,128)(2,1)S(1)}, u32[]{:S(2)}, u32[]{:S(2)}) collective-permute-start(bf16[56,384]{1,0:T(8,128)(2,1)S(1)} %get-tuple-element.80), channel_id=1, source_target_pairs={{0,16},{16,0},{1,17},{17,1},{2,18},{18,2},{3,19},{19,3},{4,20},{20... | collective-permute-start | bytes 129032 | tf_op jit(solution)/shard_map/ppermute | solution.py:47
  28.2 0.0 collective-permute-done.5.refs_1_
  28.3 0.0 collective-permute-done.6.refs_3_
  28.3 2.7 %collective-permute-start.7 = (bf16[96,384]{1,0:T(8,128)(2,1)S(1)}, bf16[96,384]{1,0:T(8,128)(2,1)S(1)}, u32[]{:S(2)}, u32[]{:S(2)}) collective-permute-start(bf16[96,384]{1,0:T(8,128)(2,1)S(1)} %get-tuple-element.63), channel_id=1, source_target_pairs={{0,8},{1,9},{2,10},{3,11},{4,12},{5,13},{6,14},{7,15},{8,0},{9,1},... | collective-permute-start | bytes 221192 | tf_op jit(solution)/shard_map/ppermute | solution.py:47
  31.0 0.0 collective-permute-done.10.got_ref
  31.0 1.5 %collective-permute-start.11 = (bf16[56,384]{1,0:T(8,128)(2,1)S(1)}, bf16[56,384]{1,0:T(8,128)(2,1)S(1)}, u32[]{:S(2)}, u32[]{:S(2)}) collective-permute-start(bf16[56,384]{1,0:T(8,128)(2,1)S(1)} %get-tuple-element.82), channel_id=1, source_target_pairs={{0,2},{1,3},{2,0},{3,1},{4,6},{5,7},{6,4},{7,5},{8,10},{9,11},{10,... | collective-permute-start | bytes 129032 | tf_op jit(solution)/shard_map/ppermute | solution.py:47
  32.5 2.6 %collective-permute-done.11.got_ref = bf16[56,384]{1,0:T(8,128)(2,1)S(1)} collective-permute-done((bf16[56,384]{1,0:T(8,128)(2,1)S(1)}, bf16[56,384]{1,0:T(8,128)(2,1)S(1)}, u32[]{:S(2)}, u32[]{:S(2)}) %collective-permute-start.11) | collective-permute-done | bytes 43040 | tf_op jit(solution)/shard_map/ppermute | solution.py:47
  35.1 0.5 %collective-permute-start.12 = (bf16[56,384]{1,0:T(8,128)(2,1)S(1)}, bf16[56,384]{1,0:T(8,128)(2,1)S(1)}, u32[]{:S(2)}, u32[]{:S(2)}) collective-permute-start(bf16[56,384]{1,0:T(8,128)(2,1)S(1)} %get-tuple-element.84), channel_id=1, source_target_pairs={{0,4},{1,5},{2,6},{3,7},{4,0},{5,1},{6,2},{7,3},{8,12},{9,13},{10,... | collective-permute-start | bytes 129032 | tf_op jit(solution)/shard_map/ppermute | solution.py:47
  35.6 0.0 collective-permute-start.14
  35.6 1.3 %collective-permute-start.15 = (bf16[4,3,8,384]{3,2,1,0:T(8,128)(2,1)S(1)}, bf16[4,3,8,384]{3,2,1,0:T(8,128)(2,1)S(1)}, u32[]{:S(2)}, u32[]{:S(2)}) collective-permute-start(bf16[4,3,8,384]{3,2,1,0:T(8,128)(2,1)S(1)} %get-tuple-element.89), channel_id=1, source_target_pairs={{0,16},{1,2},{2,1},{3,4},{4,3},{5,6},{6,5},{7,8},{8,7},{9,10},{10,... | collective-permute-start | bytes 221192 | tf_op jit(solution)/shard_map/ppermute | solution.py:60
  36.9 0.0 collective-permute-done.7.refs_1_
  36.9 0.8 %collective-permute-start.8 = (bf16[96,384]{1,0:T(8,128)(2,1)S(1)}, bf16[96,384]{1,0:T(8,128)(2,1)S(1)}, u32[]{:S(2)}, u32[]{:S(2)}) collective-permute-start(bf16[96,384]{1,0:T(8,128)(2,1)S(1)} %get-tuple-element.65), channel_id=1, source_target_pairs={{0,16},{16,0},{1,17},{17,1},{2,18},{18,2},{3,19},{19,3},{4,20},{20... | collective-permute-start | bytes 221192 | tf_op jit(solution)/shard_map/ppermute | solution.py:47
  37.8 1.4 %collective-permute-done.12.got_ref = bf16[56,384]{1,0:T(8,128)(2,1)S(1)} collective-permute-done((bf16[56,384]{1,0:T(8,128)(2,1)S(1)}, bf16[56,384]{1,0:T(8,128)(2,1)S(1)}, u32[]{:S(2)}, u32[]{:S(2)}) %collective-permute-start.12) | collective-permute-done | bytes 43040 | tf_op jit(solution)/shard_map/ppermute | solution.py:47
  39.2 2.5 %collective-permute-start.13 = (bf16[56,384]{1,0:T(8,128)(2,1)S(1)}, bf16[56,384]{1,0:T(8,128)(2,1)S(1)}, u32[]{:S(2)}, u32[]{:S(2)}) collective-permute-start(bf16[56,384]{1,0:T(8,128)(2,1)S(1)} %get-tuple-element.86), channel_id=1, source_target_pairs={{0,8},{1,9},{2,10},{3,11},{4,12},{5,13},{6,14},{7,15},{8,0},{9,1},... | collective-permute-start | bytes 129032 | tf_op jit(solution)/shard_map/ppermute | solution.py:47
  41.7 1.6 %shard_map.152.part_ref = f32[256,384]{1,0:T(8,128)S(1)} custom-call(s32[4,8]{1,0:T(4,128)S(1)} %bitcast.11, f32[256,384]{1,0:T(8,128)S(1)} %get-tuple-element.75.grad_ref, f32[7,7,384]{2,1,0:T(8,128)S(1)} %copy-done.3), custom_call_target="tpu_custom_call" | custom-call | bytes 861824 | tf_op jit(solution)/shard_map/pallas_call | solution.py:30
  43.4 0.0 collective-permute-done.14.core_ref
  43.4 0.0 collective-permute-done.15.cross_ref
  43.4 1.7 %shard_map.153 = bf16[256,384]{1,0:T(8,128)(2,1)} custom-call(s32[4,8]{1,0:T(4,128)S(1)} %bitcast.12, s32[1,1]{1,0:T(1,128)} %bitcast.place_ref, s32[1,1]{1,0:T(1,128)S(6)} %copy.15.counts_ref, f32[1,4]{1,0:T(1,128)S(1)} %copy-done.9, f32[256,384]{1,0:T(8,128)S(1)} %shard_map.152.part_ref, bf16[4,3,8,384]{3,2,1,0:T(8,128)(2,1)S(1)} %collective-permute-done.14.core_ref, ...), custom_call_target="tpu_custom_call" | custom-call | bytes 1010840 | tf_op jit(solution)/shard_map/pallas_call | solution.py:30
  45.1 0.0 collective-permute-done.13.new_ref
  45.1 0.0 collective-permute-done.8.got_ref
  45.1 0.7 %shard_map.151 = (f32[96,384]{1,0:T(8,128)}, f32[7,7,384]{2,1,0:T(8,128)}, f32[1,384]{1,0:T(1,128)}) custom-call(f32[96,384]{1,0:T(8,128)S(1)} %get-tuple-element.64.keep_ref, bf16[96,384]{1,0:T(8,128)(2,1)S(1)} %collective-permute-done.8.got_ref, f32[56,384]{1,0:T(8,128)S(1)} %get-tuple-element.85.state_ref, bf16[56,384]{1,0:T(8,128)(2,1)S(1)} %collective-permute-done.13.new_ref), custom_call_target="tpu_custom_call" | custom-call | bytes 574464 | tf_op jit(solution)/shard_map/pallas_call | solution.py:30
  (22 shorter events, 0.2 us)
Async XLA Ops:
  0.6 0.9 %copy-start.4 = (bf16[1,4,8,8,384]{4,3,2,1,0:T(8,128)(2,1)S(1)}, bf16[1,4,8,8,384]{4,3,2,1,0:T(8,128)(2,1)}, u32[]{:S(2)}) copy-start(bf16[1,4,8,8,384]{4,3,2,1,0:T(8,128)(2,1)} %param.11) | copy-start | bytes 589828
  1.6 3.9 %copy-start = (bf16[1536,384]{1,0:T(8,128)(2,1)S(1)}, bf16[1536,384]{1,0:T(8,128)(2,1)}, u32[]{:S(2)}) copy-start(bf16[1536,384]{1,0:T(8,128)(2,1)} %w_out_ref.3) | copy-start | bytes 3538948
  1.6 3.9 %copy-start.2 = (bf16[1,4,8,8,384]{4,3,2,1,0:T(8,128)(2,1)S(1)}, bf16[1,4,8,8,384]{4,3,2,1,0:T(8,128)(2,1)}, u32[]{:S(2)}) copy-start(bf16[1,4,8,8,384]{4,3,2,1,0:T(8,128)(2,1)} %param.12) | copy-start | bytes 589828
  1.6 3.9 %copy-start.3 = (f32[7,7,384]{2,1,0:T(8,128)S(1)}, f32[7,7,384]{2,1,0:T(8,128)}, u32[]{:S(2)}) copy-start(f32[7,7,384]{2,1,0:T(8,128)} %kern_ref.7) | copy-start | bytes 225796
  1.6 3.9 %copy-start.5 = (bf16[1,4,8,8,384]{4,3,2,1,0:T(8,128)(2,1)S(1)}, bf16[1,4,8,8,384]{4,3,2,1,0:T(8,128)(2,1)}, u32[]{:S(2)}) copy-start(bf16[1,4,8,8,384]{4,3,2,1,0:T(8,128)(2,1)} %param.11) | copy-start | bytes 589828
  1.6 3.9 %copy-start.6 = (s32[1,4,8]{2,1,0:T(4,128)S(1)}, s32[1,4,8]{2,1,0:T(4,128)}, u32[]{:S(2)}) copy-start(s32[1,4,8]{2,1,0:T(4,128)} %param.15) | copy-start | bytes 388
  1.6 3.9 %copy-start.7 = (f32[384]{0:T(512)S(1)}, f32[384]{0:T(512)}, u32[]{:S(2)}) copy-start(f32[384]{0:T(512)} %scale_ref.3) | copy-start | bytes 4612
  1.6 3.9 %copy-start.8 = (f32[1,384]{1,0:T(1,128)S(1)}, f32[1,384]{1,0:T(1,128)}, u32[]{:S(2)}) copy-start(f32[1,384]{1,0:T(1,128)} %cot_ref.3) | copy-start | bytes 4612
  1.6 3.9 %copy-start.9 = (f32[1,4]{1,0:T(1,128)S(1)}, f32[1,4]{1,0:T(1,128)}, u32[]{:S(2)}) copy-start(f32[1,4]{1,0:T(1,128)} %pool_ref.5) | copy-start | bytes 52
  1.7 5.9 %copy-start.1 = (bf16[384,1536]{1,0:T(8,128)(2,1)S(1)}, bf16[384,1536]{1,0:T(8,128)(2,1)}, u32[]{:S(2)}) copy-start(bf16[384,1536]{1,0:T(8,128)(2,1)} %w_in_ref.3) | copy-start | bytes 3538948
  1.7 5.9 %copy-start.10 = (f32[384]{0:T(512)S(1)}, f32[384]{0:T(512)}, u32[]{:S(2)}) copy-start(f32[384]{0:T(512)} %gain_ref.3) | copy-start | bytes 4612
  1.7 5.9 %collective-permute-start = (bf16[4,3,8,384]{3,2,1,0:T(8,128)(2,1)S(1)}, bf16[4,3,8,384]{3,2,1,0:T(8,128)(2,1)S(1)}, u32[]{:S(2)}, u32[]{:S(2)}) collective-permute-start(bf16[4,3,8,384]{3,2,1,0:T(8,128)(2,1)S(1)} %get-tuple-element.48), channel_id=1, source_target_pairs={{0,1},{1,0},{2,3},{3,2},{4,5},{5,4},{6,7},{7,6},{8,9},{9,8},{10,11... | collective-permute-start | bytes 221192 | tf_op jit(solution)/shard_map/ppermute | solution.py:47
  2.3 5.4 %collective-permute-start.1 = (bf16[4,3,8,384]{3,2,1,0:T(8,128)(2,1)S(1)}, bf16[4,3,8,384]{3,2,1,0:T(8,128)(2,1)S(1)}, u32[]{:S(2)}, u32[]{:S(2)}) collective-permute-start(bf16[4,3,8,384]{3,2,1,0:T(8,128)(2,1)S(1)} %get-tuple-element.49), channel_id=1, source_target_pairs={{0,16},{1,2},{2,1},{3,4},{4,3},{5,6},{6,5},{7,8},{8,7},{9,10},{10,... | collective-permute-start | bytes 221192 | tf_op jit(solution)/shard_map/ppermute | solution.py:60
  10.1 2.1 %collective-permute-start.2 = (bf16[768,384]{1,0:T(8,128)(2,1)S(1)}, bf16[768,384]{1,0:T(8,128)(2,1)S(1)}, u32[]{:S(2)}, u32[]{:S(2)}) collective-permute-start(bf16[768,384]{1,0:T(8,128)(2,1)S(1)} %get-tuple-element.53), channel_id=1, source_target_pairs={{0,1},{1,0},{2,3},{3,2},{4,5},{5,4},{6,7},{7,6},{8,9},{9,8},{10,11... | collective-permute-start | bytes 1769480 | tf_op jit(solution)/shard_map/ppermute | solution.py:47
  12.5 6.4 %collective-permute-start.3 = (bf16[192,384]{1,0:T(8,128)(2,1)S(1)}, bf16[192,384]{1,0:T(8,128)(2,1)S(1)}, u32[]{:S(2)}, u32[]{:S(2)}) collective-permute-start(bf16[192,384]{1,0:T(8,128)(2,1)S(1)} %get-tuple-element.55), channel_id=1, source_target_pairs={{0,2},{1,3},{2,0},{3,1},{4,6},{5,7},{6,4},{7,5},{8,10},{9,11},{10,... | collective-permute-start | bytes 442376 | tf_op jit(solution)/shard_map/ppermute | solution.py:47
  14.5 5.8 %collective-permute-start.4 = (bf16[192,384]{1,0:T(8,128)(2,1)S(1)}, bf16[192,384]{1,0:T(8,128)(2,1)S(1)}, u32[]{:S(2)}, u32[]{:S(2)}) collective-permute-start(bf16[192,384]{1,0:T(8,128)(2,1)S(1)} %get-tuple-element.57), channel_id=1, source_target_pairs={{0,4},{1,5},{2,6},{3,7},{4,0},{5,1},{6,2},{7,3},{8,12},{9,13},{10,... | collective-permute-start | bytes 442376 | tf_op jit(solution)/shard_map/ppermute | solution.py:47
  20.4 7.8 %collective-permute-start.5 = (bf16[96,384]{1,0:T(8,128)(2,1)S(1)}, bf16[96,384]{1,0:T(8,128)(2,1)S(1)}, u32[]{:S(2)}, u32[]{:S(2)}) collective-permute-start(bf16[96,384]{1,0:T(8,128)(2,1)S(1)} %get-tuple-element.59), channel_id=1, source_target_pairs={{0,4},{1,5},{2,6},{3,7},{4,0},{5,1},{6,2},{7,3},{8,12},{9,13},{10,... | collective-permute-start | bytes 221192 | tf_op jit(solution)/shard_map/ppermute | solution.py:47
  22.1 6.2 %collective-permute-start.6 = (bf16[96,384]{1,0:T(8,128)(2,1)S(1)}, bf16[96,384]{1,0:T(8,128)(2,1)S(1)}, u32[]{:S(2)}, u32[]{:S(2)}) collective-permute-start(bf16[96,384]{1,0:T(8,128)(2,1)S(1)} %get-tuple-element.61), channel_id=1, source_target_pairs={{0,2},{1,3},{2,0},{3,1},{4,6},{5,7},{6,4},{7,5},{8,10},{9,11},{10,... | collective-permute-start | bytes 221192 | tf_op jit(solution)/shard_map/ppermute | solution.py:47
  25.4 1.3 %collective-permute-start.9 = (bf16[56,384]{1,0:T(8,128)(2,1)S(1)}, bf16[56,384]{1,0:T(8,128)(2,1)S(1)}, u32[]{:S(2)}, u32[]{:S(2)}) collective-permute-start(bf16[56,384]{1,0:T(8,128)(2,1)S(1)} %get-tuple-element.78), channel_id=1, source_target_pairs={{0,1},{1,0},{2,3},{3,2},{4,5},{5,4},{6,7},{7,6},{8,9},{9,8},{10,11... | collective-permute-start | bytes 129032 | tf_op jit(solution)/shard_map/ppermute | solution.py:47
  26.7 4.3 %collective-permute-start.10 = (bf16[56,384]{1,0:T(8,128)(2,1)S(1)}, bf16[56,384]{1,0:T(8,128)(2,1)S(1)}, u32[]{:S(2)}, u32[]{:S(2)}) collective-permute-start(bf16[56,384]{1,0:T(8,128)(2,1)S(1)} %get-tuple-element.80), channel_id=1, source_target_pairs={{0,16},{16,0},{1,17},{17,1},{2,18},{18,2},{3,19},{19,3},{4,20},{20... | collective-permute-start | bytes 129032 | tf_op jit(solution)/shard_map/ppermute | solution.py:47
  28.3 8.6 %collective-permute-start.7 = (bf16[96,384]{1,0:T(8,128)(2,1)S(1)}, bf16[96,384]{1,0:T(8,128)(2,1)S(1)}, u32[]{:S(2)}, u32[]{:S(2)}) collective-permute-start(bf16[96,384]{1,0:T(8,128)(2,1)S(1)} %get-tuple-element.63), channel_id=1, source_target_pairs={{0,8},{1,9},{2,10},{3,11},{4,12},{5,13},{6,14},{7,15},{8,0},{9,1},... | collective-permute-start | bytes 221192 | tf_op jit(solution)/shard_map/ppermute | solution.py:47
  31.0 4.1 %collective-permute-start.11 = (bf16[56,384]{1,0:T(8,128)(2,1)S(1)}, bf16[56,384]{1,0:T(8,128)(2,1)S(1)}, u32[]{:S(2)}, u32[]{:S(2)}) collective-permute-start(bf16[56,384]{1,0:T(8,128)(2,1)S(1)} %get-tuple-element.82), channel_id=1, source_target_pairs={{0,2},{1,3},{2,0},{3,1},{4,6},{5,7},{6,4},{7,5},{8,10},{9,11},{10,... | collective-permute-start | bytes 129032 | tf_op jit(solution)/shard_map/ppermute | solution.py:47
  35.1 4.1 %collective-permute-start.12 = (bf16[56,384]{1,0:T(8,128)(2,1)S(1)}, bf16[56,384]{1,0:T(8,128)(2,1)S(1)}, u32[]{:S(2)}, u32[]{:S(2)}) collective-permute-start(bf16[56,384]{1,0:T(8,128)(2,1)S(1)} %get-tuple-element.84), channel_id=1, source_target_pairs={{0,4},{1,5},{2,6},{3,7},{4,0},{5,1},{6,2},{7,3},{8,12},{9,13},{10,... | collective-permute-start | bytes 129032 | tf_op jit(solution)/shard_map/ppermute | solution.py:47
  35.6 7.7 %collective-permute-start.14 = (bf16[4,3,8,384]{3,2,1,0:T(8,128)(2,1)S(1)}, bf16[4,3,8,384]{3,2,1,0:T(8,128)(2,1)S(1)}, u32[]{:S(2)}, u32[]{:S(2)}) collective-permute-start(bf16[4,3,8,384]{3,2,1,0:T(8,128)(2,1)S(1)} %get-tuple-element.88), channel_id=1, source_target_pairs={{0,1},{1,0},{2,3},{3,2},{4,5},{5,4},{6,7},{7,6},{8,9},{9,8},{10,11... | collective-permute-start | bytes 221192 | tf_op jit(solution)/shard_map/ppermute | solution.py:47
  35.6 7.7 %collective-permute-start.15 = (bf16[4,3,8,384]{3,2,1,0:T(8,128)(2,1)S(1)}, bf16[4,3,8,384]{3,2,1,0:T(8,128)(2,1)S(1)}, u32[]{:S(2)}, u32[]{:S(2)}) collective-permute-start(bf16[4,3,8,384]{3,2,1,0:T(8,128)(2,1)S(1)} %get-tuple-element.89), channel_id=1, source_target_pairs={{0,16},{1,2},{2,1},{3,4},{4,3},{5,6},{6,5},{7,8},{8,7},{9,10},{10,... | collective-permute-start | bytes 221192 | tf_op jit(solution)/shard_map/ppermute | solution.py:60
  36.9 8.2 %collective-permute-start.8 = (bf16[96,384]{1,0:T(8,128)(2,1)S(1)}, bf16[96,384]{1,0:T(8,128)(2,1)S(1)}, u32[]{:S(2)}, u32[]{:S(2)}) collective-permute-start(bf16[96,384]{1,0:T(8,128)(2,1)S(1)} %get-tuple-element.65), channel_id=1, source_target_pairs={{0,16},{16,0},{1,17},{17,1},{2,18},{18,2},{3,19},{19,3},{4,20},{20... | collective-permute-start | bytes 221192 | tf_op jit(solution)/shard_map/ppermute | solution.py:47
  39.2 5.9 %collective-permute-start.13 = (bf16[56,384]{1,0:T(8,128)(2,1)S(1)}, bf16[56,384]{1,0:T(8,128)(2,1)S(1)}, u32[]{:S(2)}, u32[]{:S(2)}) collective-permute-start(bf16[56,384]{1,0:T(8,128)(2,1)S(1)} %get-tuple-element.86), channel_id=1, source_target_pairs={{0,8},{1,9},{2,10},{3,11},{4,12},{5,13},{6,14},{7,15},{8,0},{9,1},... | collective-permute-start | bytes 129032 | tf_op jit(solution)/shard_map/ppermute | solution.py:47

commit v8 on v7

--- a/solution.py
+++ b/solution.py
@@ -17,7 +17,8 @@
 VMEM = pl.BlockSpec(memory_space=pltpu.VMEM)
 SMEM = pl.BlockSpec(memory_space=pltpu.SMEM)
 HBM = pl.BlockSpec(memory_space=pltpu.HBM)
-STATE = 56
+STATE = 64
+HALF = STATE // 2
 TAPS = 49
 CHUNK = 384
 BACK_CHUNK = 512
@@ -300,7 +301,7 @@
     emb_ref[...] = (own_sum_ref[...] + scale_ref[...].reshape(1, channels) * mixed) * 0.125
 
 
-def taps_kernel(pad_ref, edge_ref, grad_ref, emb_ref, state_ref, pack_ref, part_ref):
+def taps_kernel(place_ref, pad_ref, edge_ref, grad_ref, emb_ref, keep_ref, send_ref, part_ref, state_ref, pack_ref):
     parts, capacity = pad_ref.shape[0], pad_ref.shape[1]
     for lane in range(parts):
 
@@ -332,30 +333,31 @@
     state_ref[0:TAPS, :] = jnp.sum(part_ref[...], axis=1)
     state_ref[TAPS : TAPS + 1, :] = emb_ref[...]
     state_ref[TAPS + 1 :, :] = jnp.zeros((STATE - TAPS - 1, emb_ref.shape[1]), f32)
-    pack_ref[...] = packed(state_ref)
-
-
-def packed(state_ref):
+    pack_ref[...] = packed(state_ref, 0).astype(f32)
+    mine = lax.rem(place_ref[0, 0], 2) * HALF
+    keep_ref[...] = state_ref[pl.ds(pl.multiple_of(mine, 8), HALF), :]
+    send_ref[...] = pack_ref[pl.ds(pl.multiple_of(HALF - mine, 8), HALF), :].astype(bf16)
+
+
+def packed(state_ref, first):
     state = state_ref[...]
     high = state.astype(bf16)
     low = pltpu.roll(state - high.astype(f32), 1, 0)
-    row = lax.broadcasted_iota(jnp.int32, state.shape, 0)
+    row = lax.broadcasted_iota(jnp.int32, state.shape, 0) + first
     return jnp.where(row == TAPS + 1, low, high.astype(f32)).astype(bf16)
 
 
-def merged(state_ref, got, with_embedding=True):
-    total = packed(state_ref).astype(f32) + got.astype(f32)
-    row = lax.broadcasted_iota(jnp.int32, total.shape, 0)
+def state_kernel(with_embedding, symmetric, place_ref, state_ref, got_ref, new_ref, pack_ref):
+    first = lax.rem(place_ref[0, 0], 2) * HALF
+    own = packed(state_ref, first).astype(f32) if symmetric else state_ref[...]
+    total = own + got_ref[...].astype(f32)
+    row = lax.broadcasted_iota(jnp.int32, total.shape, 0) + first
     if with_embedding:
-        embedding = total + pltpu.roll(total, STATE - 1, 0)
+        embedding = total + pltpu.roll(total, HALF - 1, 0)
     else:
         embedding = state_ref[...]
-    return jnp.where(row < TAPS, total, jnp.where(row == TAPS, embedding, 0.0))
-
-
-def state_kernel(with_embedding, state_ref, got_ref, new_ref, pack_ref):
-    new_ref[...] = merged(state_ref, got_ref[...], with_embedding)
-    pack_ref[...] = packed(new_ref)
+    new_ref[...] = jnp.where(row < TAPS, total, jnp.where(row == TAPS, embedding, 0.0))
+    pack_ref[...] = packed(new_ref, first)
 
 
 def merge_kernel(splits, terms, place_ref, *refs):
@@ -380,12 +382,14 @@
     send_ref[...] = total.astype(bf16)
 
 
-def finish_kernel(keep_ref, got_ref, state_ref, new_ref, share_ref, taps_ref, emb_ref):
+def finish_kernel(place_ref, keep_ref, got_ref, state_ref, other_ref, share_ref, taps_ref, emb_ref, total_ref):
     share_ref[...] = keep_ref[...].astype(bf16).astype(f32) + got_ref[...].astype(f32)
-    total = merged(state_ref, new_ref[...])
+    mine = lax.rem(place_ref[0, 0], 2) * HALF
+    total_ref[pl.ds(pl.multiple_of(mine, 8), HALF), :] = state_ref[...]
+    total_ref[pl.ds(pl.multiple_of(HALF - mine, 8), HALF), :] = other_ref[...]
     for row in range(7):
-        taps_ref[row] = total[row * 7 : row * 7 + 7, :]
-    emb_ref[...] = total[TAPS : TAPS + 1, :]
+        taps_ref[row] = total_ref[row * 7 : row * 7 + 7, :]
+    emb_ref[...] = total_ref[TAPS : TAPS + 1, :]
 
 
 def middle_kernel(adj_ref, grad_ref, kern_ref, out_ref, pad_ref):
@@ -541,25 +545,25 @@
         if bit < groups:
             share, send = call(pair_kernel, [struct(share.shape), struct(send.shape, bf16)], [VMEM] * 2, [share, got])
 
+    half_shapes = [struct((HALF, channels)), struct((HALF, channels), bf16)]
     state, pack = call(
-        taps_kernel, [struct((STATE, channels)), struct((STATE, channels), bf16)],
-        [VMEM] * 4, [pad, edge, grad, emb],
-        scratch=[pltpu.VMEM((TAPS, 8, channels), f32)],
+        taps_kernel, half_shapes, [SMEM] + [VMEM] * 4, [place, pad, edge, grad, emb],
+        scratch=[pltpu.VMEM((TAPS, 8, channels), f32)] + [pltpu.VMEM((STATE, channels), f32)] * 2,
     )
     steps = [("space", 1)] + [("dp", 1 << n) for n in range(groups.bit_length() - 1)]
     steps += [("space", 1 << n) for n in range(1, stages)]
     for axis, bit in steps:
         new = swapped(pack, axis, bit)
-        if (axis, bit) != steps[-1]:
-            state, pack = call(
-                functools.partial(state_kernel, axis == "space"),
-                [struct((STATE, channels)), struct((STATE, channels), bf16)],
-                [VMEM] * 2, [state, new],
-            )
+        state, pack = call(
+            functools.partial(state_kernel, axis == "space", (axis, bit) != steps[0]), half_shapes,
+            [SMEM] + [VMEM] * 2, [place, state, new],
+        )
+    other = swapped(state, "space", 1)
 
     share, tap_grad, embedding = call(
         finish_kernel, [struct((rows, channels)), struct(kernel.shape), struct((1, channels))],
-        [VMEM] * 4, [share, got, state, new],
+        [SMEM] + [VMEM] * 4, [place, share, got, state, other],
+        scratch=[pltpu.VMEM((STATE, channels), f32)],
     )
 
     part = call(

time: 46 us -> 48.8 us (1.061)
  waiting for transfers between devices: 11.4 us -> 13.3 us
  Pallas kernels: 12.1 us -> 12.9 us
    ppermute x14 -> x15, waiting for transfers between devices: 11.4 us -> 13.3 us  [swapped(): lax.ppermute(value, axis, [(source, source ^ bit) for source in range(cou...]
    pallas_call x16 -> x17, Pallas kernels: 12.1 us -> 12.9 us  [call(): pl.pallas_call(body, out_shape=out_shape, in_specs=in_specs, out_specs=ou...]
    ppermute x14 -> x15, starting transfers between devices: 16 us -> 16.3 us  [swapped(): lax.ppermute(value, axis, [(source, source ^ bit) for source in range(cou...]
  transfers between devices with their start and end apart: 16 -> 17, of which waited for: 6 -> 7; matrix products, arithmetic and copies ran while one was open for 0% -> 0% of each run, Pallas kernels for 19% -> 19%
where the time goes in v8:
time: 48.8 us; the launch traced here: 48.6 us
  starting transfers between devices  19.9 us (41%)
  waiting for transfers between devices  13.3 us (27%)
  Pallas kernels  12.9 us (26%)
  between operations  1.55 us (3%)
  local copies, waits for them, and re-layouts  0.96 us (2%)
    ppermute x15, starting transfers between devices, swapped(): lax.ppermute(value, axis, [(source, source ^ bit) for source in range(cou...  16.3 us
    ppermute x15, waiting for transfers between devices, swapped(): lax.ppermute(value, axis, [(source, source ^ bit) for source in range(cou...  13.3 us
    pallas_call x17, Pallas kernels, call(): pl.pallas_call(body, out_shape=out_shape, in_specs=in_specs, out_specs=ou...  12.9 us
    ppermute x2, starting transfers between devices, crossed(): return lax.ppermute(value, ('dp', 'space'), targets)  3.62 us
  transfers between devices with their start and end apart: 17, of which 7 were waited for; matrix products, arithmetic and copies ran while one was open for 0% of the time, Pallas kernels for 19%

profile of v8, /device:TPU:0, one launch (start us, length us, event | category | flops | bytes accessed | tf_op | source)
XLA Modules:
  0.0 48.6 jit_solution(5258676163134525527)
XLA Ops:
  0.6 0.9 %copy-done.4 = bf16[1,4,8,8,384]{4,3,2,1,0:T(8,128)(2,1)S(1)} copy-done((bf16[1,4,8,8,384]{4,3,2,1,0:T(8,128)(2,1)S(1)}, bf16[1,4,8,8,384]{4,3,2,1,0:T(8,128)(2,1)}, u32[]{:S(2)}) %copy-start.4) | copy-done | bytes 196632
  1.6 0.1 shard_map.138
  1.7 0.0 copy-start.1
  1.7 0.0 copy-start.10
  1.7 0.6 %collective-permute-start = (bf16[4,3,8,384]{3,2,1,0:T(8,128)(2,1)S(1)}, bf16[4,3,8,384]{3,2,1,0:T(8,128)(2,1)S(1)}, u32[]{:S(2)}, u32[]{:S(2)}) collective-permute-start(bf16[4,3,8,384]{3,2,1,0:T(8,128)(2,1)S(1)} %get-tuple-element.49), channel_id=1, source_target_pairs={{0,1},{1,0},{2,3},{3,2},{4,5},{5,4},{6,7},{7,6},{8,9},{9,8},{10,11... | collective-permute-start | bytes 221192 | tf_op jit(solution)/shard_map/ppermute | solution.py:48
  2.3 2.6 %collective-permute-start.1 = (bf16[4,3,8,384]{3,2,1,0:T(8,128)(2,1)S(1)}, bf16[4,3,8,384]{3,2,1,0:T(8,128)(2,1)S(1)}, u32[]{:S(2)}, u32[]{:S(2)}) collective-permute-start(bf16[4,3,8,384]{3,2,1,0:T(8,128)(2,1)S(1)} %get-tuple-element.50), channel_id=1, source_target_pairs={{0,16},{1,2},{2,1},{3,4},{4,3},{5,6},{6,5},{7,8},{8,7},{9,10},{10,... | collective-permute-start | bytes 221192 | tf_op jit(solution)/shard_map/ppermute | solution.py:61
  5.6 2.0 %shard_map.139 = (f32[3,4,8,24,128]{4,3,2,1,0:T(8,128)S(1)}, f32[256,384]{1,0:T(8,128)S(1)}, bf16[256,512]{1,0:T(8,128)(2,1)S(1)}, f32[256,1536]{1,0:T(8,128)S(1)}, f32[1,384]{1,0:T(1,128)S(1)}) custom-call(s32[4,8]{1,0:T(4,128)S(1)} %bitcast.9, s32[1,1]{1,0:T(1,128)S(6)} %copy.15.counts_ref, f32[1,4]{1,0:T(1,128)S(1)} %copy-done.9, f32[1,384]{1,0:T(1,128)S(1)} %copy-done.8, ...), custom_call_target="tpu_custom_call" | custom-call | flops 301989888 | bytes 5060756 | tf_op jit(solution)/shard_map/pallas_call | solution.py:31
  7.6 0.0 collective-permute-done.core_ref
  7.6 0.0 collective-permute-done.1.cross_ref
  7.6 2.5 %shard_map.140 = (f32[3,4,6,24,128]{4,3,2,1,0:T(8,128)S(1)}, f32[256,384]{1,0:T(8,128)S(1)}, f32[256,1]{1,0:T(8,128)S(1)}, f32[256,1536]{1,0:T(8,128)S(1)}, f32[...) custom-call(s32[4,8]{1,0:T(4,128)S(1)} %bitcast.10, ...), custom_call_target="tpu_custom_call" | custom-call | flops 603979776 | bytes 9040004 | tf_op jit(solution)/shard_map/pallas_call | solution.py:31
  10.1 0.2 collective-permute-start.2
  10.3 1.9 %collective-permute-done.2.refs_1_ = bf16[768,384]{1,0:T(8,128)(2,1)S(1)} collective-permute-done((bf16[768,384]{1,0:T(8,128)(2,1)S(1)}, bf16[768,384]{1,0:T(8,128)(2,1)S(1)}, u32[]{:S(2)}, u32[]{:S(2)}) %collective-permute-start.2) | collective-permute-done | bytes 589856 | tf_op jit(solution)/shard_map/ppermute | solution.py:48
  12.2 0.3 shard_map.141
  12.5 2.0 %collective-permute-start.3 = (bf16[192,384]{1,0:T(8,128)(2,1)S(1)}, bf16[192,384]{1,0:T(8,128)(2,1)S(1)}, u32[]{:S(2)}, u32[]{:S(2)}) collective-permute-start(bf16[192,384]{1,0:T(8,128)(2,1)S(1)} %get-tuple-element.56), channel_id=1, source_target_pairs={{0,2},{1,3},{2,0},{3,1},{4,6},{5,7},{6,4},{7,5},{8,10},{9,11},{10,... | collective-permute-start | bytes 442376 | tf_op jit(solution)/shard_map/ppermute | solution.py:48
  14.5 1.6 %collective-permute-start.4 = (bf16[192,384]{1,0:T(8,128)(2,1)S(1)}, bf16[192,384]{1,0:T(8,128)(2,1)S(1)}, u32[]{:S(2)}, u32[]{:S(2)}) collective-permute-start(bf16[192,384]{1,0:T(8,128)(2,1)S(1)} %get-tuple-element.58), channel_id=1, source_target_pairs={{0,4},{1,5},{2,6},{3,7},{4,0},{5,1},{6,2},{7,3},{8,12},{9,13},{10,... | collective-permute-start | bytes 442376 | tf_op jit(solution)/shard_map/ppermute | solution.py:48
  16.0 2.8 %collective-permute-done.3.refs_1_ = bf16[192,384]{1,0:T(8,128)(2,1)S(1)} collective-permute-done((bf16[192,384]{1,0:T(8,128)(2,1)S(1)}, bf16[192,384]{1,0:T(8,128)(2,1)S(1)}, u32[]{:S(2)}, u32[]{:S(2)}) %collective-permute-start.3) | collective-permute-done | bytes 147488 | tf_op jit(solution)/shard_map/ppermute | solution.py:48
  18.8 1.5 %collective-permute-done.4.refs_3_ = bf16[192,384]{1,0:T(8,128)(2,1)S(1)} collective-permute-done((bf16[192,384]{1,0:T(8,128)(2,1)S(1)}, bf16[192,384]{1,0:T(8,128)(2,1)S(1)}, u32[]{:S(2)}, u32[]{:S(2)}) %collective-permute-start.4) | collective-permute-done | bytes 147488 | tf_op jit(solution)/shard_map/ppermute | solution.py:48
  20.3 0.1 shard_map.142
  20.4 1.6 %collective-permute-start.5 = (bf16[96,384]{1,0:T(8,128)(2,1)S(1)}, bf16[96,384]{1,0:T(8,128)(2,1)S(1)}, u32[]{:S(2)}, u32[]{:S(2)}) collective-permute-start(bf16[96,384]{1,0:T(8,128)(2,1)S(1)} %get-tuple-element.60), channel_id=1, source_target_pairs={{0,4},{1,5},{2,6},{3,7},{4,0},{5,1},{6,2},{7,3},{8,12},{9,13},{10,... | collective-permute-start | bytes 221192 | tf_op jit(solution)/shard_map/ppermute | solution.py:48
  22.1 0.4 collective-permute-start.6
  22.5 1.5 %shard_map.145 = (f32[256,384]{1,0:T(8,128)S(1)}, bf16[4,3,8,384]{3,2,1,0:T(8,128)(2,1)S(1)}, bf16[4,3,8,384]{3,2,1,0:T(8,128)(2,1)S(1)}, f32[1,384]{1,0:T(1,128)S(1)}) custom-call(s32[1,1]{1,0:T(1,128)} %bitcast.place_ref, s32[1,1]{1,0:T(1,128)S(6)} %copy.15.counts_ref, f32[1,4]{1,0:T(1,128)S(1)} %copy-done.9, f32[256,1536]{1,0:T(8,128)S(1)} %get-tuple-element.69.pre_ref, ...), custom_call_target="tpu_custom_call" | custom-call | flops 301989888 | bytes 8805400 | tf_op jit(solution)/shard_map/pallas_call | solution.py:31
  24.0 1.4 %shard_map.146 = (f32[32,384]{1,0:T(8,128)S(1)}, bf16[32,384]{1,0:T(8,128)(2,1)S(1)}) custom-call(s32[1,1]{1,0:T(1,128)} %bitcast.place_ref, f32[3,4,8,24,128]{4,3,2,1,0:T(8,128)S(1)} %get-tuple-element.67.pad_ref, f32[3,4,6,24,128]{4,3,2,1,0:T(8,128)S(1)} %get-tuple-element.68.edge_ref, f32[256,384]{1,0:T(8,128)S(1)} %get-tuple-element.76.grad_ref, ...), custom_call_target="tpu_custom_call" | custom-call | bytes 2532868 | tf_op jit(solution)/shard_map/pallas_call | solution.py:31
  25.4 0.1 collective-permute-start.9
  25.5 1.2 %collective-permute-done.9.got_ref = bf16[32,384]{1,0:T(8,128)(2,1)S(1)} collective-permute-done((bf16[32,384]{1,0:T(8,128)(2,1)S(1)}, bf16[32,384]{1,0:T(8,128)(2,1)S(1)}, u32[]{:S(2)}, u32[]{:S(2)}) %collective-permute-start.9) | collective-permute-done | bytes 24608 | tf_op jit(solution)/shard_map/ppermute | solution.py:48
  26.7 1.6 %collective-permute-start.10 = (bf16[32,384]{1,0:T(8,128)(2,1)S(1)}, bf16[32,384]{1,0:T(8,128)(2,1)S(1)}, u32[]{:S(2)}, u32[]{:S(2)}) collective-permute-start(bf16[32,384]{1,0:T(8,128)(2,1)S(1)} %get-tuple-element.81), channel_id=1, source_target_pairs={{0,16},{16,0},{1,17},{17,1},{2,18},{18,2},{3,19},{19,3},{4,20},{20... | collective-permute-start | bytes 73736 | tf_op jit(solution)/shard_map/ppermute | solution.py:48
  28.3 0.0 collective-permute-done.5.refs_1_
  28.3 0.0 collective-permute-done.6.refs_3_
  28.4 2.7 %collective-permute-start.7 = (bf16[96,384]{1,0:T(8,128)(2,1)S(1)}, bf16[96,384]{1,0:T(8,128)(2,1)S(1)}, u32[]{:S(2)}, u32[]{:S(2)}) collective-permute-start(bf16[96,384]{1,0:T(8,128)(2,1)S(1)} %get-tuple-element.64), channel_id=1, source_target_pairs={{0,8},{1,9},{2,10},{3,11},{4,12},{5,13},{6,14},{7,15},{8,0},{9,1},... | collective-permute-start | bytes 221192 | tf_op jit(solution)/shard_map/ppermute | solution.py:48
  31.0 0.0 collective-permute-done.10.got_ref
  31.0 1.3 %collective-permute-start.11 = (bf16[32,384]{1,0:T(8,128)(2,1)S(1)}, bf16[32,384]{1,0:T(8,128)(2,1)S(1)}, u32[]{:S(2)}, u32[]{:S(2)}) collective-permute-start(bf16[32,384]{1,0:T(8,128)(2,1)S(1)} %get-tuple-element.83), channel_id=1, source_target_pairs={{0,2},{1,3},{2,0},{3,1},{4,6},{5,7},{6,4},{7,5},{8,10},{9,11},{10,... | collective-permute-start | bytes 73736 | tf_op jit(solution)/shard_map/ppermute | solution.py:48
  32.4 2.6 %collective-permute-done.11.got_ref = bf16[32,384]{1,0:T(8,128)(2,1)S(1)} collective-permute-done((bf16[32,384]{1,0:T(8,128)(2,1)S(1)}, bf16[32,384]{1,0:T(8,128)(2,1)S(1)}, u32[]{:S(2)}, u32[]{:S(2)}) %collective-permute-start.11) | collective-permute-done | bytes 24608 | tf_op jit(solution)/shard_map/ppermute | solution.py:48
  35.0 0.5 %collective-permute-start.12 = (bf16[32,384]{1,0:T(8,128)(2,1)S(1)}, bf16[32,384]{1,0:T(8,128)(2,1)S(1)}, u32[]{:S(2)}, u32[]{:S(2)}) collective-permute-start(bf16[32,384]{1,0:T(8,128)(2,1)S(1)} %get-tuple-element.85), channel_id=1, source_target_pairs={{0,4},{1,5},{2,6},{3,7},{4,0},{5,1},{6,2},{7,3},{8,12},{9,13},{10,... | collective-permute-start | bytes 73736 | tf_op jit(solution)/shard_map/ppermute | solution.py:48
  35.5 0.0 collective-permute-start.15
  35.5 1.1 %collective-permute-start.16 = (bf16[4,3,8,384]{3,2,1,0:T(8,128)(2,1)S(1)}, bf16[4,3,8,384]{3,2,1,0:T(8,128)(2,1)S(1)}, u32[]{:S(2)}, u32[]{:S(2)}) collective-permute-start(bf16[4,3,8,384]{3,2,1,0:T(8,128)(2,1)S(1)} %get-tuple-element.91), channel_id=1, source_target_pairs={{0,16},{1,2},{2,1},{3,4},{4,3},{5,6},{6,5},{7,8},{8,7},{9,10},{10,... | collective-permute-start | bytes 221192 | tf_op jit(solution)/shard_map/ppermute | solution.py:61
  36.6 2.3 %collective-permute-done.12.got_ref = bf16[32,384]{1,0:T(8,128)(2,1)S(1)} collective-permute-done((bf16[32,384]{1,0:T(8,128)(2,1)S(1)}, bf16[32,384]{1,0:T(8,128)(2,1)S(1)}, u32[]{:S(2)}, u32[]{:S(2)}) %collective-permute-start.12) | collective-permute-done | bytes 24608 | tf_op jit(solution)/shard_map/ppermute | solution.py:48
  38.9 2.3 %collective-permute-start.13 = (bf16[32,384]{1,0:T(8,128)(2,1)S(1)}, bf16[32,384]{1,0:T(8,128)(2,1)S(1)}, u32[]{:S(2)}, u32[]{:S(2)}) collective-permute-start(bf16[32,384]{1,0:T(8,128)(2,1)S(1)} %get-tuple-element.87), channel_id=1, source_target_pairs={{0,8},{1,9},{2,10},{3,11},{4,12},{5,13},{6,14},{7,15},{8,0},{9,1},... | collective-permute-start | bytes 73736 | tf_op jit(solution)/shard_map/ppermute | solution.py:48
  41.2 0.0 collective-permute-done.7.refs_1_
  41.2 1.5 %collective-permute-start.8 = (bf16[96,384]{1,0:T(8,128)(2,1)S(1)}, bf16[96,384]{1,0:T(8,128)(2,1)S(1)}, u32[]{:S(2)}, u32[]{:S(2)}) collective-permute-start(bf16[96,384]{1,0:T(8,128)(2,1)S(1)} %get-tuple-element.66), channel_id=1, source_target_pairs={{0,16},{16,0},{1,17},{17,1},{2,18},{18,2},{3,19},{19,3},{4,20},{20... | collective-permute-start | bytes 221192 | tf_op jit(solution)/shard_map/ppermute | solution.py:48
  42.8 1.1 %collective-permute-done.13.got_ref = bf16[32,384]{1,0:T(8,128)(2,1)S(1)} collective-permute-done((bf16[32,384]{1,0:T(8,128)(2,1)S(1)}, bf16[32,384]{1,0:T(8,128)(2,1)S(1)}, u32[]{:S(2)}, u32[]{:S(2)}) %collective-permute-start.13) | collective-permute-done | bytes 24608 | tf_op jit(solution)/shard_map/ppermute | solution.py:48
  43.9 0.6 %shard_map.151 = (f32[32,384]{1,0:T(8,128)S(1)}, bf16[32,384]{1,0:T(8,128)(2,1)}) custom-call(s32[1,1]{1,0:T(1,128)} %bitcast.place_ref, f32[32,384]{1,0:T(8,128)S(1)} %get-tuple-element.86.state_ref, bf16[32,384]{1,0:T(8,128)(2,1)S(1)} %collective-permute-done.13.got_ref), custom_call_target="tpu_custom_call" | custom-call | bytes 147460 | tf_op jit(solution)/shard_map/pallas_call | solution.py:31
  44.5 0.0 collective-permute-start.14
  44.5 1.6 %shard_map.153.part_ref = f32[256,384]{1,0:T(8,128)S(1)} custom-call(s32[4,8]{1,0:T(4,128)S(1)} %bitcast.11, f32[256,384]{1,0:T(8,128)S(1)} %get-tuple-element.76.grad_ref, f32[7,7,384]{2,1,0:T(8,128)S(1)} %copy-done.3), custom_call_target="tpu_custom_call" | custom-call | bytes 861824 | tf_op jit(solution)/shard_map/pallas_call | solution.py:31
  46.2 0.0 collective-permute-done.15.core_ref
  46.2 0.0 collective-permute-done.16.cross_ref
  46.2 1.7 %shard_map.154 = bf16[256,384]{1,0:T(8,128)(2,1)} custom-call(s32[4,8]{1,0:T(4,128)S(1)} %bitcast.12, s32[1,1]{1,0:T(1,128)} %bitcast.place_ref, s32[1,1]{1,0:T(1,128)S(6)} %copy.15.counts_ref, f32[1,4]{1,0:T(1,128)S(1)} %copy-done.9, f32[256,384]{1,0:T(8,128)S(1)} %shard_map.153.part_ref, bf16[4,3,8,384]{3,2,1,0:T(8,128)(2,1)S(1)} %collective-permute-done.15.core_ref, ...), custom_call_target="tpu_custom_call" | custom-call | bytes 1010840 | tf_op jit(solution)/shard_map/pallas_call | solution.py:31
  47.9 0.0 collective-permute-done.14.other_ref
  47.9 0.0 collective-permute-done.8.got_ref
  47.9 0.7 %shard_map.152 = (f32[96,384]{1,0:T(8,128)}, f32[7,7,384]{2,1,0:T(8,128)}, f32[1,384]{1,0:T(1,128)}) custom-call(s32[1,1]{1,0:T(1,128)} %bitcast.place_ref, f32[96,384]{1,0:T(8,128)S(1)} %get-tuple-element.65.keep_ref, bf16[96,384]{1,0:T(8,128)(2,1)S(1)} %collective-permute-done.8.got_ref, f32[32,384]{1,0:T(8,128)S(1)} %get-tuple-element.88.state_ref, ...), custom_call_target="tpu_custom_call" | custom-call | bytes 543748 | tf_op jit(solution)/shard_map/pallas_call | solution.py:31
  (25 shorter events, 0.3 us)
Async XLA Ops:
  0.6 0.9 %copy-start.4 = (bf16[1,4,8,8,384]{4,3,2,1,0:T(8,128)(2,1)S(1)}, bf16[1,4,8,8,384]{4,3,2,1,0:T(8,128)(2,1)}, u32[]{:S(2)}) copy-start(bf16[1,4,8,8,384]{4,3,2,1,0:T(8,128)(2,1)} %param.11) | copy-start | bytes 589828
  1.6 3.9 %copy-start = (bf16[1536,384]{1,0:T(8,128)(2,1)S(1)}, bf16[1536,384]{1,0:T(8,128)(2,1)}, u32[]{:S(2)}) copy-start(bf16[1536,384]{1,0:T(8,128)(2,1)} %w_out_ref.3) | copy-start | bytes 3538948
  1.6 3.9 %copy-start.2 = (bf16[1,4,8,8,384]{4,3,2,1,0:T(8,128)(2,1)S(1)}, bf16[1,4,8,8,384]{4,3,2,1,0:T(8,128)(2,1)}, u32[]{:S(2)}) copy-start(bf16[1,4,8,8,384]{4,3,2,1,0:T(8,128)(2,1)} %param.12) | copy-start | bytes 589828
  1.6 3.9 %copy-start.3 = (f32[7,7,384]{2,1,0:T(8,128)S(1)}, f32[7,7,384]{2,1,0:T(8,128)}, u32[]{:S(2)}) copy-start(f32[7,7,384]{2,1,0:T(8,128)} %kern_ref.7) | copy-start | bytes 225796
  1.6 3.9 %copy-start.5 = (bf16[1,4,8,8,384]{4,3,2,1,0:T(8,128)(2,1)S(1)}, bf16[1,4,8,8,384]{4,3,2,1,0:T(8,128)(2,1)}, u32[]{:S(2)}) copy-start(bf16[1,4,8,8,384]{4,3,2,1,0:T(8,128)(2,1)} %param.11) | copy-start | bytes 589828
  1.6 3.9 %copy-start.6 = (s32[1,4,8]{2,1,0:T(4,128)S(1)}, s32[1,4,8]{2,1,0:T(4,128)}, u32[]{:S(2)}) copy-start(s32[1,4,8]{2,1,0:T(4,128)} %param.15) | copy-start | bytes 388
  1.6 3.9 %copy-start.7 = (f32[384]{0:T(512)S(1)}, f32[384]{0:T(512)}, u32[]{:S(2)}) copy-start(f32[384]{0:T(512)} %scale_ref.3) | copy-start | bytes 4612
  1.6 3.9 %copy-start.8 = (f32[1,384]{1,0:T(1,128)S(1)}, f32[1,384]{1,0:T(1,128)}, u32[]{:S(2)}) copy-start(f32[1,384]{1,0:T(1,128)} %cot_ref.3) | copy-start | bytes 4612
  1.6 3.9 %copy-start.9 = (f32[1,4]{1,0:T(1,128)S(1)}, f32[1,4]{1,0:T(1,128)}, u32[]{:S(2)}) copy-start(f32[1,4]{1,0:T(1,128)} %pool_ref.5) | copy-start | bytes 52
  1.7 5.9 %copy-start.1 = (bf16[384,1536]{1,0:T(8,128)(2,1)S(1)}, bf16[384,1536]{1,0:T(8,128)(2,1)}, u32[]{:S(2)}) copy-start(bf16[384,1536]{1,0:T(8,128)(2,1)} %w_in_ref.3) | copy-start | bytes 3538948
  1.7 5.9 %copy-start.10 = (f32[384]{0:T(512)S(1)}, f32[384]{0:T(512)}, u32[]{:S(2)}) copy-start(f32[384]{0:T(512)} %gain_ref.3) | copy-start | bytes 4612
  1.7 5.9 %collective-permute-start = (bf16[4,3,8,384]{3,2,1,0:T(8,128)(2,1)S(1)}, bf16[4,3,8,384]{3,2,1,0:T(8,128)(2,1)S(1)}, u32[]{:S(2)}, u32[]{:S(2)}) collective-permute-start(bf16[4,3,8,384]{3,2,1,0:T(8,128)(2,1)S(1)} %get-tuple-element.49), channel_id=1, source_target_pairs={{0,1},{1,0},{2,3},{3,2},{4,5},{5,4},{6,7},{7,6},{8,9},{9,8},{10,11... | collective-permute-start | bytes 221192 | tf_op jit(solution)/shard_map/ppermute | solution.py:48
  2.3 5.4 %collective-permute-start.1 = (bf16[4,3,8,384]{3,2,1,0:T(8,128)(2,1)S(1)}, bf16[4,3,8,384]{3,2,1,0:T(8,128)(2,1)S(1)}, u32[]{:S(2)}, u32[]{:S(2)}) collective-permute-start(bf16[4,3,8,384]{3,2,1,0:T(8,128)(2,1)S(1)} %get-tuple-element.50), channel_id=1, source_target_pairs={{0,16},{1,2},{2,1},{3,4},{4,3},{5,6},{6,5},{7,8},{8,7},{9,10},{10,... | collective-permute-start | bytes 221192 | tf_op jit(solution)/shard_map/ppermute | solution.py:61
  10.1 2.1 %collective-permute-start.2 = (bf16[768,384]{1,0:T(8,128)(2,1)S(1)}, bf16[768,384]{1,0:T(8,128)(2,1)S(1)}, u32[]{:S(2)}, u32[]{:S(2)}) collective-permute-start(bf16[768,384]{1,0:T(8,128)(2,1)S(1)} %get-tuple-element.54), channel_id=1, source_target_pairs={{0,1},{1,0},{2,3},{3,2},{4,5},{5,4},{6,7},{7,6},{8,9},{9,8},{10,11... | collective-permute-start | bytes 1769480 | tf_op jit(solution)/shard_map/ppermute | solution.py:48
  12.5 6.4 %collective-permute-start.3 = (bf16[192,384]{1,0:T(8,128)(2,1)S(1)}, bf16[192,384]{1,0:T(8,128)(2,1)S(1)}, u32[]{:S(2)}, u32[]{:S(2)}) collective-permute-start(bf16[192,384]{1,0:T(8,128)(2,1)S(1)} %get-tuple-element.56), channel_id=1, source_target_pairs={{0,2},{1,3},{2,0},{3,1},{4,6},{5,7},{6,4},{7,5},{8,10},{9,11},{10,... | collective-permute-start | bytes 442376 | tf_op jit(solution)/shard_map/ppermute | solution.py:48
  14.5 5.8 %collective-permute-start.4 = (bf16[192,384]{1,0:T(8,128)(2,1)S(1)}, bf16[192,384]{1,0:T(8,128)(2,1)S(1)}, u32[]{:S(2)}, u32[]{:S(2)}) collective-permute-start(bf16[192,384]{1,0:T(8,128)(2,1)S(1)} %get-tuple-element.58), channel_id=1, source_target_pairs={{0,4},{1,5},{2,6},{3,7},{4,0},{5,1},{6,2},{7,3},{8,12},{9,13},{10,... | collective-permute-start | bytes 442376 | tf_op jit(solution)/shard_map/ppermute | solution.py:48
  20.4 7.9 %collective-permute-start.5 = (bf16[96,384]{1,0:T(8,128)(2,1)S(1)}, bf16[96,384]{1,0:T(8,128)(2,1)S(1)}, u32[]{:S(2)}, u32[]{:S(2)}) collective-permute-start(bf16[96,384]{1,0:T(8,128)(2,1)S(1)} %get-tuple-element.60), channel_id=1, source_target_pairs={{0,4},{1,5},{2,6},{3,7},{4,0},{5,1},{6,2},{7,3},{8,12},{9,13},{10,... | collective-permute-start | bytes 221192 | tf_op jit(solution)/shard_map/ppermute | solution.py:48
  22.1 6.2 %collective-permute-start.6 = (bf16[96,384]{1,0:T(8,128)(2,1)S(1)}, bf16[96,384]{1,0:T(8,128)(2,1)S(1)}, u32[]{:S(2)}, u32[]{:S(2)}) collective-permute-start(bf16[96,384]{1,0:T(8,128)(2,1)S(1)} %get-tuple-element.62), channel_id=1, source_target_pairs={{0,2},{1,3},{2,0},{3,1},{4,6},{5,7},{6,4},{7,5},{8,10},{9,11},{10,... | collective-permute-start | bytes 221192 | tf_op jit(solution)/shard_map/ppermute | solution.py:48
  25.4 1.3 %collective-permute-start.9 = (bf16[32,384]{1,0:T(8,128)(2,1)S(1)}, bf16[32,384]{1,0:T(8,128)(2,1)S(1)}, u32[]{:S(2)}, u32[]{:S(2)}) collective-permute-start(bf16[32,384]{1,0:T(8,128)(2,1)S(1)} %get-tuple-element.79), channel_id=1, source_target_pairs={{0,1},{1,0},{2,3},{3,2},{4,5},{5,4},{6,7},{7,6},{8,9},{9,8},{10,11... | collective-permute-start | bytes 73736 | tf_op jit(solution)/shard_map/ppermute | solution.py:48
  26.7 4.3 %collective-permute-start.10 = (bf16[32,384]{1,0:T(8,128)(2,1)S(1)}, bf16[32,384]{1,0:T(8,128)(2,1)S(1)}, u32[]{:S(2)}, u32[]{:S(2)}) collective-permute-start(bf16[32,384]{1,0:T(8,128)(2,1)S(1)} %get-tuple-element.81), channel_id=1, source_target_pairs={{0,16},{16,0},{1,17},{17,1},{2,18},{18,2},{3,19},{19,3},{4,20},{20... | collective-permute-start | bytes 73736 | tf_op jit(solution)/shard_map/ppermute | solution.py:48
  28.4 12.9 %collective-permute-start.7 = (bf16[96,384]{1,0:T(8,128)(2,1)S(1)}, bf16[96,384]{1,0:T(8,128)(2,1)S(1)}, u32[]{:S(2)}, u32[]{:S(2)}) collective-permute-start(bf16[96,384]{1,0:T(8,128)(2,1)S(1)} %get-tuple-element.64), channel_id=1, source_target_pairs={{0,8},{1,9},{2,10},{3,11},{4,12},{5,13},{6,14},{7,15},{8,0},{9,1},... | collective-permute-start | bytes 221192 | tf_op jit(solution)/shard_map/ppermute | solution.py:48
  31.0 3.9 %collective-permute-start.11 = (bf16[32,384]{1,0:T(8,128)(2,1)S(1)}, bf16[32,384]{1,0:T(8,128)(2,1)S(1)}, u32[]{:S(2)}, u32[]{:S(2)}) collective-permute-start(bf16[32,384]{1,0:T(8,128)(2,1)S(1)} %get-tuple-element.83), channel_id=1, source_target_pairs={{0,2},{1,3},{2,0},{3,1},{4,6},{5,7},{6,4},{7,5},{8,10},{9,11},{10,... | collective-permute-start | bytes 73736 | tf_op jit(solution)/shard_map/ppermute | solution.py:48
  35.0 3.9 %collective-permute-start.12 = (bf16[32,384]{1,0:T(8,128)(2,1)S(1)}, bf16[32,384]{1,0:T(8,128)(2,1)S(1)}, u32[]{:S(2)}, u32[]{:S(2)}) collective-permute-start(bf16[32,384]{1,0:T(8,128)(2,1)S(1)} %get-tuple-element.85), channel_id=1, source_target_pairs={{0,4},{1,5},{2,6},{3,7},{4,0},{5,1},{6,2},{7,3},{8,12},{9,13},{10,... | collective-permute-start | bytes 73736 | tf_op jit(solution)/shard_map/ppermute | solution.py:48
  35.5 10.7 %collective-permute-start.15 = (bf16[4,3,8,384]{3,2,1,0:T(8,128)(2,1)S(1)}, bf16[4,3,8,384]{3,2,1,0:T(8,128)(2,1)S(1)}, u32[]{:S(2)}, u32[]{:S(2)}) collective-permute-start(bf16[4,3,8,384]{3,2,1,0:T(8,128)(2,1)S(1)} %get-tuple-element.90), channel_id=1, source_target_pairs={{0,1},{1,0},{2,3},{3,2},{4,5},{5,4},{6,7},{7,6},{8,9},{9,8},{10,11... | collective-permute-start | bytes 221192 | tf_op jit(solution)/shard_map/ppermute | solution.py:48
  35.5 10.7 %collective-permute-start.16 = (bf16[4,3,8,384]{3,2,1,0:T(8,128)(2,1)S(1)}, bf16[4,3,8,384]{3,2,1,0:T(8,128)(2,1)S(1)}, u32[]{:S(2)}, u32[]{:S(2)}) collective-permute-start(bf16[4,3,8,384]{3,2,1,0:T(8,128)(2,1)S(1)} %get-tuple-element.91), channel_id=1, source_target_pairs={{0,16},{1,2},{2,1},{3,4},{4,3},{5,6},{6,5},{7,8},{8,7},{9,10},{10,... | collective-permute-start | bytes 221192 | tf_op jit(solution)/shard_map/ppermute | solution.py:61
  38.9 4.9 %collective-permute-start.13 = (bf16[32,384]{1,0:T(8,128)(2,1)S(1)}, bf16[32,384]{1,0:T(8,128)(2,1)S(1)}, u32[]{:S(2)}, u32[]{:S(2)}) collective-permute-start(bf16[32,384]{1,0:T(8,128)(2,1)S(1)} %get-tuple-element.87), channel_id=1, source_target_pairs={{0,8},{1,9},{2,10},{3,11},{4,12},{5,13},{6,14},{7,15},{8,0},{9,1},... | collective-permute-start | bytes 73736 | tf_op jit(solution)/shard_map/ppermute | solution.py:48
  41.2 6.7 %collective-permute-start.8 = (bf16[96,384]{1,0:T(8,128)(2,1)S(1)}, bf16[96,384]{1,0:T(8,128)(2,1)S(1)}, u32[]{:S(2)}, u32[]{:S(2)}) collective-permute-start(bf16[96,384]{1,0:T(8,128)(2,1)S(1)} %get-tuple-element.66), channel_id=1, source_target_pairs={{0,16},{16,0},{1,17},{17,1},{2,18},{18,2},{3,19},{19,3},{4,20},{20... | collective-permute-start | bytes 221192 | tf_op jit(solution)/shard_map/ppermute | solution.py:48
  44.5 3.4 %collective-permute-start.14 = (f32[32,384]{1,0:T(8,128)S(1)}, f32[32,384]{1,0:T(8,128)S(1)}, u32[]{:S(2)}, u32[]{:S(2)}) collective-permute-start(f32[32,384]{1,0:T(8,128)S(1)} %get-tuple-element.88.state_ref), channel_id=1, source_target_pairs={{0,1},{1,0},{2,3},{3,2},{4,5},{5,4},{6,7},{7,6},{8,9},{9,8},{10,11... | collective-permute-start | bytes 147464 | tf_op jit(solution)/shard_map/ppermute | solution.py:48

commit v9 on v7

--- a/solution.py
+++ b/solution.py
@@ -388,12 +388,13 @@
     emb_ref[...] = total[TAPS : TAPS + 1, :]
 
 
-def middle_kernel(adj_ref, grad_ref, kern_ref, out_ref, pad_ref):
-    capacity, parts = adj_ref.shape[0], grad_ref.shape[1] // LANES
+def middle_kernel(start, adj_ref, grad_ref, kern_ref, out_ref, pad_ref):
+    capacity, parts = adj_ref.shape[0], out_ref.shape[1] // LANES
+    columns = slice(start * LANES, (start + parts) * LANES)
 
     def own_at(tile, row):
         at = tile * 64 + row * 8
-        return grad_ref[pl.ds(at if isinstance(at, int) else pl.multiple_of(at, 8), 8), :]
+        return grad_ref[pl.ds(at if isinstance(at, int) else pl.multiple_of(at, 8), 8), columns]
 
     fill_middle(pad_ref, own_at, adj_ref, capacity, 0, parts)
 
@@ -403,16 +404,16 @@
 
     convolve(
         [(pad_ref, 8, 3)],
-        lambda row, col, lane: kern_ref[6 - row, 6 - col : 7 - col, lanes(lane)],
+        lambda row, col, lane: kern_ref[6 - row, 6 - col : 7 - col, lanes(start + lane)],
         finish, capacity, parts,
     )
 
 
 def outer_kernel(
-    adj_ref, place_ref, counts_ref, pool_ref, part_ref, core_ref, cross_ref, kern_ref, up_ref, cot_ref,
+    adj_ref, place_ref, counts_ref, pool_ref, first_ref, other_ref, core_ref, cross_ref, kern_ref, up_ref, cot_ref,
     out_ref, pad_ref,
 ):
-    capacity, parts = adj_ref.shape[0], part_ref.shape[1] // LANES
+    capacity, parts = adj_ref.shape[0], up_ref.shape[1] // LANES
     fill_edges(pad_ref, core_ref, cross_ref, place_ref, adj_ref, capacity, parts)
 
     def finish(tile, lane, sums):
@@ -420,7 +421,8 @@
         extra = pool_ref[0, tile] * cot_ref[:, lanes(lane)] * 0.125
         for row in range(8):
             at = pl.ds(tile * 64 + row * 8, 8)
-            total = live * (up_ref[at, lanes(lane)].astype(f32) + extra) + part_ref[at, lanes(lane)]
+            part = first_ref[at, :] if lane == 0 else other_ref[at, lanes(lane - 1)]
+            total = live * (up_ref[at, lanes(lane)].astype(f32) + extra) + part
             if sums[row] is not None:
                 total = total + sums[row]
             out_ref[at, lanes(lane)] = (live * total).astype(bf16)
@@ -521,9 +523,8 @@
     got_a = swapped(send_a, "space", 2)
     got_b = swapped(send_b, "space", 4)
     half //= 2
-    (keep_a, send_a), (keep_b, send_b) = merge(
-        [(keep_a, got_a), (keep_b, got_b)], [(0, half, rows, 2), (half, half, rows, 1)]
-    )
+    ((keep_a, send_a),) = merge([(keep_a, got_a)], [(0, half, rows, 2)])
+    ((keep_b, send_b),) = merge([(keep_b, got_b)], [(0, half, rows, 1)])
     got_a = swapped(send_a, "space", 4)
     got_b = swapped(send_b, "space", 2)
     held = [(keep_a, got_a), (keep_b, got_b)]
@@ -547,7 +548,7 @@
         scratch=[pltpu.VMEM((TAPS, 8, channels), f32)],
     )
     steps = [("space", 1)] + [("dp", 1 << n) for n in range(groups.bit_length() - 1)]
-    steps += [("space", 1 << n) for n in range(1, stages)]
+    steps += [("space", 4), ("space", 2)] + [("space", 1 << n) for n in range(3, stages)]
     for axis, bit in steps:
         new = swapped(pack, axis, bit)
         if (axis, bit) != steps[-1]:
@@ -562,14 +563,17 @@
         [VMEM] * 4, [share, got, state, new],
     )
 
-    part = call(
-        middle_kernel, struct((pixels, channels)), [SMEM] + [VMEM] * 2, [wanted, grad, kernel],
-        scratch=[pltpu.VMEM((parts, capacity, 8, 24, LANES), f32)],
-    )
+    middle = []
+    for start, width in ((0, 1), (1, parts - 1)):
+        middle.append(call(
+            functools.partial(middle_kernel, start), struct((pixels, width * LANES)),
+            [SMEM] + [VMEM] * 2, [wanted, grad, kernel],
+            scratch=[pltpu.VMEM((width, capacity, 8, 24, LANES), f32)],
+        ))
     grad_tiles = call(
         outer_kernel, struct((pixels, channels), bf16),
-        [SMEM] * 2 + [VMEM, SMEM] + [VMEM] * 6,
-        [wanted, place, counts, pool_weight, part, core, cross, kernel, up, slide_cot],
+        [SMEM] * 2 + [VMEM, SMEM] + [VMEM] * 7,
+        [wanted, place, counts, pool_weight, *middle, core, cross, kernel, up, slide_cot],
         scratch=[pltpu.VMEM((parts, capacity, 6, 24, LANES), f32)],
     )
     return (

time: 46 us -> 45.9 us (level)
  starting transfers between devices: 19.8 us -> 18.5 us
  Pallas kernels: 12.1 us -> 12.8 us
  waiting for transfers between devices: 11.4 us -> 12 us
    ppermute x14, starting transfers between devices: 16 us -> 14.9 us  [swapped(): lax.ppermute(value, axis, [(source, source ^ bit) for source in range(cou...]
    ppermute x14, waiting for transfers between devices: 11.4 us -> 12 us  [swapped(): lax.ppermute(value, axis, [(source, source ^ bit) for source in range(cou...]
    pallas_call x16 -> x18, Pallas kernels: 12.1 us -> 12.8 us  [call(): pl.pallas_call(body, out_shape=out_shape, in_specs=in_specs, out_specs=ou...]
  transfers between devices with their start and end apart: 16 -> 16, of which waited for: 6 -> 6; matrix products, arithmetic and copies ran while one was open for 0% -> 0% of each run, Pallas kernels for 19% -> 20%
where the time goes in v9:
time: 45.9 us; the launch traced here: 45.8 us
  starting transfers between devices  18.5 us (40%)
  Pallas kernels  12.8 us (28%)
  waiting for transfers between devices  12 us (26%)
  between operations  1.56 us (3%)
  local copies, waits for them, and re-layouts  0.96 us (2%)
    ppermute x14, starting transfers between devices, swapped(): lax.ppermute(value, axis, [(source, source ^ bit) for source in range(cou...  14.9 us
    pallas_call x18, Pallas kernels, call(): pl.pallas_call(body, out_shape=out_shape, in_specs=in_specs, out_specs=ou...  12.8 us
    ppermute x14, waiting for transfers between devices, swapped(): lax.ppermute(value, axis, [(source, source ^ bit) for source in range(cou...  12 us
    ppermute x2, starting transfers between devices, crossed(): return lax.ppermute(value, ('dp', 'space'), targets)  3.57 us
    unnamed x22, local copies, waits for them, and re-layouts  0.96 us
  transfers between devices with their start and end apart: 16, of which 6 were waited for; matrix products, arithmetic and copies ran while one was open for 0% of the time, Pallas kernels for 20%

profile of v9, /device:TPU:0, one launch (start us, length us, event | category | flops | bytes accessed | tf_op | source)
XLA Modules:
  0.0 45.8 jit_solution(3282132350209435401)
XLA Ops:
  0.6 0.9 %copy-done.4 = bf16[1,4,8,8,384]{4,3,2,1,0:T(8,128)(2,1)S(1)} copy-done((bf16[1,4,8,8,384]{4,3,2,1,0:T(8,128)(2,1)S(1)}, bf16[1,4,8,8,384]{4,3,2,1,0:T(8,128)(2,1)}, u32[]{:S(2)}) %copy-start.4) | copy-done | bytes 196632
  1.6 0.0 copy-start.6
  1.6 0.1 shard_map.138
  1.7 0.0 copy-start.2
  1.7 0.0 copy-start.10
  1.7 0.6 %collective-permute-start = (bf16[4,3,8,384]{3,2,1,0:T(8,128)(2,1)S(1)}, bf16[4,3,8,384]{3,2,1,0:T(8,128)(2,1)S(1)}, u32[]{:S(2)}, u32[]{:S(2)}) collective-permute-start(bf16[4,3,8,384]{3,2,1,0:T(8,128)(2,1)S(1)} %get-tuple-element.48), channel_id=1, source_target_pairs={{0,1},{1,0},{2,3},{3,2},{4,5},{5,4},{6,7},{7,6},{8,9},{9,8},{10,11... | collective-permute-start | bytes 221192 | tf_op jit(solution)/shard_map/ppermute | solution.py:47
  2.3 2.6 %collective-permute-start.1 = (bf16[4,3,8,384]{3,2,1,0:T(8,128)(2,1)S(1)}, bf16[4,3,8,384]{3,2,1,0:T(8,128)(2,1)S(1)}, u32[]{:S(2)}, u32[]{:S(2)}) collective-permute-start(bf16[4,3,8,384]{3,2,1,0:T(8,128)(2,1)S(1)} %get-tuple-element.49), channel_id=1, source_target_pairs={{0,16},{1,2},{2,1},{3,4},{4,3},{5,6},{6,5},{7,8},{8,7},{9,10},{10,... | collective-permute-start | bytes 221192 | tf_op jit(solution)/shard_map/ppermute | solution.py:60
  5.6 2.0 %shard_map.139 = (f32[3,4,8,24,128]{4,3,2,1,0:T(8,128)S(1)}, f32[256,384]{1,0:T(8,128)S(1)}, bf16[256,512]{1,0:T(8,128)(2,1)S(1)}, f32[256,1536]{1,0:T(8,128)S(1)}, f32[1,384]{1,0:T(1,128)S(1)}) custom-call(s32[4,8]{1,0:T(4,128)S(1)} %bitcast.9, s32[1,1]{1,0:T(1,128)S(6)} %copy.15.counts_ref, f32[1,4]{1,0:T(1,128)S(1)} %copy-done.9, f32[1,384]{1,0:T(1,128)S(1)} %copy-done.8, ...), custom_call_target="tpu_custom_call" | custom-call | flops 301989888 | bytes 5060756 | tf_op jit(solution)/shard_map/pallas_call | solution.py:30
  7.6 0.0 collective-permute-done.core_ref
  7.6 0.0 collective-permute-done.1.cross_ref
  7.6 2.5 %shard_map.140 = (f32[3,4,6,24,128]{4,3,2,1,0:T(8,128)S(1)}, f32[256,384]{1,0:T(8,128)S(1)}, f32[256,1]{1,0:T(8,128)S(1)}, f32[256,1536]{1,0:T(8,128)S(1)}, f32[...) custom-call(s32[4,8]{1,0:T(4,128)S(1)} %bitcast.10, ...), custom_call_target="tpu_custom_call" | custom-call | flops 603979776 | bytes 9040004 | tf_op jit(solution)/shard_map/pallas_call | solution.py:30
  10.1 0.2 collective-permute-start.2
  10.3 1.9 %collective-permute-done.2.refs_1_ = bf16[768,384]{1,0:T(8,128)(2,1)S(1)} collective-permute-done((bf16[768,384]{1,0:T(8,128)(2,1)S(1)}, bf16[768,384]{1,0:T(8,128)(2,1)S(1)}, u32[]{:S(2)}, u32[]{:S(2)}) %collective-permute-start.2) | collective-permute-done | bytes 589856 | tf_op jit(solution)/shard_map/ppermute | solution.py:47
  12.2 0.3 shard_map.141
  12.5 2.0 %collective-permute-start.3 = (bf16[192,384]{1,0:T(8,128)(2,1)S(1)}, bf16[192,384]{1,0:T(8,128)(2,1)S(1)}, u32[]{:S(2)}, u32[]{:S(2)}) collective-permute-start(bf16[192,384]{1,0:T(8,128)(2,1)S(1)} %get-tuple-element.55), channel_id=1, source_target_pairs={{0,2},{1,3},{2,0},{3,1},{4,6},{5,7},{6,4},{7,5},{8,10},{9,11},{10,... | collective-permute-start | bytes 442376 | tf_op jit(solution)/shard_map/ppermute | solution.py:47
  14.5 1.6 %collective-permute-start.5 = (bf16[192,384]{1,0:T(8,128)(2,1)S(1)}, bf16[192,384]{1,0:T(8,128)(2,1)S(1)}, u32[]{:S(2)}, u32[]{:S(2)}) collective-permute-start(bf16[192,384]{1,0:T(8,128)(2,1)S(1)} %get-tuple-element.59), channel_id=1, source_target_pairs={{0,4},{1,5},{2,6},{3,7},{4,0},{5,1},{6,2},{7,3},{8,12},{9,13},{10,... | collective-permute-start | bytes 442376 | tf_op jit(solution)/shard_map/ppermute | solution.py:47
  16.0 2.8 %collective-permute-done.3.refs_1_ = bf16[192,384]{1,0:T(8,128)(2,1)S(1)} collective-permute-done((bf16[192,384]{1,0:T(8,128)(2,1)S(1)}, bf16[192,384]{1,0:T(8,128)(2,1)S(1)}, u32[]{:S(2)}, u32[]{:S(2)}) %collective-permute-start.3) | collective-permute-done | bytes 147488 | tf_op jit(solution)/shard_map/ppermute | solution.py:47
  18.8 0.1 shard_map.142
  18.9 1.7 %collective-permute-start.4 = (bf16[96,384]{1,0:T(8,128)(2,1)S(1)}, bf16[96,384]{1,0:T(8,128)(2,1)S(1)}, u32[]{:S(2)}, u32[]{:S(2)}) collective-permute-start(bf16[96,384]{1,0:T(8,128)(2,1)S(1)} %get-tuple-element.57), channel_id=1, source_target_pairs={{0,4},{1,5},{2,6},{3,7},{4,0},{5,1},{6,2},{7,3},{8,12},{9,13},{10,... | collective-permute-start | bytes 221192 | tf_op jit(solution)/shard_map/ppermute | solution.py:47
  20.7 0.0 collective-permute-done.5.refs_1_
  20.7 0.1 shard_map.143
  20.7 1.7 %collective-permute-start.6 = (bf16[96,384]{1,0:T(8,128)(2,1)S(1)}, bf16[96,384]{1,0:T(8,128)(2,1)S(1)}, u32[]{:S(2)}, u32[]{:S(2)}) collective-permute-start(bf16[96,384]{1,0:T(8,128)(2,1)S(1)} %get-tuple-element.61), channel_id=1, source_target_pairs={{0,2},{1,3},{2,0},{3,1},{4,6},{5,7},{6,4},{7,5},{8,10},{9,11},{10,... | collective-permute-start | bytes 221192 | tf_op jit(solution)/shard_map/ppermute | solution.py:47
  22.4 1.5 %shard_map.146 = (f32[256,384]{1,0:T(8,128)S(1)}, bf16[4,3,8,384]{3,2,1,0:T(8,128)(2,1)S(1)}, bf16[4,3,8,384]{3,2,1,0:T(8,128)(2,1)S(1)}, f32[1,384]{1,0:T(1,128)S(1)}) custom-call(s32[1,1]{1,0:T(1,128)} %bitcast.place_ref, s32[1,1]{1,0:T(1,128)S(6)} %copy.15.counts_ref, f32[1,4]{1,0:T(1,128)S(1)} %copy-done.9, f32[256,1536]{1,0:T(8,128)S(1)} %get-tuple-element.68.pre_ref, ...), custom_call_target="tpu_custom_call" | custom-call | flops 301989888 | bytes 8805400 | tf_op jit(solution)/shard_map/pallas_call | solution.py:30
  24.0 1.4 %shard_map.147 = (f32[56,384]{1,0:T(8,128)S(1)}, bf16[56,384]{1,0:T(8,128)(2,1)S(1)}) custom-call(f32[3,4,8,24,128]{4,3,2,1,0:T(8,128)S(1)} %get-tuple-element.66.pad_ref, f32[3,4,6,24,128]{4,3,2,1,0:T(8,128)S(1)} %get-tuple-element.67.edge_ref, f32[256,384]{1,0:T(8,128)S(1)} %get-tuple-element.75.grad_ref, f32[1,384]{1,0:T(1,128)S(1)} %get-tuple-element.76.emb_ref), custom_call_target="tpu_custom_call" | custom-call | bytes 2588160 | tf_op jit(solution)/shard_map/pallas_call | solution.py:30
  25.4 0.1 collective-permute-start.9
  25.5 1.2 %collective-permute-done.9.got_ref = bf16[56,384]{1,0:T(8,128)(2,1)S(1)} collective-permute-done((bf16[56,384]{1,0:T(8,128)(2,1)S(1)}, bf16[56,384]{1,0:T(8,128)(2,1)S(1)}, u32[]{:S(2)}, u32[]{:S(2)}) %collective-permute-start.9) | collective-permute-done | bytes 43040 | tf_op jit(solution)/shard_map/ppermute | solution.py:47
  26.7 1.6 %collective-permute-start.10 = (bf16[56,384]{1,0:T(8,128)(2,1)S(1)}, bf16[56,384]{1,0:T(8,128)(2,1)S(1)}, u32[]{:S(2)}, u32[]{:S(2)}) collective-permute-start(bf16[56,384]{1,0:T(8,128)(2,1)S(1)} %get-tuple-element.80), channel_id=1, source_target_pairs={{0,16},{16,0},{1,17},{17,1},{2,18},{18,2},{3,19},{19,3},{4,20},{20... | collective-permute-start | bytes 129032 | tf_op jit(solution)/shard_map/ppermute | solution.py:47
  28.3 0.0 collective-permute-done.4.refs_1_
  28.3 0.0 collective-permute-done.6.refs_3_
  28.3 1.5 %collective-permute-start.7 = (bf16[96,384]{1,0:T(8,128)(2,1)S(1)}, bf16[96,384]{1,0:T(8,128)(2,1)S(1)}, u32[]{:S(2)}, u32[]{:S(2)}) collective-permute-start(bf16[96,384]{1,0:T(8,128)(2,1)S(1)} %get-tuple-element.63), channel_id=1, source_target_pairs={{0,8},{1,9},{2,10},{3,11},{4,12},{5,13},{6,14},{7,15},{8,0},{9,1},... | collective-permute-start | bytes 221192 | tf_op jit(solution)/shard_map/ppermute | solution.py:47
  29.8 1.0 %collective-permute-done.10.got_ref = bf16[56,384]{1,0:T(8,128)(2,1)S(1)} collective-permute-done((bf16[56,384]{1,0:T(8,128)(2,1)S(1)}, bf16[56,384]{1,0:T(8,128)(2,1)S(1)}, u32[]{:S(2)}, u32[]{:S(2)}) %collective-permute-start.10) | collective-permute-done | bytes 43040 | tf_op jit(solution)/shard_map/ppermute | solution.py:47
  30.8 0.7 %collective-permute-start.11 = (bf16[56,384]{1,0:T(8,128)(2,1)S(1)}, bf16[56,384]{1,0:T(8,128)(2,1)S(1)}, u32[]{:S(2)}, u32[]{:S(2)}) collective-permute-start(bf16[56,384]{1,0:T(8,128)(2,1)S(1)} %get-tuple-element.82), channel_id=1, source_target_pairs={{0,4},{1,5},{2,6},{3,7},{4,0},{5,1},{6,2},{7,3},{8,12},{9,13},{10,... | collective-permute-start | bytes 129032 | tf_op jit(solution)/shard_map/ppermute | solution.py:47
  31.5 3.7 %collective-permute-done.11.got_ref = bf16[56,384]{1,0:T(8,128)(2,1)S(1)} collective-permute-done((bf16[56,384]{1,0:T(8,128)(2,1)S(1)}, bf16[56,384]{1,0:T(8,128)(2,1)S(1)}, u32[]{:S(2)}, u32[]{:S(2)}) %collective-permute-start.11) | collective-permute-done | bytes 43040 | tf_op jit(solution)/shard_map/ppermute | solution.py:47
  35.3 0.6 %collective-permute-start.12 = (bf16[56,384]{1,0:T(8,128)(2,1)S(1)}, bf16[56,384]{1,0:T(8,128)(2,1)S(1)}, u32[]{:S(2)}, u32[]{:S(2)}) collective-permute-start(bf16[56,384]{1,0:T(8,128)(2,1)S(1)} %get-tuple-element.84), channel_id=1, source_target_pairs={{0,2},{1,3},{2,0},{3,1},{4,6},{5,7},{6,4},{7,5},{8,10},{9,11},{10,... | collective-permute-start | bytes 129032 | tf_op jit(solution)/shard_map/ppermute | solution.py:47
  35.9 0.0 collective-permute-start.14
  35.9 1.0 %collective-permute-start.15 = (bf16[4,3,8,384]{3,2,1,0:T(8,128)(2,1)S(1)}, bf16[4,3,8,384]{3,2,1,0:T(8,128)(2,1)S(1)}, u32[]{:S(2)}, u32[]{:S(2)}) collective-permute-start(bf16[4,3,8,384]{3,2,1,0:T(8,128)(2,1)S(1)} %get-tuple-element.89), channel_id=1, source_target_pairs={{0,16},{1,2},{2,1},{3,4},{4,3},{5,6},{6,5},{7,8},{8,7},{9,10},{10,... | collective-permute-start | bytes 221192 | tf_op jit(solution)/shard_map/ppermute | solution.py:60
  36.9 0.0 collective-permute-done.7.refs_1_
  36.9 1.1 %collective-permute-start.8 = (bf16[96,384]{1,0:T(8,128)(2,1)S(1)}, bf16[96,384]{1,0:T(8,128)(2,1)S(1)}, u32[]{:S(2)}, u32[]{:S(2)}) collective-permute-start(bf16[96,384]{1,0:T(8,128)(2,1)S(1)} %get-tuple-element.65), channel_id=1, source_target_pairs={{0,16},{16,0},{1,17},{17,1},{2,18},{18,2},{3,19},{19,3},{4,20},{20... | collective-permute-start | bytes 221192 | tf_op jit(solution)/shard_map/ppermute | solution.py:47
  38.0 1.4 %collective-permute-done.12.got_ref = bf16[56,384]{1,0:T(8,128)(2,1)S(1)} collective-permute-done((bf16[56,384]{1,0:T(8,128)(2,1)S(1)}, bf16[56,384]{1,0:T(8,128)(2,1)S(1)}, u32[]{:S(2)}, u32[]{:S(2)}) %collective-permute-start.12) | collective-permute-done | bytes 43040 | tf_op jit(solution)/shard_map/ppermute | solution.py:47
  39.4 1.7 %collective-permute-start.13 = (bf16[56,384]{1,0:T(8,128)(2,1)S(1)}, bf16[56,384]{1,0:T(8,128)(2,1)S(1)}, u32[]{:S(2)}, u32[]{:S(2)}) collective-permute-start(bf16[56,384]{1,0:T(8,128)(2,1)S(1)} %get-tuple-element.86), channel_id=1, source_target_pairs={{0,8},{1,9},{2,10},{3,11},{4,12},{5,13},{6,14},{7,15},{8,0},{9,1},... | collective-permute-start | bytes 129032 | tf_op jit(solution)/shard_map/ppermute | solution.py:47
  41.1 0.9 %shard_map.153.first_ref = f32[256,128]{1,0:T(8,128)S(1)} custom-call(s32[4,8]{1,0:T(4,128)S(1)} %bitcast.11, f32[256,384]{1,0:T(8,128)S(1)} %get-tuple-element.75.grad_ref, f32[7,7,384]{2,1,0:T(8,128)S(1)} %copy-done.1), custom_call_target="tpu_custom_call" | custom-call | bytes 599680 | tf_op jit(solution)/shard_map/pallas_call | solution.py:30
  42.0 1.3 %shard_map.154.other_ref = f32[256,256]{1,0:T(8,128)S(1)} custom-call(s32[4,8]{1,0:T(4,128)S(1)} %bitcast.12, f32[256,384]{1,0:T(8,128)S(1)} %get-tuple-element.75.grad_ref, f32[7,7,384]{2,1,0:T(8,128)S(1)} %copy-done.1), custom_call_target="tpu_custom_call" | custom-call | bytes 730752 | tf_op jit(solution)/shard_map/pallas_call | solution.py:30
  43.3 0.0 collective-permute-done.14.core_ref
  43.3 0.0 collective-permute-done.15.cross_ref
  43.3 1.7 %shard_map.155 = bf16[256,384]{1,0:T(8,128)(2,1)} custom-call(s32[4,8]{1,0:T(4,128)S(1)} %bitcast.13, s32[1,1]{1,0:T(1,128)} %bitcast.place_ref, s32[1,1]{1,0:T(1,128)S(6)} %copy.15.counts_ref, f32[1,4]{1,0:T(1,128)S(1)} %copy-done.9, f32[256,128]{1,0:T(8,128)S(1)} %shard_map.153.first_ref, f32[256,256]{1,0:T(8,128)S(1)} %shard_map.154.other_ref, ...), custom_call_target="tpu_custom_call" | custom-call | bytes 1010840 | tf_op jit(solution)/shard_map/pallas_call | solution.py:30
  45.1 0.0 collective-permute-done.13.new_ref
  45.1 0.0 collective-permute-done.8.got_ref
  45.1 0.7 %shard_map.152 = (f32[96,384]{1,0:T(8,128)}, f32[7,7,384]{2,1,0:T(8,128)}, f32[1,384]{1,0:T(1,128)}) custom-call(f32[96,384]{1,0:T(8,128)S(1)} %get-tuple-element.64.keep_ref, bf16[96,384]{1,0:T(8,128)(2,1)S(1)} %collective-permute-done.8.got_ref, f32[56,384]{1,0:T(8,128)S(1)} %get-tuple-element.85.state_ref, bf16[56,384]{1,0:T(8,128)(2,1)S(1)} %collective-permute-done.13.new_ref), custom_call_target="tpu_custom_call" | custom-call | bytes 574464 | tf_op jit(solution)/shard_map/pallas_call | solution.py:30
  (24 shorter events, 0.2 us)
Async XLA Ops:
  0.6 0.9 %copy-start.4 = (bf16[1,4,8,8,384]{4,3,2,1,0:T(8,128)(2,1)S(1)}, bf16[1,4,8,8,384]{4,3,2,1,0:T(8,128)(2,1)}, u32[]{:S(2)}) copy-start(bf16[1,4,8,8,384]{4,3,2,1,0:T(8,128)(2,1)} %param.11) | copy-start | bytes 589828
  1.6 3.9 %copy-start = (bf16[1536,384]{1,0:T(8,128)(2,1)S(1)}, bf16[1536,384]{1,0:T(8,128)(2,1)}, u32[]{:S(2)}) copy-start(bf16[1536,384]{1,0:T(8,128)(2,1)} %w_out_ref.3) | copy-start | bytes 3538948
  1.6 3.9 %copy-start.1 = (f32[7,7,384]{2,1,0:T(8,128)S(1)}, f32[7,7,384]{2,1,0:T(8,128)}, u32[]{:S(2)}) copy-start(f32[7,7,384]{2,1,0:T(8,128)} %kern_ref.9) | copy-start | bytes 225796
  1.6 3.9 %copy-start.3 = (bf16[1,4,8,8,384]{4,3,2,1,0:T(8,128)(2,1)S(1)}, bf16[1,4,8,8,384]{4,3,2,1,0:T(8,128)(2,1)}, u32[]{:S(2)}) copy-start(bf16[1,4,8,8,384]{4,3,2,1,0:T(8,128)(2,1)} %param.12) | copy-start | bytes 589828
  1.6 3.9 %copy-start.5 = (bf16[1,4,8,8,384]{4,3,2,1,0:T(8,128)(2,1)S(1)}, bf16[1,4,8,8,384]{4,3,2,1,0:T(8,128)(2,1)}, u32[]{:S(2)}) copy-start(bf16[1,4,8,8,384]{4,3,2,1,0:T(8,128)(2,1)} %param.11) | copy-start | bytes 589828
  1.6 3.9 %copy-start.6 = (s32[1,4,8]{2,1,0:T(4,128)S(1)}, s32[1,4,8]{2,1,0:T(4,128)}, u32[]{:S(2)}) copy-start(s32[1,4,8]{2,1,0:T(4,128)} %param.15) | copy-start | bytes 388
  1.6 3.9 %copy-start.7 = (f32[384]{0:T(512)S(1)}, f32[384]{0:T(512)}, u32[]{:S(2)}) copy-start(f32[384]{0:T(512)} %scale_ref.3) | copy-start | bytes 4612
  1.6 3.9 %copy-start.8 = (f32[1,384]{1,0:T(1,128)S(1)}, f32[1,384]{1,0:T(1,128)}, u32[]{:S(2)}) copy-start(f32[1,384]{1,0:T(1,128)} %cot_ref.3) | copy-start | bytes 4612
  1.6 3.9 %copy-start.9 = (f32[1,4]{1,0:T(1,128)S(1)}, f32[1,4]{1,0:T(1,128)}, u32[]{:S(2)}) copy-start(f32[1,4]{1,0:T(1,128)} %pool_ref.5) | copy-start | bytes 52
  1.7 5.9 %copy-start.2 = (bf16[384,1536]{1,0:T(8,128)(2,1)S(1)}, bf16[384,1536]{1,0:T(8,128)(2,1)}, u32[]{:S(2)}) copy-start(bf16[384,1536]{1,0:T(8,128)(2,1)} %w_in_ref.3) | copy-start | bytes 3538948
  1.7 5.9 %copy-start.10 = (f32[384]{0:T(512)S(1)}, f32[384]{0:T(512)}, u32[]{:S(2)}) copy-start(f32[384]{0:T(512)} %gain_ref.3) | copy-start | bytes 4612
  1.7 5.9 %collective-permute-start = (bf16[4,3,8,384]{3,2,1,0:T(8,128)(2,1)S(1)}, bf16[4,3,8,384]{3,2,1,0:T(8,128)(2,1)S(1)}, u32[]{:S(2)}, u32[]{:S(2)}) collective-permute-start(bf16[4,3,8,384]{3,2,1,0:T(8,128)(2,1)S(1)} %get-tuple-element.48), channel_id=1, source_target_pairs={{0,1},{1,0},{2,3},{3,2},{4,5},{5,4},{6,7},{7,6},{8,9},{9,8},{10,11... | collective-permute-start | bytes 221192 | tf_op jit(solution)/shard_map/ppermute | solution.py:47
  2.3 5.4 %collective-permute-start.1 = (bf16[4,3,8,384]{3,2,1,0:T(8,128)(2,1)S(1)}, bf16[4,3,8,384]{3,2,1,0:T(8,128)(2,1)S(1)}, u32[]{:S(2)}, u32[]{:S(2)}) collective-permute-start(bf16[4,3,8,384]{3,2,1,0:T(8,128)(2,1)S(1)} %get-tuple-element.49), channel_id=1, source_target_pairs={{0,16},{1,2},{2,1},{3,4},{4,3},{5,6},{6,5},{7,8},{8,7},{9,10},{10,... | collective-permute-start | bytes 221192 | tf_op jit(solution)/shard_map/ppermute | solution.py:60
  10.1 2.1 %collective-permute-start.2 = (bf16[768,384]{1,0:T(8,128)(2,1)S(1)}, bf16[768,384]{1,0:T(8,128)(2,1)S(1)}, u32[]{:S(2)}, u32[]{:S(2)}) collective-permute-start(bf16[768,384]{1,0:T(8,128)(2,1)S(1)} %get-tuple-element.53), channel_id=1, source_target_pairs={{0,1},{1,0},{2,3},{3,2},{4,5},{5,4},{6,7},{7,6},{8,9},{9,8},{10,11... | collective-permute-start | bytes 1769480 | tf_op jit(solution)/shard_map/ppermute | solution.py:47
  12.5 6.4 %collective-permute-start.3 = (bf16[192,384]{1,0:T(8,128)(2,1)S(1)}, bf16[192,384]{1,0:T(8,128)(2,1)S(1)}, u32[]{:S(2)}, u32[]{:S(2)}) collective-permute-start(bf16[192,384]{1,0:T(8,128)(2,1)S(1)} %get-tuple-element.55), channel_id=1, source_target_pairs={{0,2},{1,3},{2,0},{3,1},{4,6},{5,7},{6,4},{7,5},{8,10},{9,11},{10,... | collective-permute-start | bytes 442376 | tf_op jit(solution)/shard_map/ppermute | solution.py:47
  14.5 6.2 %collective-permute-start.5 = (bf16[192,384]{1,0:T(8,128)(2,1)S(1)}, bf16[192,384]{1,0:T(8,128)(2,1)S(1)}, u32[]{:S(2)}, u32[]{:S(2)}) collective-permute-start(bf16[192,384]{1,0:T(8,128)(2,1)S(1)} %get-tuple-element.59), channel_id=1, source_target_pairs={{0,4},{1,5},{2,6},{3,7},{4,0},{5,1},{6,2},{7,3},{8,12},{9,13},{10,... | collective-permute-start | bytes 442376 | tf_op jit(solution)/shard_map/ppermute | solution.py:47
  18.9 9.4 %collective-permute-start.4 = (bf16[96,384]{1,0:T(8,128)(2,1)S(1)}, bf16[96,384]{1,0:T(8,128)(2,1)S(1)}, u32[]{:S(2)}, u32[]{:S(2)}) collective-permute-start(bf16[96,384]{1,0:T(8,128)(2,1)S(1)} %get-tuple-element.57), channel_id=1, source_target_pairs={{0,4},{1,5},{2,6},{3,7},{4,0},{5,1},{6,2},{7,3},{8,12},{9,13},{10,... | collective-permute-start | bytes 221192 | tf_op jit(solution)/shard_map/ppermute | solution.py:47
  20.7 7.6 %collective-permute-start.6 = (bf16[96,384]{1,0:T(8,128)(2,1)S(1)}, bf16[96,384]{1,0:T(8,128)(2,1)S(1)}, u32[]{:S(2)}, u32[]{:S(2)}) collective-permute-start(bf16[96,384]{1,0:T(8,128)(2,1)S(1)} %get-tuple-element.61), channel_id=1, source_target_pairs={{0,2},{1,3},{2,0},{3,1},{4,6},{5,7},{6,4},{7,5},{8,10},{9,11},{10,... | collective-permute-start | bytes 221192 | tf_op jit(solution)/shard_map/ppermute | solution.py:47
  25.4 1.3 %collective-permute-start.9 = (bf16[56,384]{1,0:T(8,128)(2,1)S(1)}, bf16[56,384]{1,0:T(8,128)(2,1)S(1)}, u32[]{:S(2)}, u32[]{:S(2)}) collective-permute-start(bf16[56,384]{1,0:T(8,128)(2,1)S(1)} %get-tuple-element.78), channel_id=1, source_target_pairs={{0,1},{1,0},{2,3},{3,2},{4,5},{5,4},{6,7},{7,6},{8,9},{9,8},{10,11... | collective-permute-start | bytes 129032 | tf_op jit(solution)/shard_map/ppermute | solution.py:47
  26.7 4.1 %collective-permute-start.10 = (bf16[56,384]{1,0:T(8,128)(2,1)S(1)}, bf16[56,384]{1,0:T(8,128)(2,1)S(1)}, u32[]{:S(2)}, u32[]{:S(2)}) collective-permute-start(bf16[56,384]{1,0:T(8,128)(2,1)S(1)} %get-tuple-element.80), channel_id=1, source_target_pairs={{0,16},{16,0},{1,17},{17,1},{2,18},{18,2},{3,19},{19,3},{4,20},{20... | collective-permute-start | bytes 129032 | tf_op jit(solution)/shard_map/ppermute | solution.py:47
  28.3 8.6 %collective-permute-start.7 = (bf16[96,384]{1,0:T(8,128)(2,1)S(1)}, bf16[96,384]{1,0:T(8,128)(2,1)S(1)}, u32[]{:S(2)}, u32[]{:S(2)}) collective-permute-start(bf16[96,384]{1,0:T(8,128)(2,1)S(1)} %get-tuple-element.63), channel_id=1, source_target_pairs={{0,8},{1,9},{2,10},{3,11},{4,12},{5,13},{6,14},{7,15},{8,0},{9,1},... | collective-permute-start | bytes 221192 | tf_op jit(solution)/shard_map/ppermute | solution.py:47
  30.8 4.4 %collective-permute-start.11 = (bf16[56,384]{1,0:T(8,128)(2,1)S(1)}, bf16[56,384]{1,0:T(8,128)(2,1)S(1)}, u32[]{:S(2)}, u32[]{:S(2)}) collective-permute-start(bf16[56,384]{1,0:T(8,128)(2,1)S(1)} %get-tuple-element.82), channel_id=1, source_target_pairs={{0,4},{1,5},{2,6},{3,7},{4,0},{5,1},{6,2},{7,3},{8,12},{9,13},{10,... | collective-permute-start | bytes 129032 | tf_op jit(solution)/shard_map/ppermute | solution.py:47
  35.3 4.1 %collective-permute-start.12 = (bf16[56,384]{1,0:T(8,128)(2,1)S(1)}, bf16[56,384]{1,0:T(8,128)(2,1)S(1)}, u32[]{:S(2)}, u32[]{:S(2)}) collective-permute-start(bf16[56,384]{1,0:T(8,128)(2,1)S(1)} %get-tuple-element.84), channel_id=1, source_target_pairs={{0,2},{1,3},{2,0},{3,1},{4,6},{5,7},{6,4},{7,5},{8,10},{9,11},{10,... | collective-permute-start | bytes 129032 | tf_op jit(solution)/shard_map/ppermute | solution.py:47
  35.9 7.4 %collective-permute-start.14 = (bf16[4,3,8,384]{3,2,1,0:T(8,128)(2,1)S(1)}, bf16[4,3,8,384]{3,2,1,0:T(8,128)(2,1)S(1)}, u32[]{:S(2)}, u32[]{:S(2)}) collective-permute-start(bf16[4,3,8,384]{3,2,1,0:T(8,128)(2,1)S(1)} %get-tuple-element.88), channel_id=1, source_target_pairs={{0,1},{1,0},{2,3},{3,2},{4,5},{5,4},{6,7},{7,6},{8,9},{9,8},{10,11... | collective-permute-start | bytes 221192 | tf_op jit(solution)/shard_map/ppermute | solution.py:47
  35.9 7.4 %collective-permute-start.15 = (bf16[4,3,8,384]{3,2,1,0:T(8,128)(2,1)S(1)}, bf16[4,3,8,384]{3,2,1,0:T(8,128)(2,1)S(1)}, u32[]{:S(2)}, u32[]{:S(2)}) collective-permute-start(bf16[4,3,8,384]{3,2,1,0:T(8,128)(2,1)S(1)} %get-tuple-element.89), channel_id=1, source_target_pairs={{0,16},{1,2},{2,1},{3,4},{4,3},{5,6},{6,5},{7,8},{8,7},{9,10},{10,... | collective-permute-start | bytes 221192 | tf_op jit(solution)/shard_map/ppermute | solution.py:60
  36.9 8.1 %collective-permute-start.8 = (bf16[96,384]{1,0:T(8,128)(2,1)S(1)}, bf16[96,384]{1,0:T(8,128)(2,1)S(1)}, u32[]{:S(2)}, u32[]{:S(2)}) collective-permute-start(bf16[96,384]{1,0:T(8,128)(2,1)S(1)} %get-tuple-element.65), channel_id=1, source_target_pairs={{0,16},{16,0},{1,17},{17,1},{2,18},{18,2},{3,19},{19,3},{4,20},{20... | collective-permute-start | bytes 221192 | tf_op jit(solution)/shard_map/ppermute | solution.py:47
  39.4 5.6 %collective-permute-start.13 = (bf16[56,384]{1,0:T(8,128)(2,1)S(1)}, bf16[56,384]{1,0:T(8,128)(2,1)S(1)}, u32[]{:S(2)}, u32[]{:S(2)}) collective-permute-start(bf16[56,384]{1,0:T(8,128)(2,1)S(1)} %get-tuple-element.86), channel_id=1, source_target_pairs={{0,8},{1,9},{2,10},{3,11},{4,12},{5,13},{6,14},{7,15},{8,0},{9,1},... | collective-permute-start | bytes 129032 | tf_op jit(solution)/shard_map/ppermute | solution.py:47

commit v10 on v7

--- a/solution.py
+++ b/solution.py
@@ -19,7 +19,7 @@
 HBM = pl.BlockSpec(memory_space=pltpu.HBM)
 STATE = 56
 TAPS = 49
-CHUNK = 384
+CHUNK = 768
 BACK_CHUNK = 512
 EDGE_COST = 5_000_000_000
 
@@ -521,9 +521,8 @@
     got_a = swapped(send_a, "space", 2)
     got_b = swapped(send_b, "space", 4)
     half //= 2
-    (keep_a, send_a), (keep_b, send_b) = merge(
-        [(keep_a, got_a), (keep_b, got_b)], [(0, half, rows, 2), (half, half, rows, 1)]
-    )
+    ((keep_a, send_a),) = merge([(keep_a, got_a)], [(0, half, rows, 2)])
+    ((keep_b, send_b),) = merge([(keep_b, got_b)], [(0, half, rows, 1)])
     got_a = swapped(send_a, "space", 4)
     got_b = swapped(send_b, "space", 2)
     held = [(keep_a, got_a), (keep_b, got_b)]

time: 46 us -> 45.1 us (0.980)
  starting transfers between devices: 19.8 us -> 18.9 us
    ppermute x14, starting transfers between devices: 16 us -> 15.1 us  [swapped(): lax.ppermute(value, axis, [(source, source ^ bit) for source in range(cou...]
    pallas_call x16 -> x17, Pallas kernels: 12.1 us -> 11.9 us  [call(): pl.pallas_call(body, out_shape=out_shape, in_specs=in_specs, out_specs=ou...]
where the time goes in v10:
time: 45.1 us; the launch traced here: 45 us
  starting transfers between devices  18.9 us (42%)
  Pallas kernels  11.9 us (26%)
  waiting for transfers between devices  11.6 us (26%)
  between operations  1.56 us (3%)
  local copies, waits for them, and re-layouts  0.96 us (2%)
    ppermute x14, starting transfers between devices, swapped(): lax.ppermute(value, axis, [(source, source ^ bit) for source in range(cou...  15.1 us
    pallas_call x17, Pallas kernels, call(): pl.pallas_call(body, out_shape=out_shape, in_specs=in_specs, out_specs=ou...  11.9 us
    ppermute x14, waiting for transfers between devices, swapped(): lax.ppermute(value, axis, [(source, source ^ bit) for source in range(cou...  11.6 us
    ppermute x2, starting transfers between devices, crossed(): return lax.ppermute(value, ('dp', 'space'), targets)  3.85 us
    unnamed x22, local copies, waits for them, and re-layouts  0.96 us
  transfers between devices with their start and end apart: 16, of which 6 were waited for; matrix products, arithmetic and copies ran while one was open for 0% of the time, Pallas kernels for 19%

profile of v10, /device:TPU:0, one launch (start us, length us, event | category | flops | bytes accessed | tf_op | source)
XLA Modules:
  0.0 45.0 jit_solution(6451983591984677156)
XLA Ops:
  0.6 0.9 %copy-done.4 = bf16[1,4,8,8,384]{4,3,2,1,0:T(8,128)(2,1)S(1)} copy-done((bf16[1,4,8,8,384]{4,3,2,1,0:T(8,128)(2,1)S(1)}, bf16[1,4,8,8,384]{4,3,2,1,0:T(8,128)(2,1)}, u32[]{:S(2)}) %copy-start.4) | copy-done | bytes 196632
  1.6 0.0 copy-start.6
  1.6 0.1 shard_map.138
  1.7 0.0 copy-start.1
  1.7 0.0 copy-start.10
  1.7 0.6 %collective-permute-start = (bf16[4,3,8,384]{3,2,1,0:T(8,128)(2,1)S(1)}, bf16[4,3,8,384]{3,2,1,0:T(8,128)(2,1)S(1)}, u32[]{:S(2)}, u32[]{:S(2)}) collective-permute-start(bf16[4,3,8,384]{3,2,1,0:T(8,128)(2,1)S(1)} %get-tuple-element.48), channel_id=1, source_target_pairs={{0,1},{1,0},{2,3},{3,2},{4,5},{5,4},{6,7},{7,6},{8,9},{9,8},{10,11... | collective-permute-start | bytes 221192 | tf_op jit(solution)/shard_map/ppermute | solution.py:47
  2.3 2.6 %collective-permute-start.1 = (bf16[4,3,8,384]{3,2,1,0:T(8,128)(2,1)S(1)}, bf16[4,3,8,384]{3,2,1,0:T(8,128)(2,1)S(1)}, u32[]{:S(2)}, u32[]{:S(2)}) collective-permute-start(bf16[4,3,8,384]{3,2,1,0:T(8,128)(2,1)S(1)} %get-tuple-element.49), channel_id=1, source_target_pairs={{0,16},{1,2},{2,1},{3,4},{4,3},{5,6},{6,5},{7,8},{8,7},{9,10},{10,... | collective-permute-start | bytes 221192 | tf_op jit(solution)/shard_map/ppermute | solution.py:60
  5.6 2.0 %shard_map.139 = (f32[3,4,8,24,128]{4,3,2,1,0:T(8,128)S(1)}, f32[256,384]{1,0:T(8,128)S(1)}, bf16[256,512]{1,0:T(8,128)(2,1)S(1)}, f32[256,1536]{1,0:T(8,128)S(1)}, f32[1,384]{1,0:T(1,128)S(1)}) custom-call(s32[4,8]{1,0:T(4,128)S(1)} %bitcast.9, s32[1,1]{1,0:T(1,128)S(6)} %copy.15.counts_ref, f32[1,4]{1,0:T(1,128)S(1)} %copy-done.9, f32[1,384]{1,0:T(1,128)S(1)} %copy-done.8, ...), custom_call_target="tpu_custom_call" | custom-call | flops 301989888 | bytes 5060756 | tf_op jit(solution)/shard_map/pallas_call | solution.py:30
  7.6 0.0 collective-permute-done.core_ref
  7.6 0.0 collective-permute-done.1.cross_ref
  7.6 2.3 %shard_map.140 = (f32[3,4,6,24,128]{4,3,2,1,0:T(8,128)S(1)}, f32[256,384]{1,0:T(8,128)S(1)}, f32[256,1]{1,0:T(8,128)S(1)}, f32[256,1536]{1,0:T(8,128)S(1)}, f32[...) custom-call(s32[4,8]{1,0:T(4,128)S(1)} %bitcast.10, ...), custom_call_target="tpu_custom_call" | custom-call | flops 603979776 | bytes 9040004 | tf_op jit(solution)/shard_map/pallas_call | solution.py:30
  9.9 0.2 collective-permute-start.2
  10.1 1.9 %collective-permute-done.2.refs_1_ = bf16[768,384]{1,0:T(8,128)(2,1)S(1)} collective-permute-done((bf16[768,384]{1,0:T(8,128)(2,1)S(1)}, bf16[768,384]{1,0:T(8,128)(2,1)S(1)}, u32[]{:S(2)}, u32[]{:S(2)}) %collective-permute-start.2) | collective-permute-done | bytes 589856 | tf_op jit(solution)/shard_map/ppermute | solution.py:47
  12.0 0.3 shard_map.141
  12.2 2.0 %collective-permute-start.3 = (bf16[192,384]{1,0:T(8,128)(2,1)S(1)}, bf16[192,384]{1,0:T(8,128)(2,1)S(1)}, u32[]{:S(2)}, u32[]{:S(2)}) collective-permute-start(bf16[192,384]{1,0:T(8,128)(2,1)S(1)} %get-tuple-element.55), channel_id=1, source_target_pairs={{0,2},{1,3},{2,0},{3,1},{4,6},{5,7},{6,4},{7,5},{8,10},{9,11},{10,... | collective-permute-start | bytes 442376 | tf_op jit(solution)/shard_map/ppermute | solution.py:47
  14.2 1.6 %collective-permute-start.5 = (bf16[192,384]{1,0:T(8,128)(2,1)S(1)}, bf16[192,384]{1,0:T(8,128)(2,1)S(1)}, u32[]{:S(2)}, u32[]{:S(2)}) collective-permute-start(bf16[192,384]{1,0:T(8,128)(2,1)S(1)} %get-tuple-element.59), channel_id=1, source_target_pairs={{0,4},{1,5},{2,6},{3,7},{4,0},{5,1},{6,2},{7,3},{8,12},{9,13},{10,... | collective-permute-start | bytes 442376 | tf_op jit(solution)/shard_map/ppermute | solution.py:47
  15.8 2.8 %collective-permute-done.3.refs_1_ = bf16[192,384]{1,0:T(8,128)(2,1)S(1)} collective-permute-done((bf16[192,384]{1,0:T(8,128)(2,1)S(1)}, bf16[192,384]{1,0:T(8,128)(2,1)S(1)}, u32[]{:S(2)}, u32[]{:S(2)}) %collective-permute-start.3) | collective-permute-done | bytes 147488 | tf_op jit(solution)/shard_map/ppermute | solution.py:47
  18.6 0.1 shard_map.142
  18.7 1.8 %collective-permute-start.4 = (bf16[96,384]{1,0:T(8,128)(2,1)S(1)}, bf16[96,384]{1,0:T(8,128)(2,1)S(1)}, u32[]{:S(2)}, u32[]{:S(2)}) collective-permute-start(bf16[96,384]{1,0:T(8,128)(2,1)S(1)} %get-tuple-element.57), channel_id=1, source_target_pairs={{0,4},{1,5},{2,6},{3,7},{4,0},{5,1},{6,2},{7,3},{8,12},{9,13},{10,... | collective-permute-start | bytes 221192 | tf_op jit(solution)/shard_map/ppermute | solution.py:47
  20.4 0.0 collective-permute-done.5.refs_1_
  20.4 0.1 shard_map.143
  20.5 1.7 %collective-permute-start.6 = (bf16[96,384]{1,0:T(8,128)(2,1)S(1)}, bf16[96,384]{1,0:T(8,128)(2,1)S(1)}, u32[]{:S(2)}, u32[]{:S(2)}) collective-permute-start(bf16[96,384]{1,0:T(8,128)(2,1)S(1)} %get-tuple-element.61), channel_id=1, source_target_pairs={{0,2},{1,3},{2,0},{3,1},{4,6},{5,7},{6,4},{7,5},{8,10},{9,11},{10,... | collective-permute-start | bytes 221192 | tf_op jit(solution)/shard_map/ppermute | solution.py:47
  22.2 1.5 %shard_map.146 = (f32[256,384]{1,0:T(8,128)S(1)}, bf16[4,3,8,384]{3,2,1,0:T(8,128)(2,1)S(1)}, bf16[4,3,8,384]{3,2,1,0:T(8,128)(2,1)S(1)}, f32[1,384]{1,0:T(1,128)S(1)}) custom-call(s32[1,1]{1,0:T(1,128)} %bitcast.place_ref, s32[1,1]{1,0:T(1,128)S(6)} %copy.15.counts_ref, f32[1,4]{1,0:T(1,128)S(1)} %copy-done.9, f32[256,1536]{1,0:T(8,128)S(1)} %get-tuple-element.68.pre_ref, ...), custom_call_target="tpu_custom_call" | custom-call | flops 301989888 | bytes 8805400 | tf_op jit(solution)/shard_map/pallas_call | solution.py:30
  23.7 1.4 %shard_map.147 = (f32[56,384]{1,0:T(8,128)S(1)}, bf16[56,384]{1,0:T(8,128)(2,1)S(1)}) custom-call(f32[3,4,8,24,128]{4,3,2,1,0:T(8,128)S(1)} %get-tuple-element.66.pad_ref, f32[3,4,6,24,128]{4,3,2,1,0:T(8,128)S(1)} %get-tuple-element.67.edge_ref, f32[256,384]{1,0:T(8,128)S(1)} %get-tuple-element.75.grad_ref, f32[1,384]{1,0:T(1,128)S(1)} %get-tuple-element.76.emb_ref), custom_call_target="tpu_custom_call" | custom-call | bytes 2588160 | tf_op jit(solution)/shard_map/pallas_call | solution.py:30
  25.1 0.1 collective-permute-start.9
  25.2 1.2 %collective-permute-done.9.got_ref = bf16[56,384]{1,0:T(8,128)(2,1)S(1)} collective-permute-done((bf16[56,384]{1,0:T(8,128)(2,1)S(1)}, bf16[56,384]{1,0:T(8,128)(2,1)S(1)}, u32[]{:S(2)}, u32[]{:S(2)}) %collective-permute-start.9) | collective-permute-done | bytes 43040 | tf_op jit(solution)/shard_map/ppermute | solution.py:47
  26.4 1.6 %collective-permute-start.10 = (bf16[56,384]{1,0:T(8,128)(2,1)S(1)}, bf16[56,384]{1,0:T(8,128)(2,1)S(1)}, u32[]{:S(2)}, u32[]{:S(2)}) collective-permute-start(bf16[56,384]{1,0:T(8,128)(2,1)S(1)} %get-tuple-element.80), channel_id=1, source_target_pairs={{0,16},{16,0},{1,17},{17,1},{2,18},{18,2},{3,19},{19,3},{4,20},{20... | collective-permute-start | bytes 129032 | tf_op jit(solution)/shard_map/ppermute | solution.py:47
  28.0 0.0 collective-permute-done.4.refs_1_
  28.0 0.0 collective-permute-done.6.refs_3_
  28.0 0.1 shard_map.144
  28.0 1.5 %collective-permute-start.7 = (bf16[96,384]{1,0:T(8,128)(2,1)S(1)}, bf16[96,384]{1,0:T(8,128)(2,1)S(1)}, u32[]{:S(2)}, u32[]{:S(2)}) collective-permute-start(bf16[96,384]{1,0:T(8,128)(2,1)S(1)} %get-tuple-element.63), channel_id=1, source_target_pairs={{0,8},{1,9},{2,10},{3,11},{4,12},{5,13},{6,14},{7,15},{8,0},{9,1},... | collective-permute-start | bytes 221192 | tf_op jit(solution)/shard_map/ppermute | solution.py:47
  29.5 1.0 %collective-permute-done.10.got_ref = bf16[56,384]{1,0:T(8,128)(2,1)S(1)} collective-permute-done((bf16[56,384]{1,0:T(8,128)(2,1)S(1)}, bf16[56,384]{1,0:T(8,128)(2,1)S(1)}, u32[]{:S(2)}, u32[]{:S(2)}) %collective-permute-start.10) | collective-permute-done | bytes 43040 | tf_op jit(solution)/shard_map/ppermute | solution.py:47
  30.5 0.7 %collective-permute-start.11 = (bf16[56,384]{1,0:T(8,128)(2,1)S(1)}, bf16[56,384]{1,0:T(8,128)(2,1)S(1)}, u32[]{:S(2)}, u32[]{:S(2)}) collective-permute-start(bf16[56,384]{1,0:T(8,128)(2,1)S(1)} %get-tuple-element.82), channel_id=1, source_target_pairs={{0,2},{1,3},{2,0},{3,1},{4,6},{5,7},{6,4},{7,5},{8,10},{9,11},{10,... | collective-permute-start | bytes 129032 | tf_op jit(solution)/shard_map/ppermute | solution.py:47
  31.2 3.4 %collective-permute-done.11.got_ref = bf16[56,384]{1,0:T(8,128)(2,1)S(1)} collective-permute-done((bf16[56,384]{1,0:T(8,128)(2,1)S(1)}, bf16[56,384]{1,0:T(8,128)(2,1)S(1)}, u32[]{:S(2)}, u32[]{:S(2)}) %collective-permute-start.11) | collective-permute-done | bytes 43040 | tf_op jit(solution)/shard_map/ppermute | solution.py:47
  34.7 0.7 %collective-permute-start.12 = (bf16[56,384]{1,0:T(8,128)(2,1)S(1)}, bf16[56,384]{1,0:T(8,128)(2,1)S(1)}, u32[]{:S(2)}, u32[]{:S(2)}) collective-permute-start(bf16[56,384]{1,0:T(8,128)(2,1)S(1)} %get-tuple-element.84), channel_id=1, source_target_pairs={{0,4},{1,5},{2,6},{3,7},{4,0},{5,1},{6,2},{7,3},{8,12},{9,13},{10,... | collective-permute-start | bytes 129032 | tf_op jit(solution)/shard_map/ppermute | solution.py:47
  35.4 0.0 collective-permute-start.14
  35.4 1.3 %collective-permute-start.15 = (bf16[4,3,8,384]{3,2,1,0:T(8,128)(2,1)S(1)}, bf16[4,3,8,384]{3,2,1,0:T(8,128)(2,1)S(1)}, u32[]{:S(2)}, u32[]{:S(2)}) collective-permute-start(bf16[4,3,8,384]{3,2,1,0:T(8,128)(2,1)S(1)} %get-tuple-element.89), channel_id=1, source_target_pairs={{0,16},{1,2},{2,1},{3,4},{4,3},{5,6},{6,5},{7,8},{8,7},{9,10},{10,... | collective-permute-start | bytes 221192 | tf_op jit(solution)/shard_map/ppermute | solution.py:60
  36.7 0.0 collective-permute-done.7.refs_1_
  36.7 0.8 %collective-permute-start.8 = (bf16[96,384]{1,0:T(8,128)(2,1)S(1)}, bf16[96,384]{1,0:T(8,128)(2,1)S(1)}, u32[]{:S(2)}, u32[]{:S(2)}) collective-permute-start(bf16[96,384]{1,0:T(8,128)(2,1)S(1)} %get-tuple-element.65), channel_id=1, source_target_pairs={{0,16},{16,0},{1,17},{17,1},{2,18},{18,2},{3,19},{19,3},{4,20},{20... | collective-permute-start | bytes 221192 | tf_op jit(solution)/shard_map/ppermute | solution.py:47
  37.5 1.3 %collective-permute-done.12.got_ref = bf16[56,384]{1,0:T(8,128)(2,1)S(1)} collective-permute-done((bf16[56,384]{1,0:T(8,128)(2,1)S(1)}, bf16[56,384]{1,0:T(8,128)(2,1)S(1)}, u32[]{:S(2)}, u32[]{:S(2)}) %collective-permute-start.12) | collective-permute-done | bytes 43040 | tf_op jit(solution)/shard_map/ppermute | solution.py:47
  38.8 2.0 %collective-permute-start.13 = (bf16[56,384]{1,0:T(8,128)(2,1)S(1)}, bf16[56,384]{1,0:T(8,128)(2,1)S(1)}, u32[]{:S(2)}, u32[]{:S(2)}) collective-permute-start(bf16[56,384]{1,0:T(8,128)(2,1)S(1)} %get-tuple-element.86), channel_id=1, source_target_pairs={{0,8},{1,9},{2,10},{3,11},{4,12},{5,13},{6,14},{7,15},{8,0},{9,1},... | collective-permute-start | bytes 129032 | tf_op jit(solution)/shard_map/ppermute | solution.py:47
  40.8 1.6 %shard_map.153.part_ref = f32[256,384]{1,0:T(8,128)S(1)} custom-call(s32[4,8]{1,0:T(4,128)S(1)} %bitcast.11, f32[256,384]{1,0:T(8,128)S(1)} %get-tuple-element.75.grad_ref, f32[7,7,384]{2,1,0:T(8,128)S(1)} %copy-done.3), custom_call_target="tpu_custom_call" | custom-call | bytes 861824 | tf_op jit(solution)/shard_map/pallas_call | solution.py:30
  42.5 0.0 collective-permute-done.14.core_ref
  42.5 0.0 collective-permute-done.15.cross_ref
  42.5 1.7 %shard_map.154 = bf16[256,384]{1,0:T(8,128)(2,1)} custom-call(s32[4,8]{1,0:T(4,128)S(1)} %bitcast.12, s32[1,1]{1,0:T(1,128)} %bitcast.place_ref, s32[1,1]{1,0:T(1,128)S(6)} %copy.15.counts_ref, f32[1,4]{1,0:T(1,128)S(1)} %copy-done.9, f32[256,384]{1,0:T(8,128)S(1)} %shard_map.153.part_ref, bf16[4,3,8,384]{3,2,1,0:T(8,128)(2,1)S(1)} %collective-permute-done.14.core_ref, ...), custom_call_target="tpu_custom_call" | custom-call | bytes 1010840 | tf_op jit(solution)/shard_map/pallas_call | solution.py:30
  44.2 0.0 collective-permute-done.13.new_ref
  44.2 0.0 collective-permute-done.8.got_ref
  44.2 0.7 %shard_map.152 = (f32[96,384]{1,0:T(8,128)}, f32[7,7,384]{2,1,0:T(8,128)}, f32[1,384]{1,0:T(1,128)}) custom-call(f32[96,384]{1,0:T(8,128)S(1)} %get-tuple-element.64.keep_ref, bf16[96,384]{1,0:T(8,128)(2,1)S(1)} %collective-permute-done.8.got_ref, f32[56,384]{1,0:T(8,128)S(1)} %get-tuple-element.85.state_ref, bf16[56,384]{1,0:T(8,128)(2,1)S(1)} %collective-permute-done.13.new_ref), custom_call_target="tpu_custom_call" | custom-call | bytes 574464 | tf_op jit(solution)/shard_map/pallas_call | solution.py:30
  (23 shorter events, 0.2 us)
Async XLA Ops:
  0.6 0.9 %copy-start.4 = (bf16[1,4,8,8,384]{4,3,2,1,0:T(8,128)(2,1)S(1)}, bf16[1,4,8,8,384]{4,3,2,1,0:T(8,128)(2,1)}, u32[]{:S(2)}) copy-start(bf16[1,4,8,8,384]{4,3,2,1,0:T(8,128)(2,1)} %param.11) | copy-start | bytes 589828
  1.6 3.9 %copy-start = (bf16[1536,384]{1,0:T(8,128)(2,1)S(1)}, bf16[1536,384]{1,0:T(8,128)(2,1)}, u32[]{:S(2)}) copy-start(bf16[1536,384]{1,0:T(8,128)(2,1)} %w_out_ref.3) | copy-start | bytes 3538948
  1.6 3.9 %copy-start.2 = (bf16[1,4,8,8,384]{4,3,2,1,0:T(8,128)(2,1)S(1)}, bf16[1,4,8,8,384]{4,3,2,1,0:T(8,128)(2,1)}, u32[]{:S(2)}) copy-start(bf16[1,4,8,8,384]{4,3,2,1,0:T(8,128)(2,1)} %param.12) | copy-start | bytes 589828
  1.6 3.9 %copy-start.3 = (f32[7,7,384]{2,1,0:T(8,128)S(1)}, f32[7,7,384]{2,1,0:T(8,128)}, u32[]{:S(2)}) copy-start(f32[7,7,384]{2,1,0:T(8,128)} %kern_ref.7) | copy-start | bytes 225796
  1.6 3.9 %copy-start.5 = (bf16[1,4,8,8,384]{4,3,2,1,0:T(8,128)(2,1)S(1)}, bf16[1,4,8,8,384]{4,3,2,1,0:T(8,128)(2,1)}, u32[]{:S(2)}) copy-start(bf16[1,4,8,8,384]{4,3,2,1,0:T(8,128)(2,1)} %param.11) | copy-start | bytes 589828
  1.6 3.9 %copy-start.6 = (s32[1,4,8]{2,1,0:T(4,128)S(1)}, s32[1,4,8]{2,1,0:T(4,128)}, u32[]{:S(2)}) copy-start(s32[1,4,8]{2,1,0:T(4,128)} %param.15) | copy-start | bytes 388
  1.6 3.9 %copy-start.7 = (f32[384]{0:T(512)S(1)}, f32[384]{0:T(512)}, u32[]{:S(2)}) copy-start(f32[384]{0:T(512)} %scale_ref.3) | copy-start | bytes 4612
  1.6 3.9 %copy-start.8 = (f32[1,384]{1,0:T(1,128)S(1)}, f32[1,384]{1,0:T(1,128)}, u32[]{:S(2)}) copy-start(f32[1,384]{1,0:T(1,128)} %cot_ref.3) | copy-start | bytes 4612
  1.6 3.9 %copy-start.9 = (f32[1,4]{1,0:T(1,128)S(1)}, f32[1,4]{1,0:T(1,128)}, u32[]{:S(2)}) copy-start(f32[1,4]{1,0:T(1,128)} %pool_ref.5) | copy-start | bytes 52
  1.7 5.9 %copy-start.1 = (bf16[384,1536]{1,0:T(8,128)(2,1)S(1)}, bf16[384,1536]{1,0:T(8,128)(2,1)}, u32[]{:S(2)}) copy-start(bf16[384,1536]{1,0:T(8,128)(2,1)} %w_in_ref.3) | copy-start | bytes 3538948
  1.7 5.9 %copy-start.10 = (f32[384]{0:T(512)S(1)}, f32[384]{0:T(512)}, u32[]{:S(2)}) copy-start(f32[384]{0:T(512)} %gain_ref.3) | copy-start | bytes 4612
  1.7 5.9 %collective-permute-start = (bf16[4,3,8,384]{3,2,1,0:T(8,128)(2,1)S(1)}, bf16[4,3,8,384]{3,2,1,0:T(8,128)(2,1)S(1)}, u32[]{:S(2)}, u32[]{:S(2)}) collective-permute-start(bf16[4,3,8,384]{3,2,1,0:T(8,128)(2,1)S(1)} %get-tuple-element.48), channel_id=1, source_target_pairs={{0,1},{1,0},{2,3},{3,2},{4,5},{5,4},{6,7},{7,6},{8,9},{9,8},{10,11... | collective-permute-start | bytes 221192 | tf_op jit(solution)/shard_map/ppermute | solution.py:47
  2.3 5.4 %collective-permute-start.1 = (bf16[4,3,8,384]{3,2,1,0:T(8,128)(2,1)S(1)}, bf16[4,3,8,384]{3,2,1,0:T(8,128)(2,1)S(1)}, u32[]{:S(2)}, u32[]{:S(2)}) collective-permute-start(bf16[4,3,8,384]{3,2,1,0:T(8,128)(2,1)S(1)} %get-tuple-element.49), channel_id=1, source_target_pairs={{0,16},{1,2},{2,1},{3,4},{4,3},{5,6},{6,5},{7,8},{8,7},{9,10},{10,... | collective-permute-start | bytes 221192 | tf_op jit(solution)/shard_map/ppermute | solution.py:60
  9.9 2.1 %collective-permute-start.2 = (bf16[768,384]{1,0:T(8,128)(2,1)S(1)}, bf16[768,384]{1,0:T(8,128)(2,1)S(1)}, u32[]{:S(2)}, u32[]{:S(2)}) collective-permute-start(bf16[768,384]{1,0:T(8,128)(2,1)S(1)} %get-tuple-element.53), channel_id=1, source_target_pairs={{0,1},{1,0},{2,3},{3,2},{4,5},{5,4},{6,7},{7,6},{8,9},{9,8},{10,11... | collective-permute-start | bytes 1769480 | tf_op jit(solution)/shard_map/ppermute | solution.py:47
  12.2 6.4 %collective-permute-start.3 = (bf16[192,384]{1,0:T(8,128)(2,1)S(1)}, bf16[192,384]{1,0:T(8,128)(2,1)S(1)}, u32[]{:S(2)}, u32[]{:S(2)}) collective-permute-start(bf16[192,384]{1,0:T(8,128)(2,1)S(1)} %get-tuple-element.55), channel_id=1, source_target_pairs={{0,2},{1,3},{2,0},{3,1},{4,6},{5,7},{6,4},{7,5},{8,10},{9,11},{10,... | collective-permute-start | bytes 442376 | tf_op jit(solution)/shard_map/ppermute | solution.py:47
  14.2 6.2 %collective-permute-start.5 = (bf16[192,384]{1,0:T(8,128)(2,1)S(1)}, bf16[192,384]{1,0:T(8,128)(2,1)S(1)}, u32[]{:S(2)}, u32[]{:S(2)}) collective-permute-start(bf16[192,384]{1,0:T(8,128)(2,1)S(1)} %get-tuple-element.59), channel_id=1, source_target_pairs={{0,4},{1,5},{2,6},{3,7},{4,0},{5,1},{6,2},{7,3},{8,12},{9,13},{10,... | collective-permute-start | bytes 442376 | tf_op jit(solution)/shard_map/ppermute | solution.py:47
  18.7 9.3 %collective-permute-start.4 = (bf16[96,384]{1,0:T(8,128)(2,1)S(1)}, bf16[96,384]{1,0:T(8,128)(2,1)S(1)}, u32[]{:S(2)}, u32[]{:S(2)}) collective-permute-start(bf16[96,384]{1,0:T(8,128)(2,1)S(1)} %get-tuple-element.57), channel_id=1, source_target_pairs={{0,4},{1,5},{2,6},{3,7},{4,0},{5,1},{6,2},{7,3},{8,12},{9,13},{10,... | collective-permute-start | bytes 221192 | tf_op jit(solution)/shard_map/ppermute | solution.py:47
  20.5 7.5 %collective-permute-start.6 = (bf16[96,384]{1,0:T(8,128)(2,1)S(1)}, bf16[96,384]{1,0:T(8,128)(2,1)S(1)}, u32[]{:S(2)}, u32[]{:S(2)}) collective-permute-start(bf16[96,384]{1,0:T(8,128)(2,1)S(1)} %get-tuple-element.61), channel_id=1, source_target_pairs={{0,2},{1,3},{2,0},{3,1},{4,6},{5,7},{6,4},{7,5},{8,10},{9,11},{10,... | collective-permute-start | bytes 221192 | tf_op jit(solution)/shard_map/ppermute | solution.py:47
  25.1 1.3 %collective-permute-start.9 = (bf16[56,384]{1,0:T(8,128)(2,1)S(1)}, bf16[56,384]{1,0:T(8,128)(2,1)S(1)}, u32[]{:S(2)}, u32[]{:S(2)}) collective-permute-start(bf16[56,384]{1,0:T(8,128)(2,1)S(1)} %get-tuple-element.78), channel_id=1, source_target_pairs={{0,1},{1,0},{2,3},{3,2},{4,5},{5,4},{6,7},{7,6},{8,9},{9,8},{10,11... | collective-permute-start | bytes 129032 | tf_op jit(solution)/shard_map/ppermute | solution.py:47
  26.4 4.1 %collective-permute-start.10 = (bf16[56,384]{1,0:T(8,128)(2,1)S(1)}, bf16[56,384]{1,0:T(8,128)(2,1)S(1)}, u32[]{:S(2)}, u32[]{:S(2)}) collective-permute-start(bf16[56,384]{1,0:T(8,128)(2,1)S(1)} %get-tuple-element.80), channel_id=1, source_target_pairs={{0,16},{16,0},{1,17},{17,1},{2,18},{18,2},{3,19},{19,3},{4,20},{20... | collective-permute-start | bytes 129032 | tf_op jit(solution)/shard_map/ppermute | solution.py:47
  28.0 8.6 %collective-permute-start.7 = (bf16[96,384]{1,0:T(8,128)(2,1)S(1)}, bf16[96,384]{1,0:T(8,128)(2,1)S(1)}, u32[]{:S(2)}, u32[]{:S(2)}) collective-permute-start(bf16[96,384]{1,0:T(8,128)(2,1)S(1)} %get-tuple-element.63), channel_id=1, source_target_pairs={{0,8},{1,9},{2,10},{3,11},{4,12},{5,13},{6,14},{7,15},{8,0},{9,1},... | collective-permute-start | bytes 221192 | tf_op jit(solution)/shard_map/ppermute | solution.py:47
  30.5 4.1 %collective-permute-start.11 = (bf16[56,384]{1,0:T(8,128)(2,1)S(1)}, bf16[56,384]{1,0:T(8,128)(2,1)S(1)}, u32[]{:S(2)}, u32[]{:S(2)}) collective-permute-start(bf16[56,384]{1,0:T(8,128)(2,1)S(1)} %get-tuple-element.82), channel_id=1, source_target_pairs={{0,2},{1,3},{2,0},{3,1},{4,6},{5,7},{6,4},{7,5},{8,10},{9,11},{10,... | collective-permute-start | bytes 129032 | tf_op jit(solution)/shard_map/ppermute | solution.py:47
  34.7 4.1 %collective-permute-start.12 = (bf16[56,384]{1,0:T(8,128)(2,1)S(1)}, bf16[56,384]{1,0:T(8,128)(2,1)S(1)}, u32[]{:S(2)}, u32[]{:S(2)}) collective-permute-start(bf16[56,384]{1,0:T(8,128)(2,1)S(1)} %get-tuple-element.84), channel_id=1, source_target_pairs={{0,4},{1,5},{2,6},{3,7},{4,0},{5,1},{6,2},{7,3},{8,12},{9,13},{10,... | collective-permute-start | bytes 129032 | tf_op jit(solution)/shard_map/ppermute | solution.py:47
  35.4 7.1 %collective-permute-start.14 = (bf16[4,3,8,384]{3,2,1,0:T(8,128)(2,1)S(1)}, bf16[4,3,8,384]{3,2,1,0:T(8,128)(2,1)S(1)}, u32[]{:S(2)}, u32[]{:S(2)}) collective-permute-start(bf16[4,3,8,384]{3,2,1,0:T(8,128)(2,1)S(1)} %get-tuple-element.88), channel_id=1, source_target_pairs={{0,1},{1,0},{2,3},{3,2},{4,5},{5,4},{6,7},{7,6},{8,9},{9,8},{10,11... | collective-permute-start | bytes 221192 | tf_op jit(solution)/shard_map/ppermute | solution.py:47
  35.4 7.1 %collective-permute-start.15 = (bf16[4,3,8,384]{3,2,1,0:T(8,128)(2,1)S(1)}, bf16[4,3,8,384]{3,2,1,0:T(8,128)(2,1)S(1)}, u32[]{:S(2)}, u32[]{:S(2)}) collective-permute-start(bf16[4,3,8,384]{3,2,1,0:T(8,128)(2,1)S(1)} %get-tuple-element.89), channel_id=1, source_target_pairs={{0,16},{1,2},{2,1},{3,4},{4,3},{5,6},{6,5},{7,8},{8,7},{9,10},{10,... | collective-permute-start | bytes 221192 | tf_op jit(solution)/shard_map/ppermute | solution.py:60
  36.7 7.5 %collective-permute-start.8 = (bf16[96,384]{1,0:T(8,128)(2,1)S(1)}, bf16[96,384]{1,0:T(8,128)(2,1)S(1)}, u32[]{:S(2)}, u32[]{:S(2)}) collective-permute-start(bf16[96,384]{1,0:T(8,128)(2,1)S(1)} %get-tuple-element.65), channel_id=1, source_target_pairs={{0,16},{16,0},{1,17},{17,1},{2,18},{18,2},{3,19},{19,3},{4,20},{20... | collective-permute-start | bytes 221192 | tf_op jit(solution)/shard_map/ppermute | solution.py:47
  38.8 5.4 %collective-permute-start.13 = (bf16[56,384]{1,0:T(8,128)(2,1)S(1)}, bf16[56,384]{1,0:T(8,128)(2,1)S(1)}, u32[]{:S(2)}, u32[]{:S(2)}) collective-permute-start(bf16[56,384]{1,0:T(8,128)(2,1)S(1)} %get-tuple-element.86), channel_id=1, source_target_pairs={{0,8},{1,9},{2,10},{3,11},{4,12},{5,13},{6,14},{7,15},{8,0},{9,1},... | collective-permute-start | bytes 129032 | tf_op jit(solution)/shard_map/ppermute | solution.py:47
